TPU v7x, 32 devices: a whole 2x2x4 slice. The times are simulated.
32 devices in a mesh: vel: 4 (over x, core), strip: 8 (over z, y).
Axes of the slice: x: 2, y: 2, z: 4, core: 2. Of those that a mesh axis runs over, the one named last changes fastest.
Arguments:
- dist: float32 [13824, 32, 128], P('vel', 'strip'), may hold values from -25 to 25
- cell_type: int32 [32, 128], P('strip'), may hold values 0 or 1
- collision_rate: float32 [32, 128], P('strip'), may hold values from 0.05 to 0.5
- vel_index: int32 [3, 13824], P(None, 'vel'), may hold values from 0 to 23, as said below
Outputs:
- dist_out: float32 [13824, 32, 128], P('vel', 'strip')
- state: float32 [5, 32, 128], P(None, 'strip')
Inputs may be any that keep to these rules, and one draw needn't show every extreme that they name: `vel_index`: each point of the 24 x 24 x 24 velocity grid is listed once. In every aligned block of 3456 velocities, the first half have x index at least 12 and the second half below it.
All inputs are finite; a program needn't handle non-finite values. No bound on the sum of `cell_type` on one device may be relied on, other than what follows from the above.
Results may differ from a plain program's by a relative error of at most 0.0003.
Values sent between devices are 32-bit elements; how exact they have to be, the bound alone decides.
No kernel may reach another device: no remote copies, remote signals or barrier semaphores. Data moves between devices by JAX's collectives and lax.ppermute only.
A program may use at most 128 MiB of HBM per device.

v0:
```python
import math

import jax
import jax.numpy as jnp
from jax import lax
from jax.sharding import PartitionSpec as P

GV = 24
ITERS = 2
SWEEPS = 3


STEP_RATIO = 0.1
SOURCE_WEIGHT = 0.5
HEAT_WEIGHT = 4.0 / 15.0
HIGH = lax.Precision.HIGHEST


def from_behind(shard, axis, by):
    count = lax.axis_size(axis)
    pairs = [(i, i + by) for i in range(count) if 0 <= i + by < count]
    return lax.ppermute(shard, axis, pairs)


def with_halo(cells, sides, width):
    for axis, dim in sides:
        count = lax.axis_size(axis)
        ends = count - 1
        head = lax.slice_in_dim(cells, 0, width, axis=dim)
        tail = lax.slice_in_dim(cells, cells.shape[dim] - width, cells.shape[dim], axis=dim)
        cells = jnp.concatenate(
            [
                lax.ppermute(tail, axis, [(i, (i + 1) % count) for i in range(ends)]),
                cells,
                lax.ppermute(head, axis, [((i + 1) % count, i) for i in range(ends)]),
            ],
            axis=dim,
        )
    return cells


def speeds(vel_index):
    return (vel_index.astype(jnp.float32) - (GV - 1) / 2.0) * (8.0 / GV)


def moment_table(comps):
    vel_x, vel_y, vel_z = (comps[0], comps[1], comps[2])
    energy = vel_x * vel_x + vel_y * vel_y + vel_z * vel_z
    volume = (8.0 / GV) ** 3
    weight = volume * math.pi ** (-1.5) * jnp.exp(-energy)
    rows = [
        jnp.ones_like(vel_x),
        vel_x,
        vel_y,
        vel_z,
        energy,
        vel_x * vel_x,
        vel_y * vel_y,
        vel_x * vel_y,
        vel_x * vel_z,
        vel_y * vel_z,
        energy * vel_x,
        energy * vel_y,
        energy * vel_z,
    ]
    return jnp.stack(rows) * weight


def state_table(comps):
    vel_x, vel_y, vel_z = (comps[0], comps[1], comps[2])
    energy = vel_x * vel_x + vel_y * vel_y + vel_z * vel_z
    shape_heat = HEAT_WEIGHT * (energy - 2.5)
    columns = [
        jnp.ones_like(vel_x),
        2.0 * vel_x,
        2.0 * vel_y,
        2.0 * vel_z,
        energy - 1.5,
        shape_heat * vel_x,
        shape_heat * vel_y,
        shape_heat * vel_z,
    ]
    return jnp.stack(columns, axis=1)


def macro_parts(moments):
    third = moments[4] * (2.0 / 3.0)
    start = jnp.stack([moments[0], moments[1], moments[2], moments[3], third - moments[0]])
    heat = jnp.stack(
        [
            moments[10] - 2.5 * moments[1],
            moments[11] - 2.5 * moments[2],
            moments[12] - 2.5 * moments[3],
        ]
    )
    flux_fields = jnp.stack(
        [
            moments[1],
            moments[2],
            2.0 * moments[5] - third,
            2.0 * moments[7],
            2.0 * moments[6] - third,
            2.0 * moments[8],
            2.0 * moments[9],
            heat[0],
            heat[1],
        ]
    )
    return (start, flux_fields, heat)


def source_terms(start, framed):
    diff_x = 0.5 * (framed[:, 2:, 1:-1] - framed[:, :-2, 1:-1])
    diff_y = 0.5 * (framed[:, 1:-1, 2:] - framed[:, 1:-1, :-2])
    spread = jnp.stack(
        [
            diff_x[0] + diff_y[1],
            diff_x[2] + diff_y[3],
            diff_x[3] + diff_y[4],
            diff_x[5] + diff_y[6],
            diff_x[7] + diff_y[8],
        ]
    )
    return start - SOURCE_WEIGHT * spread


def neighbour_sum(framed):
    return framed[:, 2:, 1:-1] + framed[:, :-2, 1:-1] + framed[:, 1:-1, 2:] + framed[:, 1:-1, :-2]


def limiter(left, right):
    return jnp.where(
        left * right > 0, jnp.sign(left) * jnp.minimum(jnp.abs(left), jnp.abs(right)), 0.0
    )


def interface_diff(extended, speed, axis, count):

    def part(lower, upper):
        return lax.slice_in_dim(extended, lower, upper, axis=axis)

    left = part(1, count + 3) - part(0, count + 2)
    right = part(2, count + 4) - part(1, count + 3)
    slope = limiter(left, right)
    upwind = part(1, count + 2) + 0.5 * lax.slice_in_dim(slope, 0, count + 1, axis=axis)
    downwind = part(2, count + 3) - 0.5 * lax.slice_in_dim(slope, 1, count + 2, axis=axis)
    flux = speed * jnp.where(speed > 0, upwind, downwind)
    return lax.slice_in_dim(flux, 1, count + 1, axis=axis) - lax.slice_in_dim(
        flux, 0, count, axis=axis
    )


def relax(dist, extended, vel_x, vel_y, table, fields, wall, rate):
    count_x = dist.shape[1]
    count_y = dist.shape[2]
    wide = jnp.pad(dist, ((0, 0), (0, 0), (2, 2)))
    drift = interface_diff(extended, vel_x[:, None, None], 1, count_x)
    drift = drift + interface_diff(wide, vel_y[:, None, None], 2, count_y)
    target = jnp.dot(table, fields.reshape(8, -1), precision=HIGH).reshape(dist.shape)
    moved = dist - STEP_RATIO * drift + rate * (target - dist)
    return jnp.where(wall, target, moved)


def extend_rows(dist):
    half_count = dist.shape[0] // 2
    forward = dist[:half_count]
    backward = dist[half_count:]
    from_left = from_behind((forward[:, -2:], backward[:, -1:]), "strip", 1)
    from_right = from_behind((backward[:, :2], forward[:, :1]), "strip", -1)
    blank = jnp.zeros((half_count, 1, dist.shape[2]), dist.dtype)
    upper_rows = jnp.concatenate(
        [from_left[0], jnp.concatenate([blank, from_left[1]], axis=1)], axis=0
    )
    lower_rows = jnp.concatenate(
        [jnp.concatenate([from_right[1], blank], axis=1), from_right[0]], axis=0
    )
    return jnp.concatenate([upper_rows, dist, lower_rows], axis=1)


def per_device(dist, cell_type, collision_rate, vel_index):
    comps = speeds(vel_index)
    weights = moment_table(comps)
    table = state_table(comps)
    wall = cell_type == 1
    kappa = 0.5 / collision_rate
    count_v, rows, cols = dist.shape

    def partial_sum(field):
        return jnp.dot(weights, field.reshape(count_v, rows * cols), precision=HIGH).reshape(
            13, rows, cols
        )

    start, flux_fields, heat = macro_parts(lax.psum(partial_sum(dist), "vel"))
    fields = jnp.concatenate([start, heat])
    state = start
    for iteration in range(ITERS):
        extended = extend_rows(dist)
        post = relax(dist, extended, comps[0], comps[1], table, fields, wall, collision_rate)
        partial_value = partial_sum(post)
        start, flux_fields, heat = macro_parts(lax.psum(partial_value, "vel"))
        framed = with_halo(flux_fields, (("strip", 1),), 1)
        source = source_terms(start, jnp.pad(framed, ((0, 0), (0, 0), (1, 1))))
        state = start
        for sweep in range(SWEEPS):
            framed = with_halo(state, (("strip", 1),), 1)
            framed = jnp.pad(framed, ((0, 0), (0, 0), (1, 1)))
            state = (source + kappa * neighbour_sum(framed)) / (1.0 + 4.0 * kappa)
        delta = state - start
        change = jnp.dot(table[:, :5], delta.reshape(5, rows * cols), precision=HIGH)
        dist = post + change.reshape(dist.shape)
        fields = jnp.concatenate([state, heat])
    return (dist, state)


def solution(mesh):
    in_specs = (P("vel", "strip", None), P("strip", None), P("strip", None), P(None, "vel"))
    out_specs = (P("vel", "strip", None), P(None, "strip", None))
    return jax.shard_map(
        per_device, mesh=mesh, in_specs=in_specs, out_specs=out_specs, check_vma=False
    )
```

profile of v0, /device:TPU:24, one launch (start us, length us, event | category | flops | bytes accessed | tf_op | source)
XLA Modules:
  0.0 523.4 jit_solution(12473169336976819734)
XLA Ops:
  0.6 3.5 copy.30
  4.1 2.1 fusion.126
  6.3 3.4 collective-permute-start
  9.7 3.3 collective-permute-start.3
  13.1 4.0 collective-permute-start.1
  17.1 3.0 collective-permute-start.2
  20.4 10.3 %multiply_select_fusion.1 = f32[3456,4,130]{2,0,1:T(8,128)} fusion(f32[3456,4,128]{2,0,1:T(8,128)S(1)} %copy.30), kind=kLoop, calls=%fused_computation.28 | loop fusion | flops 17971200 | bytes 14266368 | tf_op jit(solution)/shard_map/jit(_where)/select_n | solution.py:132
  30.8 3.7 copy.42
  34.5 8.0 %copy.21 = f32[512,3456]{1,0:T(8,128)} copy(f32[512,3456]{0,1:T(8,128)} %bitcast.105) | data formatting | bytes 14155776 | tf_op jit(solution)/shard_map/dot_general | solution.py:189
  42.8 7.9 %fusion.38 = f32[13,4,128]{2,0,1:T(8,128)S(1)} fusion(f32[4,128,3456]{2,1,0:T(8,128)} %bitcast.106, f32[13,3456]{1,0:T(8,128)S(1)} %stack.24, f32[3456]{0:T(1024)S(1)} %get-tuple-element.10), kind=kOutput, calls=%fused_computation.81 | convolution fusion | flops 276082560 | bytes 7298048 | tf_op jit(solution)/shard_map/dot_general | solution.py:189
  50.7 11.3 %psum.21 = f32[13,4,128]{2,0,1:T(8,128)S(1)} all-reduce(f32[13,4,128]{2,0,1:T(8,128)S(1)} %fusion.38), channel_id=1, replica_groups=mesh['vel'=4,'strip'=8] {'vel'}, use_global_device_ids=true, to_apply=%region_0.0 | all-reduce | flops 6656 | bytes 53248 | tf_op jit(solution)/shard_map/psum | solution.py:193
  62.6 20.0 %fusion.2 = f32[3456,4,129]{2,0,1:T(8,128)} fusion(f32[3456,4,128]{2,0,1:T(8,128)} %copy-done.1, f32[3456,4,130]{2,0,1:T(8,128)} %multiply_select_fusion.1, f32[3456]{0:T(1024)S(1)} %get-tuple-element.43, pred[3456]{0:T(1024)(128)(4,1)S(1)} %get-tuple-element.91), kind=kLoop, calls=%fused_computation.12 | loop fusion | flops 10699776 | bytes 28494720 | tf_op jit(solution)/shard_map/mul | solution.py:147
  82.8 0.6 concatenate.151
  83.4 0.8 stack.23
  84.7 0.6 multiply_add_fusion.1
  85.5 40.0 %collective-permute-done.2 = f32[1728,1,128]{2,0,1:T(8,128)} collective-permute-done((f32[1728,1,128]{2,0,1:T(8,128)S(1)}, f32[1728,1,128]{2,0,1:T(8,128)}, u32[]{:S(2)}, u32[]{:S(2)}) %collective-permute-start.2) | collective-permute-done | bytes 884768 | tf_op jit(solution)/shard_map/ppermute | solution.py:22
  125.5 1.3 concatenate.155
  126.8 21.2 %pad_maximum_fusion.6 = (f32[3456,6,128]{2,0,1:T(8,128)}, f32[3456,6,128]{2,0,1:T(8,128)}, f32[3456,6,128]{2,0,1:T(8,128)}) fusion(f32[3456,4,128]{2,0,1:T(8,128)} %copy-done.1, f32[1728,2,128]{2,0,1:T(8,128)S(1)} %concatenate.152, f32[1728,2,128]{2,0,1:T(8,128)} %collective-permute-done, f32[1728,2,128]{2,0,1:T(8,128)} %collective-permute-done.3, ...), kind=kLoop, calls=%fused_computation.38 | loop fusion | flops 47775744 | bytes 46006272 | tf_op jit(solution)/shard_map/concatenate | solution.py:177
  148.1 16.1 %fusion.20 = f32[3456,5,128]{2,0,1:T(8,128)} fusion(f32[3456,6,128]{2,0,1:T(8,128)} %get-tuple-element.18, f32[3456,6,128]{2,0,1:T(8,128)} %get-tuple-element.19, f32[3456,6,128]{2,0,1:T(8,128)} %get-tuple-element.17, f32[3456]{0:T(1024)} %copy-done.9, pred[3456]{0:T(1024)(128)(4,1)} %get-tuple-element.92), kind=kLoop, calls=%fused_computation.55 | loop fusion | flops 13271040 | bytes 44254080 | tf_op jit(solution)/shard_map/mul | solution.py:147
  164.2 19.3 %fusion.31 = f32[3456,4,128]{2,0,1:T(8,128)} fusion(f32[3456,4,129]{2,0,1:T(8,128)} %fusion.2, f32[3456,5,128]{2,0,1:T(8,128)} %fusion.20, f32[4,128]{1,0:T(4,128)S(1)} %copy-done.37, pred[4,128]{1,0:T(4,128)(4,1)S(1)} %copy-done.40, f32[3456,8]{0,1:T(8,128)S(1)} %copy-done.7, f32[8,512]{1,0:T(8,128)S(1)} %copy-done.28, f32[3456,4,128]{2,1,0:T(4,128)} %param.4), kind=kOutput, calls=%fused_computation.71 | convolution fusion | flops 185794560 | bytes 42596864 | tf_op jit(solution)/shard_map/dot_general | solution.py:159
  183.5 8.2 %copy.32 = f32[3456,4,128]{0,2,1:T(8,128)} copy(f32[3456,4,128]{2,0,1:T(8,128)} %fusion.31) | data formatting | bytes 14155776 | tf_op jit(solution)/shard_map/jit(_where)/select_n | solution.py:161
  191.7 7.9 %fusion.34 = f32[13,4,128]{2,0,1:T(8,128)S(1)} fusion(f32[3456,4,128]{0,2,1:T(8,128)} %copy.32, f32[13,3456]{1,0:T(8,128)S(1)} %copy-done.3, f32[3456]{0:T(1024)S(1)} %get-tuple-element.10), kind=kOutput, calls=%fused_computation.75 | convolution fusion | flops 276082560 | bytes 7298048 | tf_op jit(solution)/shard_map/dot_general | solution.py:189
  199.6 11.4 %psum.22 = f32[13,4,128]{2,0,1:T(8,128)S(1)} all-reduce(f32[13,4,128]{2,0,1:T(8,128)S(1)} %fusion.34), channel_id=1, replica_groups=mesh['vel'=4,'strip'=8] {'vel'}, use_global_device_ids=true, to_apply=%region_1.2 | all-reduce | flops 6656 | bytes 53248 | tf_op jit(solution)/shard_map/psum | solution.py:200
  211.6 1.9 collective-permute-start.6
  213.5 3.9 collective-permute-start.7
  217.5 2.8 collective-permute-start.4
  220.3 3.0 collective-permute-start.5
  223.5 3.3 collective-permute-done.5
  227.1 2.0 collective-permute-start.8
  229.1 3.8 collective-permute-start.9
  233.0 2.6 collective-permute-done.9
  235.7 2.8 collective-permute-start.10
  238.5 3.0 collective-permute-start.11
  241.8 3.2 collective-permute-done.11
  245.1 8.2 %convolution_add_fusion.1 = f32[3456,4,128]{2,0,1:T(8,128)S(1)} fusion(f32[3456,4,128]{2,0,1:T(8,128)} %fusion.31, f32[3456,5]{0,1:T(8,128)S(1)} %stack.28, f32[5,4,128]{2,0,1:T(8,128)S(1)} %fusion.80, f32[1,4,128]{2,0,1:T(1,128)S(1)} %get-tuple-element.71, f32[4,4,128]{2,0,1:T(4,128)S(1)} %slice.705), kind=kOutput, calls=%fused_computation.78 | convolution fusion | flops 107942912 | bytes 14245376 | tf_op jit(solution)/shard_map/dot_general | solution.py:209
  253.3 1.6 fusion.124
  255.0 8.6 %multiply_select_fusion = f32[3456,4,130]{2,0,1:T(8,128)S(1)} fusion(f32[3456,4,128]{2,0,1:T(8,128)S(1)} %convolution_add_fusion.1), kind=kLoop, calls=%fused_computation.26 | loop fusion | flops 17971200 | bytes 14266368 | tf_op jit(solution)/shard_map/jit(_where)/select_n | solution.py:132
  263.7 2.1 collective-permute-start.12
  265.8 4.6 collective-permute-start.15
  270.5 2.4 collective-permute-start.13
  272.9 4.3 collective-permute-start.14
  277.2 10.4 %fusion.8 = f32[3456,4,129]{2,0,1:T(8,128)} fusion(f32[3456,4,128]{2,0,1:T(8,128)S(1)} %convolution_add_fusion.1, f32[3456,4,130]{2,0,1:T(8,128)S(1)} %multiply_select_fusion, f32[3456]{0:T(1024)S(1)} %copy-done.11, pred[3456]{0:T(1024)(128)(4,1)S(1)} %copy-done.31), kind=kLoop, calls=%fused_computation.18 | loop fusion | flops 10699776 | bytes 28494720 | tf_op jit(solution)/shard_map/mul | solution.py:147
  287.6 33.3 %collective-permute-done.13 = f32[1728,1,128]{2,0,1:T(8,128)S(1)} collective-permute-done((f32[1728,1,128]{2,0,1:T(8,128)S(1)}, f32[1728,1,128]{2,0,1:T(8,128)S(1)}, u32[]{:S(2)}, u32[]{:S(2)}) %collective-permute-start.13) | collective-permute-done | bytes 884768 | tf_op jit(solution)/shard_map/ppermute | solution.py:22
  321.1 56.8 %collective-permute-done.14 = f32[1728,1,128]{2,0,1:T(8,128)} collective-permute-done((f32[1728,1,128]{2,0,1:T(8,128)S(1)}, f32[1728,1,128]{2,0,1:T(8,128)}, u32[]{:S(2)}, u32[]{:S(2)}) %collective-permute-start.14) | collective-permute-done | bytes 884768 | tf_op jit(solution)/shard_map/ppermute | solution.py:22
  377.8 1.3 concatenate.179
  379.1 21.2 %pad_maximum_fusion.7 = (f32[3456,6,128]{2,0,1:T(8,128)}, f32[3456,6,128]{2,0,1:T(8,128)}, f32[3456,6,128]{2,0,1:T(8,128)}) fusion(f32[3456,4,128]{2,0,1:T(8,128)} %copy-done, f32[1728,2,128]{2,0,1:T(8,128)S(1)} %concatenate.176, f32[1728,2,128]{2,0,1:T(8,128)} %collective-permute-done.12, f32[1728,2,128]{2,0,1:T(8,128)} %collective-permute-done.15, ...), kind=kLoop, calls=%fused_computation.40 | loop fusion | flops 47775744 | bytes 46006272 | tf_op jit(solution)/shard_map/concatenate | solution.py:177
  400.4 16.1 %fusion.16 = f32[3456,5,128]{2,0,1:T(8,128)} fusion(f32[3456,6,128]{2,0,1:T(8,128)} %get-tuple-element.15, f32[3456,6,128]{2,0,1:T(8,128)} %get-tuple-element.16, f32[3456,6,128]{2,0,1:T(8,128)} %get-tuple-element.14, f32[3456]{0:T(1024)} %copy-done.9, pred[3456]{0:T(1024)(128)(4,1)} %get-tuple-element.92), kind=kLoop, calls=%fused_computation.49 | loop fusion | flops 13271040 | bytes 44254080 | tf_op jit(solution)/shard_map/mul | solution.py:147
  416.5 20.4 %fusion.26 = f32[3456,4,128]{2,0,1:T(8,128)} fusion(f32[3456,4,128]{2,0,1:T(8,128)} %copy-done, f32[3456,4,129]{2,0,1:T(8,128)} %fusion.8, f32[3456,5,128]{2,0,1:T(8,128)} %fusion.16, f32[4,128]{1,0:T(4,128)S(1)} %copy-done.38, pred[4,128]{1,0:T(4,128)(4,1)S(1)} %copy-done.41, f32[3456,8]{0,1:T(8,128)S(1)} %copy-done.8, f32[1,512]{1,0:T(1,128)S(1)} %copy-done.39, ...), kind=kOutput, calls=%fused_computation.64 | convolution fusion | flops 185806848 | bytes 42596864 | tf_op jit(solution)/shard_map/dot_general | solution.py:159
  436.9 8.1 %copy.35 = f32[3456,4,128]{0,2,1:T(8,128)} copy(f32[3456,4,128]{2,0,1:T(8,128)} %fusion.26) | data formatting | bytes 14155776 | tf_op jit(solution)/shard_map/jit(_where)/select_n | solution.py:161
  445.0 8.0 %fusion.32 = f32[13,4,128]{2,0,1:T(8,128)S(1)} fusion(f32[3456,4,128]{0,2,1:T(8,128)} %copy.35, f32[13,3456]{1,0:T(8,128)S(1)} %copy-done.4, f32[3456]{0:T(1024)S(1)} %get-tuple-element.10), kind=kOutput, calls=%fused_computation.73 | convolution fusion | flops 276082560 | bytes 7298048 | tf_op jit(solution)/shard_map/dot_general | solution.py:189
  453.0 11.2 %psum.23 = f32[13,4,128]{2,0,1:T(8,128)S(1)} all-reduce(f32[13,4,128]{2,0,1:T(8,128)S(1)} %fusion.32), channel_id=1, replica_groups=mesh['vel'=4,'strip'=8] {'vel'}, use_global_device_ids=true, to_apply=%region_2.3 | all-reduce | flops 6656 | bytes 53248 | tf_op jit(solution)/shard_map/psum | solution.py:200
  464.4 1.9 collective-permute-start.18
  466.3 3.9 collective-permute-start.19
  470.3 2.8 collective-permute-start.16
  473.1 3.0 collective-permute-start.17
  476.3 3.3 collective-permute-done.17
  479.9 2.0 collective-permute-start.20
  481.9 3.8 collective-permute-start.21
  485.8 2.6 collective-permute-done.21
  488.5 2.8 collective-permute-start.22
  491.3 3.0 collective-permute-start.23
  494.3 3.4 collective-permute-done.23
  497.9 8.6 %convolution_add_fusion = f32[3456,4,128]{2,0,1:T(8,128)S(1)} fusion(f32[3456,4,128]{2,0,1:T(8,128)} %fusion.26, f32[3456,5]{0,1:T(8,128)S(1)} %copy-done.6, f32[5,4,128]{2,0,1:T(8,128)S(1)} %fusion.68, f32[1,4,128]{2,0,1:T(1,128)S(1)} %get-tuple-element.61, f32[4,4,128]{2,0,1:T(4,128)S(1)} %slice.762), kind=kOutput, calls=%fused_computation.77 | convolution fusion | flops 107942912 | bytes 14245376 | tf_op jit(solution)/shard_map/dot_general | solution.py:209
  507.1 15.8 %copy.36 = f32[3456,4,128]{2,1,0:T(4,128)} copy(f32[3456,4,128]{2,0,1:T(8,128)S(1)} %convolution_add_fusion) | data formatting | bytes 14155776
  (162 shorter events, 5.3 us)
Async XLA Ops:
  4.1 26.5 %copy-start.1 = (f32[3456,4,128]{2,0,1:T(8,128)}, f32[3456,4,128]{2,0,1:T(8,128)S(1)}, u32[]{:S(2)}) copy-start(f32[3456,4,128]{2,0,1:T(8,128)S(1)} %copy.30) | copy-start | bytes 21233668
  4.1 16.1 %copy-start.29 = (s32[3,3456]{1,0:T(4,128)S(1)}, s32[3,3456]{1,0:T(4,128)}, u32[]{:S(2)}) copy-start(s32[3,3456]{1,0:T(4,128)} %param.7) | copy-start | bytes 124420
  6.3 120.6 %collective-permute-start = (f32[1728,2,128]{2,0,1:T(8,128)}, f32[1728,2,128]{2,0,1:T(8,128)}, u32[]{:S(2)}, u32[]{:S(2)}) collective-permute-start(f32[1728,2,128]{2,0,1:T(8,128)} %get-tuple-element.24), channel_id=1, source_target_pairs={{0,1},{1,2},{2,3},{3,4},{4,5},{5,6},{6,7},{8,9},{9,10},{10,11},{11... | collective-permute-start | bytes 5308424 | tf_op jit(solution)/shard_map/ppermute | solution.py:22
  9.7 117.2 %collective-permute-start.3 = (f32[1728,2,128]{2,0,1:T(8,128)}, f32[1728,2,128]{2,0,1:T(8,128)}, u32[]{:S(2)}, u32[]{:S(2)}) collective-permute-start(f32[1728,2,128]{2,0,1:T(8,128)} %get-tuple-element.25), channel_id=1, source_target_pairs={{1,0},{2,1},{3,2},{4,3},{5,4},{6,5},{7,6},{9,8},{10,9},{11,10},{12... | collective-permute-start | bytes 5308424 | tf_op jit(solution)/shard_map/ppermute | solution.py:22
  13.0 17.8 %slice-start = ((s8[7077888]{0:T(1024)(128)(4,1)}), s8[4194304]{0:T(1024)(128)(4,1)S(1)}, s32[]{:S(2)}) async-start(s8[7077888]{0:T(1024)(128)(4,1)} %bitcast.102), calls=%async_computation | async-start | bytes 8388608
  13.1 72.2 %collective-permute-start.1 = (f32[1728,1,128]{2,0,1:T(8,128)S(1)}, f32[1728,1,128]{2,0,1:T(8,128)S(1)}, u32[]{:S(2)}, u32[]{:S(2)}) collective-permute-start(f32[1728,1,128]{2,0,1:T(8,128)S(1)} %get-tuple-element.26), channel_id=1, source_target_pairs={{0,1},{1,2},{2,3},{3,4},{4,5},{5,6},{6,7},{8,9},{9,10},{10,11},{11... | collective-permute-start | bytes 2654216 | tf_op jit(solution)/shard_map/ppermute | solution.py:22
  17.1 108.4 %collective-permute-start.2 = (f32[1728,1,128]{2,0,1:T(8,128)S(1)}, f32[1728,1,128]{2,0,1:T(8,128)}, u32[]{:S(2)}, u32[]{:S(2)}) collective-permute-start(f32[1728,1,128]{2,0,1:T(8,128)S(1)} %get-tuple-element.27), channel_id=1, source_target_pairs={{1,0},{2,1},{3,2},{4,3},{5,4},{6,5},{7,6},{9,8},{10,9},{11,10},{12... | collective-permute-start | bytes 2654216 | tf_op jit(solution)/shard_map/ppermute | solution.py:22
  20.3 10.4 %slice-start.1 = ((s8[7077888]{0:T(1024)(128)(4,1)}), s8[2883584]{0:T(1024)(128)(4,1)S(1)}, s32[]{:S(2)}) async-start(s8[7077888]{0:T(1024)(128)(4,1)} %bitcast.102), calls=%async_computation.1 | async-start | bytes 5767168
  30.7 31.2 %copy-start.9 = (f32[3456]{0:T(1024)}, f32[3456]{0:T(1024)S(1)}, u32[]{:S(2)}) copy-start(f32[3456]{0:T(1024)S(1)} %get-tuple-element.44) | copy-start | bytes 41476
  30.7 31.8 %copy-start.10 = (f32[3456]{0:T(1024)}, f32[3456]{0:T(1024)S(1)}, u32[]{:S(2)}) copy-start(f32[3456]{0:T(1024)S(1)} %get-tuple-element.43) | copy-start | bytes 41476
  42.8 39.8 %copy-start.2 = (f32[13,3456]{1,0:T(8,128)}, f32[13,3456]{1,0:T(8,128)S(1)}, u32[]{:S(2)}) copy-start(f32[13,3456]{1,0:T(8,128)S(1)} %stack.24) | copy-start | bytes 539140
  62.6 20.0 %copy-start.30 = (pred[3456]{0:T(1024)(128)(4,1)}, pred[3456]{0:T(1024)(128)(4,1)S(1)}, u32[]{:S(2)}) copy-start(pred[3456]{0:T(1024)(128)(4,1)S(1)} %get-tuple-element.91) | copy-start | bytes 10372
  62.6 21.6 %copy-start.42 = (s32[4,128]{1,0:T(4,128)S(1)}, s32[4,128]{1,0:T(4,128)}, u32[]{:S(2)}) copy-start(s32[4,128]{1,0:T(4,128)} %param.5) | copy-start | bytes 6148
  62.6 22.1 %copy-start.36 = (f32[4,128]{1,0:T(4,128)S(1)}, f32[4,128]{1,0:T(4,128)}, u32[]{:S(2)}) copy-start(f32[4,128]{1,0:T(4,128)} %param.6) | copy-start | bytes 6148
  148.1 16.1 %copy-start.7 = (f32[3456,8]{0,1:T(8,128)S(1)}, f32[3456,8]{0,1:T(8,128)}, u32[]{:S(2)}) copy-start(f32[3456,8]{0,1:T(8,128)} %stack.23) | copy-start | bytes 331780
  148.1 16.1 %copy-start.28 = (f32[8,512]{1,0:T(8,128)S(1)}, f32[8,512]{1,0:T(8,128)}, u32[]{:S(2)}) copy-start(f32[8,512]{1,0:T(8,128)} %concatenate.151) | copy-start | bytes 49156
  148.1 16.1 %copy-start.37 = (f32[4,128]{1,0:T(4,128)S(1)}, f32[4,128]{1,0:T(4,128)}, u32[]{:S(2)}) copy-start(f32[4,128]{1,0:T(4,128)} %param.6) | copy-start | bytes 6148
  148.1 16.1 %copy-start.40 = (pred[4,128]{1,0:T(4,128)(4,1)S(1)}, pred[4,128]{1,0:T(4,128)(4,1)}, u32[]{:S(2)}) copy-start(pred[4,128]{1,0:T(4,128)(4,1)} %broadcast_compare_fusion.2) | copy-start | bytes 1540
  183.5 8.2 %copy-start.3 = (f32[13,3456]{1,0:T(8,128)S(1)}, f32[13,3456]{1,0:T(8,128)}, u32[]{:S(2)}) copy-start(f32[13,3456]{1,0:T(8,128)} %copy-done.2) | copy-start | bytes 539140
  183.5 43.6 %copy-start.24 = (f32[4,128]{1,0:T(4,128)S(1)}, f32[4,128]{1,0:T(4,128)}, u32[]{:S(2)}) copy-start(f32[4,128]{1,0:T(4,128)} %get-tuple-element.8) | copy-start | bytes 6148
  183.5 43.6 %copy-start.26 = (f32[4,128]{1,0:T(4,128)S(1)}, f32[4,128]{1,0:T(4,128)}, u32[]{:S(2)}) copy-start(f32[4,128]{1,0:T(4,128)} %get-tuple-element.9) | copy-start | bytes 6148
  183.5 58.1 %copy-start.15 = (f32[3456,1]{0,1:T(1,128)S(1)}, f32[3456,1]{0,1:T(1,128)}, u32[]{:S(2)}) copy-start(f32[3456,1]{0,1:T(1,128)} %copy-done.14) | copy-start | bytes 41476
  183.5 58.1 %copy-start.17 = (f32[3456,1]{0,1:T(1,128)S(1)}, f32[3456,1]{0,1:T(1,128)}, u32[]{:S(2)}) copy-start(f32[3456,1]{0,1:T(1,128)} %copy-done.16) | copy-start | bytes 41476
  183.5 58.1 %copy-start.19 = (f32[3456,1]{0,1:T(1,128)S(1)}, f32[3456,1]{0,1:T(1,128)}, u32[]{:S(2)}) copy-start(f32[3456,1]{0,1:T(1,128)} %copy-done.18) | copy-start | bytes 41476
  183.5 58.1 %copy-start.21 = (f32[3456,1]{0,1:T(1,128)S(1)}, f32[3456,1]{0,1:T(1,128)}, u32[]{:S(2)}) copy-start(f32[3456,1]{0,1:T(1,128)} %copy-done.20) | copy-start | bytes 41476
  183.5 58.1 %copy-start.23 = (f32[3456,1]{0,1:T(1,128)S(1)}, f32[3456,1]{0,1:T(1,128)}, u32[]{:S(2)}) copy-start(f32[3456,1]{0,1:T(1,128)} %copy-done.22) | copy-start | bytes 41476
  211.6 15.2 %copy-start.32 = (f32[1,4,128]{2,0,1:T(1,128)}, f32[1,4,128]{2,0,1:T(1,128)S(1)}, u32[]{:S(2)}) copy-start(f32[1,4,128]{2,0,1:T(1,128)S(1)} %get-tuple-element.64) | copy-start | bytes 6148
  211.6 15.2 %copy-start.34 = (f32[1,4,128]{2,0,1:T(1,128)}, f32[1,4,128]{2,0,1:T(1,128)S(1)}, u32[]{:S(2)}) copy-start(f32[1,4,128]{2,0,1:T(1,128)S(1)} %get-tuple-element.65) | copy-start | bytes 6148
  211.6 11.8 %collective-permute-start.6 = (f32[5,1,128]{2,0,1:T(8,128)S(1)}, f32[5,1,128]{2,0,1:T(8,128)S(1)}, u32[]{:S(2)}, u32[]{:S(2)}) collective-permute-start(f32[5,1,128]{2,0,1:T(8,128)S(1)} %get-tuple-element.90), channel_id=1, source_target_pairs={{1,0},{2,1},{3,2},{4,3},{5,4},{6,5},{7,6},{9,8},{10,9},{11,10},{12... | collective-permute-start | bytes 7688 | tf_op jit(solution)/shard_map/ppermute | solution.py:35
  213.5 9.8 %collective-permute-start.7 = (f32[5,1,128]{2,0,1:T(8,128)S(1)}, f32[5,1,128]{2,0,1:T(8,128)S(1)}, u32[]{:S(2)}, u32[]{:S(2)}) collective-permute-start(f32[5,1,128]{2,0,1:T(8,128)S(1)} %get-tuple-element.89), channel_id=1, source_target_pairs={{0,1},{1,2},{2,3},{3,4},{4,5},{5,6},{6,7},{8,9},{9,10},{10,11},{11... | collective-permute-start | bytes 7688 | tf_op jit(solution)/shard_map/ppermute | solution.py:33
  217.5 6.0 %collective-permute-start.4 = (f32[9,1,128]{2,0,1:T(8,128)S(1)}, f32[9,1,128]{2,0,1:T(8,128)S(1)}, u32[]{:S(2)}, u32[]{:S(2)}) collective-permute-start(f32[9,1,128]{2,0,1:T(8,128)S(1)} %get-tuple-element.73), channel_id=1, source_target_pairs={{1,0},{2,1},{3,2},{4,3},{5,4},{6,5},{7,6},{9,8},{10,9},{11,10},{12... | collective-permute-start | bytes 13832 | tf_op jit(solution)/shard_map/ppermute | solution.py:35
  220.3 6.4 %collective-permute-start.5 = (f32[9,1,128]{2,0,1:T(8,128)S(1)}, f32[9,1,128]{2,0,1:T(8,128)S(1)}, u32[]{:S(2)}, u32[]{:S(2)}) collective-permute-start(f32[9,1,128]{2,0,1:T(8,128)S(1)} %get-tuple-element.72), channel_id=1, source_target_pairs={{0,1},{1,2},{2,3},{3,4},{4,5},{5,6},{6,7},{8,9},{9,10},{10,11},{11... | collective-permute-start | bytes 13832 | tf_op jit(solution)/shard_map/ppermute | solution.py:33
  227.1 5.8 %collective-permute-start.8 = (f32[5,1,128]{2,0,1:T(8,128)S(1)}, f32[5,1,128]{2,0,1:T(8,128)S(1)}, u32[]{:S(2)}, u32[]{:S(2)}) collective-permute-start(f32[5,1,128]{2,0,1:T(8,128)S(1)} %get-tuple-element.85), channel_id=1, source_target_pairs={{1,0},{2,1},{3,2},{4,3},{5,4},{6,5},{7,6},{9,8},{10,9},{11,10},{12... | collective-permute-start | bytes 7688 | tf_op jit(solution)/shard_map/ppermute | solution.py:35
  229.1 6.4 %collective-permute-start.9 = (f32[5,1,128]{2,0,1:T(8,128)S(1)}, f32[5,1,128]{2,0,1:T(8,128)S(1)}, u32[]{:S(2)}, u32[]{:S(2)}) collective-permute-start(f32[5,1,128]{2,0,1:T(8,128)S(1)} %get-tuple-element.84), channel_id=1, source_target_pairs={{0,1},{1,2},{2,3},{3,4},{4,5},{5,6},{6,7},{8,9},{9,10},{10,11},{11... | collective-permute-start | bytes 7688 | tf_op jit(solution)/shard_map/ppermute | solution.py:33
  235.7 6.0 %collective-permute-start.10 = (f32[5,1,128]{2,0,1:T(8,128)S(1)}, f32[5,1,128]{2,0,1:T(8,128)S(1)}, u32[]{:S(2)}, u32[]{:S(2)}) collective-permute-start(f32[5,1,128]{2,0,1:T(8,128)S(1)} %get-tuple-element.83), channel_id=1, source_target_pairs={{1,0},{2,1},{3,2},{4,3},{5,4},{6,5},{7,6},{9,8},{10,9},{11,10},{12... | collective-permute-start | bytes 7688 | tf_op jit(solution)/shard_map/ppermute | solution.py:35
  238.5 6.4 %collective-permute-start.11 = (f32[5,1,128]{2,0,1:T(8,128)S(1)}, f32[5,1,128]{2,0,1:T(8,128)S(1)}, u32[]{:S(2)}, u32[]{:S(2)}) collective-permute-start(f32[5,1,128]{2,0,1:T(8,128)S(1)} %get-tuple-element.82), channel_id=1, source_target_pairs={{0,1},{1,2},{2,3},{3,4},{4,5},{5,6},{6,7},{8,9},{9,10},{10,11},{11... | collective-permute-start | bytes 7688 | tf_op jit(solution)/shard_map/ppermute | solution.py:33
  241.7 13.2 %copy-start.5 = (f32[3456,5]{0,1:T(8,128)}, f32[3456,5]{0,1:T(8,128)S(1)}, u32[]{:S(2)}) copy-start(f32[3456,5]{0,1:T(8,128)S(1)} %stack.28) | copy-start | bytes 207364
  245.1 8.2 %copy-start.12 = (f32[5,4,128]{2,0,1:T(8,128)}, f32[5,4,128]{2,0,1:T(8,128)S(1)}, u32[]{:S(2)}) copy-start(f32[5,4,128]{2,0,1:T(8,128)S(1)} %fusion.80) | copy-start | bytes 30724
  253.3 23.9 %copy-start = (f32[3456,4,128]{2,0,1:T(8,128)}, f32[3456,4,128]{2,0,1:T(8,128)S(1)}, u32[]{:S(2)}) copy-start(f32[3456,4,128]{2,0,1:T(8,128)S(1)} %convolution_add_fusion.1) | copy-start | bytes 21233668
  255.0 22.2 %copy-start.11 = (f32[3456]{0:T(1024)S(1)}, f32[3456]{0:T(1024)}, u32[]{:S(2)}) copy-start(f32[3456]{0:T(1024)} %copy-done.10) | copy-start | bytes 41476
  255.0 22.2 %copy-start.31 = (pred[3456]{0:T(1024)(128)(4,1)S(1)}, pred[3456]{0:T(1024)(128)(4,1)}, u32[]{:S(2)}) copy-start(pred[3456]{0:T(1024)(128)(4,1)} %copy-done.30) | copy-start | bytes 10372
  263.7 115.4 %collective-permute-start.12 = (f32[1728,2,128]{2,0,1:T(8,128)}, f32[1728,2,128]{2,0,1:T(8,128)}, u32[]{:S(2)}, u32[]{:S(2)}) collective-permute-start(f32[1728,2,128]{2,0,1:T(8,128)} %get-tuple-element.20), channel_id=1, source_target_pairs={{0,1},{1,2},{2,3},{3,4},{4,5},{5,6},{6,7},{8,9},{9,10},{10,11},{11... | collective-permute-start | bytes 5308424 | tf_op jit(solution)/shard_map/ppermute | solution.py:22
  265.8 113.3 %collective-permute-start.15 = (f32[1728,2,128]{2,0,1:T(8,128)S(1)}, f32[1728,2,128]{2,0,1:T(8,128)}, u32[]{:S(2)}, u32[]{:S(2)}) collective-permute-start(f32[1728,2,128]{2,0,1:T(8,128)S(1)} %get-tuple-element.21), channel_id=1, source_target_pairs={{1,0},{2,1},{3,2},{4,3},{5,4},{6,5},{7,6},{9,8},{10,9},{11,10},{12... | collective-permute-start | bytes 5308424 | tf_op jit(solution)/shard_map/ppermute | solution.py:22
  270.5 50.5 %collective-permute-start.13 = (f32[1728,1,128]{2,0,1:T(8,128)S(1)}, f32[1728,1,128]{2,0,1:T(8,128)S(1)}, u32[]{:S(2)}, u32[]{:S(2)}) collective-permute-start(f32[1728,1,128]{2,0,1:T(8,128)S(1)} %get-tuple-element.22), channel_id=1, source_target_pairs={{0,1},{1,2},{2,3},{3,4},{4,5},{5,6},{6,7},{8,9},{9,10},{10,11},{11... | collective-permute-start | bytes 2654216 | tf_op jit(solution)/shard_map/ppermute | solution.py:22
  272.9 104.9 %collective-permute-start.14 = (f32[1728,1,128]{2,0,1:T(8,128)S(1)}, f32[1728,1,128]{2,0,1:T(8,128)}, u32[]{:S(2)}, u32[]{:S(2)}) collective-permute-start(f32[1728,1,128]{2,0,1:T(8,128)S(1)} %get-tuple-element.23), channel_id=1, source_target_pairs={{1,0},{2,1},{3,2},{4,3},{5,4},{6,5},{7,6},{9,8},{10,9},{11,10},{12... | collective-permute-start | bytes 2654216 | tf_op jit(solution)/shard_map/ppermute | solution.py:22
  400.4 16.1 %copy-start.8 = (f32[3456,8]{0,1:T(8,128)S(1)}, f32[3456,8]{0,1:T(8,128)}, u32[]{:S(2)}) copy-start(f32[3456,8]{0,1:T(8,128)} %stack.23) | copy-start | bytes 331780
  400.4 16.1 %copy-start.13 = (f32[5,4,128]{2,0,1:T(8,128)S(1)}, f32[5,4,128]{2,0,1:T(8,128)}, u32[]{:S(2)}) copy-start(f32[5,4,128]{2,0,1:T(8,128)} %copy-done.12) | copy-start | bytes 30724
  400.4 16.1 %copy-start.33 = (f32[1,4,128]{2,0,1:T(1,128)S(1)}, f32[1,4,128]{2,0,1:T(1,128)}, u32[]{:S(2)}) copy-start(f32[1,4,128]{2,0,1:T(1,128)} %copy-done.32) | copy-start | bytes 6148
  400.4 16.1 %copy-start.35 = (f32[1,4,128]{2,0,1:T(1,128)S(1)}, f32[1,4,128]{2,0,1:T(1,128)}, u32[]{:S(2)}) copy-start(f32[1,4,128]{2,0,1:T(1,128)} %copy-done.34) | copy-start | bytes 6148
  400.4 16.1 %copy-start.38 = (f32[4,128]{1,0:T(4,128)S(1)}, f32[4,128]{1,0:T(4,128)}, u32[]{:S(2)}) copy-start(f32[4,128]{1,0:T(4,128)} %param.6) | copy-start | bytes 6148
  400.4 16.1 %copy-start.39 = (f32[1,512]{1,0:T(1,128)S(1)}, f32[1,512]{1,0:T(1,128)}, u32[]{:S(2)}) copy-start(f32[1,512]{1,0:T(1,128)} %get-tuple-element.63) | copy-start | bytes 6148
  400.4 16.1 %copy-start.41 = (pred[4,128]{1,0:T(4,128)(4,1)S(1)}, pred[4,128]{1,0:T(4,128)(4,1)}, u32[]{:S(2)}) copy-start(pred[4,128]{1,0:T(4,128)(4,1)} %broadcast_compare_fusion.2) | copy-start | bytes 1540
  436.9 8.1 %copy-start.4 = (f32[13,3456]{1,0:T(8,128)S(1)}, f32[13,3456]{1,0:T(8,128)}, u32[]{:S(2)}) copy-start(f32[13,3456]{1,0:T(8,128)} %copy-done.2) | copy-start | bytes 539140
  436.9 42.9 %copy-start.25 = (f32[4,128]{1,0:T(4,128)S(1)}, f32[4,128]{1,0:T(4,128)}, u32[]{:S(2)}) copy-start(f32[4,128]{1,0:T(4,128)} %get-tuple-element.8) | copy-start | bytes 6148
  436.9 42.9 %copy-start.27 = (f32[4,128]{1,0:T(4,128)S(1)}, f32[4,128]{1,0:T(4,128)}, u32[]{:S(2)}) copy-start(f32[4,128]{1,0:T(4,128)} %get-tuple-element.9) | copy-start | bytes 6148
  436.9 60.9 %copy-start.6 = (f32[3456,5]{0,1:T(8,128)S(1)}, f32[3456,5]{0,1:T(8,128)}, u32[]{:S(2)}) copy-start(f32[3456,5]{0,1:T(8,128)} %copy-done.5) | copy-start | bytes 207364
  464.4 11.8 %collective-permute-start.18 = (f32[5,1,128]{2,0,1:T(8,128)S(1)}, f32[5,1,128]{2,0,1:T(8,128)S(1)}, u32[]{:S(2)}, u32[]{:S(2)}) collective-permute-start(f32[5,1,128]{2,0,1:T(8,128)S(1)} %get-tuple-element.88), channel_id=1, source_target_pairs={{1,0},{2,1},{3,2},{4,3},{5,4},{6,5},{7,6},{9,8},{10,9},{11,10},{12... | collective-permute-start | bytes 7688 | tf_op jit(solution)/shard_map/ppermute | solution.py:35
  466.3 9.8 %collective-permute-start.19 = (f32[5,1,128]{2,0,1:T(8,128)S(1)}, f32[5,1,128]{2,0,1:T(8,128)S(1)}, u32[]{:S(2)}, u32[]{:S(2)}) collective-permute-start(f32[5,1,128]{2,0,1:T(8,128)S(1)} %get-tuple-element.87), channel_id=1, source_target_pairs={{0,1},{1,2},{2,3},{3,4},{4,5},{5,6},{6,7},{8,9},{9,10},{10,11},{11... | collective-permute-start | bytes 7688 | tf_op jit(solution)/shard_map/ppermute | solution.py:33
  470.3 6.0 %collective-permute-start.16 = (f32[9,1,128]{2,0,1:T(8,128)S(1)}, f32[9,1,128]{2,0,1:T(8,128)S(1)}, u32[]{:S(2)}, u32[]{:S(2)}) collective-permute-start(f32[9,1,128]{2,0,1:T(8,128)S(1)} %get-tuple-element.54), channel_id=1, source_target_pairs={{1,0},{2,1},{3,2},{4,3},{5,4},{6,5},{7,6},{9,8},{10,9},{11,10},{12... | collective-permute-start | bytes 13832 | tf_op jit(solution)/shard_map/ppermute | solution.py:35
  473.1 6.4 %collective-permute-start.17 = (f32[9,1,128]{2,0,1:T(8,128)S(1)}, f32[9,1,128]{2,0,1:T(8,128)S(1)}, u32[]{:S(2)}, u32[]{:S(2)}) collective-permute-start(f32[9,1,128]{2,0,1:T(8,128)S(1)} %get-tuple-element.53), channel_id=1, source_target_pairs={{0,1},{1,2},{2,3},{3,4},{4,5},{5,6},{6,7},{8,9},{9,10},{10,11},{11... | collective-permute-start | bytes 13832 | tf_op jit(solution)/shard_map/ppermute | solution.py:33
  479.9 5.8 %collective-permute-start.20 = (f32[5,1,128]{2,0,1:T(8,128)S(1)}, f32[5,1,128]{2,0,1:T(8,128)S(1)}, u32[]{:S(2)}, u32[]{:S(2)}) collective-permute-start(f32[5,1,128]{2,0,1:T(8,128)S(1)} %get-tuple-element.81), channel_id=1, source_target_pairs={{1,0},{2,1},{3,2},{4,3},{5,4},{6,5},{7,6},{9,8},{10,9},{11,10},{12... | collective-permute-start | bytes 7688 | tf_op jit(solution)/shard_map/ppermute | solution.py:35
  481.9 6.4 %collective-permute-start.21 = (f32[5,1,128]{2,0,1:T(8,128)S(1)}, f32[5,1,128]{2,0,1:T(8,128)S(1)}, u32[]{:S(2)}, u32[]{:S(2)}) collective-permute-start(f32[5,1,128]{2,0,1:T(8,128)S(1)} %get-tuple-element.80), channel_id=1, source_target_pairs={{0,1},{1,2},{2,3},{3,4},{4,5},{5,6},{6,7},{8,9},{9,10},{10,11},{11... | collective-permute-start | bytes 7688 | tf_op jit(solution)/shard_map/ppermute | solution.py:33
  488.5 5.8 %collective-permute-start.22 = (f32[5,1,128]{2,0,1:T(8,128)S(1)}, f32[5,1,128]{2,0,1:T(8,128)S(1)}, u32[]{:S(2)}, u32[]{:S(2)}) collective-permute-start(f32[5,1,128]{2,0,1:T(8,128)S(1)} %get-tuple-element.79), channel_id=1, source_target_pairs={{1,0},{2,1},{3,2},{4,3},{5,4},{6,5},{7,6},{9,8},{10,9},{11,10},{12... | collective-permute-start | bytes 7688 | tf_op jit(solution)/shard_map/ppermute | solution.py:35
  491.3 6.4 %collective-permute-start.23 = (f32[5,1,128]{2,0,1:T(8,128)S(1)}, f32[5,1,128]{2,0,1:T(8,128)S(1)}, u32[]{:S(2)}, u32[]{:S(2)}) collective-permute-start(f32[5,1,128]{2,0,1:T(8,128)S(1)} %get-tuple-element.78), channel_id=1, source_target_pairs={{0,1},{1,2},{2,3},{3,4},{4,5},{5,6},{6,7},{8,9},{9,10},{10,11},{11... | collective-permute-start | bytes 7688 | tf_op jit(solution)/shard_map/ppermute | solution.py:33
  (5 other events, 12.5 us)
where the time goes:
time: 530 us; the launch traced here: 523 us
  waiting for transfers between devices  148 us (28%)
  other arithmetic  128 us (24%)
  matrix products  80.3 us (15%)
  starting transfers between devices  73.9 us (14%)
  local copies, waits for them, and re-layouts  56.8 us (11%)
  blocking collectives  33.9 us (6%)
    ppermute x8, waiting for transfers between devices, from_behind(): return lax.ppermute(shard, axis, pairs)  130 us
    mul x4, other arithmetic, interface_diff(): flux = speed * jnp.where(speed > 0, upwind, downwind)  62.5 us
    concatenate x2, other arithmetic, extend_rows(): return jnp.concatenate([upper_rows, dist, lower_rows], axis=1)  42.5 us
    dot_general x2, matrix products, relax(): jnp.dot(table, fields.reshape(8, -1), precision=HIGH).reshape(dist.shape)  39.6 us
    ppermute x8, starting transfers between devices, with_halo(): lax.ppermute(tail, axis, [(i, (i + 1) % count) for i in range(ends)])  27.6 us
    ppermute x8, starting transfers between devices, from_behind(): return lax.ppermute(shard, axis, pairs)  27.2 us
    dot_general x3, matrix products, partial_sum(): jnp.dot(weights, field.reshape(count_v, rows * cols), precision=HIGH)  23.8 us
    unnamed x94, local copies, waits for them, and re-layouts  23.8 us
  transfers between devices with their start and end apart: 24, of which 9 were waited for; matrix products, arithmetic and copies ran while one was open for 13% of the time, Pallas kernels for 0%

commit v1 on v0

v1 whole, which is shorter than its diff:
```python
import functools
import math

import jax
import jax.numpy as jnp
import numpy as np
from jax import lax
from jax.experimental import pallas as pl
from jax.experimental.pallas import tpu as pltpu
from jax.sharding import PartitionSpec as P

STEP_RATIO = 0.1
SOURCE_WEIGHT = 0.5
HEAT_WEIGHT = 4.0 / 15.0
SWEEPS = 3
HIGH = lax.Precision.HIGHEST
LANES = 128
STRIP_ROWS = 4
BLOCK_ROWS = 2 * STRIP_ROWS
SPAN = 3 * BLOCK_ROWS
GROUP = 16
F32 = jnp.float32
BF16 = jnp.bfloat16


def params(**more):
    return pltpu.CompilerParams(vmem_limit_bytes=40 * 1024 * 1024, **more)


def moment_rows(vel_x, vel_y, vel_z, volume, lib):
    energy = vel_x * vel_x + vel_y * vel_y + vel_z * vel_z
    weight = volume * math.pi ** (-1.5) * lib.exp(-energy)
    rows = [
        lib.ones_like(vel_x),
        vel_x,
        vel_y,
        vel_z,
        energy,
        vel_x * vel_x,
        vel_y * vel_y,
        vel_x * vel_y,
        vel_x * vel_z,
        vel_y * vel_z,
        energy * vel_x,
        energy * vel_y,
        energy * vel_z,
    ]
    return lib.stack(rows) * weight


def state_rows(vel_x, vel_y, vel_z, lib):
    energy = vel_x * vel_x + vel_y * vel_y + vel_z * vel_z
    shape_heat = HEAT_WEIGHT * (energy - 2.5)
    rows = [
        lib.ones_like(vel_x),
        2.0 * vel_x,
        2.0 * vel_y,
        2.0 * vel_z,
        energy - 1.5,
        shape_heat * vel_x,
        shape_heat * vel_y,
        shape_heat * vel_z,
    ]
    return lib.stack(rows)


def target_moments(points):
    line = (np.arange(points) - (points - 1) / 2.0) * (8.0 / points)
    comps = [a.reshape(-1) for a in np.meshgrid(line, line, line, indexing="ij")]
    gram = moment_rows(*comps, (8.0 / points) ** 3, np) @ state_rows(*comps, np).T
    gram[np.abs(gram) < 1e-12] = 0.0
    full = np.zeros((16, 8), np.float32)
    full[:13] = gram
    return full


def macro_matrix():
    third = 2.0 / 3.0
    unit = np.eye(16, dtype=np.float64)
    start = [unit[0], unit[1], unit[2], unit[3], third * unit[4] - unit[0]]
    heat = [unit[10] - 2.5 * unit[1], unit[11] - 2.5 * unit[2], unit[12] - 2.5 * unit[3]]
    flux = [
        unit[1],
        unit[2],
        2.0 * unit[5] - third * unit[4],
        2.0 * unit[7],
        2.0 * unit[6] - third * unit[4],
        2.0 * unit[8],
        2.0 * unit[9],
        heat[0],
        heat[1],
    ]
    out = np.zeros((32, 16), np.float64)
    for row in range(5):
        out[row] = start[row]
        out[8 + row] = flux[(0, 2, 3, 5, 7)[row]]
        out[16 + row] = flux[(1, 3, 4, 6, 8)[row]]
    for row in range(3):
        out[24 + 5 + row] = heat[row]
    return out.astype(np.float32)


def rounded(value):
    return lax.reduce_precision(value, 8, 7)


def minmod(left, right):
    low = jnp.minimum(left, right)
    high = jnp.maximum(left, right)
    return jnp.maximum(low, 0.0) + jnp.minimum(high, 0.0)


def strided(start, count):
    return pl.ds(start, count, stride=STRIP_ROWS)


def pack_kernel(size, side_ref, far_ref, own_ref, mid_ref, edge_ref, down_ref):
    side = side_ref[0]
    for i in range(4):
        row = jnp.where(side == 1, i, 3 - i)
        part = far_ref[strided(row, size), :]
        if i < 2:
            mid_ref[i] = part
        else:
            edge_ref[i - 2] = part
    down_ref[...] = own_ref[strided(jnp.where(side == 1, 3, 0), size), :]


def pack(side, flat, half, chunk, first, size):
    steps = chunk // size
    shift = half // size
    begin = first // size
    return pl.pallas_call(
        functools.partial(pack_kernel, size),
        out_shape=(
            jax.ShapeDtypeStruct((2, chunk, LANES), F32),
            jax.ShapeDtypeStruct((2, chunk, LANES), F32),
            jax.ShapeDtypeStruct((chunk, LANES), F32),
        ),
        grid_spec=pltpu.PrefetchScalarGridSpec(
            num_scalar_prefetch=1,
            grid=(steps,),
            in_specs=[
                pl.BlockSpec((4 * size, LANES), lambda i, s: ((1 - s[0]) * shift + begin + i, 0)),
                pl.BlockSpec((4 * size, LANES), lambda i, s: (s[0] * shift + begin + i, 0)),
            ],
            out_specs=[
                pl.BlockSpec((2, size, LANES), lambda i, s: (0, i, 0)),
                pl.BlockSpec((2, size, LANES), lambda i, s: (0, i, 0)),
                pl.BlockSpec((size, LANES), lambda i, s: (i, 0)),
            ],
        ),
        compiler_params=params(),
        name="pack",
        cost_estimate=pl.CostEstimate(
            flops=0, transcendentals=0, bytes_accessed=chunk * LANES * 4 * 13
        ),
    )(side, flat, flat)


def split_store(value, first_ref, second_ref, rows, columns):
    first = value.astype(BF16)
    first_ref[rows, columns] = first
    second_ref[rows, columns] = (value - first.astype(F32)).astype(BF16)


def weighted(weights, first, second):
    both = jnp.dot(weights, first, preferred_element_type=F32)
    return both[:16] + both[16:] + jnp.dot(weights[:16], second, preferred_element_type=F32)


def moment_kernel(size, dist_ref, weight_ref, out_ref, first_ref, second_ref):
    @pl.when(pl.program_id(0) == 0)
    def _():
        out_ref[...] = jnp.zeros_like(out_ref)

    for row in range(STRIP_ROWS):
        columns = pl.ds(row * LANES, LANES)
        split_store(
            dist_ref[strided(row, size), :], first_ref, second_ref, pl.ds(0, size), columns
        )
    out_ref[...] += weighted(weight_ref[0], first_ref[...], second_ref[...])


def home_moments(flat, weights, size):
    count = flat.shape[0] // STRIP_ROWS
    width = STRIP_ROWS * LANES
    return pl.pallas_call(
        functools.partial(moment_kernel, size),
        out_shape=jax.ShapeDtypeStruct((16, width), F32),
        grid=(count // size,),
        in_specs=[
            pl.BlockSpec((4 * size, LANES), lambda i: (i, 0)),
            pl.BlockSpec((1, 32, size), lambda i: (i, 0, 0)),
        ],
        out_specs=pl.BlockSpec((16, width), lambda i: (0, 0)),
        scratch_shapes=[pltpu.VMEM((size, width), BF16), pltpu.VMEM((size, width), BF16)],
        compiler_params=params(),
        name="home_moments",
        cost_estimate=pl.CostEstimate(
            flops=2 * 48 * count * width, transcendentals=0, bytes_accessed=count * width * 4
        ),
    )(flat, weights)


def transport_kernel(size, second_pass, side_ref, *refs):
    if second_pass:
        (table_ref, change_ref, q_first, q_mid, q_edge, up_ref, down_ref, *rest) = refs
    else:
        (own_ref, mid_ref, edge_ref, up_ref, down_ref, *rest) = refs
    (const_ref, weight_ref, cell_ref, sum_in_ref, *rest) = rest
    if second_pass:
        (near_out, far_out, sum_ref, first_ref, second_ref, lift_ref) = rest
    else:
        (first_out, mid_out, edge_out, sum_ref, first_ref, second_ref) = rest
    side = side_ref[0]

    @pl.when(pl.program_id(0) == 0)
    def _():
        sum_ref[...] = sum_in_ref[...]

    if second_pass:
        lift_ref[...] = jnp.dot(table_ref[...], change_ref[...], preferred_element_type=F32)

    lane = lax.broadcasted_iota(jnp.int32, (GROUP, LANES), 1)
    inner_low = jnp.where(lane == 0, 0.0, 1.0)
    inner_high = jnp.where(lane == LANES - 1, 0.0, 1.0)

    def body(group, carry):
        base = pl.multiple_of(group * GROUP, GROUP)
        rows = pl.ds(base, GROUP)

        def load(row):
            if row < 0:
                value = up_ref[row + 2, rows, :]
            elif row == 8:
                value = down_ref[rows, :]
            elif second_pass:
                if row == 0:
                    value = q_first[rows, :]
                elif row < 6:
                    value = q_mid[row - 1, rows, :]
                else:
                    value = q_edge[row - 6, rows, :]
            elif row < 4:
                value = own_ref[
                    strided(base * STRIP_ROWS + jnp.where(side == 1, 3 - row, row), GROUP), :
                ]
            elif row < 6:
                value = mid_ref[row - 4, rows, :]
            else:
                value = edge_ref[row - 6, rows, :]
            if second_pass:
                value = value + lift_ref[rows, pl.ds((row + 2) * LANES, LANES)]
            return value

        def wide(column):
            return jnp.broadcast_to(const_ref[rows, column : column + 1], (GROUP, LANES))

        speed_x = wide(0)
        speed_y = wide(1)
        half_sign = wide(2)
        forward = half_sign > 0.0
        open_end = jnp.where(forward, inner_low, inner_high)

        behind = load(-2)
        here = load(-1)
        ahead = load(0)
        step = ahead - here
        upwind = here + 0.5 * minmod(here - behind, step)
        here = ahead
        for row in range(BLOCK_ROWS):
            ahead = load(row + 1)
            next_step = ahead - here
            next_upwind = here + 0.5 * minmod(step, next_step)
            drift = speed_x * (next_upwind - upwind)
            step = next_step
            upwind = next_upwind
            left = here - pltpu.roll(here, 1, 1) * inner_low
            right = pltpu.roll(here, LANES - 1, 1) * inner_high - here
            face = here + half_sign * minmod(left, right)
            other = jnp.where(forward, pltpu.roll(face, 1, 1), pltpu.roll(face, LANES - 1, 1))
            drift = drift + speed_y * (face - other * open_end)
            keep = jnp.broadcast_to(cell_ref[row : row + 1, :], (GROUP, LANES))
            fluid = jnp.broadcast_to(cell_ref[row + 8 : row + 9, :], (GROUP, LANES))
            value = keep * here - fluid * drift
            split_store(value, first_ref, second_ref, rows, pl.ds(row * LANES, LANES))
            if second_pass:
                if row < 4:
                    near_out[row, rows, :] = value
                else:
                    far_out[row - 4, rows, :] = value
            elif row == 0:
                first_out[rows, :] = value
            elif row < 6:
                mid_out[row - 1, rows, :] = value
            else:
                edge_out[row - 6, rows, :] = value
            here = ahead
        return carry

    lax.fori_loop(0, size // GROUP, body, 0)
    part = weighted(weight_ref[0], first_ref[...], second_ref[...])
    for row in range(BLOCK_ROWS):
        place = jnp.where(side == 1, 7 - row, row)
        columns = pl.ds(pl.multiple_of(place * LANES, LANES), LANES)
        sum_ref[:, columns] += part[:, row * LANES : (row + 1) * LANES]


def transport(side, sources, tables, cells, sums, half, chunk, first, size, change=None):
    second_pass = change is not None
    steps = chunk // size
    shift = half // size
    begin = first // size
    table, const, weights = tables
    width = BLOCK_ROWS * LANES

    def mine(i, s):
        return s[0] * shift + begin + i

    two = pl.BlockSpec((2, size, LANES), lambda i, s: (0, i, 0))
    one = pl.BlockSpec((size, LANES), lambda i, s: (i, 0))
    if second_pass:
        args = [table, change]
        specs = [
            pl.BlockSpec((size, 48), lambda i, s: (mine(i, s), 0)),
            pl.BlockSpec(change.shape, lambda i, s: (0, 0)),
            one,
            pl.BlockSpec((5, size, LANES), lambda i, s: (0, i, 0)),
            two,
            two,
            one,
        ]
        four = pl.BlockSpec((4, size, LANES), lambda i, s: (0, i, 0))
        outs = [jax.ShapeDtypeStruct((4, chunk, LANES), F32)] * 2
        out_specs = [four, four]
        scratch = [pltpu.VMEM((size, 11 * LANES), F32)]
    else:
        args = []
        specs = [
            pl.BlockSpec((4 * size, LANES), lambda i, s: (mine(i, s), 0)),
            two,
            two,
            two,
            one,
        ]
        outs = [
            jax.ShapeDtypeStruct((chunk, LANES), F32),
            jax.ShapeDtypeStruct((5, chunk, LANES), F32),
            jax.ShapeDtypeStruct((2, chunk, LANES), F32),
        ]
        out_specs = [one, pl.BlockSpec((5, size, LANES), lambda i, s: (0, i, 0)), two]
        scratch = []
    whole = pl.BlockSpec((16, width), lambda i, s: (0, 0))
    return pl.pallas_call(
        functools.partial(transport_kernel, size, second_pass),
        out_shape=(*outs, jax.ShapeDtypeStruct((16, width), F32)),
        grid_spec=pltpu.PrefetchScalarGridSpec(
            num_scalar_prefetch=1,
            grid=(steps,),
            in_specs=[
                *specs,
                pl.BlockSpec((size, 8), lambda i, s: (mine(i, s), 0)),
                pl.BlockSpec((1, 32, size), lambda i, s: (mine(i, s), 0, 0)),
                pl.BlockSpec((16, LANES), lambda i, s: (0, 0)),
                whole,
            ],
            out_specs=[*out_specs, whole],
            scratch_shapes=[
                pltpu.VMEM((size, width), BF16),
                pltpu.VMEM((size, width), BF16),
                *scratch,
            ],
        ),
        compiler_params=params(),
        name="transport_second" if second_pass else "transport_first",
        cost_estimate=pl.CostEstimate(
            flops=60 * chunk * width, transcendentals=0, bytes_accessed=chunk * LANES * 4 * 19
        ),
    )(side, *args, *sources, const, weights, cells, sums)


def sweep_block(inputs, relax, rate):
    start, flux_x, flux_y = inputs
    lane = lax.broadcasted_iota(jnp.int32, (8, LANES), 1)
    inner_low = jnp.where(lane == 0, 0.0, 1.0)
    inner_high = jnp.where(lane == LANES - 1, 0.0, 1.0)

    def block(array, row):
        if row < 0 or row >= SPAN:
            return jnp.zeros((8, LANES), F32)
        return array[:, row * LANES : (row + 1) * LANES]

    def lower(value):
        return pltpu.roll(value, 1, 1) * inner_low

    def upper(value):
        return pltpu.roll(value, LANES - 1, 1) * inner_high

    source = []
    for row in range(SPAN):
        diff_x = 0.5 * (block(flux_x, row + 1) - block(flux_x, row - 1))
        side = block(flux_y, row)
        diff_y = 0.5 * (upper(side) - lower(side))
        source.append(block(start, row) - SOURCE_WEIGHT * (diff_x + diff_y))
    zero = jnp.zeros((8, LANES), F32)
    kappa = [block(rate, row) for row in range(SPAN)]
    scale = [block(relax, row) for row in range(SPAN)]
    state = [block(start, row) for row in range(SPAN)]
    for _ in range(SWEEPS):
        near = [zero, *state, zero]
        state = [
            (source[row] + kappa[row] * (near[row] + near[row + 2] + lower(near[row + 1]) + upper(near[row + 1])))
            * scale[row]
            for row in range(SPAN)
        ]
    return jnp.concatenate(state, axis=1)


def stacked(value):
    first = value.astype(BF16)
    rest = value - first.astype(F32)
    second = rest.astype(BF16)
    third = (rest - second.astype(F32)).astype(BF16)
    return jnp.concatenate([first, second, third, first, second, first], axis=0)


def relax_rows(rate):
    inside = rate > 0.0
    kappa = jnp.where(inside, 0.5 / jnp.where(inside, rate, 1.0), 0.0)
    scale = jnp.where(inside, 1.0 / (1.0 + 4.0 * kappa), 0.0)
    width = rate.shape[1]
    return jnp.broadcast_to(kappa, (8, width)), jnp.broadcast_to(scale, (8, width))


def place_blocks(info_ref, span_ref, own, pair_a, pair_b):
    odd = info_ref[1]
    width = BLOCK_ROWS * LANES
    span_ref[:, width : 2 * width] = own
    place_a = pl.multiple_of((1 - odd) * 2 * width, width)
    place_b = pl.multiple_of(odd * 2 * width, width)
    span_ref[:, pl.ds(place_a, width)] = pair_a
    span_ref[:, pl.ds(place_b, width)] = pair_b


def first_macro_kernel(
    info_ref, sum_ref, sum_a_ref, sum_b_ref, near_ref, far_ref, gram_ref, mat_ref,
    change_ref, keep_ref, span_ref, home_ref,
):
    side = info_ref[0]
    odd = info_ref[1]
    width = BLOCK_ROWS * LANES
    part = STRIP_ROWS * LANES
    place_blocks(info_ref, span_ref, sum_ref[...], sum_a_ref[...], sum_b_ref[...])
    for ref, where in ((near_ref, side), (far_ref, 1 - side)):
        for index, block in enumerate((1, (1 - odd) * 2, odd * 2)):
            spot = pl.multiple_of(block * width + where * part, part)
            home_ref[:, pl.ds(spot, part)] = ref[index]
    home = home_ref[...]
    rate = home[13:14, :]
    ratio = jnp.where(home[14:15, :] > 0.5, 1.0, rate)
    mat = mat_ref[...]
    first = jnp.dot(mat, jnp.where(lax.broadcasted_iota(jnp.int32, home.shape, 0) < 13, home, 0.0), precision=HIGH)
    fields = first[:8] + first[24:]
    moments = span_ref[...] + ratio * jnp.dot(gram_ref[...], fields, precision=HIGH)
    all_parts = jnp.dot(mat, moments, precision=HIGH)
    start = all_parts[:8]
    kappa, scale = relax_rows(rate)
    state = sweep_block((start, all_parts[8:16], all_parts[16:24]), scale, kappa)
    change = ratio * fields + (state - start)
    span_ref[0:8, :] = change
    keep_ref[0:8, :] = state + all_parts[24:]
    keep_ref[8:9, :] = rate
    keep_ref[9:10, :] = ratio
    keep_ref[10:16, :] = jnp.zeros((6, SPAN * LANES), F32)
    for row in range(-2, 9):
        spot = jnp.where(side == 1, 15 - row, 8 + row)
        piece = span_ref[0:8, pl.ds(pl.multiple_of(spot * LANES, LANES), LANES)]
        change_ref[:, (row + 2) * LANES : (row + 3) * LANES] = stacked(piece)


def second_macro_kernel(
    info_ref, sum_ref, sum_a_ref, sum_b_ref, keep_ref, gram_ref, mat_ref,
    change_ref, state_ref, span_ref,
):
    side = info_ref[0]
    place_blocks(info_ref, span_ref, sum_ref[...], sum_a_ref[...], sum_b_ref[...])
    fields = keep_ref[0:8, :]
    rate = keep_ref[8:9, :]
    ratio = keep_ref[9:10, :]
    moments = span_ref[...] + ratio * jnp.dot(gram_ref[...], fields, precision=HIGH)
    all_parts = jnp.dot(mat_ref[...], moments, precision=HIGH)
    start = all_parts[:8]
    kappa, scale = relax_rows(rate)
    state = sweep_block((start, all_parts[8:16], all_parts[16:24]), scale, kappa)
    span_ref[0:8, :] = ratio * fields + (state - start)
    span_ref[8:16, :] = state
    part = STRIP_ROWS * LANES
    spot = pl.ds(pl.multiple_of(2 * part + side * part, part), part)
    change_ref[...] = stacked(span_ref[0:8, spot])
    state_ref[...] = span_ref[8:16, spot]


def macro(kernel, info, args, outs, scratch, name):
    vmem = pl.BlockSpec(memory_space=pltpu.VMEM)
    return pl.pallas_call(
        kernel,
        out_shape=outs,
        in_specs=[pl.BlockSpec(memory_space=pltpu.SMEM)] + [vmem] * len(args),
        out_specs=[vmem] * len(outs),
        scratch_shapes=scratch,
        compiler_params=params(),
        name=name,
        cost_estimate=pl.CostEstimate(flops=4000000, transcendentals=0, bytes_accessed=1000000),
    )(info, *args)


def finish_kernel(size, side_ref, near_ref, back_ref, table_ref, change_ref, *rest):
    out_ref = rest[-1]
    side = side_ref[0]
    lift = jnp.dot(table_ref[...], change_ref[...], preferred_element_type=F32)

    def write(ref, flipped):
        for row in range(STRIP_ROWS):
            index = jnp.where(side == flipped, 3 - row, row)
            out_ref[strided(row, size), :] = (
                ref[index] + lift[:, row * LANES : (row + 1) * LANES]
            )

    @pl.when(pl.program_id(0) == 0)
    def _():
        write(near_ref, 1)

    @pl.when(pl.program_id(0) == 1)
    def _():
        write(back_ref, 0)


def finish(side, out, near, back, table, change, half, chunk, first, size):
    steps = chunk // size
    shift = half // size
    begin = first // size

    def place(h, i, s):
        return jnp.where(h == 0, s[0], 1 - s[0]) * shift + begin + i

    specs = [
        pl.BlockSpec((4, size, LANES), lambda h, i, s: (0, jnp.where(h == 0, i, steps - 1), 0)),
        pl.BlockSpec((4, size, LANES), lambda h, i, s: (0, jnp.where(h == 0, 0, i), 0)),
        pl.BlockSpec((size, 48), lambda h, i, s: (place(h, i, s), 0)),
        pl.BlockSpec(change.shape, lambda h, i, s: (0, 0)),
    ]
    args = [side, near, back, table, change]
    aliases = {}
    if out is not None:
        specs.append(pl.BlockSpec(memory_space=pl.ANY))
        args.append(out)
        aliases = {5: 0}
    return pl.pallas_call(
        functools.partial(finish_kernel, size),
        out_shape=jax.ShapeDtypeStruct((2 * half * STRIP_ROWS, LANES), F32),
        grid_spec=pltpu.PrefetchScalarGridSpec(
            num_scalar_prefetch=1,
            grid=(2, steps),
            in_specs=specs,
            out_specs=pl.BlockSpec((4 * size, LANES), lambda h, i, s: (place(h, i, s), 0)),
        ),
        input_output_aliases=aliases,
        compiler_params=params(),
        name="finish",
        cost_estimate=pl.CostEstimate(
            flops=2 * 48 * 8 * LANES * chunk,
            transcendentals=0,
            bytes_accessed=chunk * LANES * 4 * 16,
        ),
    )(*args)


def per_device(points, dist, cell_type, collision_rate, vel_index):
    count, rows, cols = dist.shape
    half = count // 2
    strips = lax.axis_size("strip")
    groups = lax.axis_size("vel")
    strip = lax.axis_index("strip")
    size = 144
    pieces = next(k for k in (4, 3, 2, 1) if (half // size) % k == 0)
    chunk = half // pieces
    side = (strip % 2).astype(jnp.int32).reshape(1)
    info = jnp.stack([strip % 2, (strip // 2) % 2]).astype(jnp.int32)

    swap_pairs = [(s, s ^ 1) for s in range(strips)]
    down_pairs = [
        (s, s + (2 if s % 2 == 0 else -2))
        for s in range(strips)
        if 0 <= s + (2 if s % 2 == 0 else -2) < strips
    ]
    up_pairs = [(b, a) for a, b in down_pairs]
    pair_a = [
        (s, s + (2 if (s // 2) % 2 == 0 else -2))
        for s in range(strips)
        if 0 <= s + (2 if (s // 2) % 2 == 0 else -2) < strips
    ]
    pair_b = [
        (s, s + (-2 if (s // 2) % 2 == 0 else 2))
        for s in range(strips)
        if 0 <= s + (-2 if (s // 2) % 2 == 0 else 2) < strips
    ]

    def swap(value):
        return lax.ppermute(value, "strip", swap_pairs)

    def with_flow(value):
        return lax.ppermute(value, "strip", down_pairs)

    def against_flow(value):
        return lax.ppermute(value, "strip", up_pairs)

    def both_z(value):
        return lax.ppermute(value, "strip", pair_a), lax.ppermute(value, "strip", pair_b)

    def sum_groups(value):
        total = value
        for shift in range(1, groups):
            total = total + lax.ppermute(
                value, "vel", [(g, (g + shift) % groups) for g in range(groups)]
            )
        return total

    flat = dist.reshape(count * rows, cols)
    wall = (cell_type == 1).astype(F32)
    cell_pair = jnp.concatenate([collision_rate, wall])
    other_cells = swap(cell_pair)

    packed = [pack(side, flat, half, chunk, c * chunk, size) for c in range(pieces)]
    got = []
    for mid, edge, down in packed:
        edge_here = swap(edge)
        mid_here = swap(mid)
        got.append((mid_here, edge_here, with_flow(edge_here), against_flow(down)))

    comps = (vel_index.astype(F32) - (points - 1) / 2.0) * (8.0 / points)
    moment_table = jnp.pad(moment_rows(comps[0], comps[1], comps[2], (8.0 / points) ** 3, jnp), ((0, 3), (0, 0)))
    weight_high = rounded(moment_table)
    weight_low = rounded(moment_table - weight_high)
    weights = (
        jnp.concatenate([weight_high, weight_low])
        .astype(BF16)
        .reshape(32, count // size, size)
        .transpose(1, 0, 2)
    )
    shape_rows = state_rows(comps[0], comps[1], comps[2], jnp)
    part_a = rounded(shape_rows)
    part_b = rounded(shape_rows - part_a)
    part_c = rounded(shape_rows - part_a - part_b)
    table = jnp.concatenate([part_a, part_a, part_a, part_b, part_b, part_c]).astype(BF16).T
    zero = jnp.zeros_like(comps[0])
    const = jnp.stack(
        [
            STEP_RATIO * jnp.abs(comps[0]),
            STEP_RATIO * jnp.abs(comps[1]),
            jnp.where(comps[1] > 0, 0.5, -0.5),
            zero,
            zero,
            zero,
            zero,
            zero,
        ]
    ).T
    tables = (table, const, weights)
    gram = jnp.asarray(target_moments(points))
    mat = jnp.asarray(macro_matrix())

    def flow(own, other):
        odd = strip % 2 == 1
        return jnp.concatenate(
            [jnp.where(odd, own[::-1], own), jnp.where(odd, other[::-1], other)]
        )

    flow_rate = flow(collision_rate, other_cells[:rows])
    flow_fluid = 1.0 - flow(wall, other_cells[rows:])
    cells = jnp.concatenate([flow_fluid * (1.0 - flow_rate), flow_fluid])

    home = sum_groups(home_moments(flat, weights, size))
    home = jnp.concatenate(
        [home[:13], collision_rate.reshape(1, -1), wall.reshape(1, -1), jnp.zeros((1, rows * cols), F32)]
    )
    near_home = jnp.stack([home, *both_z(home)])
    far_home = swap(near_home)

    width = BLOCK_ROWS * LANES
    sums = jnp.zeros((16, width), F32)
    kept = []
    for c in range(pieces):
        mid_here, edge_here, above, below = got[c]
        first, middle, edge, sums = transport(
            side, [flat, mid_here, edge_here, above, below], tables, cells, sums,
            half, chunk, c * chunk, size,
        )
        kept.append((first, middle, edge, with_flow(edge), against_flow(first)))

    def exchange(value):
        value = sum_groups(value)
        value = value + swap(value)
        return value, both_z(value)

    own_sum, (sum_a, sum_b) = exchange(sums)
    change, keep = macro(
        first_macro_kernel, info,
        [own_sum, sum_a, sum_b, near_home, far_home, gram, mat],
        [
            jax.ShapeDtypeStruct((48, 11 * LANES), BF16),
            jax.ShapeDtypeStruct((16, SPAN * LANES), F32),
        ],
        [pltpu.VMEM((16, SPAN * LANES), F32)] * 2,
        "first_macro",
    )

    sums = jnp.zeros((16, width), F32)
    near, far = [], []
    for c in range(pieces):
        near_part, far_part, sums = transport(
            side, list(kept[c]), tables, cells, sums, half, chunk, c * chunk, size, change
        )
        near.append(near_part)
        far.append(far_part)
    back = [swap(part) for part in far[:-1]]
    own_sum, (sum_a, sum_b) = exchange(sums)
    last, own_sum = lax.optimization_barrier((far[-1], own_sum))
    back.append(swap(last))
    change, state = macro(
        second_macro_kernel, info,
        [own_sum, sum_a, sum_b, keep, gram, mat],
        [
            jax.ShapeDtypeStruct((48, STRIP_ROWS * LANES), BF16),
            jax.ShapeDtypeStruct((8, STRIP_ROWS * LANES), F32),
        ],
        [pltpu.VMEM((16, SPAN * LANES), F32)],
        "second_macro",
    )
    out = None
    for c in range(pieces):
        out = finish(side, out, near[c], back[c], table, change, half, chunk, c * chunk, size)
    return out.reshape(dist.shape), state[:5].reshape(5, rows, cols)


def solution(mesh):
    groups = mesh.shape["vel"]

    def whole(dist, cell_type, collision_rate, vel_index):
        points = round(vel_index.shape[1] ** (1.0 / 3.0))
        in_specs = (P("vel", "strip", None), P("strip", None), P("strip", None), P(None, "vel"))
        out_specs = (P("vel", "strip", None), P(None, "strip", None))
        return jax.shard_map(
            functools.partial(per_device, points),
            mesh=mesh,
            in_specs=in_specs,
            out_specs=out_specs,
            check_vma=False,
        )(dist, cell_type, collision_rate, vel_index)

    return whole
```

time: 530 us -> 348 us (0.66)
  other arithmetic: 128 us -> 5.37 us
  Pallas kernels: 0 us -> 97.6 us
  matrix products: 80.3 us -> 0 us
  waiting for transfers between devices: 148 us -> 114 us
  blocking collectives: 33.9 us -> 0 us
  local copies, waits for them, and re-layouts: 56.8 us -> 49.5 us
    pallas_call x0 -> x19, Pallas kernels: none -> 97.6 us  [the longest x8 71.1 us: transport(): pl.pallas_call(functools.partial(transport_kernel, size, second_pass), ou...]
    dot_general x7 -> x0, matrix products: 80.3 us -> none  [the longest x2 39.6 us: relax(): jnp.dot(table, fields.reshape(8, -1), precision=HIGH).reshape(dist.shape)]
    mul x13 -> x5, other arithmetic: 63 us -> 1.1 us  [the longest x1 0.84 us: per_device(): comps = (vel_index.astype(F32) - (points - 1) / 2.0) * (8.0 / points)]
    concatenate x12 -> x4, other arithmetic: 43.7 us -> 0.73 us  [the longest x1 0.64 us: per_device(): jnp.concatenate([part_a, part_a, part_a, part_b, part_b, part_c])]
    ppermute x24 -> x47, waiting for transfers between devices: 148 us -> 114 us  [the longest x16 96.5 us: swap(): return lax.ppermute(value, 'strip', swap_pairs)]
    psum x3 -> x0, blocking collectives: 33.9 us -> none  [the longest x2 22.6 us: per_device(): start, flux_fields, heat = macro_parts(lax.psum(partial_value, 'vel'))]
    unnamed x94 -> x118, local copies, waits for them, and re-layouts: 23.8 us -> 44.9 us
    select_n x2 -> x3, other arithmetic: 18.9 us -> 0.01 us  [the longest x2 0.01 us: flow(): jnp.where(odd, other[::-1], other)]
  transfers between devices with their start and end apart: 24 -> 47, of which waited for: 9 -> 20; matrix products, arithmetic and copies ran while one was open for 13% -> 2% of each run, Pallas kernels for 0% -> 23%
where the time goes in v1:
time: 348 us; the launch traced here: 344 us
  waiting for transfers between devices  114 us (33%)
  Pallas kernels  97.6 us (28%)
  starting transfers between devices  76 us (22%)
  local copies, waits for them, and re-layouts  49.5 us (14%)
  other arithmetic  5.37 us (2%)
    ppermute x16, waiting for transfers between devices, swap(): return lax.ppermute(value, 'strip', swap_pairs)  96.5 us
    pallas_call x8, Pallas kernels, transport(): pl.pallas_call(functools.partial(transport_kernel, size, second_pass), ou...  71.1 us
    unnamed x118, local copies, waits for them, and re-layouts  44.9 us
    ppermute x8, starting transfers between devices, against_flow(): return lax.ppermute(value, 'strip', up_pairs)  31.4 us
    ppermute x16, starting transfers between devices, swap(): return lax.ppermute(value, 'strip', swap_pairs)  19 us
    pallas_call x4, Pallas kernels, finish(): pl.pallas_call(functools.partial(finish_kernel, size), out_shape=jax.Shap...  16 us
    ppermute x8, starting transfers between devices, with_flow(): return lax.ppermute(value, 'strip', down_pairs)  10.3 us
    ppermute x3, starting transfers between devices, both_z(): lax.ppermute(value, 'strip', pair_a)  9.2 us
  transfers between devices with their start and end apart: 47, of which 20 were waited for; matrix products, arithmetic and copies ran while one was open for 2% of the time, Pallas kernels for 23%

profile of v1, /device:TPU:24, one launch (start us, length us, event | category | flops | bytes accessed | tf_op | source)
XLA Modules:
  0.0 343.8 jit_solution(331970203760231292)
XLA Ops:
  2.8 3.0 copy-done
  5.8 4.7 %home_moments.1 = f32[16,512]{1,0:T(8,128)S(1)} custom-call(f32[13824,128]{1,0:T(8,128)S(1)} %bitcast.16, bf16[24,32,144]{2,1,0:T(8,128)(2,1)S(1)} %maximum_bitcast_fusion.refs_6_.weight_ref.refs_8_), custom_call_target="tpu_custom_call" | custom-call | flops 169869312 | bytes 7077888 | tf_op jit(solution)/shard_map/home_moments/pallas_call | solution.py:188
  12.3 1.6 collective-permute-start.4
  13.9 3.0 copy-done.1
  16.9 1.5 pack.7
  19.2 2.4 collective-permute-start.16
  23.7 3.0 copy-done.2
  35.1 2.1 collective-permute-start.14
  37.1 3.0 collective-permute-start.12
  40.2 2.3 collective-permute-start.8
  42.6 3.0 collective-permute-done.12.refs_4_
  45.6 2.1 collective-permute-start.10
  47.7 1.9 collective-permute-done.8.refs_4_
  49.6 2.4 collective-permute-start.6
  52.1 5.7 %collective-permute-done.14.refs_2_ = f32[2,432,128]{2,1,0:T(8,128)S(1)} collective-permute-done((f32[2,432,128]{2,1,0:T(8,128)}, f32[2,432,128]{2,1,0:T(8,128)S(1)}, u32[]{:S(2)}, u32[]{:S(2)}) %collective-permute-start.14) | collective-permute-done | bytes 442400 | tf_op jit(solution)/shard_map/ppermute | solution.py:610
  57.8 9.5 %collective-permute-done.9.refs_1_ = f32[2,432,128]{2,1,0:T(8,128)S(1)} collective-permute-done((f32[2,432,128]{2,1,0:T(8,128)}, f32[2,432,128]{2,1,0:T(8,128)S(1)}, u32[]{:S(2)}, u32[]{:S(2)}) %collective-permute-start.9) | collective-permute-done | bytes 442400 | tf_op jit(solution)/shard_map/ppermute | solution.py:610
  67.2 1.3 collective-permute-start.15
  68.5 8.2 %collective-permute-done.10.refs_2_ = f32[2,432,128]{2,1,0:T(8,128)S(1)} collective-permute-done((f32[2,432,128]{2,1,0:T(8,128)}, f32[2,432,128]{2,1,0:T(8,128)S(1)}, u32[]{:S(2)}, u32[]{:S(2)}) %collective-permute-start.10) | collective-permute-done | bytes 442400 | tf_op jit(solution)/shard_map/ppermute | solution.py:610
  76.7 1.3 collective-permute-start.11
  78.0 8.2 %collective-permute-done.6.refs_2_ = f32[2,432,128]{2,1,0:T(8,128)S(1)} collective-permute-done((f32[2,432,128]{2,1,0:T(8,128)}, f32[2,432,128]{2,1,0:T(8,128)S(1)}, u32[]{:S(2)}, u32[]{:S(2)}) %collective-permute-start.6) | collective-permute-done | bytes 442400 | tf_op jit(solution)/shard_map/ppermute | solution.py:610
  86.2 1.3 collective-permute-start.7
  87.5 8.2 %collective-permute-done.5.refs_1_ = f32[2,432,128]{2,1,0:T(8,128)S(1)} collective-permute-done((f32[2,432,128]{2,1,0:T(8,128)}, f32[2,432,128]{2,1,0:T(8,128)S(1)}, u32[]{:S(2)}, u32[]{:S(2)}) %collective-permute-start.5) | collective-permute-done | bytes 442400 | tf_op jit(solution)/shard_map/ppermute | solution.py:610
  95.7 9.5 %collective-permute-done.1.refs_2_ = f32[2,432,128]{2,1,0:T(8,128)S(1)} collective-permute-done((f32[2,432,128]{2,1,0:T(8,128)}, f32[2,432,128]{2,1,0:T(8,128)S(1)}, u32[]{:S(2)}, u32[]{:S(2)}) %collective-permute-start.1) | collective-permute-done | bytes 442400 | tf_op jit(solution)/shard_map/ppermute | solution.py:610
  105.1 1.3 collective-permute-start.2
  106.5 4.5 %collective-permute-start.3 = (f32[432,128]{1,0:T(8,128)}, f32[432,128]{1,0:T(8,128)S(1)}, u32[]{:S(2)}, u32[]{:S(2)}) collective-permute-start(f32[432,128]{1,0:T(8,128)} %copy-done.52), channel_id=1, source_target_pairs={{2,0},{4,2},{1,3},{6,4},{3,5},{5,7},{10,8},{12,10},{9,11},{14,12},... | collective-permute-start | bytes 663560 | tf_op jit(solution)/shard_map/ppermute | solution.py:616
  112.3 3.0 copy-done.3
  115.3 7.4 %transport_first.4 = (f32[432,128]{1,0:T(8,128)S(1)}, f32[5,432,128]{2,1,0:T(8,128)S(1)}, f32[2,432,128]{2,1,0:T(8,128)S(1)}, f32[16,1024]{1,0:T(8,128)S(1)}) custom-call(s32[1]{0:T(128)} %bitcast.side_ref, f32[13824,128]{1,0:T(8,128)S(1)} %bitcast.25, f32[2,432,128]{2,1,0:T(8,128)S(1)} %collective-permute-done.13.refs_1_, ...), custom_call_target="tpu_custom_call" | custom-call | flops 26542080 | bytes 4202496 | tf_op jit(solution)/shard_map/transport_first/pallas_call | solution.py:355
  123.7 8.9 %transport_first.5 = (f32[432,128]{1,0:T(8,128)S(1)}, f32[5,432,128]{2,1,0:T(8,128)S(1)}, f32[2,432,128]{2,1,0:T(8,128)}, f32[16,1024]{1,0:T(8,128)S(1)}) custom-call(s32[1]{0:T(128)} %bitcast.side_ref, f32[13824,128]{1,0:T(8,128)S(1)} %bitcast.26, f32[2,432,128]{2,1,0:T(8,128)S(1)} %collective-permute-done.9.refs_1_, ...), custom_call_target="tpu_custom_call" | custom-call | flops 26542080 | bytes 4202496 | tf_op jit(solution)/shard_map/transport_first/pallas_call | solution.py:355
  133.6 8.9 %transport_first.6 = (f32[432,128]{1,0:T(8,128)S(1)}, f32[5,432,128]{2,1,0:T(8,128)S(1)}, f32[2,432,128]{2,1,0:T(8,128)}, f32[16,1024]{1,0:T(8,128)S(1)}) custom-call(s32[1]{0:T(128)} %bitcast.side_ref, f32[13824,128]{1,0:T(8,128)S(1)} %bitcast.27, f32[2,432,128]{2,1,0:T(8,128)S(1)} %collective-permute-done.5.refs_1_, ...), custom_call_target="tpu_custom_call" | custom-call | flops 26542080 | bytes 4202496 | tf_op jit(solution)/shard_map/transport_first/pallas_call | solution.py:355
  143.5 8.0 %transport_first.7 = (f32[432,128]{1,0:T(8,128)}, f32[5,432,128]{2,1,0:T(8,128)S(1)}, f32[2,432,128]{2,1,0:T(8,128)}, f32[16,1024]{1,0:T(8,128)S(1)}) custom-call(s32[1]{0:T(128)} %bitcast.side_ref, f32[13824,128]{1,0:T(8,128)S(1)} %bitcast.28, f32[2,432,128]{2,1,0:T(8,128)S(1)} %collective-permute-done.refs_1_, ...), custom_call_target="tpu_custom_call" | custom-call | flops 26542080 | bytes 4202496 | tf_op jit(solution)/shard_map/transport_first/pallas_call | solution.py:355
  154.1 1.7 collective-permute-start.28
  155.8 2.1 collective-permute-done.18
  158.2 1.7 collective-permute-start.20
  160.5 4.0 %collective-permute-start.34 = (f32[432,128]{1,0:T(8,128)S(1)}, f32[432,128]{1,0:T(8,128)S(1)}, u32[]{:S(2)}, u32[]{:S(2)}) collective-permute-start(f32[432,128]{1,0:T(8,128)S(1)} %get-tuple-element.71.refs_2_), channel_id=1, source_target_pairs={{2,0},{4,2},{1,3},{6,4},{3,5},{5,7},{10,8},{12,10},{9,11},{14,12},... | collective-permute-start | bytes 663560 | tf_op jit(solution)/shard_map/ppermute | solution.py:616
  164.6 3.1 collective-permute-start.36
  167.7 1.3 collective-permute-start.35
  169.7 4.0 %collective-permute-start.21 = (f32[16,1024]{1,0:T(8,128)S(1)}, f32[16,1024]{1,0:T(8,128)S(1)}, u32[]{:S(2)}, u32[]{:S(2)}) collective-permute-start(f32[16,1024]{1,0:T(8,128)S(1)} %add.86.sum_ref), channel_id=1, source_target_pairs={{0,2},{1,3},{2,0},{3,1},{4,6},{5,7},{6,4},{7,5},{8,10},{9,11},{10,... | collective-permute-start | bytes 196616 | tf_op jit(solution)/shard_map/ppermute | solution.py:619
  175.0 10.0 %collective-permute-start.30 = (f32[432,128]{1,0:T(8,128)}, f32[432,128]{1,0:T(8,128)}, u32[]{:S(2)}, u32[]{:S(2)}) collective-permute-start(f32[432,128]{1,0:T(8,128)} %get-tuple-element.65.refs_2_), channel_id=1, source_target_pairs={{2,0},{4,2},{1,3},{6,4},{3,5},{5,7},{10,8},{12,10},{9,11},{14,12},... | collective-permute-start | bytes 663560 | tf_op jit(solution)/shard_map/ppermute | solution.py:616
  185.6 2.0 collective-permute-start.32
  188.3 1.3 collective-permute-start.29
  190.3 1.3 collective-permute-start.31
  194.3 1.4 copy.29
  198.5 2.0 first_macro.1
  205.6 8.8 %transport_second.4 = (f32[4,432,128]{2,1,0:T(8,128)S(1)}, f32[4,432,128]{2,1,0:T(8,128)}, f32[16,1024]{1,0:T(8,128)S(1)}) custom-call(s32[1]{0:T(128)} %bitcast.side_ref, bf16[3456,48]{1,0:T(8,128)(2,1)S(1)} %bitcast.37, bf16[48,1408]{1,0:T(8,128)(2,1)S(1)} %get-tuple-element.64.refs_1_, f32[432,128]{1,0:T(8,128)S(1)} %copy-done.30, ...), custom_call_target="tpu_custom_call" | custom-call | flops 26542080 | bytes 4202496 | tf_op jit(solution)/shard_map/transport_second/pallas_call | solution.py:355
  215.3 3.7 %collective-permute-done.33.refs_5_ = f32[2,432,128]{2,1,0:T(8,128)} collective-permute-done((f32[2,432,128]{2,1,0:T(8,128)}, f32[2,432,128]{2,1,0:T(8,128)}, u32[]{:S(2)}, u32[]{:S(2)}) %collective-permute-start.33) | collective-permute-done | bytes 442400 | tf_op jit(solution)/shard_map/ppermute | solution.py:613
  222.2 9.6 %transport_second.5 = (f32[4,432,128]{2,1,0:T(8,128)S(1)}, f32[4,432,128]{2,1,0:T(8,128)}, f32[16,1024]{1,0:T(8,128)S(1)}) custom-call(s32[1]{0:T(128)} %bitcast.side_ref, bf16[3456,48]{1,0:T(8,128)(2,1)S(1)} %bitcast.38, bf16[48,1408]{1,0:T(8,128)(2,1)S(1)} %get-tuple-element.64.refs_1_, f32[432,128]{1,0:T(8,128)S(1)} %copy-done.28, ...), custom_call_target="tpu_custom_call" | custom-call | flops 26542080 | bytes 4202496 | tf_op jit(solution)/shard_map/transport_second/pallas_call | solution.py:355
  232.8 9.8 %transport_second.6 = (f32[4,432,128]{2,1,0:T(8,128)S(1)}, f32[4,432,128]{2,1,0:T(8,128)}, f32[16,1024]{1,0:T(8,128)S(1)}) custom-call(s32[1]{0:T(128)} %bitcast.side_ref, bf16[3456,48]{1,0:T(8,128)(2,1)S(1)} %bitcast.39, bf16[48,1408]{1,0:T(8,128)(2,1)S(1)} %get-tuple-element.64.refs_1_, f32[432,128]{1,0:T(8,128)S(1)} %get-tuple-element.68.refs_2_, ...), custom_call_target="tpu_custom_call" | custom-call | flops 26542080 | bytes 4202496 | tf_op jit(solution)/shard_map/transport_second/pallas_call | solution.py:355
  243.5 9.7 %transport_second.7 = (f32[4,432,128]{2,1,0:T(8,128)S(1)}, f32[4,432,128]{2,1,0:T(8,128)}, f32[16,1024]{1,0:T(8,128)S(1)}) custom-call(s32[1]{0:T(128)} %bitcast.side_ref, bf16[3456,48]{1,0:T(8,128)(2,1)S(1)} %bitcast.40, bf16[48,1408]{1,0:T(8,128)(2,1)S(1)} %get-tuple-element.64.refs_1_, f32[432,128]{1,0:T(8,128)} %get-tuple-element.65.refs_2_, ...), custom_call_target="tpu_custom_call" | custom-call | flops 26542080 | bytes 4202496 | tf_op jit(solution)/shard_map/transport_second/pallas_call | solution.py:355
  256.5 2.7 collective-permute-done.38
  259.5 3.1 collective-permute-start.40
  262.7 1.9 collective-permute-start.45
  265.6 2.1 collective-permute-start.41
  268.3 4.7 %collective-permute-start.42 = (f32[16,1024]{1,0:T(8,128)S(1)}, f32[16,1024]{1,0:T(8,128)S(1)}, u32[]{:S(2)}, u32[]{:S(2)}) collective-permute-start(f32[16,1024]{1,0:T(8,128)S(1)} %add.93.sum_ref), channel_id=1, source_target_pairs={{0,2},{1,3},{2,0},{3,1},{4,6},{5,7},{6,4},{7,5},{8,10},{9,11},{10,... | collective-permute-start | bytes 196616 | tf_op jit(solution)/shard_map/ppermute | solution.py:619
  273.1 2.2 collective-permute-done.42.sum_a_ref
  275.3 1.5 second_macro.1
  278.0 1.3 reshape.32
  279.3 6.0 %collective-permute-done.46.back_ref = f32[4,432,128]{2,1,0:T(8,128)S(1)} collective-permute-done((f32[4,432,128]{2,1,0:T(8,128)}, f32[4,432,128]{2,1,0:T(8,128)S(1)}, u32[]{:S(2)}, u32[]{:S(2)}) %collective-permute-start.46) | collective-permute-done | bytes 884768 | tf_op jit(solution)/shard_map/ppermute | solution.py:610
  287.3 3.2 finish.4.rest_0_
  290.5 13.9 %collective-permute-done.45.back_ref = f32[4,432,128]{2,1,0:T(8,128)} collective-permute-done((f32[4,432,128]{2,1,0:T(8,128)}, f32[4,432,128]{2,1,0:T(8,128)}, u32[]{:S(2)}, u32[]{:S(2)}) %collective-permute-start.45) | collective-permute-done | bytes 884768 | tf_op jit(solution)/shard_map/ppermute | solution.py:610
  304.4 4.8 %finish.5.rest_0_ = f32[13824,128]{1,0:T(8,128)} custom-call(s32[1]{0:T(128)} %bitcast.side_ref, f32[4,432,128]{2,1,0:T(8,128)S(1)} %copy-done.15, f32[4,432,128]{2,1,0:T(8,128)} %collective-permute-done.45.back_ref, bf16[3456,48]{1,0:T(8,128)(2,1)S(1)} %bitcast.42, bf16[48,512]{1,0:T(8,128)(2,1)S(1)} %copy-done.21, ...), custom_call_target="tpu_custom_call", output_to_operand_aliasing={{}: (5, {})} | custom-call | flops 42467328 | bytes 3538944 | tf_op jit(solution)/shard_map/finish/pallas_call | solution.py:559
  309.2 14.1 %collective-permute-done.44.back_ref = f32[4,432,128]{2,1,0:T(8,128)} collective-permute-done((f32[4,432,128]{2,1,0:T(8,128)}, f32[4,432,128]{2,1,0:T(8,128)}, u32[]{:S(2)}, u32[]{:S(2)}) %collective-permute-start.44) | collective-permute-done | bytes 884768 | tf_op jit(solution)/shard_map/ppermute | solution.py:610
  323.4 4.8 %finish.6.rest_0_ = f32[13824,128]{1,0:T(8,128)} custom-call(s32[1]{0:T(128)} %bitcast.side_ref, f32[4,432,128]{2,1,0:T(8,128)S(1)} %copy-done.17, f32[4,432,128]{2,1,0:T(8,128)} %collective-permute-done.44.back_ref, bf16[3456,48]{1,0:T(8,128)(2,1)S(1)} %bitcast.43, bf16[48,512]{1,0:T(8,128)(2,1)S(1)} %copy-done.22, ...), custom_call_target="tpu_custom_call", output_to_operand_aliasing={{}: (5, {})} | custom-call | flops 42467328 | bytes 3538944 | tf_op jit(solution)/shard_map/finish/pallas_call | solution.py:559
  328.2 12.4 %collective-permute-done.41.back_ref = f32[4,432,128]{2,1,0:T(8,128)S(1)} collective-permute-done((f32[4,432,128]{2,1,0:T(8,128)}, f32[4,432,128]{2,1,0:T(8,128)S(1)}, u32[]{:S(2)}, u32[]{:S(2)}) %collective-permute-start.41) | collective-permute-done | bytes 884768 | tf_op jit(solution)/shard_map/ppermute | solution.py:610
  340.6 3.2 finish.7
  (215 shorter events, 51.9 us)
Async XLA Ops:
  0.6 11.7 %copy-start.58 = (s32[4,128]{1,0:T(4,128)S(1)}, s32[4,128]{1,0:T(4,128)}, u32[]{:S(2)}) copy-start(s32[4,128]{1,0:T(4,128)} %param.7) | copy-start | bytes 6148
  0.6 11.7 %copy-start.57 = (f32[4,128]{1,0:T(4,128)S(1)}, f32[4,128]{1,0:T(4,128)}, u32[]{:S(2)}) copy-start(f32[4,128]{1,0:T(4,128)} %param.8) | copy-start | bytes 6148
  10.6 24.5 %collective-permute-start.25 = (f32[16,512]{1,0:T(8,128)S(1)}, f32[16,512]{1,0:T(8,128)S(1)}, u32[]{:S(2)}, u32[]{:S(2)}) collective-permute-start(f32[16,512]{1,0:T(8,128)S(1)} %home_moments.1), channel_id=1, source_target_pairs={{0,24},{8,0},{16,8},{24,16},{1,25},{9,1},{17,9},{25,17},{2,26},{10... | collective-permute-start | bytes 98312 | tf_op jit(solution)/shard_map/ppermute | solution.py:624
  11.5 25.6 %collective-permute-start.24 = (f32[16,512]{1,0:T(8,128)S(1)}, f32[16,512]{1,0:T(8,128)S(1)}, u32[]{:S(2)}, u32[]{:S(2)}) collective-permute-start(f32[16,512]{1,0:T(8,128)S(1)} %home_moments.1), channel_id=1, source_target_pairs={{0,16},{8,24},{16,0},{24,8},{1,17},{9,25},{17,1},{25,9},{2,18},{10... | collective-permute-start | bytes 98312 | tf_op jit(solution)/shard_map/ppermute | solution.py:624
  12.1 28.0 %collective-permute-start.23 = (f32[16,512]{1,0:T(8,128)S(1)}, f32[16,512]{1,0:T(8,128)S(1)}, u32[]{:S(2)}, u32[]{:S(2)}) collective-permute-start(f32[16,512]{1,0:T(8,128)S(1)} %home_moments.1), channel_id=1, source_target_pairs={{0,8},{8,16},{16,24},{24,0},{1,9},{9,17},{17,25},{25,1},{2,10},{10... | collective-permute-start | bytes 98312 | tf_op jit(solution)/shard_map/ppermute | solution.py:624
  12.3 22.7 %collective-permute-start.4 = (f32[8,128]{1,0:T(8,128)S(1)}, f32[8,128]{1,0:T(8,128)S(1)}, u32[]{:S(2)}, u32[]{:S(2)}) collective-permute-start(f32[8,128]{1,0:T(8,128)S(1)} %pad_maximum_fusion.2), channel_id=1, source_target_pairs={{0,1},{1,0},{2,3},{3,2},{4,5},{5,4},{6,7},{7,6},{8,9},{9,8},{10,11... | collective-permute-start | bytes 12296 | tf_op jit(solution)/shard_map/ppermute | solution.py:610
  19.2 23.4 %collective-permute-start.16 = (f32[432,128]{1,0:T(8,128)}, f32[432,128]{1,0:T(8,128)S(1)}, u32[]{:S(2)}, u32[]{:S(2)}) collective-permute-start(f32[432,128]{1,0:T(8,128)} %get-tuple-element.59), channel_id=1, source_target_pairs={{2,0},{4,2},{1,3},{6,4},{3,5},{5,7},{10,8},{12,10},{9,11},{14,12},... | collective-permute-start | bytes 663560 | tf_op jit(solution)/shard_map/ppermute | solution.py:616
  21.8 5.2 %copy-start.55 = (f32[8,3456]{1,0:T(8,128)}, f32[8,3456]{1,0:T(8,128)S(1)}, u32[]{:S(2)}) copy-start(f32[8,3456]{1,0:T(8,128)S(1)} %stack.21) | copy-start | bytes 331780
  35.0 17.0 %collective-permute-start.13 = (f32[2,432,128]{2,1,0:T(8,128)}, f32[2,432,128]{2,1,0:T(8,128)S(1)}, u32[]{:S(2)}, u32[]{:S(2)}) collective-permute-start(f32[2,432,128]{2,1,0:T(8,128)} %get-tuple-element.57), channel_id=1, source_target_pairs={{0,1},{1,0},{2,3},{3,2},{4,5},{5,4},{6,7},{7,6},{8,9},{9,8},{10,11... | collective-permute-start | bytes 1327112 | tf_op jit(solution)/shard_map/ppermute | solution.py:610
  35.1 22.7 %collective-permute-start.14 = (f32[2,432,128]{2,1,0:T(8,128)}, f32[2,432,128]{2,1,0:T(8,128)S(1)}, u32[]{:S(2)}, u32[]{:S(2)}) collective-permute-start(f32[2,432,128]{2,1,0:T(8,128)} %copy-done.49), channel_id=1, source_target_pairs={{0,1},{1,0},{2,3},{3,2},{4,5},{5,4},{6,7},{7,6},{8,9},{9,8},{10,11... | collective-permute-start | bytes 1327112 | tf_op jit(solution)/shard_map/ppermute | solution.py:610
  37.1 8.5 %collective-permute-start.12 = (f32[432,128]{1,0:T(8,128)}, f32[432,128]{1,0:T(8,128)}, u32[]{:S(2)}, u32[]{:S(2)}) collective-permute-start(f32[432,128]{1,0:T(8,128)} %copy-done.54), channel_id=1, source_target_pairs={{2,0},{4,2},{1,3},{6,4},{3,5},{5,7},{10,8},{12,10},{9,11},{14,12},... | collective-permute-start | bytes 663560 | tf_op jit(solution)/shard_map/ppermute | solution.py:616
  40.2 9.4 %collective-permute-start.8 = (f32[432,128]{1,0:T(8,128)}, f32[432,128]{1,0:T(8,128)}, u32[]{:S(2)}, u32[]{:S(2)}) collective-permute-start(f32[432,128]{1,0:T(8,128)} %copy-done.53), channel_id=1, source_target_pairs={{2,0},{4,2},{1,3},{6,4},{3,5},{5,7},{10,8},{12,10},{9,11},{14,12},... | collective-permute-start | bytes 663560 | tf_op jit(solution)/shard_map/ppermute | solution.py:616
  42.6 24.7 %collective-permute-start.9 = (f32[2,432,128]{2,1,0:T(8,128)}, f32[2,432,128]{2,1,0:T(8,128)S(1)}, u32[]{:S(2)}, u32[]{:S(2)}) collective-permute-start(f32[2,432,128]{2,1,0:T(8,128)} %copy-done.51), channel_id=1, source_target_pairs={{0,1},{1,0},{2,3},{3,2},{4,5},{5,4},{6,7},{7,6},{8,9},{9,8},{10,11... | collective-permute-start | bytes 1327112 | tf_op jit(solution)/shard_map/ppermute | solution.py:610
  45.6 31.1 %collective-permute-start.10 = (f32[2,432,128]{2,1,0:T(8,128)}, f32[2,432,128]{2,1,0:T(8,128)S(1)}, u32[]{:S(2)}, u32[]{:S(2)}) collective-permute-start(f32[2,432,128]{2,1,0:T(8,128)} %copy-done.50), channel_id=1, source_target_pairs={{0,1},{1,0},{2,3},{3,2},{4,5},{5,4},{6,7},{7,6},{8,9},{9,8},{10,11... | collective-permute-start | bytes 1327112 | tf_op jit(solution)/shard_map/ppermute | solution.py:610
  49.6 36.6 %collective-permute-start.6 = (f32[2,432,128]{2,1,0:T(8,128)}, f32[2,432,128]{2,1,0:T(8,128)S(1)}, u32[]{:S(2)}, u32[]{:S(2)}) collective-permute-start(f32[2,432,128]{2,1,0:T(8,128)} %copy-done.48), channel_id=1, source_target_pairs={{0,1},{1,0},{2,3},{3,2},{4,5},{5,4},{6,7},{7,6},{8,9},{9,8},{10,11... | collective-permute-start | bytes 1327112 | tf_op jit(solution)/shard_map/ppermute | solution.py:610
  52.0 43.7 %collective-permute-start.5 = (f32[2,432,128]{2,1,0:T(8,128)}, f32[2,432,128]{2,1,0:T(8,128)S(1)}, u32[]{:S(2)}, u32[]{:S(2)}) collective-permute-start(f32[2,432,128]{2,1,0:T(8,128)} %copy-done.47), channel_id=1, source_target_pairs={{0,1},{1,0},{2,3},{3,2},{4,5},{5,4},{6,7},{7,6},{8,9},{9,8},{10,11... | collective-permute-start | bytes 1327112 | tf_op jit(solution)/shard_map/ppermute | solution.py:610
  57.7 47.4 %collective-permute-start.1 = (f32[2,432,128]{2,1,0:T(8,128)}, f32[2,432,128]{2,1,0:T(8,128)S(1)}, u32[]{:S(2)}, u32[]{:S(2)}) collective-permute-start(f32[2,432,128]{2,1,0:T(8,128)} %copy-done.46), channel_id=1, source_target_pairs={{0,1},{1,0},{2,3},{3,2},{4,5},{5,4},{6,7},{7,6},{8,9},{9,8},{10,11... | collective-permute-start | bytes 1327112 | tf_op jit(solution)/shard_map/ppermute | solution.py:610
  67.2 39.3 %collective-permute-start.15 = (f32[2,432,128]{2,1,0:T(8,128)S(1)}, f32[2,432,128]{2,1,0:T(8,128)S(1)}, u32[]{:S(2)}, u32[]{:S(2)}) collective-permute-start(f32[2,432,128]{2,1,0:T(8,128)S(1)} %collective-permute-done.14.refs_2_), channel_id=1, source_target_pairs={{0,2},{2,4},{3,1},{4,6},{5,3},{7,5},{8,10},{10,12},{11,9},{12,14},... | collective-permute-start | bytes 1327112 | tf_op jit(solution)/shard_map/ppermute | solution.py:613
  76.7 34.4 %collective-permute-start.11 = (f32[2,432,128]{2,1,0:T(8,128)S(1)}, f32[2,432,128]{2,1,0:T(8,128)S(1)}, u32[]{:S(2)}, u32[]{:S(2)}) collective-permute-start(f32[2,432,128]{2,1,0:T(8,128)S(1)} %collective-permute-done.10.refs_2_), channel_id=1, source_target_pairs={{0,2},{2,4},{3,1},{4,6},{5,3},{7,5},{8,10},{10,12},{11,9},{12,14},... | collective-permute-start | bytes 1327112 | tf_op jit(solution)/shard_map/ppermute | solution.py:613
  86.2 25.4 %collective-permute-start.7 = (f32[2,432,128]{2,1,0:T(8,128)S(1)}, f32[2,432,128]{2,1,0:T(8,128)S(1)}, u32[]{:S(2)}, u32[]{:S(2)}) collective-permute-start(f32[2,432,128]{2,1,0:T(8,128)S(1)} %collective-permute-done.6.refs_2_), channel_id=1, source_target_pairs={{0,2},{2,4},{3,1},{4,6},{5,3},{7,5},{8,10},{10,12},{11,9},{12,14},... | collective-permute-start | bytes 1327112 | tf_op jit(solution)/shard_map/ppermute | solution.py:613
  95.7 47.9 %collective-permute-start = (f32[2,432,128]{2,1,0:T(8,128)}, f32[2,432,128]{2,1,0:T(8,128)S(1)}, u32[]{:S(2)}, u32[]{:S(2)}) collective-permute-start(f32[2,432,128]{2,1,0:T(8,128)} %copy-done.45), channel_id=1, source_target_pairs={{0,1},{1,0},{2,3},{3,2},{4,5},{5,4},{6,7},{7,6},{8,9},{9,8},{10,11... | collective-permute-start | bytes 1327112 | tf_op jit(solution)/shard_map/ppermute | solution.py:610
  105.1 38.4 %collective-permute-start.2 = (f32[2,432,128]{2,1,0:T(8,128)S(1)}, f32[2,432,128]{2,1,0:T(8,128)S(1)}, u32[]{:S(2)}, u32[]{:S(2)}) collective-permute-start(f32[2,432,128]{2,1,0:T(8,128)S(1)} %collective-permute-done.1.refs_2_), channel_id=1, source_target_pairs={{0,2},{2,4},{3,1},{4,6},{5,3},{7,5},{8,10},{10,12},{11,9},{12,14},... | collective-permute-start | bytes 1327112 | tf_op jit(solution)/shard_map/ppermute | solution.py:613
  106.5 37.0 %collective-permute-start.3 = (f32[432,128]{1,0:T(8,128)}, f32[432,128]{1,0:T(8,128)S(1)}, u32[]{:S(2)}, u32[]{:S(2)}) collective-permute-start(f32[432,128]{1,0:T(8,128)} %copy-done.52), channel_id=1, source_target_pairs={{2,0},{4,2},{1,3},{6,4},{3,5},{5,7},{10,8},{12,10},{9,11},{14,12},... | collective-permute-start | bytes 663560 | tf_op jit(solution)/shard_map/ppermute | solution.py:616
  111.1 43.0 %collective-permute-start.26 = (f32[16,512]{1,0:T(8,128)S(1)}, f32[16,512]{1,0:T(8,128)S(1)}, u32[]{:S(2)}, u32[]{:S(2)}) collective-permute-start(f32[16,512]{1,0:T(8,128)S(1)} %maximum_maximum_fusion), channel_id=1, source_target_pairs={{0,2},{1,3},{2,0},{3,1},{4,6},{5,7},{6,4},{7,5},{8,10},{9,11},{10,... | collective-permute-start | bytes 98312 | tf_op jit(solution)/shard_map/ppermute | solution.py:619
  111.6 42.5 %collective-permute-start.27 = (f32[16,512]{1,0:T(8,128)S(1)}, f32[16,512]{1,0:T(8,128)S(1)}, u32[]{:S(2)}, u32[]{:S(2)}) collective-permute-start(f32[16,512]{1,0:T(8,128)S(1)} %maximum_maximum_fusion), channel_id=1, source_target_pairs={{2,4},{3,5},{4,2},{5,3},{10,12},{11,13},{12,10},{13,11},{18,20},{1... | collective-permute-start | bytes 98312 | tf_op jit(solution)/shard_map/ppermute | solution.py:619
  123.7 40.9 %copy-start.29 = (f32[432,128]{1,0:T(8,128)}, f32[432,128]{1,0:T(8,128)S(1)}, u32[]{:S(2)}) copy-start(f32[432,128]{1,0:T(8,128)S(1)} %get-tuple-element.74.refs_2_) | copy-start | bytes 663556
  123.7 44.0 %copy-start.23 = (f32[2,432,128]{2,1,0:T(8,128)}, f32[2,432,128]{2,1,0:T(8,128)S(1)}, u32[]{:S(2)}) copy-start(f32[2,432,128]{2,1,0:T(8,128)S(1)} %get-tuple-element.76.refs_4_) | copy-start | bytes 1327108
  133.6 26.9 %copy-start.27 = (f32[432,128]{1,0:T(8,128)}, f32[432,128]{1,0:T(8,128)S(1)}, u32[]{:S(2)}) copy-start(f32[432,128]{1,0:T(8,128)S(1)} %get-tuple-element.71.refs_2_) | copy-start | bytes 663556
  143.5 16.4 %copy-start.56 = (f32[8,3456]{1,0:T(8,128)S(1)}, f32[8,3456]{1,0:T(8,128)}, u32[]{:S(2)}) copy-start(f32[8,3456]{1,0:T(8,128)} %copy-done.55) | copy-start | bytes 331780
  143.5 52.3 %copy-start.41 = (f32[32,16]{1,0:T(8,128)S(1)}, f32[32,16]{1,0:T(8,128)}, u32[]{:S(2)}) copy-start(f32[32,16]{1,0:T(8,128)} %constant.79.clone.mat_ref) | copy-start | bytes 6148
  143.5 52.3 %copy-start.42 = (f32[16,8]{1,0:T(8,128)S(1)}, f32[16,8]{1,0:T(8,128)}, u32[]{:S(2)}) copy-start(f32[16,8]{1,0:T(8,128)} %constant.78.clone.gram_ref) | copy-start | bytes 1540
  152.6 3.2 collective-permute-start.19
  152.6 5.3 %collective-permute-start.18 = (f32[16,1024]{1,0:T(8,128)S(1)}, f32[16,1024]{1,0:T(8,128)S(1)}, u32[]{:S(2)}, u32[]{:S(2)}) collective-permute-start(f32[16,1024]{1,0:T(8,128)S(1)} %get-tuple-element.63), channel_id=1, source_target_pairs={{0,16},{8,24},{16,0},{24,8},{1,17},{9,25},{17,1},{25,9},{2,18},{10... | collective-permute-start | bytes 196616 | tf_op jit(solution)/shard_map/ppermute | solution.py:624
  153.8 4.3 %collective-permute-start.17 = (f32[16,1024]{1,0:T(8,128)S(1)}, f32[16,1024]{1,0:T(8,128)S(1)}, u32[]{:S(2)}, u32[]{:S(2)}) collective-permute-start(f32[16,1024]{1,0:T(8,128)S(1)} %get-tuple-element.63), channel_id=1, source_target_pairs={{0,8},{8,16},{16,24},{24,0},{1,9},{9,17},{17,25},{25,1},{2,10},{10... | collective-permute-start | bytes 196616 | tf_op jit(solution)/shard_map/ppermute | solution.py:624
  154.1 15.6 %collective-permute-start.28 = (f32[3,16,512]{2,1,0:T(8,128)S(1)}, f32[3,16,512]{2,1,0:T(8,128)S(1)}, u32[]{:S(2)}, u32[]{:S(2)}) collective-permute-start(f32[3,16,512]{2,1,0:T(8,128)S(1)} %pad_maximum_fusion.near_ref), channel_id=1, source_target_pairs={{0,1},{1,0},{2,3},{3,2},{4,5},{5,4},{6,7},{7,6},{8,9},{9,8},{10,11... | collective-permute-start | bytes 294920 | tf_op jit(solution)/shard_map/ppermute | solution.py:610
  158.2 10.8 %collective-permute-start.20 = (f32[16,1024]{1,0:T(8,128)S(1)}, f32[16,1024]{1,0:T(8,128)S(1)}, u32[]{:S(2)}, u32[]{:S(2)}) collective-permute-start(f32[16,1024]{1,0:T(8,128)S(1)} %add_add_fusion.1), channel_id=1, source_target_pairs={{0,1},{1,0},{2,3},{3,2},{4,5},{5,4},{6,7},{7,6},{8,9},{9,8},{10,11... | collective-permute-start | bytes 196616 | tf_op jit(solution)/shard_map/ppermute | solution.py:610
  160.5 27.0 %collective-permute-start.34 = (f32[432,128]{1,0:T(8,128)S(1)}, f32[432,128]{1,0:T(8,128)S(1)}, u32[]{:S(2)}, u32[]{:S(2)}) collective-permute-start(f32[432,128]{1,0:T(8,128)S(1)} %get-tuple-element.71.refs_2_), channel_id=1, source_target_pairs={{2,0},{4,2},{1,3},{6,4},{3,5},{5,7},{10,8},{12,10},{9,11},{14,12},... | collective-permute-start | bytes 663560 | tf_op jit(solution)/shard_map/ppermute | solution.py:616
  164.6 25.0 %collective-permute-start.36 = (f32[432,128]{1,0:T(8,128)S(1)}, f32[432,128]{1,0:T(8,128)S(1)}, u32[]{:S(2)}, u32[]{:S(2)}) collective-permute-start(f32[432,128]{1,0:T(8,128)S(1)} %get-tuple-element.74.refs_2_), channel_id=1, source_target_pairs={{2,0},{4,2},{1,3},{6,4},{3,5},{5,7},{10,8},{12,10},{9,11},{14,12},... | collective-permute-start | bytes 663560 | tf_op jit(solution)/shard_map/ppermute | solution.py:616
  167.7 23.9 %collective-permute-start.35 = (f32[2,432,128]{2,1,0:T(8,128)S(1)}, f32[2,432,128]{2,1,0:T(8,128)S(1)}, u32[]{:S(2)}, u32[]{:S(2)}) collective-permute-start(f32[2,432,128]{2,1,0:T(8,128)S(1)} %get-tuple-element.76.refs_4_), channel_id=1, source_target_pairs={{0,2},{2,4},{3,1},{4,6},{5,3},{7,5},{8,10},{10,12},{11,9},{12,14},... | collective-permute-start | bytes 1327112 | tf_op jit(solution)/shard_map/ppermute | solution.py:613
  169.0 5.3 %collective-permute-start.22 = (f32[16,1024]{1,0:T(8,128)S(1)}, f32[16,1024]{1,0:T(8,128)S(1)}, u32[]{:S(2)}, u32[]{:S(2)}) collective-permute-start(f32[16,1024]{1,0:T(8,128)S(1)} %add.86.sum_ref), channel_id=1, source_target_pairs={{2,4},{3,5},{4,2},{5,3},{10,12},{11,13},{12,10},{13,11},{18,20},{1... | collective-permute-start | bytes 196616 | tf_op jit(solution)/shard_map/ppermute | solution.py:619
  169.7 21.9 %copy-start.35 = (f32[3,16,512]{2,1,0:T(8,128)}, f32[3,16,512]{2,1,0:T(8,128)S(1)}, u32[]{:S(2)}) copy-start(f32[3,16,512]{2,1,0:T(8,128)S(1)} %collective-permute-done.28.far_ref) | copy-start | bytes 294916
  169.7 15.2 %collective-permute-start.21 = (f32[16,1024]{1,0:T(8,128)S(1)}, f32[16,1024]{1,0:T(8,128)S(1)}, u32[]{:S(2)}, u32[]{:S(2)}) collective-permute-start(f32[16,1024]{1,0:T(8,128)S(1)} %add.86.sum_ref), channel_id=1, source_target_pairs={{0,2},{1,3},{2,0},{3,1},{4,6},{5,7},{6,4},{7,5},{8,10},{9,11},{10,... | collective-permute-start | bytes 196616 | tf_op jit(solution)/shard_map/ppermute | solution.py:619
  175.0 68.6 %collective-permute-start.30 = (f32[432,128]{1,0:T(8,128)}, f32[432,128]{1,0:T(8,128)}, u32[]{:S(2)}, u32[]{:S(2)}) collective-permute-start(f32[432,128]{1,0:T(8,128)} %get-tuple-element.65.refs_2_), channel_id=1, source_target_pairs={{2,0},{4,2},{1,3},{6,4},{3,5},{5,7},{10,8},{12,10},{9,11},{14,12},... | collective-permute-start | bytes 663560 | tf_op jit(solution)/shard_map/ppermute | solution.py:616
  185.6 47.2 %collective-permute-start.32 = (f32[432,128]{1,0:T(8,128)S(1)}, f32[432,128]{1,0:T(8,128)}, u32[]{:S(2)}, u32[]{:S(2)}) collective-permute-start(f32[432,128]{1,0:T(8,128)S(1)} %get-tuple-element.68.refs_2_), channel_id=1, source_target_pairs={{2,0},{4,2},{1,3},{6,4},{3,5},{5,7},{10,8},{12,10},{9,11},{14,12},... | collective-permute-start | bytes 663560 | tf_op jit(solution)/shard_map/ppermute | solution.py:616
  188.3 55.2 %collective-permute-start.29 = (f32[2,432,128]{2,1,0:T(8,128)}, f32[2,432,128]{2,1,0:T(8,128)}, u32[]{:S(2)}, u32[]{:S(2)}) collective-permute-start(f32[2,432,128]{2,1,0:T(8,128)} %get-tuple-element.67.refs_4_), channel_id=1, source_target_pairs={{0,2},{2,4},{3,1},{4,6},{5,3},{7,5},{8,10},{10,12},{11,9},{12,14},... | collective-permute-start | bytes 1327112 | tf_op jit(solution)/shard_map/ppermute | solution.py:613
  190.3 42.5 %collective-permute-start.31 = (f32[2,432,128]{2,1,0:T(8,128)}, f32[2,432,128]{2,1,0:T(8,128)}, u32[]{:S(2)}, u32[]{:S(2)}) collective-permute-start(f32[2,432,128]{2,1,0:T(8,128)} %get-tuple-element.70.refs_4_), channel_id=1, source_target_pairs={{0,2},{2,4},{3,1},{4,6},{5,3},{7,5},{8,10},{10,12},{11,9},{12,14},... | collective-permute-start | bytes 1327112 | tf_op jit(solution)/shard_map/ppermute | solution.py:613
  192.4 26.6 %collective-permute-start.33 = (f32[2,432,128]{2,1,0:T(8,128)}, f32[2,432,128]{2,1,0:T(8,128)}, u32[]{:S(2)}, u32[]{:S(2)}) collective-permute-start(f32[2,432,128]{2,1,0:T(8,128)} %get-tuple-element.73.refs_4_), channel_id=1, source_target_pairs={{0,2},{2,4},{3,1},{4,6},{5,3},{7,5},{8,10},{10,12},{11,9},{12,14},... | collective-permute-start | bytes 1327112 | tf_op jit(solution)/shard_map/ppermute | solution.py:613
  195.7 37.0 %copy-start.5 = (f32[5,432,128]{2,1,0:T(8,128)S(1)}, f32[5,432,128]{2,1,0:T(8,128)}, u32[]{:S(2)}) copy-start(f32[5,432,128]{2,1,0:T(8,128)} %copy-done.4) | copy-start | bytes 3317764
  215.3 28.2 %copy-start.7 = (f32[5,432,128]{2,1,0:T(8,128)S(1)}, f32[5,432,128]{2,1,0:T(8,128)}, u32[]{:S(2)}) copy-start(f32[5,432,128]{2,1,0:T(8,128)} %copy-done.6) | copy-start | bytes 3317764
  232.8 42.6 %copy-start.43 = (f32[16,8]{1,0:T(8,128)S(1)}, f32[16,8]{1,0:T(8,128)}, u32[]{:S(2)}) copy-start(f32[16,8]{1,0:T(8,128)} %constant.78.clone.gram_ref) | copy-start | bytes 1540
  254.3 50.1 %copy-start.15 = (f32[4,432,128]{2,1,0:T(8,128)S(1)}, f32[4,432,128]{2,1,0:T(8,128)}, u32[]{:S(2)}) copy-start(f32[4,432,128]{2,1,0:T(8,128)} %copy-done.14) | copy-start | bytes 2654212
  254.3 2.2 collective-permute-start.39
  254.3 5.0 %collective-permute-start.38 = (f32[16,1024]{1,0:T(8,128)S(1)}, f32[16,1024]{1,0:T(8,128)S(1)}, u32[]{:S(2)}, u32[]{:S(2)}) collective-permute-start(f32[16,1024]{1,0:T(8,128)S(1)} %get-tuple-element.82), channel_id=1, source_target_pairs={{0,16},{8,24},{16,0},{24,8},{1,17},{9,25},{17,1},{25,9},{2,18},{10... | collective-permute-start | bytes 196616 | tf_op jit(solution)/shard_map/ppermute | solution.py:624
  255.0 4.5 %collective-permute-start.37 = (f32[16,1024]{1,0:T(8,128)S(1)}, f32[16,1024]{1,0:T(8,128)S(1)}, u32[]{:S(2)}, u32[]{:S(2)}) collective-permute-start(f32[16,1024]{1,0:T(8,128)S(1)} %get-tuple-element.82), channel_id=1, source_target_pairs={{0,8},{8,16},{16,24},{24,0},{1,9},{9,17},{17,25},{25,1},{2,10},{10... | collective-permute-start | bytes 196616 | tf_op jit(solution)/shard_map/ppermute | solution.py:624
  259.5 6.0 %collective-permute-start.40 = (f32[16,1024]{1,0:T(8,128)S(1)}, f32[16,1024]{1,0:T(8,128)S(1)}, u32[]{:S(2)}, u32[]{:S(2)}) collective-permute-start(f32[16,1024]{1,0:T(8,128)S(1)} %add_add_fusion), channel_id=1, source_target_pairs={{0,1},{1,0},{2,3},{3,2},{4,5},{5,4},{6,7},{7,6},{8,9},{9,8},{10,11... | collective-permute-start | bytes 196616 | tf_op jit(solution)/shard_map/ppermute | solution.py:610
  262.6 22.7 %collective-permute-start.46 = (f32[4,432,128]{2,1,0:T(8,128)}, f32[4,432,128]{2,1,0:T(8,128)S(1)}, u32[]{:S(2)}, u32[]{:S(2)}) collective-permute-start(f32[4,432,128]{2,1,0:T(8,128)} %get-tuple-element.92), channel_id=1, source_target_pairs={{0,1},{1,0},{2,3},{3,2},{4,5},{5,4},{6,7},{7,6},{8,9},{9,8},{10,11... | collective-permute-start | bytes 2654216 | tf_op jit(solution)/shard_map/ppermute | solution.py:610
  262.7 41.7 %collective-permute-start.45 = (f32[4,432,128]{2,1,0:T(8,128)}, f32[4,432,128]{2,1,0:T(8,128)}, u32[]{:S(2)}, u32[]{:S(2)}) collective-permute-start(f32[4,432,128]{2,1,0:T(8,128)} %get-tuple-element.90), channel_id=1, source_target_pairs={{0,1},{1,0},{2,3},{3,2},{4,5},{5,4},{6,7},{7,6},{8,9},{9,8},{10,11... | collective-permute-start | bytes 2654216 | tf_op jit(solution)/shard_map/ppermute | solution.py:610
  264.6 58.7 %collective-permute-start.44 = (f32[4,432,128]{2,1,0:T(8,128)}, f32[4,432,128]{2,1,0:T(8,128)}, u32[]{:S(2)}, u32[]{:S(2)}) collective-permute-start(f32[4,432,128]{2,1,0:T(8,128)} %get-tuple-element.88), channel_id=1, source_target_pairs={{0,1},{1,0},{2,3},{3,2},{4,5},{5,4},{6,7},{7,6},{8,9},{9,8},{10,11... | collective-permute-start | bytes 2654216 | tf_op jit(solution)/shard_map/ppermute | solution.py:610
  265.6 75.1 %collective-permute-start.41 = (f32[4,432,128]{2,1,0:T(8,128)}, f32[4,432,128]{2,1,0:T(8,128)S(1)}, u32[]{:S(2)}, u32[]{:S(2)}) collective-permute-start(f32[4,432,128]{2,1,0:T(8,128)} %get-tuple-element.83), channel_id=1, source_target_pairs={{0,1},{1,0},{2,3},{3,2},{4,5},{5,4},{6,7},{7,6},{8,9},{9,8},{10,11... | collective-permute-start | bytes 2654216 | tf_op jit(solution)/shard_map/ppermute | solution.py:610
  267.7 0.7 collective-permute-start.43
  268.3 7.0 %collective-permute-start.42 = (f32[16,1024]{1,0:T(8,128)S(1)}, f32[16,1024]{1,0:T(8,128)S(1)}, u32[]{:S(2)}, u32[]{:S(2)}) collective-permute-start(f32[16,1024]{1,0:T(8,128)S(1)} %add.93.sum_ref), channel_id=1, source_target_pairs={{0,2},{1,3},{2,0},{3,1},{4,6},{5,7},{6,4},{7,5},{8,10},{9,11},{10,... | collective-permute-start | bytes 196616 | tf_op jit(solution)/shard_map/ppermute | solution.py:619
  304.4 19.0 %copy-start.17 = (f32[4,432,128]{2,1,0:T(8,128)S(1)}, f32[4,432,128]{2,1,0:T(8,128)}, u32[]{:S(2)}) copy-start(f32[4,432,128]{2,1,0:T(8,128)} %copy-done.16) | copy-start | bytes 2654212
  304.4 19.0 %copy-start.22 = (bf16[48,512]{1,0:T(8,128)(2,1)S(1)}, bf16[48,512]{1,0:T(8,128)(2,1)}, u32[]{:S(2)}) copy-start(bf16[48,512]{1,0:T(8,128)(2,1)} %copy-done.20) | copy-start | bytes 147460
  323.4 17.3 %copy-start.19 = (f32[4,432,128]{2,1,0:T(8,128)S(1)}, f32[4,432,128]{2,1,0:T(8,128)}, u32[]{:S(2)}) copy-start(f32[4,432,128]{2,1,0:T(8,128)} %copy-done.18) | copy-start | bytes 2654212
  (42 other events, 44.9 us)

commit v2 on v1

--- a/solution.py
+++ b/solution.py
@@ -8,6 +8,7 @@
 from jax.experimental import pallas as pl
 from jax.experimental.pallas import tpu as pltpu
 from jax.sharding import PartitionSpec as P
+
 
 STEP_RATIO = 0.1
 SOURCE_WEIGHT = 0.5
@@ -19,12 +20,20 @@
 BLOCK_ROWS = 2 * STRIP_ROWS
 SPAN = 3 * BLOCK_ROWS
 GROUP = 16
+BLOCK = 144
 F32 = jnp.float32
 BF16 = jnp.bfloat16
 
 
 def params(**more):
-    return pltpu.CompilerParams(vmem_limit_bytes=40 * 1024 * 1024, **more)
+    return pltpu.CompilerParams(vmem_limit_bytes=62 * 1024 * 1024, **more)
+
+
+def chunk_blocks(blocks):
+    if blocks % 12 == 0:
+        unit = blocks // 12
+        return [4 * unit, 4 * unit, 3 * unit, unit]
+    return [1] * blocks if blocks < 4 else [blocks - blocks // 2, blocks // 2]
 
 
 def moment_rows(vel_x, vel_y, vel_z, volume, lib):
@@ -45,7 +54,7 @@
         energy * vel_y,
         energy * vel_z,
     ]
-    return lib.stack(rows) * weight
+    return lib.stack([row * weight for row in rows])
 
 
 def state_rows(vel_x, vel_y, vel_z, lib):
@@ -100,10 +109,6 @@
     return out.astype(np.float32)
 
 
-def rounded(value):
-    return lax.reduce_precision(value, 8, 7)
-
-
 def minmod(left, right):
     low = jnp.minimum(left, right)
     high = jnp.maximum(left, right)
@@ -114,7 +119,8 @@
     return pl.ds(start, count, stride=STRIP_ROWS)
 
 
-def pack_kernel(size, side_ref, far_ref, own_ref, mid_ref, edge_ref, down_ref):
+def pack_kernel(size, side_ref, far_ref, own_ref, *rest):
+    mid_ref, edge_ref, down_ref = rest[-3:]
     side = side_ref[0]
     for i in range(4):
         row = jnp.where(side == 1, i, 3 - i)
@@ -126,7 +132,7 @@
     down_ref[...] = own_ref[strided(jnp.where(side == 1, 3, 0), size), :]
 
 
-def pack(side, flat, half, chunk, first, size):
+def pack(side, flat, half, chunk, first, size, earlier):
     steps = chunk // size
     shift = half // size
     begin = first // size
@@ -143,6 +149,7 @@
             in_specs=[
                 pl.BlockSpec((4 * size, LANES), lambda i, s: ((1 - s[0]) * shift + begin + i, 0)),
                 pl.BlockSpec((4 * size, LANES), lambda i, s: (s[0] * shift + begin + i, 0)),
+                *[pl.BlockSpec(memory_space=pl.ANY)] * len(earlier),
             ],
             out_specs=[
                 pl.BlockSpec((2, size, LANES), lambda i, s: (0, i, 0)),
@@ -155,7 +162,63 @@
         cost_estimate=pl.CostEstimate(
             flops=0, transcendentals=0, bytes_accessed=chunk * LANES * 4 * 13
         ),
-    )(side, flat, flat)
+    )(side, flat, flat, *earlier)
+
+
+def prepare_kernel(points, vel_ref, earlier_ref, table_ref, const_ref, weight_ref):
+    comps = (vel_ref[0].astype(F32) - (points - 1) / 2.0) * (8.0 / points)
+    vel_x, vel_y, vel_z = comps[0:1], comps[1:2], comps[2:3]
+    moments = jnp.concatenate(
+        [row[0] for row in moment_rows(vel_x, vel_y, vel_z, (8.0 / points) ** 3, jnp)[:, None]]
+        + [jnp.zeros_like(vel_x)] * 3
+    )
+    high = moments.astype(BF16)
+    weight_ref[0, 0:16] = high
+    weight_ref[0, 16:32] = (moments - high.astype(F32)).astype(BF16)
+    shapes = jnp.concatenate([row[0] for row in state_rows(vel_x, vel_y, vel_z, jnp)[:, None]])
+    part_a = shapes.astype(BF16).astype(F32)
+    part_b = (shapes - part_a).astype(BF16).astype(F32)
+    part_c = shapes - part_a - part_b
+    factors = jnp.concatenate(
+        [
+            STEP_RATIO * jnp.abs(vel_x),
+            STEP_RATIO * jnp.abs(vel_y),
+            jnp.where(vel_y > 0, 0.5, -0.5),
+            jnp.zeros((13, vel_x.shape[1]), F32),
+        ]
+    )
+    rows = jnp.concatenate([part_a, part_a, part_a, part_b, part_b, part_c, factors])
+    columns = rows.T
+    table_ref[...] = columns[:, :48].astype(BF16)
+    const_ref[...] = columns[:, 48:56]
+
+
+def prepare(points, vel_index, size, earlier):
+    count = vel_index.shape[1]
+    blocks = vel_index.reshape(3, count // size, size).transpose(1, 0, 2)
+    return pl.pallas_call(
+        functools.partial(prepare_kernel, points),
+        out_shape=(
+            jax.ShapeDtypeStruct((count, 48), BF16),
+            jax.ShapeDtypeStruct((count, 8), F32),
+            jax.ShapeDtypeStruct((count // size, 32, size), BF16),
+        ),
+        grid=(count // size,),
+        in_specs=[
+            pl.BlockSpec((1, 3, size), lambda i: (i, 0, 0)),
+            pl.BlockSpec(memory_space=pl.ANY),
+        ],
+        out_specs=[
+            pl.BlockSpec((size, 48), lambda i: (i, 0)),
+            pl.BlockSpec((size, 8), lambda i: (i, 0)),
+            pl.BlockSpec((1, 32, size), lambda i: (i, 0, 0)),
+        ],
+        compiler_params=params(),
+        name="prepare",
+        cost_estimate=pl.CostEstimate(
+            flops=200 * count, transcendentals=count, bytes_accessed=count * 2000
+        ),
+    )(blocks, earlier)
 
 
 def split_store(value, first_ref, second_ref, rows, columns):
@@ -501,7 +564,7 @@
     state_ref[...] = span_ref[8:16, spot]
 
 
-def macro(kernel, info, args, outs, scratch, name):
+def macro(kernel, info, args, outs, scratch):
     vmem = pl.BlockSpec(memory_space=pltpu.VMEM)
     return pl.pallas_call(
         kernel,
@@ -510,7 +573,6 @@
         out_specs=[vmem] * len(outs),
         scratch_shapes=scratch,
         compiler_params=params(),
-        name=name,
         cost_estimate=pl.CostEstimate(flops=4000000, transcendentals=0, bytes_accessed=1000000),
     )(info, *args)
 
@@ -582,9 +644,10 @@
     strips = lax.axis_size("strip")
     groups = lax.axis_size("vel")
     strip = lax.axis_index("strip")
-    size = 144
-    pieces = next(k for k in (4, 3, 2, 1) if (half // size) % k == 0)
-    chunk = half // pieces
+    size = BLOCK
+    chunks = [size * n for n in chunk_blocks(half // size)]
+    firsts = [sum(chunks[:c]) for c in range(len(chunks))]
+    order = range(len(chunks))
     side = (strip % 2).astype(jnp.int32).reshape(1)
     info = jnp.stack([strip % 2, (strip // 2) % 2]).astype(jnp.int32)
 
@@ -631,42 +694,18 @@
     cell_pair = jnp.concatenate([collision_rate, wall])
     other_cells = swap(cell_pair)
 
-    packed = [pack(side, flat, half, chunk, c * chunk, size) for c in range(pieces)]
     got = []
-    for mid, edge, down in packed:
+    earlier = []
+    for c in order:
+        mid, edge, down = pack(side, flat, half, chunks[c], firsts[c], size, earlier)
+        earlier = [down]
         edge_here = swap(edge)
         mid_here = swap(mid)
-        got.append((mid_here, edge_here, with_flow(edge_here), against_flow(down)))
-
-    comps = (vel_index.astype(F32) - (points - 1) / 2.0) * (8.0 / points)
-    moment_table = jnp.pad(moment_rows(comps[0], comps[1], comps[2], (8.0 / points) ** 3, jnp), ((0, 3), (0, 0)))
-    weight_high = rounded(moment_table)
-    weight_low = rounded(moment_table - weight_high)
-    weights = (
-        jnp.concatenate([weight_high, weight_low])
-        .astype(BF16)
-        .reshape(32, count // size, size)
-        .transpose(1, 0, 2)
-    )
-    shape_rows = state_rows(comps[0], comps[1], comps[2], jnp)
-    part_a = rounded(shape_rows)
-    part_b = rounded(shape_rows - part_a)
-    part_c = rounded(shape_rows - part_a - part_b)
-    table = jnp.concatenate([part_a, part_a, part_a, part_b, part_b, part_c]).astype(BF16).T
-    zero = jnp.zeros_like(comps[0])
-    const = jnp.stack(
-        [
-            STEP_RATIO * jnp.abs(comps[0]),
-            STEP_RATIO * jnp.abs(comps[1]),
-            jnp.where(comps[1] > 0, 0.5, -0.5),
-            zero,
-            zero,
-            zero,
-            zero,
-            zero,
-        ]
-    ).T
-    tables = (table, const, weights)
+        below = against_flow(down)
+        got.append((edge_here, mid_here, below))
+
+    tables = prepare(points, vel_index, size, earlier[0])
+    table, _, weights = tables
     gram = jnp.asarray(target_moments(points))
     mat = jnp.asarray(macro_matrix())
 
@@ -690,72 +729,67 @@
     width = BLOCK_ROWS * LANES
     sums = jnp.zeros((16, width), F32)
     kept = []
-    for c in range(pieces):
-        mid_here, edge_here, above, below = got[c]
+    for c in order:
+        edge_here, mid_here, below = got[c]
+        above = with_flow(edge_here)
         first, middle, edge, sums = transport(
-            side, [flat, mid_here, edge_here, above, below], tables, cells, sums,
-            half, chunk, c * chunk, size,
+            side, [flat, mid_here, edge_here, above, below],
+            tables, cells, sums, half, chunks[c], firsts[c], size,
         )
-        kept.append((first, middle, edge, with_flow(edge), against_flow(first)))
-
-    def exchange(value):
-        value = sum_groups(value)
-        value = value + swap(value)
-        return value, both_z(value)
-
-    own_sum, (sum_a, sum_b) = exchange(sums)
+        above = with_flow(edge)
+        below = against_flow(first)
+        kept.append((first, middle, edge, above, below))
+
+    total = sum_groups(sums)
+    total = total + swap(total)
+    sum_a, sum_b = both_z(total)
     change, keep = macro(
         first_macro_kernel, info,
-        [own_sum, sum_a, sum_b, near_home, far_home, gram, mat],
+        [total, sum_a, sum_b, near_home, far_home, gram, mat],
         [
             jax.ShapeDtypeStruct((48, 11 * LANES), BF16),
             jax.ShapeDtypeStruct((16, SPAN * LANES), F32),
         ],
         [pltpu.VMEM((16, SPAN * LANES), F32)] * 2,
-        "first_macro",
     )
 
     sums = jnp.zeros((16, width), F32)
-    near, far = [], []
-    for c in range(pieces):
-        near_part, far_part, sums = transport(
-            side, list(kept[c]), tables, cells, sums, half, chunk, c * chunk, size, change
+    near, far, back = {}, {}, {}
+    for c in reversed(order):
+        near[c], far[c], sums = transport(
+            side, list(kept[c]), tables, cells, sums, half, chunks[c], firsts[c], size, change
         )
-        near.append(near_part)
-        far.append(far_part)
-    back = [swap(part) for part in far[:-1]]
-    own_sum, (sum_a, sum_b) = exchange(sums)
-    last, own_sum = lax.optimization_barrier((far[-1], own_sum))
-    back.append(swap(last))
+        back[c] = swap(far[c])
+    total = sum_groups(sums)
+    total = total + swap(total)
+    sum_a, sum_b = both_z(total)
     change, state = macro(
         second_macro_kernel, info,
-        [own_sum, sum_a, sum_b, keep, gram, mat],
+        [total, sum_a, sum_b, keep, gram, mat],
         [
             jax.ShapeDtypeStruct((48, STRIP_ROWS * LANES), BF16),
             jax.ShapeDtypeStruct((8, STRIP_ROWS * LANES), F32),
         ],
         [pltpu.VMEM((16, SPAN * LANES), F32)],
-        "second_macro",
     )
     out = None
-    for c in range(pieces):
-        out = finish(side, out, near[c], back[c], table, change, half, chunk, c * chunk, size)
+    for c in reversed(order):
+        out = finish(side, out, near[c], back[c], table, change, half, chunks[c], firsts[c], size)
     return out.reshape(dist.shape), state[:5].reshape(5, rows, cols)
 
 
 def solution(mesh):
-    groups = mesh.shape["vel"]
-
     def whole(dist, cell_type, collision_rate, vel_index):
         points = round(vel_index.shape[1] ** (1.0 / 3.0))
         in_specs = (P("vel", "strip", None), P("strip", None), P("strip", None), P(None, "vel"))
         out_specs = (P("vel", "strip", None), P(None, "strip", None))
-        return jax.shard_map(
-            functools.partial(per_device, points),
-            mesh=mesh,
-            in_specs=in_specs,
-            out_specs=out_specs,
-            check_vma=False,
-        )(dist, cell_type, collision_rate, vel_index)
+
+        def body(*args):
+            return per_device(points, *args)
+
+        run = jax.shard_map(
+            body, mesh=mesh, in_specs=in_specs, out_specs=out_specs, check_vma=False
+        )
+        return run(dist, cell_type, collision_rate, vel_index)
 
     return whole

time: 348 us -> 386 us (1.11)
  Pallas kernels: 97.6 us -> 144 us
  local copies, waits for them, and re-layouts: 49.5 us -> 8.14 us
  starting transfers between devices: 76 us -> 105 us
    unnamed x118 -> x58, local copies, waits for them, and re-layouts: 44.9 us -> 5.2 us
    ppermute x3, starting transfers between devices: 9.2 us -> 36 us  [both_z(): lax.ppermute(value, 'strip', pair_a)]
    pallas_call x0 -> x1, Pallas kernels: none -> 12.9 us  [prepare(): pl.pallas_call(functools.partial(prepare_kernel, points), out_shape=(jax....]
    pallas_call x4, Pallas kernels: 2.29 us -> 12.7 us  [pack(): pl.pallas_call(functools.partial(pack_kernel, size), out_shape=(jax.Shape...]
    pallas_call x1, Pallas kernels: 4.72 us -> 15 us  [home_moments(): pl.pallas_call(functools.partial(moment_kernel, size), out_shape=jax.Shap...]
    pallas_call x8, Pallas kernels: 71.1 us -> 77.7 us  [transport(): pl.pallas_call(functools.partial(transport_kernel, size, second_pass), ou...]
    ppermute x16, starting transfers between devices: 19 us -> 24.1 us  [swap(): return lax.ppermute(value, 'strip', swap_pairs)]
    pallas_call x4, Pallas kernels: 16 us -> 20.5 us  [finish(): pl.pallas_call(functools.partial(finish_kernel, size), out_shape=jax.Shap...]
  transfers between devices with their start and end apart: 47 -> 47, of which waited for: 20 -> 13; matrix products, arithmetic and copies ran while one was open for 2% -> 2% of each run, Pallas kernels for 23% -> 33%
where the time goes in v2:
time: 386 us; the launch traced here: 380 us
  Pallas kernels  144 us (37%)
  waiting for transfers between devices  117 us (30%)
  starting transfers between devices  105 us (27%)
  local copies, waits for them, and re-layouts  8.14 us (2%)
  other arithmetic  3.92 us (1%)
    ppermute x16, waiting for transfers between devices, swap(): return lax.ppermute(value, 'strip', swap_pairs)  100 us
    pallas_call x8, Pallas kernels, transport(): pl.pallas_call(functools.partial(transport_kernel, size, second_pass), ou...  77.7 us
    ppermute x3, starting transfers between devices, both_z(): lax.ppermute(value, 'strip', pair_a)  36 us
    ppermute x8, starting transfers between devices, against_flow(): return lax.ppermute(value, 'strip', up_pairs)  28 us
    ppermute x16, starting transfers between devices, swap(): return lax.ppermute(value, 'strip', swap_pairs)  24.1 us
    pallas_call x4, Pallas kernels, finish(): pl.pallas_call(functools.partial(finish_kernel, size), out_shape=jax.Shap...  20.5 us
    pallas_call x1, Pallas kernels, home_moments(): pl.pallas_call(functools.partial(moment_kernel, size), out_shape=jax.Shap...  15 us
    pallas_call x1, Pallas kernels, prepare(): pl.pallas_call(functools.partial(prepare_kernel, points), out_shape=(jax....  12.9 us
  transfers between devices with their start and end apart: 47, of which 13 were waited for; matrix products, arithmetic and copies ran while one was open for 2% of the time, Pallas kernels for 33%

profile of v2, /device:TPU:24, one launch (start us, length us, event | category | flops | bytes accessed | tf_op | source)
XLA Modules:
  0.0 380.4 jit_solution(3219670939584443513)
XLA Ops:
  0.6 3.8 pack.4
  4.4 3.8 pack.5
  8.2 3.3 pack.6
  11.5 2.5 collective-permute-start.8
  14.0 1.8 pack.7
  16.6 12.9 %prepare.1 = (bf16[3456,48]{1,0:T(8,128)(2,1)}, f32[3456,8]{1,0:T(8,128)}, bf16[24,32,144]{2,1,0:T(8,128)(2,1)}) custom-call(s32[24,3,144]{2,1,0:T(4,128)} %bitcast.29, f32[144,128]{1,0:T(8,128)} %get-tuple-element.52.earlier_ref), custom_call_target="tpu_custom_call" | custom-call | flops 691200 | bytes 6912000 | tf_op jit(solution)/shard_map/prepare/pallas_call | solution.py:199
  29.5 15.0 %home_moments.1 = f32[16,512]{1,0:T(8,128)} custom-call(f32[13824,128]{1,0:T(8,128)} %bitcast.23, bf16[24,32,144]{2,1,0:T(8,128)(2,1)} %get-tuple-element.57.refs_6_.weight_ref.refs_8_), custom_call_target="tpu_custom_call" | custom-call | flops 169869312 | bytes 7077888 | tf_op jit(solution)/shard_map/home_moments/pallas_call | solution.py:251
  47.1 1.4 collective-permute-start.1
  49.4 1.0 collective-permute-start.5
  51.2 2.1 collective-permute-start.26
  54.0 1.2 collective-permute-done.26
  56.2 1.1 collective-permute-start.10
  57.2 4.8 %collective-permute-start.16 = (f32[576,128]{1,0:T(8,128)S(1)}, f32[576,128]{1,0:T(8,128)S(1)}, u32[]{:S(2)}, u32[]{:S(2)}) collective-permute-start(f32[576,128]{1,0:T(8,128)S(1)} %copy-done.15), channel_id=1, source_target_pairs={{2,0},{4,2},{1,3},{6,4},{3,5},{5,7},{10,8},{12,10},{9,11},{14,12},... | collective-permute-start | bytes 884744 | tf_op jit(solution)/shard_map/ppermute | solution.py:679
  62.0 2.1 collective-permute-start.12
  64.3 5.1 %collective-permute-done.16.refs_4_ = f32[576,128]{1,0:T(8,128)S(1)} collective-permute-done((f32[576,128]{1,0:T(8,128)S(1)}, f32[576,128]{1,0:T(8,128)S(1)}, u32[]{:S(2)}, u32[]{:S(2)}) %collective-permute-start.16) | collective-permute-done | bytes 294944 | tf_op jit(solution)/shard_map/ppermute | solution.py:679
  69.4 1.6 collective-permute-start.13
  70.9 2.1 collective-permute-done.12.refs_4_
  73.8 1.7 collective-permute-start.9
  76.3 1.3 collective-permute-start.15
  77.5 11.1 %collective-permute-done.10.refs_2_ = f32[2,576,128]{2,1,0:T(8,128)S(1)} collective-permute-done((f32[2,576,128]{2,1,0:T(8,128)}, f32[2,576,128]{2,1,0:T(8,128)S(1)}, u32[]{:S(2)}, u32[]{:S(2)}) %collective-permute-start.10) | collective-permute-done | bytes 589856 | tf_op jit(solution)/shard_map/ppermute | solution.py:673
  88.6 1.3 collective-permute-start.11
  89.9 33.5 %collective-permute-done.6.refs_2_ = f32[2,432,128]{2,1,0:T(8,128)} collective-permute-done((f32[2,432,128]{2,1,0:T(8,128)}, f32[2,432,128]{2,1,0:T(8,128)}, u32[]{:S(2)}, u32[]{:S(2)}) %collective-permute-start.6) | collective-permute-done | bytes 442400 | tf_op jit(solution)/shard_map/ppermute | solution.py:673
  123.5 1.3 collective-permute-start.7
  124.8 4.5 %collective-permute-start = (f32[2,144,128]{2,1,0:T(8,128)}, f32[2,144,128]{2,1,0:T(8,128)}, u32[]{:S(2)}, u32[]{:S(2)}) collective-permute-start(f32[2,144,128]{2,1,0:T(8,128)} %get-tuple-element.54), channel_id=1, source_target_pairs={{0,1},{1,0},{2,3},{3,2},{4,5},{5,4},{6,7},{7,6},{8,9},{9,8},{10,11... | collective-permute-start | bytes 442376 | tf_op jit(solution)/shard_map/ppermute | solution.py:673
  129.4 1.3 collective-permute-start.2
  130.7 5.2 %collective-permute-start.3 = (f32[144,128]{1,0:T(8,128)}, f32[144,128]{1,0:T(8,128)}, u32[]{:S(2)}, u32[]{:S(2)}) collective-permute-start(f32[144,128]{1,0:T(8,128)} %get-tuple-element.52.earlier_ref), channel_id=1, source_target_pairs={{2,0},{4,2},{1,3},{6,4},{3,5},{5,7},{10,8},{12,10},{9,11},{14,12},... | collective-permute-start | bytes 221192 | tf_op jit(solution)/shard_map/ppermute | solution.py:679
  137.9 11.8 %transport_first.4 = (f32[576,128]{1,0:T(8,128)}, f32[5,576,128]{2,1,0:T(8,128)}, f32[2,576,128]{2,1,0:T(8,128)}, f32[16,1024]{1,0:T(8,128)}) custom-call(s32[1]{0:T(128)} %bitcast.side_ref, f32[13824,128]{1,0:T(8,128)} %bitcast.24, f32[2,576,128]{2,1,0:T(8,128)} %copy-done.6, f32[2,576,128]{2,1,0:T(8,128)} %copy-done.4, f32[2,576,128]{2,1,0:T(8,128)} %copy-done.9, ...), custom_call_target="tpu_custom_call" | custom-call | flops 35389440 | bytes 5603328 | tf_op jit(solution)/shard_map/transport_first/pallas_call | solution.py:418
  149.8 11.7 %transport_first.5 = (f32[576,128]{1,0:T(8,128)}, f32[5,576,128]{2,1,0:T(8,128)}, f32[2,576,128]{2,1,0:T(8,128)}, f32[16,1024]{1,0:T(8,128)}) custom-call(s32[1]{0:T(128)} %bitcast.side_ref, f32[13824,128]{1,0:T(8,128)} %bitcast.25, f32[2,576,128]{2,1,0:T(8,128)} %copy-done.7, f32[2,576,128]{2,1,0:T(8,128)} %copy-done.3, f32[2,576,128]{2,1,0:T(8,128)} %copy-done.8, ...), custom_call_target="tpu_custom_call" | custom-call | flops 35389440 | bytes 5603328 | tf_op jit(solution)/shard_map/transport_first/pallas_call | solution.py:418
  161.5 9.3 %transport_first.6 = (f32[432,128]{1,0:T(8,128)}, f32[5,432,128]{2,1,0:T(8,128)}, f32[2,432,128]{2,1,0:T(8,128)}, f32[16,1024]{1,0:T(8,128)}) custom-call(s32[1]{0:T(128)} %bitcast.side_ref, f32[13824,128]{1,0:T(8,128)} %bitcast.26, f32[2,432,128]{2,1,0:T(8,128)} %copy-done.10, f32[2,432,128]{2,1,0:T(8,128)} %collective-permute-done.6.refs_2_, ...), custom_call_target="tpu_custom_call" | custom-call | flops 26542080 | bytes 4202496 | tf_op jit(solution)/shard_map/transport_first/pallas_call | solution.py:418
  170.9 4.3 %transport_first.7 = (f32[144,128]{1,0:T(8,128)}, f32[5,144,128]{2,1,0:T(8,128)}, f32[2,144,128]{2,1,0:T(8,128)}, f32[16,1024]{1,0:T(8,128)}) custom-call(s32[1]{0:T(128)} %bitcast.side_ref, f32[13824,128]{1,0:T(8,128)} %bitcast.27, f32[2,144,128]{2,1,0:T(8,128)} %collective-permute-done.refs_1_, f32[2,144,128]{2,1,0:T(8,128)} %copy-done.20, ...), custom_call_target="tpu_custom_call" | custom-call | flops 8847360 | bytes 1400832 | tf_op jit(solution)/shard_map/transport_first/pallas_call | solution.py:418
  175.2 1.0 collective-permute-start.18
  176.4 1.6 collective-permute-start.36
  178.1 1.3 collective-permute-start.35
  179.4 5.2 %collective-permute-start.34 = (f32[432,128]{1,0:T(8,128)}, f32[432,128]{1,0:T(8,128)}, u32[]{:S(2)}, u32[]{:S(2)}) collective-permute-start(f32[432,128]{1,0:T(8,128)} %get-tuple-element.75.refs_2_), channel_id=1, source_target_pairs={{2,0},{4,2},{1,3},{6,4},{3,5},{5,7},{10,8},{12,10},{9,11},{14,12},... | collective-permute-start | bytes 663560 | tf_op jit(solution)/shard_map/ppermute | solution.py:679
  184.7 1.3 collective-permute-start.31
  186.0 1.3 collective-permute-start.29
  188.1 5.0 %collective-permute-start.20 = (f32[16,1024]{1,0:T(8,128)S(1)}, f32[16,1024]{1,0:T(8,128)S(1)}, u32[]{:S(2)}, u32[]{:S(2)}) collective-permute-start(f32[16,1024]{1,0:T(8,128)S(1)} %add_add_fusion.1), channel_id=1, source_target_pairs={{0,1},{1,0},{2,3},{3,2},{4,5},{5,4},{6,7},{7,6},{8,9},{9,8},{10,11... | collective-permute-start | bytes 196616 | tf_op jit(solution)/shard_map/ppermute | solution.py:673
  193.2 2.2 collective-permute-done.20
  195.4 1.3 collective-permute-start.33
  197.4 28.8 %collective-permute-start.21 = (f32[16,1024]{1,0:T(8,128)S(1)}, f32[16,1024]{1,0:T(8,128)S(1)}, u32[]{:S(2)}, u32[]{:S(2)}) collective-permute-start(f32[16,1024]{1,0:T(8,128)S(1)} %add.49.sum_ref), channel_id=1, source_target_pairs={{0,2},{1,3},{2,0},{3,1},{4,6},{5,7},{6,4},{7,5},{8,10},{9,11},{10,... | collective-permute-start | bytes 196616 | tf_op jit(solution)/shard_map/ppermute | solution.py:682
  226.3 2.2 collective-permute-done.21.sum_a_ref
  228.5 4.6 %collective-permute-start.32 = (f32[576,128]{1,0:T(8,128)}, f32[576,128]{1,0:T(8,128)}, u32[]{:S(2)}, u32[]{:S(2)}) collective-permute-start(f32[576,128]{1,0:T(8,128)} %get-tuple-element.72.refs_2_), channel_id=1, source_target_pairs={{2,0},{4,2},{1,3},{6,4},{3,5},{5,7},{10,8},{12,10},{9,11},{14,12},... | collective-permute-start | bytes 884744 | tf_op jit(solution)/shard_map/ppermute | solution.py:679
  233.2 2.0 collective-permute-start.30
  235.8 3.2 shard_map.77
  239.0 4.5 %transport_second.4 = (f32[4,144,128]{2,1,0:T(8,128)}, f32[4,144,128]{2,1,0:T(8,128)}, f32[16,1024]{1,0:T(8,128)}) custom-call(s32[1]{0:T(128)} %bitcast.side_ref, bf16[3456,48]{1,0:T(8,128)(2,1)} %get-tuple-element.53.refs_0_.table_ref, bf16[48,1408]{1,0:T(8,128)(2,1)} %get-tuple-element.68.refs_1_, f32[144,128]{1,0:T(8,128)} %get-tuple-element.78.refs_2_, ...), custom_call_target="tpu_custom_call" | custom-call | flops 8847360 | bytes 1400832 | tf_op jit(solution)/shard_map/transport_second/pallas_call | solution.py:418
  243.5 10.2 %transport_second.5 = (f32[4,432,128]{2,1,0:T(8,128)}, f32[4,432,128]{2,1,0:T(8,128)}, f32[16,1024]{1,0:T(8,128)}) custom-call(s32[1]{0:T(128)} %bitcast.side_ref, bf16[3456,48]{1,0:T(8,128)(2,1)} %get-tuple-element.53.refs_0_.table_ref, bf16[48,1408]{1,0:T(8,128)(2,1)} %get-tuple-element.68.refs_1_, f32[432,128]{1,0:T(8,128)} %get-tuple-element.75.refs_2_, ...), custom_call_target="tpu_custom_call" | custom-call | flops 26542080 | bytes 4202496 | tf_op jit(solution)/shard_map/transport_second/pallas_call | solution.py:418
  254.5 12.9 %transport_second.6 = (f32[4,576,128]{2,1,0:T(8,128)}, f32[4,576,128]{2,1,0:T(8,128)}, f32[16,1024]{1,0:T(8,128)}) custom-call(s32[1]{0:T(128)} %bitcast.side_ref, bf16[3456,48]{1,0:T(8,128)(2,1)} %get-tuple-element.53.refs_0_.table_ref, bf16[48,1408]{1,0:T(8,128)(2,1)} %get-tuple-element.68.refs_1_, f32[576,128]{1,0:T(8,128)} %get-tuple-element.72.refs_2_, ...), custom_call_target="tpu_custom_call" | custom-call | flops 35389440 | bytes 5603328 | tf_op jit(solution)/shard_map/transport_second/pallas_call | solution.py:418
  267.5 13.0 %transport_second.7 = (f32[4,576,128]{2,1,0:T(8,128)}, f32[4,576,128]{2,1,0:T(8,128)}, f32[16,1024]{1,0:T(8,128)}) custom-call(s32[1]{0:T(128)} %bitcast.side_ref, bf16[3456,48]{1,0:T(8,128)(2,1)} %get-tuple-element.53.refs_0_.table_ref, bf16[48,1408]{1,0:T(8,128)(2,1)} %get-tuple-element.68.refs_1_, f32[576,128]{1,0:T(8,128)} %get-tuple-element.69.refs_2_, ...), custom_call_target="tpu_custom_call" | custom-call | flops 35389440 | bytes 5603328 | tf_op jit(solution)/shard_map/transport_second/pallas_call | solution.py:418
  280.5 2.0 collective-permute-start.37
  283.4 1.6 collective-permute-done.40
  285.0 1.0 collective-permute-start.38
  286.0 1.3 collective-permute-done.39
  287.3 1.9 collective-permute-start.46
  290.1 2.0 collective-permute-start.41
  292.1 53.5 %collective-permute-done.41 = f32[16,1024]{1,0:T(8,128)S(1)} collective-permute-done((f32[16,1024]{1,0:T(8,128)S(1)}, f32[16,1024]{1,0:T(8,128)S(1)}, u32[]{:S(2)}, u32[]{:S(2)}) %collective-permute-start.41) | collective-permute-done | bytes 65568 | tf_op jit(solution)/shard_map/ppermute | solution.py:673
  346.3 5.0 %collective-permute-start.42 = (f32[16,1024]{1,0:T(8,128)S(1)}, f32[16,1024]{1,0:T(8,128)S(1)}, u32[]{:S(2)}, u32[]{:S(2)}) collective-permute-start(f32[16,1024]{1,0:T(8,128)S(1)} %add.56.sum_ref), channel_id=1, source_target_pairs={{0,2},{1,3},{2,0},{3,1},{4,6},{5,7},{6,4},{7,5},{8,10},{9,11},{10,... | collective-permute-start | bytes 196616 | tf_op jit(solution)/shard_map/ppermute | solution.py:682
  351.3 2.2 collective-permute-done.42.sum_a_ref
  354.2 2.6 shard_map.78
  356.8 1.3 reshape.31
  358.9 2.2 finish.4.rest_0_
  361.1 5.2 %finish.5.rest_0_ = f32[13824,128]{1,0:T(8,128)} custom-call(s32[1]{0:T(128)} %bitcast.side_ref, f32[4,432,128]{2,1,0:T(8,128)} %get-tuple-element.91.near_ref, f32[4,432,128]{2,1,0:T(8,128)} %collective-permute-done.45.back_ref, bf16[3456,48]{1,0:T(8,128)(2,1)} %get-tuple-element.53.refs_0_.table_ref, ...), custom_call_target="tpu_custom_call", output_to_operand_aliasing={{}: (5, {})} | custom-call | flops 42467328 | bytes 3538944 | tf_op jit(solution)/shard_map/finish/pallas_call | solution.py:621
  366.3 1.0 copy-done
  367.3 6.5 %finish.6.rest_0_ = f32[13824,128]{1,0:T(8,128)} custom-call(s32[1]{0:T(128)} %bitcast.side_ref, f32[4,576,128]{2,1,0:T(8,128)} %get-tuple-element.89.near_ref, f32[4,576,128]{2,1,0:T(8,128)} %copy-done, bf16[3456,48]{1,0:T(8,128)(2,1)} %get-tuple-element.53.refs_0_.table_ref, ...), custom_call_target="tpu_custom_call", output_to_operand_aliasing={{}: (5, {})} | custom-call | flops 56623104 | bytes 4718592 | tf_op jit(solution)/shard_map/finish/pallas_call | solution.py:621
  373.8 6.5 %finish.7 = f32[13824,128]{1,0:T(8,128)} custom-call(s32[1]{0:T(128)} %bitcast.side_ref, f32[4,576,128]{2,1,0:T(8,128)} %get-tuple-element.84.near_ref, f32[4,576,128]{2,1,0:T(8,128)} %collective-permute-done.37.back_ref, bf16[3456,48]{1,0:T(8,128)(2,1)} %get-tuple-element.53.refs_0_.table_ref, ...), custom_call_target="tpu_custom_call", output_to_operand_aliasing={{}: (5, {})} | custom-call | flops 56623104 | bytes 4718592 | tf_op jit(solution)/shard_map/finish/pallas_call | solution.py:621
  (134 shorter events, 17.7 us)
Async XLA Ops:
  11.5 50.5 %collective-permute-start.8 = (f32[432,128]{1,0:T(8,128)}, f32[432,128]{1,0:T(8,128)S(1)}, u32[]{:S(2)}, u32[]{:S(2)}) collective-permute-start(f32[432,128]{1,0:T(8,128)} %get-tuple-element.51.rest_0_), channel_id=1, source_target_pairs={{2,0},{4,2},{1,3},{6,4},{3,5},{5,7},{10,8},{12,10},{9,11},{14,12},... | collective-permute-start | bytes 663560 | tf_op jit(solution)/shard_map/ppermute | solution.py:679
  29.5 16.8 %copy-start.28 = (s32[4,128]{1,0:T(4,128)S(1)}, s32[4,128]{1,0:T(4,128)}, u32[]{:S(2)}) copy-start(s32[4,128]{1,0:T(4,128)} %param.7) | copy-start | bytes 6148
  29.5 16.8 %copy-start.27 = (f32[4,128]{1,0:T(4,128)S(1)}, f32[4,128]{1,0:T(4,128)}, u32[]{:S(2)}) copy-start(f32[4,128]{1,0:T(4,128)} %param.8) | copy-start | bytes 6148
  29.5 27.8 %copy-start.15 = (f32[576,128]{1,0:T(8,128)S(1)}, f32[576,128]{1,0:T(8,128)}, u32[]{:S(2)}) copy-start(f32[576,128]{1,0:T(8,128)} %get-tuple-element.49.rest_0_) | copy-start | bytes 884740
  44.5 2.6 collective-permute-start.25
  45.2 4.2 %collective-permute-start.24 = (f32[16,512]{1,0:T(8,128)}, f32[16,512]{1,0:T(8,128)S(1)}, u32[]{:S(2)}, u32[]{:S(2)}) collective-permute-start(f32[16,512]{1,0:T(8,128)} %home_moments.1), channel_id=1, source_target_pairs={{0,16},{8,24},{16,0},{24,8},{1,17},{9,25},{17,1},{25,9},{2,18},{10... | collective-permute-start | bytes 98312 | tf_op jit(solution)/shard_map/ppermute | solution.py:687
  46.0 4.3 %collective-permute-start.23 = (f32[16,512]{1,0:T(8,128)}, f32[16,512]{1,0:T(8,128)S(1)}, u32[]{:S(2)}, u32[]{:S(2)}) collective-permute-start(f32[16,512]{1,0:T(8,128)} %home_moments.1), channel_id=1, source_target_pairs={{0,8},{8,16},{16,24},{24,0},{1,9},{9,17},{17,25},{25,1},{2,10},{10... | collective-permute-start | bytes 98312 | tf_op jit(solution)/shard_map/ppermute | solution.py:687
  46.3 7.1 %collective-permute-start.4 = (f32[8,128]{1,0:T(8,128)S(1)}, f32[8,128]{1,0:T(8,128)S(1)}, u32[]{:S(2)}, u32[]{:S(2)}) collective-permute-start(f32[8,128]{1,0:T(8,128)S(1)} %pad_maximum_fusion.2), channel_id=1, source_target_pairs={{0,1},{1,0},{2,3},{3,2},{4,5},{5,4},{6,7},{7,6},{8,9},{9,8},{10,11... | collective-permute-start | bytes 12296 | tf_op jit(solution)/shard_map/ppermute | solution.py:673
  47.1 10.2 %collective-permute-start.1 = (f32[2,144,128]{2,1,0:T(8,128)}, f32[2,144,128]{2,1,0:T(8,128)S(1)}, u32[]{:S(2)}, u32[]{:S(2)}) collective-permute-start(f32[2,144,128]{2,1,0:T(8,128)} %get-tuple-element.55), channel_id=1, source_target_pairs={{0,1},{1,0},{2,3},{3,2},{4,5},{5,4},{6,7},{7,6},{8,9},{9,8},{10,11... | collective-permute-start | bytes 442376 | tf_op jit(solution)/shard_map/ppermute | solution.py:673
  49.4 26.1 %collective-permute-start.5 = (f32[2,432,128]{2,1,0:T(8,128)}, f32[2,432,128]{2,1,0:T(8,128)S(1)}, u32[]{:S(2)}, u32[]{:S(2)}) collective-permute-start(f32[2,432,128]{2,1,0:T(8,128)} %get-tuple-element.58), channel_id=1, source_target_pairs={{0,1},{1,0},{2,3},{3,2},{4,5},{5,4},{6,7},{7,6},{8,9},{9,8},{10,11... | collective-permute-start | bytes 1327112 | tf_op jit(solution)/shard_map/ppermute | solution.py:673
  51.2 4.0 %collective-permute-start.26 = (f32[16,512]{1,0:T(8,128)S(1)}, f32[16,512]{1,0:T(8,128)S(1)}, u32[]{:S(2)}, u32[]{:S(2)}) collective-permute-start(f32[16,512]{1,0:T(8,128)S(1)} %maximum_maximum_fusion), channel_id=1, source_target_pairs={{0,2},{1,3},{2,0},{3,1},{4,6},{5,7},{6,4},{7,5},{8,10},{9,11},{10,... | collective-permute-start | bytes 98312 | tf_op jit(solution)/shard_map/ppermute | solution.py:682
  53.3 2.9 collective-permute-start.27
  55.2 21.0 %collective-permute-start.14 = (f32[2,576,128]{2,1,0:T(8,128)}, f32[2,576,128]{2,1,0:T(8,128)S(1)}, u32[]{:S(2)}, u32[]{:S(2)}) collective-permute-start(f32[2,576,128]{2,1,0:T(8,128)} %get-tuple-element.63), channel_id=1, source_target_pairs={{0,1},{1,0},{2,3},{3,2},{4,5},{5,4},{6,7},{7,6},{8,9},{9,8},{10,11... | collective-permute-start | bytes 1769480 | tf_op jit(solution)/shard_map/ppermute | solution.py:673
  56.2 32.4 %collective-permute-start.10 = (f32[2,576,128]{2,1,0:T(8,128)}, f32[2,576,128]{2,1,0:T(8,128)S(1)}, u32[]{:S(2)}, u32[]{:S(2)}) collective-permute-start(f32[2,576,128]{2,1,0:T(8,128)} %get-tuple-element.61), channel_id=1, source_target_pairs={{0,1},{1,0},{2,3},{3,2},{4,5},{5,4},{6,7},{7,6},{8,9},{9,8},{10,11... | collective-permute-start | bytes 1769480 | tf_op jit(solution)/shard_map/ppermute | solution.py:673
  57.2 92.5 %copy-start.20 = (f32[2,144,128]{2,1,0:T(8,128)}, f32[2,144,128]{2,1,0:T(8,128)S(1)}, u32[]{:S(2)}) copy-start(f32[2,144,128]{2,1,0:T(8,128)S(1)} %collective-permute-done.1.refs_2_) | copy-start | bytes 442372
  57.2 12.1 %collective-permute-start.16 = (f32[576,128]{1,0:T(8,128)S(1)}, f32[576,128]{1,0:T(8,128)S(1)}, u32[]{:S(2)}, u32[]{:S(2)}) collective-permute-start(f32[576,128]{1,0:T(8,128)S(1)} %copy-done.15), channel_id=1, source_target_pairs={{2,0},{4,2},{1,3},{6,4},{3,5},{5,7},{10,8},{12,10},{9,11},{14,12},... | collective-permute-start | bytes 884744 | tf_op jit(solution)/shard_map/ppermute | solution.py:679
  62.0 7.4 %copy-start.18 = (f32[432,128]{1,0:T(8,128)}, f32[432,128]{1,0:T(8,128)S(1)}, u32[]{:S(2)}) copy-start(f32[432,128]{1,0:T(8,128)S(1)} %collective-permute-done.8.refs_4_) | copy-start | bytes 663556
  62.0 11.0 %collective-permute-start.12 = (f32[576,128]{1,0:T(8,128)}, f32[576,128]{1,0:T(8,128)S(1)}, u32[]{:S(2)}, u32[]{:S(2)}) collective-permute-start(f32[576,128]{1,0:T(8,128)} %get-tuple-element.50.rest_0_), channel_id=1, source_target_pairs={{2,0},{4,2},{1,3},{6,4},{3,5},{5,7},{10,8},{12,10},{9,11},{14,12},... | collective-permute-start | bytes 884744 | tf_op jit(solution)/shard_map/ppermute | solution.py:679
  69.4 55.5 %collective-permute-start.13 = (f32[2,576,128]{2,1,0:T(8,128)}, f32[2,576,128]{2,1,0:T(8,128)S(1)}, u32[]{:S(2)}, u32[]{:S(2)}) collective-permute-start(f32[2,576,128]{2,1,0:T(8,128)} %get-tuple-element.62), channel_id=1, source_target_pairs={{0,1},{1,0},{2,3},{3,2},{4,5},{5,4},{6,7},{7,6},{8,9},{9,8},{10,11... | collective-permute-start | bytes 1769480 | tf_op jit(solution)/shard_map/ppermute | solution.py:673
  73.8 55.6 %collective-permute-start.9 = (f32[2,576,128]{2,1,0:T(8,128)}, f32[2,576,128]{2,1,0:T(8,128)S(1)}, u32[]{:S(2)}, u32[]{:S(2)}) collective-permute-start(f32[2,576,128]{2,1,0:T(8,128)} %get-tuple-element.60), channel_id=1, source_target_pairs={{0,1},{1,0},{2,3},{3,2},{4,5},{5,4},{6,7},{7,6},{8,9},{9,8},{10,11... | collective-permute-start | bytes 1769480 | tf_op jit(solution)/shard_map/ppermute | solution.py:673
  75.5 48.0 %collective-permute-start.6 = (f32[2,432,128]{2,1,0:T(8,128)}, f32[2,432,128]{2,1,0:T(8,128)}, u32[]{:S(2)}, u32[]{:S(2)}) collective-permute-start(f32[2,432,128]{2,1,0:T(8,128)} %get-tuple-element.59), channel_id=1, source_target_pairs={{0,1},{1,0},{2,3},{3,2},{4,5},{5,4},{6,7},{7,6},{8,9},{9,8},{10,11... | collective-permute-start | bytes 1327112 | tf_op jit(solution)/shard_map/ppermute | solution.py:673
  76.3 61.7 %copy-start.4 = (f32[2,576,128]{2,1,0:T(8,128)}, f32[2,576,128]{2,1,0:T(8,128)S(1)}, u32[]{:S(2)}) copy-start(f32[2,576,128]{2,1,0:T(8,128)S(1)} %collective-permute-done.14.refs_2_) | copy-start | bytes 1769476
  76.3 54.4 %collective-permute-start.15 = (f32[2,576,128]{2,1,0:T(8,128)S(1)}, f32[2,576,128]{2,1,0:T(8,128)S(1)}, u32[]{:S(2)}, u32[]{:S(2)}) collective-permute-start(f32[2,576,128]{2,1,0:T(8,128)S(1)} %collective-permute-done.14.refs_2_), channel_id=1, source_target_pairs={{0,2},{2,4},{3,1},{4,6},{5,3},{7,5},{8,10},{10,12},{11,9},{12,14},... | collective-permute-start | bytes 1769480 | tf_op jit(solution)/shard_map/ppermute | solution.py:676
  88.6 61.1 %copy-start.3 = (f32[2,576,128]{2,1,0:T(8,128)}, f32[2,576,128]{2,1,0:T(8,128)S(1)}, u32[]{:S(2)}) copy-start(f32[2,576,128]{2,1,0:T(8,128)S(1)} %collective-permute-done.10.refs_2_) | copy-start | bytes 1769476
  88.6 47.3 %collective-permute-start.11 = (f32[2,576,128]{2,1,0:T(8,128)S(1)}, f32[2,576,128]{2,1,0:T(8,128)S(1)}, u32[]{:S(2)}, u32[]{:S(2)}) collective-permute-start(f32[2,576,128]{2,1,0:T(8,128)S(1)} %collective-permute-done.10.refs_2_), channel_id=1, source_target_pairs={{0,2},{2,4},{3,1},{4,6},{5,3},{7,5},{8,10},{10,12},{11,9},{12,14},... | collective-permute-start | bytes 1769480 | tf_op jit(solution)/shard_map/ppermute | solution.py:676
  123.5 38.0 %collective-permute-start.7 = (f32[2,432,128]{2,1,0:T(8,128)}, f32[2,432,128]{2,1,0:T(8,128)}, u32[]{:S(2)}, u32[]{:S(2)}) collective-permute-start(f32[2,432,128]{2,1,0:T(8,128)} %collective-permute-done.6.refs_2_), channel_id=1, source_target_pairs={{0,2},{2,4},{3,1},{4,6},{5,3},{7,5},{8,10},{10,12},{11,9},{12,14},... | collective-permute-start | bytes 1327112 | tf_op jit(solution)/shard_map/ppermute | solution.py:676
  124.8 13.1 %copy-start.6 = (f32[2,576,128]{2,1,0:T(8,128)}, f32[2,576,128]{2,1,0:T(8,128)S(1)}, u32[]{:S(2)}) copy-start(f32[2,576,128]{2,1,0:T(8,128)S(1)} %collective-permute-done.13.refs_1_) | copy-start | bytes 1769476
  124.8 46.0 %collective-permute-start = (f32[2,144,128]{2,1,0:T(8,128)}, f32[2,144,128]{2,1,0:T(8,128)}, u32[]{:S(2)}, u32[]{:S(2)}) collective-permute-start(f32[2,144,128]{2,1,0:T(8,128)} %get-tuple-element.54), channel_id=1, source_target_pairs={{0,1},{1,0},{2,3},{3,2},{4,5},{5,4},{6,7},{7,6},{8,9},{9,8},{10,11... | collective-permute-start | bytes 442376 | tf_op jit(solution)/shard_map/ppermute | solution.py:673
  129.4 41.5 %collective-permute-start.2 = (f32[2,144,128]{2,1,0:T(8,128)S(1)}, f32[2,144,128]{2,1,0:T(8,128)}, u32[]{:S(2)}, u32[]{:S(2)}) collective-permute-start(f32[2,144,128]{2,1,0:T(8,128)S(1)} %collective-permute-done.1.refs_2_), channel_id=1, source_target_pairs={{0,2},{2,4},{3,1},{4,6},{5,3},{7,5},{8,10},{10,12},{11,9},{12,14},... | collective-permute-start | bytes 442376 | tf_op jit(solution)/shard_map/ppermute | solution.py:676
  130.7 19.1 %copy-start.11 = (f32[3,16,512]{2,1,0:T(8,128)}, f32[3,16,512]{2,1,0:T(8,128)S(1)}, u32[]{:S(2)}) copy-start(f32[3,16,512]{2,1,0:T(8,128)S(1)} %pad_maximum_fusion.near_ref) | copy-start | bytes 294916
  130.7 40.2 %collective-permute-start.3 = (f32[144,128]{1,0:T(8,128)}, f32[144,128]{1,0:T(8,128)}, u32[]{:S(2)}, u32[]{:S(2)}) collective-permute-start(f32[144,128]{1,0:T(8,128)} %get-tuple-element.52.earlier_ref), channel_id=1, source_target_pairs={{2,0},{4,2},{1,3},{6,4},{3,5},{5,7},{10,8},{12,10},{9,11},{14,12},... | collective-permute-start | bytes 221192 | tf_op jit(solution)/shard_map/ppermute | solution.py:679
  135.9 42.2 %collective-permute-start.28 = (f32[3,16,512]{2,1,0:T(8,128)S(1)}, f32[3,16,512]{2,1,0:T(8,128)}, u32[]{:S(2)}, u32[]{:S(2)}) collective-permute-start(f32[3,16,512]{2,1,0:T(8,128)S(1)} %pad_maximum_fusion.near_ref), channel_id=1, source_target_pairs={{0,1},{1,0},{2,3},{3,2},{4,5},{5,4},{6,7},{7,6},{8,9},{9,8},{10,11... | collective-permute-start | bytes 294920 | tf_op jit(solution)/shard_map/ppermute | solution.py:673
  170.9 13.8 %copy-start.2 = (f32[2,576,128]{2,1,0:T(8,128)S(1)}, f32[2,576,128]{2,1,0:T(8,128)}, u32[]{:S(2)}) copy-start(f32[2,576,128]{2,1,0:T(8,128)} %get-tuple-element.74.refs_4_) | copy-start | bytes 1769476
  170.9 15.1 %copy-start.1 = (f32[2,576,128]{2,1,0:T(8,128)S(1)}, f32[2,576,128]{2,1,0:T(8,128)}, u32[]{:S(2)}) copy-start(f32[2,576,128]{2,1,0:T(8,128)} %get-tuple-element.71.refs_4_) | copy-start | bytes 1769476
  175.2 4.2 %collective-permute-start.19 = (f32[16,1024]{1,0:T(8,128)}, f32[16,1024]{1,0:T(8,128)S(1)}, u32[]{:S(2)}, u32[]{:S(2)}) collective-permute-start(f32[16,1024]{1,0:T(8,128)} %get-tuple-element.67), channel_id=1, source_target_pairs={{0,24},{8,0},{16,8},{24,16},{1,25},{9,1},{17,9},{25,17},{2,26},{10... | collective-permute-start | bytes 196616 | tf_op jit(solution)/shard_map/ppermute | solution.py:687
  175.2 9.4 %collective-permute-start.18 = (f32[16,1024]{1,0:T(8,128)}, f32[16,1024]{1,0:T(8,128)S(1)}, u32[]{:S(2)}, u32[]{:S(2)}) collective-permute-start(f32[16,1024]{1,0:T(8,128)} %get-tuple-element.67), channel_id=1, source_target_pairs={{0,16},{8,24},{16,0},{24,8},{1,17},{9,25},{17,1},{25,9},{2,18},{10... | collective-permute-start | bytes 196616 | tf_op jit(solution)/shard_map/ppermute | solution.py:687
  176.3 9.7 %collective-permute-start.17 = (f32[16,1024]{1,0:T(8,128)}, f32[16,1024]{1,0:T(8,128)S(1)}, u32[]{:S(2)}, u32[]{:S(2)}) collective-permute-start(f32[16,1024]{1,0:T(8,128)} %get-tuple-element.67), channel_id=1, source_target_pairs={{0,8},{8,16},{16,24},{24,0},{1,9},{9,17},{17,25},{25,1},{2,10},{10... | collective-permute-start | bytes 196616 | tf_op jit(solution)/shard_map/ppermute | solution.py:687
  176.4 11.7 %collective-permute-start.36 = (f32[144,128]{1,0:T(8,128)}, f32[144,128]{1,0:T(8,128)S(1)}, u32[]{:S(2)}, u32[]{:S(2)}) collective-permute-start(f32[144,128]{1,0:T(8,128)} %get-tuple-element.78.refs_2_), channel_id=1, source_target_pairs={{2,0},{4,2},{1,3},{6,4},{3,5},{5,7},{10,8},{12,10},{9,11},{14,12},... | collective-permute-start | bytes 221192 | tf_op jit(solution)/shard_map/ppermute | solution.py:679
  178.1 18.6 %collective-permute-start.35 = (f32[2,144,128]{2,1,0:T(8,128)}, f32[2,144,128]{2,1,0:T(8,128)S(1)}, u32[]{:S(2)}, u32[]{:S(2)}) collective-permute-start(f32[2,144,128]{2,1,0:T(8,128)} %get-tuple-element.80.refs_4_), channel_id=1, source_target_pairs={{0,2},{2,4},{3,1},{4,6},{5,3},{7,5},{8,10},{10,12},{11,9},{12,14},... | collective-permute-start | bytes 442376 | tf_op jit(solution)/shard_map/ppermute | solution.py:676
  179.4 53.8 %collective-permute-start.34 = (f32[432,128]{1,0:T(8,128)}, f32[432,128]{1,0:T(8,128)}, u32[]{:S(2)}, u32[]{:S(2)}) collective-permute-start(f32[432,128]{1,0:T(8,128)} %get-tuple-element.75.refs_2_), channel_id=1, source_target_pairs={{2,0},{4,2},{1,3},{6,4},{3,5},{5,7},{10,8},{12,10},{9,11},{14,12},... | collective-permute-start | bytes 663560 | tf_op jit(solution)/shard_map/ppermute | solution.py:679
  184.7 69.0 %collective-permute-start.31 = (f32[2,576,128]{2,1,0:T(8,128)S(1)}, f32[2,576,128]{2,1,0:T(8,128)S(1)}, u32[]{:S(2)}, u32[]{:S(2)}) collective-permute-start(f32[2,576,128]{2,1,0:T(8,128)S(1)} %copy-done.2), channel_id=1, source_target_pairs={{0,2},{2,4},{3,1},{4,6},{5,3},{7,5},{8,10},{10,12},{11,9},{12,14},... | collective-permute-start | bytes 1769480 | tf_op jit(solution)/shard_map/ppermute | solution.py:676
  186.0 81.5 %collective-permute-start.29 = (f32[2,576,128]{2,1,0:T(8,128)S(1)}, f32[2,576,128]{2,1,0:T(8,128)}, u32[]{:S(2)}, u32[]{:S(2)}) collective-permute-start(f32[2,576,128]{2,1,0:T(8,128)S(1)} %copy-done.1), channel_id=1, source_target_pairs={{0,2},{2,4},{3,1},{4,6},{5,3},{7,5},{8,10},{10,12},{11,9},{12,14},... | collective-permute-start | bytes 1769480 | tf_op jit(solution)/shard_map/ppermute | solution.py:676
  188.1 40.4 %copy-start.21 = (f32[144,128]{1,0:T(8,128)}, f32[144,128]{1,0:T(8,128)S(1)}, u32[]{:S(2)}) copy-start(f32[144,128]{1,0:T(8,128)S(1)} %collective-permute-done.36.refs_6_) | copy-start | bytes 221188
  188.1 7.3 %collective-permute-start.20 = (f32[16,1024]{1,0:T(8,128)S(1)}, f32[16,1024]{1,0:T(8,128)S(1)}, u32[]{:S(2)}, u32[]{:S(2)}) collective-permute-start(f32[16,1024]{1,0:T(8,128)S(1)} %add_add_fusion.1), channel_id=1, source_target_pairs={{0,1},{1,0},{2,3},{3,2},{4,5},{5,4},{6,7},{7,6},{8,9},{9,8},{10,11... | collective-permute-start | bytes 196616 | tf_op jit(solution)/shard_map/ppermute | solution.py:673
  195.4 48.1 %collective-permute-start.33 = (f32[2,432,128]{2,1,0:T(8,128)}, f32[2,432,128]{2,1,0:T(8,128)}, u32[]{:S(2)}, u32[]{:S(2)}) collective-permute-start(f32[2,432,128]{2,1,0:T(8,128)} %get-tuple-element.77.refs_4_), channel_id=1, source_target_pairs={{0,2},{2,4},{3,1},{4,6},{5,3},{7,5},{8,10},{10,12},{11,9},{12,14},... | collective-permute-start | bytes 1327112 | tf_op jit(solution)/shard_map/ppermute | solution.py:676
  196.7 39.1 %copy-start.16 = (f32[16,1024]{1,0:T(8,128)}, f32[16,1024]{1,0:T(8,128)S(1)}, u32[]{:S(2)}) copy-start(f32[16,1024]{1,0:T(8,128)S(1)} %add.49.sum_ref) | copy-start | bytes 196612
  196.7 42.3 %copy-start.19 = (f32[2,144,128]{2,1,0:T(8,128)}, f32[2,144,128]{2,1,0:T(8,128)S(1)}, u32[]{:S(2)}) copy-start(f32[2,144,128]{2,1,0:T(8,128)S(1)} %collective-permute-done.35.refs_5_) | copy-start | bytes 442372
  196.8 0.7 collective-permute-start.22
  197.4 31.1 %copy-start.22 = (f32[16,1024]{1,0:T(8,128)}, f32[16,1024]{1,0:T(8,128)S(1)}, u32[]{:S(2)}) copy-start(f32[16,1024]{1,0:T(8,128)S(1)} %collective-permute-done.22.sum_b_ref) | copy-start | bytes 196612
  197.4 31.1 %collective-permute-start.21 = (f32[16,1024]{1,0:T(8,128)S(1)}, f32[16,1024]{1,0:T(8,128)S(1)}, u32[]{:S(2)}, u32[]{:S(2)}) collective-permute-start(f32[16,1024]{1,0:T(8,128)S(1)} %add.49.sum_ref), channel_id=1, source_target_pairs={{0,2},{1,3},{2,0},{3,1},{4,6},{5,7},{6,4},{7,5},{8,10},{9,11},{10,... | collective-permute-start | bytes 196616 | tf_op jit(solution)/shard_map/ppermute | solution.py:682
  228.5 25.2 %collective-permute-start.32 = (f32[576,128]{1,0:T(8,128)}, f32[576,128]{1,0:T(8,128)}, u32[]{:S(2)}, u32[]{:S(2)}) collective-permute-start(f32[576,128]{1,0:T(8,128)} %get-tuple-element.72.refs_2_), channel_id=1, source_target_pairs={{2,0},{4,2},{1,3},{6,4},{3,5},{5,7},{10,8},{12,10},{9,11},{14,12},... | collective-permute-start | bytes 884744 | tf_op jit(solution)/shard_map/ppermute | solution.py:679
  233.2 34.3 %collective-permute-start.30 = (f32[576,128]{1,0:T(8,128)}, f32[576,128]{1,0:T(8,128)}, u32[]{:S(2)}, u32[]{:S(2)}) collective-permute-start(f32[576,128]{1,0:T(8,128)} %get-tuple-element.69.refs_2_), channel_id=1, source_target_pairs={{2,0},{4,2},{1,3},{6,4},{3,5},{5,7},{10,8},{12,10},{9,11},{14,12},... | collective-permute-start | bytes 884744 | tf_op jit(solution)/shard_map/ppermute | solution.py:679
  267.4 98.9 %collective-permute-start.44 = (f32[4,576,128]{2,1,0:T(8,128)}, f32[4,576,128]{2,1,0:T(8,128)S(1)}, u32[]{:S(2)}, u32[]{:S(2)}) collective-permute-start(f32[4,576,128]{2,1,0:T(8,128)} %get-tuple-element.90), channel_id=1, source_target_pairs={{0,1},{1,0},{2,3},{3,2},{4,5},{5,4},{6,7},{7,6},{8,9},{9,8},{10,11... | collective-permute-start | bytes 3538952 | tf_op jit(solution)/shard_map/ppermute | solution.py:673
  280.5 93.4 %collective-permute-start.37 = (f32[4,576,128]{2,1,0:T(8,128)}, f32[4,576,128]{2,1,0:T(8,128)}, u32[]{:S(2)}, u32[]{:S(2)}) collective-permute-start(f32[4,576,128]{2,1,0:T(8,128)} %get-tuple-element.85), channel_id=1, source_target_pairs={{0,1},{1,0},{2,3},{3,2},{4,5},{5,4},{6,7},{7,6},{8,9},{9,8},{10,11... | collective-permute-start | bytes 3538952 | tf_op jit(solution)/shard_map/ppermute | solution.py:673
  282.5 78.6 %collective-permute-start.45 = (f32[4,432,128]{2,1,0:T(8,128)}, f32[4,432,128]{2,1,0:T(8,128)}, u32[]{:S(2)}, u32[]{:S(2)}) collective-permute-start(f32[4,432,128]{2,1,0:T(8,128)} %get-tuple-element.92), channel_id=1, source_target_pairs={{0,1},{1,0},{2,3},{3,2},{4,5},{5,4},{6,7},{7,6},{8,9},{9,8},{10,11... | collective-permute-start | bytes 2654216 | tf_op jit(solution)/shard_map/ppermute | solution.py:673
  282.6 2.4 collective-permute-start.40
  282.6 4.7 %collective-permute-start.39 = (f32[16,1024]{1,0:T(8,128)}, f32[16,1024]{1,0:T(8,128)S(1)}, u32[]{:S(2)}, u32[]{:S(2)}) collective-permute-start(f32[16,1024]{1,0:T(8,128)} %get-tuple-element.86), channel_id=1, source_target_pairs={{0,16},{8,24},{16,0},{24,8},{1,17},{9,25},{17,1},{25,9},{2,18},{10... | collective-permute-start | bytes 196616 | tf_op jit(solution)/shard_map/ppermute | solution.py:687
  285.0 4.3 %collective-permute-start.38 = (f32[16,1024]{1,0:T(8,128)}, f32[16,1024]{1,0:T(8,128)S(1)}, u32[]{:S(2)}, u32[]{:S(2)}) collective-permute-start(f32[16,1024]{1,0:T(8,128)} %get-tuple-element.86), channel_id=1, source_target_pairs={{0,8},{8,16},{16,24},{24,0},{1,9},{9,17},{17,25},{25,1},{2,10},{10... | collective-permute-start | bytes 196616 | tf_op jit(solution)/shard_map/ppermute | solution.py:687
  287.3 70.8 %collective-permute-start.46 = (f32[4,144,128]{2,1,0:T(8,128)}, f32[4,144,128]{2,1,0:T(8,128)S(1)}, u32[]{:S(2)}, u32[]{:S(2)}) collective-permute-start(f32[4,144,128]{2,1,0:T(8,128)} %get-tuple-element.94), channel_id=1, source_target_pairs={{0,1},{1,0},{2,3},{3,2},{4,5},{5,4},{6,7},{7,6},{8,9},{9,8},{10,11... | collective-permute-start | bytes 884744 | tf_op jit(solution)/shard_map/ppermute | solution.py:673
  290.1 55.5 %collective-permute-start.41 = (f32[16,1024]{1,0:T(8,128)S(1)}, f32[16,1024]{1,0:T(8,128)S(1)}, u32[]{:S(2)}, u32[]{:S(2)}) collective-permute-start(f32[16,1024]{1,0:T(8,128)S(1)} %add_add_fusion), channel_id=1, source_target_pairs={{0,1},{1,0},{2,3},{3,2},{4,5},{5,4},{6,7},{7,6},{8,9},{9,8},{10,11... | collective-permute-start | bytes 196616 | tf_op jit(solution)/shard_map/ppermute | solution.py:673
  345.6 8.0 %copy-start.17 = (f32[16,1024]{1,0:T(8,128)}, f32[16,1024]{1,0:T(8,128)S(1)}, u32[]{:S(2)}) copy-start(f32[16,1024]{1,0:T(8,128)S(1)} %add.56.sum_ref) | copy-start | bytes 196612
  345.6 0.7 collective-permute-start.43
  346.3 7.3 %copy-start.24 = (f32[16,1024]{1,0:T(8,128)}, f32[16,1024]{1,0:T(8,128)S(1)}, u32[]{:S(2)}) copy-start(f32[16,1024]{1,0:T(8,128)S(1)} %collective-permute-done.43.sum_b_ref) | copy-start | bytes 196612
  346.3 7.3 %collective-permute-start.42 = (f32[16,1024]{1,0:T(8,128)S(1)}, f32[16,1024]{1,0:T(8,128)S(1)}, u32[]{:S(2)}, u32[]{:S(2)}) collective-permute-start(f32[16,1024]{1,0:T(8,128)S(1)} %add.56.sum_ref), channel_id=1, source_target_pairs={{0,2},{1,3},{2,0},{3,1},{4,6},{5,7},{6,4},{7,5},{8,10},{9,11},{10,... | collective-permute-start | bytes 196616 | tf_op jit(solution)/shard_map/ppermute | solution.py:682
  (12 other events, 30.7 us)

commit v3 on v2

--- a/solution.py
+++ b/solution.py
@@ -20,7 +20,6 @@
 BLOCK_ROWS = 2 * STRIP_ROWS
 SPAN = 3 * BLOCK_ROWS
 GROUP = 16
-BLOCK = 144
 F32 = jnp.float32
 BF16 = jnp.bfloat16
 
@@ -29,11 +28,13 @@
     return pltpu.CompilerParams(vmem_limit_bytes=62 * 1024 * 1024, **more)
 
 
-def chunk_blocks(blocks):
-    if blocks % 12 == 0:
-        unit = blocks // 12
-        return [4 * unit, 4 * unit, 3 * unit, unit]
-    return [1] * blocks if blocks < 4 else [blocks - blocks // 2, blocks // 2]
+def plan(half):
+    block = 288 if half % 288 == 0 else 144
+    blocks = half // block
+    if blocks % 6 == 0:
+        unit = block * (blocks // 6)
+        return block, [unit, 2 * unit, 2 * unit, unit]
+    return block, [block * (blocks - 2), block, block]
 
 
 def moment_rows(vel_x, vel_y, vel_z, volume, lib):
@@ -54,7 +55,7 @@
         energy * vel_y,
         energy * vel_z,
     ]
-    return lib.stack([row * weight for row in rows])
+    return lib.concatenate([(row * weight).reshape(1, -1) for row in rows])
 
 
 def state_rows(vel_x, vel_y, vel_z, lib):
@@ -70,7 +71,7 @@
         shape_heat * vel_y,
         shape_heat * vel_z,
     ]
-    return lib.stack(rows)
+    return lib.concatenate([row.reshape(1, -1) for row in rows])
 
 
 def target_moments(points):
@@ -110,115 +111,89 @@
 
 
 def minmod(left, right):
-    low = jnp.minimum(left, right)
-    high = jnp.maximum(left, right)
-    return jnp.maximum(low, 0.0) + jnp.minimum(high, 0.0)
+    return jnp.maximum(jnp.minimum(right, jnp.maximum(left, 0.0)), jnp.minimum(left, 0.0))
 
 
 def strided(start, count):
     return pl.ds(start, count, stride=STRIP_ROWS)
 
 
-def pack_kernel(size, side_ref, far_ref, own_ref, *rest):
-    mid_ref, edge_ref, down_ref = rest[-3:]
+def pick_kernel(size, picks, side_ref, strip_ref, *rest):
+    out_ref = rest[-1]
     side = side_ref[0]
-    for i in range(4):
-        row = jnp.where(side == 1, i, 3 - i)
-        part = far_ref[strided(row, size), :]
-        if i < 2:
-            mid_ref[i] = part
-        else:
-            edge_ref[i - 2] = part
-    down_ref[...] = own_ref[strided(jnp.where(side == 1, 3, 0), size), :]
-
-
-def pack(side, flat, half, chunk, first, size, earlier):
-    steps = chunk // size
-    shift = half // size
-    begin = first // size
+    for index, (even, odd) in enumerate(picks):
+        out_ref[index] = strip_ref[strided(jnp.where(side == 1, odd, even), size), :]
+
+
+def pick(side, flat, start, count, size, picks, earlier=()):
     return pl.pallas_call(
-        functools.partial(pack_kernel, size),
-        out_shape=(
-            jax.ShapeDtypeStruct((2, chunk, LANES), F32),
-            jax.ShapeDtypeStruct((2, chunk, LANES), F32),
-            jax.ShapeDtypeStruct((chunk, LANES), F32),
-        ),
+        functools.partial(pick_kernel, size, picks),
+        out_shape=jax.ShapeDtypeStruct((len(picks), count, LANES), F32),
         grid_spec=pltpu.PrefetchScalarGridSpec(
             num_scalar_prefetch=1,
-            grid=(steps,),
+            grid=(count // size,),
             in_specs=[
-                pl.BlockSpec((4 * size, LANES), lambda i, s: ((1 - s[0]) * shift + begin + i, 0)),
-                pl.BlockSpec((4 * size, LANES), lambda i, s: (s[0] * shift + begin + i, 0)),
+                pl.BlockSpec((4 * size, LANES), lambda i, s: (start(s[0]) + i, 0)),
                 *[pl.BlockSpec(memory_space=pl.ANY)] * len(earlier),
             ],
-            out_specs=[
-                pl.BlockSpec((2, size, LANES), lambda i, s: (0, i, 0)),
-                pl.BlockSpec((2, size, LANES), lambda i, s: (0, i, 0)),
-                pl.BlockSpec((size, LANES), lambda i, s: (i, 0)),
-            ],
+            out_specs=pl.BlockSpec((len(picks), size, LANES), lambda i, s: (0, i, 0)),
         ),
         compiler_params=params(),
-        name="pack",
         cost_estimate=pl.CostEstimate(
-            flops=0, transcendentals=0, bytes_accessed=chunk * LANES * 4 * 13
-        ),
-    )(side, flat, flat, *earlier)
-
-
-def prepare_kernel(points, vel_ref, earlier_ref, table_ref, const_ref, weight_ref):
-    comps = (vel_ref[0].astype(F32) - (points - 1) / 2.0) * (8.0 / points)
+            flops=0, transcendentals=0, bytes_accessed=count * LANES * 4 * (4 + len(picks))
+        ),
+    )(side, flat, *earlier)
+
+
+def prepare_kernel(points, vel_ref, table_ref, const_ref, weight_ref):
+    comps = (vel_ref[...].astype(F32) - (points - 1) / 2.0) * (8.0 / points)
     vel_x, vel_y, vel_z = comps[0:1], comps[1:2], comps[2:3]
-    moments = jnp.concatenate(
-        [row[0] for row in moment_rows(vel_x, vel_y, vel_z, (8.0 / points) ** 3, jnp)[:, None]]
-        + [jnp.zeros_like(vel_x)] * 3
-    )
-    high = moments.astype(BF16)
-    weight_ref[0, 0:16] = high
-    weight_ref[0, 16:32] = (moments - high.astype(F32)).astype(BF16)
-    shapes = jnp.concatenate([row[0] for row in state_rows(vel_x, vel_y, vel_z, jnp)[:, None]])
+    moments = moment_rows(vel_x, vel_y, vel_z, (8.0 / points) ** 3, jnp)
+    high = moments.astype(BF16).astype(F32)
+    shapes = state_rows(vel_x, vel_y, vel_z, jnp)
     part_a = shapes.astype(BF16).astype(F32)
     part_b = (shapes - part_a).astype(BF16).astype(F32)
     part_c = shapes - part_a - part_b
-    factors = jnp.concatenate(
+    width = vel_x.shape[1]
+    rows = jnp.concatenate(
         [
+            *[part_a] * 3,
+            *[part_b] * 2,
+            part_c,
+            high,
+            jnp.zeros((3, width), F32),
+            moments - high,
+            jnp.zeros((3, width), F32),
             STEP_RATIO * jnp.abs(vel_x),
             STEP_RATIO * jnp.abs(vel_y),
             jnp.where(vel_y > 0, 0.5, -0.5),
-            jnp.zeros((13, vel_x.shape[1]), F32),
+            jnp.zeros((45, width), F32),
         ]
     )
-    rows = jnp.concatenate([part_a, part_a, part_a, part_b, part_b, part_c, factors])
     columns = rows.T
     table_ref[...] = columns[:, :48].astype(BF16)
-    const_ref[...] = columns[:, 48:56]
-
-
-def prepare(points, vel_index, size, earlier):
+    weight_ref[...] = columns[:, 48:80].astype(BF16)
+    const_ref[...] = columns[:, 80:88]
+
+
+def prepare(points, vel_index):
     count = vel_index.shape[1]
-    blocks = vel_index.reshape(3, count // size, size).transpose(1, 0, 2)
+    vmem = pl.BlockSpec(memory_space=pltpu.VMEM)
     return pl.pallas_call(
         functools.partial(prepare_kernel, points),
         out_shape=(
             jax.ShapeDtypeStruct((count, 48), BF16),
             jax.ShapeDtypeStruct((count, 8), F32),
-            jax.ShapeDtypeStruct((count // size, 32, size), BF16),
-        ),
-        grid=(count // size,),
-        in_specs=[
-            pl.BlockSpec((1, 3, size), lambda i: (i, 0, 0)),
-            pl.BlockSpec(memory_space=pl.ANY),
-        ],
-        out_specs=[
-            pl.BlockSpec((size, 48), lambda i: (i, 0)),
-            pl.BlockSpec((size, 8), lambda i: (i, 0)),
-            pl.BlockSpec((1, 32, size), lambda i: (i, 0, 0)),
-        ],
+            jax.ShapeDtypeStruct((count, 32), BF16),
+        ),
+        in_specs=[vmem],
+        out_specs=[vmem] * 3,
         compiler_params=params(),
         name="prepare",
         cost_estimate=pl.CostEstimate(
-            flops=200 * count, transcendentals=count, bytes_accessed=count * 2000
-        ),
-    )(blocks, earlier)
+            flops=200 * count, transcendentals=count, bytes_accessed=count * 1000
+        ),
+    )(vel_index)
 
 
 def split_store(value, first_ref, second_ref, rows, columns):
@@ -228,8 +203,10 @@
 
 
 def weighted(weights, first, second):
-    both = jnp.dot(weights, first, preferred_element_type=F32)
-    return both[:16] + both[16:] + jnp.dot(weights[:16], second, preferred_element_type=F32)
+    over_rows = (((0,), (0,)), ((), ()))
+    both = lax.dot_general(weights, first, over_rows, preferred_element_type=F32)
+    rest = lax.dot_general(weights, second, over_rows, preferred_element_type=F32)
+    return both[:16] + both[16:] + rest[:16]
 
 
 def moment_kernel(size, dist_ref, weight_ref, out_ref, first_ref, second_ref):
@@ -242,7 +219,7 @@
         split_store(
             dist_ref[strided(row, size), :], first_ref, second_ref, pl.ds(0, size), columns
         )
-    out_ref[...] += weighted(weight_ref[0], first_ref[...], second_ref[...])
+    out_ref[...] += weighted(weight_ref[...], first_ref[...], second_ref[...])
 
 
 def home_moments(flat, weights, size):
@@ -254,7 +231,7 @@
         grid=(count // size,),
         in_specs=[
             pl.BlockSpec((4 * size, LANES), lambda i: (i, 0)),
-            pl.BlockSpec((1, 32, size), lambda i: (i, 0, 0)),
+            pl.BlockSpec((size, 32), lambda i: (i, 0)),
         ],
         out_specs=pl.BlockSpec((16, width), lambda i: (0, 0)),
         scratch_shapes=[pltpu.VMEM((size, width), BF16), pltpu.VMEM((size, width), BF16)],
@@ -270,12 +247,12 @@
     if second_pass:
         (table_ref, change_ref, q_first, q_mid, q_edge, up_ref, down_ref, *rest) = refs
     else:
-        (own_ref, mid_ref, edge_ref, up_ref, down_ref, *rest) = refs
+        (own_ref, got_ref, up_ref, down_ref, *rest) = refs
     (const_ref, weight_ref, cell_ref, sum_in_ref, *rest) = rest
     if second_pass:
         (near_out, far_out, sum_ref, first_ref, second_ref, lift_ref) = rest
     else:
-        (first_out, mid_out, edge_out, sum_ref, first_ref, second_ref) = rest
+        (first_out, mid_out, edge_out, sum_ref, first_ref, second_ref) = rest[-6:]
     side = side_ref[0]
 
     @pl.when(pl.program_id(0) == 0)
@@ -305,14 +282,10 @@
                     value = q_mid[row - 1, rows, :]
                 else:
                     value = q_edge[row - 6, rows, :]
-            elif row < 4:
-                value = own_ref[
-                    strided(base * STRIP_ROWS + jnp.where(side == 1, 3 - row, row), GROUP), :
-                ]
-            elif row < 6:
-                value = mid_ref[row - 4, rows, :]
             else:
-                value = edge_ref[row - 6, rows, :]
+                ref = own_ref if row < 4 else got_ref
+                local = jnp.where(side == 1, 3 - row % 4, row % 4)
+                value = ref[strided(base * STRIP_ROWS + local, GROUP), :]
             if second_pass:
                 value = value + lift_ref[rows, pl.ds((row + 2) * LANES, LANES)]
             return value
@@ -363,71 +336,76 @@
         return carry
 
     lax.fori_loop(0, size // GROUP, body, 0)
-    part = weighted(weight_ref[0], first_ref[...], second_ref[...])
+    part = weighted(weight_ref[...], first_ref[...], second_ref[...])
     for row in range(BLOCK_ROWS):
         place = jnp.where(side == 1, 7 - row, row)
         columns = pl.ds(pl.multiple_of(place * LANES, LANES), LANES)
         sum_ref[:, columns] += part[:, row * LANES : (row + 1) * LANES]
 
 
-def transport(side, sources, tables, cells, sums, half, chunk, first, size, change=None):
+def transport(
+    side, sources, tables, cells, sums, half, chunk, first, size, change=None, skip=0, group=None, into=None
+):
     second_pass = change is not None
     steps = chunk // size
     shift = half // size
     begin = first // size
+    offset = skip // size
     table, const, weights = tables
     width = BLOCK_ROWS * LANES
 
     def mine(i, s):
         return s[0] * shift + begin + i
 
-    two = pl.BlockSpec((2, size, LANES), lambda i, s: (0, i, 0))
-    one = pl.BlockSpec((size, LANES), lambda i, s: (i, 0))
+    def stack_of(count, at):
+        return pl.BlockSpec((count, size, LANES), lambda i, s: (0, at + i, 0))
+
+    aliases = {}
     if second_pass:
         args = [table, change]
         specs = [
             pl.BlockSpec((size, 48), lambda i, s: (mine(i, s), 0)),
             pl.BlockSpec(change.shape, lambda i, s: (0, 0)),
-            one,
-            pl.BlockSpec((5, size, LANES), lambda i, s: (0, i, 0)),
-            two,
-            two,
-            one,
+            stack_of(None, offset),
+            stack_of(5, offset),
+            stack_of(2, offset),
+            stack_of(2, offset),
+            stack_of(None, offset),
         ]
-        four = pl.BlockSpec((4, size, LANES), lambda i, s: (0, i, 0))
         outs = [jax.ShapeDtypeStruct((4, chunk, LANES), F32)] * 2
-        out_specs = [four, four]
+        out_specs = [stack_of(4, 0)] * 2
         scratch = [pltpu.VMEM((size, 11 * LANES), F32)]
     else:
         args = []
         specs = [
             pl.BlockSpec((4 * size, LANES), lambda i, s: (mine(i, s), 0)),
-            two,
-            two,
-            two,
-            one,
+            pl.BlockSpec((4 * size, LANES), lambda i, s: (i, 0)),
+            stack_of(2, 0),
+            stack_of(None, begin),
         ]
-        outs = [
-            jax.ShapeDtypeStruct((chunk, LANES), F32),
-            jax.ShapeDtypeStruct((5, chunk, LANES), F32),
-            jax.ShapeDtypeStruct((2, chunk, LANES), F32),
-        ]
-        out_specs = [one, pl.BlockSpec((5, size, LANES), lambda i, s: (0, i, 0)), two]
+        outs = [jax.ShapeDtypeStruct((n, group, LANES), F32) for n in (1, 5, 2)]
+        out_specs = [stack_of(None, offset), stack_of(5, offset), stack_of(2, offset)]
         scratch = []
     whole = pl.BlockSpec((16, width), lambda i, s: (0, 0))
+    args = [side, *args, *sources, const, weights, cells, sums]
+    specs = [
+        *specs,
+        pl.BlockSpec((size, 8), lambda i, s: (mine(i, s), 0)),
+        pl.BlockSpec((size, 32), lambda i, s: (mine(i, s), 0)),
+        pl.BlockSpec((16, LANES), lambda i, s: (0, 0)),
+        whole,
+    ]
+    if into is not None:
+        aliases = {len(args) + n: n for n in range(3)}
+        args = [*args, *into]
+        specs = [*specs, *[pl.BlockSpec(memory_space=pl.ANY)] * 3]
     return pl.pallas_call(
         functools.partial(transport_kernel, size, second_pass),
         out_shape=(*outs, jax.ShapeDtypeStruct((16, width), F32)),
         grid_spec=pltpu.PrefetchScalarGridSpec(
             num_scalar_prefetch=1,
             grid=(steps,),
-            in_specs=[
-                *specs,
-                pl.BlockSpec((size, 8), lambda i, s: (mine(i, s), 0)),
-                pl.BlockSpec((1, 32, size), lambda i, s: (mine(i, s), 0, 0)),
-                pl.BlockSpec((16, LANES), lambda i, s: (0, 0)),
-                whole,
-            ],
+            in_specs=specs,
             out_specs=[*out_specs, whole],
             scratch_shapes=[
                 pltpu.VMEM((size, width), BF16),
@@ -435,12 +413,13 @@
                 *scratch,
             ],
         ),
+        input_output_aliases=aliases,
         compiler_params=params(),
         name="transport_second" if second_pass else "transport_first",
         cost_estimate=pl.CostEstimate(
             flops=60 * chunk * width, transcendentals=0, bytes_accessed=chunk * LANES * 4 * 19
         ),
-    )(side, *args, *sources, const, weights, cells, sums)
+    )(*args)
 
 
 def sweep_block(inputs, relax, rate):
@@ -577,63 +556,49 @@
     )(info, *args)
 
 
-def finish_kernel(size, side_ref, near_ref, back_ref, table_ref, change_ref, *rest):
+def finish_kernel(size, own, side_ref, rows_ref, table_ref, change_ref, *rest):
     out_ref = rest[-1]
-    side = side_ref[0]
+    flipped = side_ref[0] == (1 if own else 0)
     lift = jnp.dot(table_ref[...], change_ref[...], preferred_element_type=F32)
-
-    def write(ref, flipped):
-        for row in range(STRIP_ROWS):
-            index = jnp.where(side == flipped, 3 - row, row)
-            out_ref[strided(row, size), :] = (
-                ref[index] + lift[:, row * LANES : (row + 1) * LANES]
-            )
-
-    @pl.when(pl.program_id(0) == 0)
-    def _():
-        write(near_ref, 1)
-
-    @pl.when(pl.program_id(0) == 1)
-    def _():
-        write(back_ref, 0)
-
-
-def finish(side, out, near, back, table, change, half, chunk, first, size):
-    steps = chunk // size
+    for row in range(STRIP_ROWS):
+        index = jnp.where(flipped, 3 - row, row)
+        out_ref[strided(row, size), :] = (
+            rows_ref[index] + lift[:, row * LANES : (row + 1) * LANES]
+        )
+
+
+def finish(side, out, rows, own, table, change, half, chunk, first, size):
     shift = half // size
     begin = first // size
 
-    def place(h, i, s):
-        return jnp.where(h == 0, s[0], 1 - s[0]) * shift + begin + i
+    def place(i, s):
+        return (s[0] if own else 1 - s[0]) * shift + begin + i
 
     specs = [
-        pl.BlockSpec((4, size, LANES), lambda h, i, s: (0, jnp.where(h == 0, i, steps - 1), 0)),
-        pl.BlockSpec((4, size, LANES), lambda h, i, s: (0, jnp.where(h == 0, 0, i), 0)),
-        pl.BlockSpec((size, 48), lambda h, i, s: (place(h, i, s), 0)),
-        pl.BlockSpec(change.shape, lambda h, i, s: (0, 0)),
+        pl.BlockSpec((4, size, LANES), lambda i, s: (0, i, 0)),
+        pl.BlockSpec((size, 48), lambda i, s: (place(i, s), 0)),
+        pl.BlockSpec(change.shape, lambda i, s: (0, 0)),
     ]
-    args = [side, near, back, table, change]
+    args = [side, rows, table, change]
     aliases = {}
     if out is not None:
         specs.append(pl.BlockSpec(memory_space=pl.ANY))
         args.append(out)
-        aliases = {5: 0}
+        aliases = {4: 0}
     return pl.pallas_call(
-        functools.partial(finish_kernel, size),
+        functools.partial(finish_kernel, size, own),
         out_shape=jax.ShapeDtypeStruct((2 * half * STRIP_ROWS, LANES), F32),
         grid_spec=pltpu.PrefetchScalarGridSpec(
             num_scalar_prefetch=1,
-            grid=(2, steps),
+            grid=(chunk // size,),
             in_specs=specs,
-            out_specs=pl.BlockSpec((4 * size, LANES), lambda h, i, s: (place(h, i, s), 0)),
+            out_specs=pl.BlockSpec((4 * size, LANES), lambda i, s: (place(i, s), 0)),
         ),
         input_output_aliases=aliases,
         compiler_params=params(),
         name="finish",
         cost_estimate=pl.CostEstimate(
-            flops=2 * 48 * 8 * LANES * chunk,
-            transcendentals=0,
-            bytes_accessed=chunk * LANES * 4 * 16,
+            flops=2 * 48 * 4 * LANES * chunk, transcendentals=0, bytes_accessed=chunk * LANES * 4 * 8
         ),
     )(*args)
 
@@ -644,10 +609,11 @@
     strips = lax.axis_size("strip")
     groups = lax.axis_size("vel")
     strip = lax.axis_index("strip")
-    size = BLOCK
-    chunks = [size * n for n in chunk_blocks(half // size)]
+    size, chunks = plan(half)
     firsts = [sum(chunks[:c]) for c in range(len(chunks))]
     order = range(len(chunks))
+    cut = len(chunks) // 2
+    groups_of = [order[:cut], order[cut:]]
     side = (strip % 2).astype(jnp.int32).reshape(1)
     info = jnp.stack([strip % 2, (strip // 2) % 2]).astype(jnp.int32)
 
@@ -695,17 +661,14 @@
     other_cells = swap(cell_pair)
 
     got = []
-    earlier = []
     for c in order:
-        mid, edge, down = pack(side, flat, half, chunks[c], firsts[c], size, earlier)
-        earlier = [down]
-        edge_here = swap(edge)
-        mid_here = swap(mid)
-        below = against_flow(down)
-        got.append((edge_here, mid_here, below))
-
-    tables = prepare(points, vel_index, size, earlier[0])
+        far_start = ((1 - strip % 2) * half + firsts[c]) * rows
+        part = lax.dynamic_slice_in_dim(flat, far_start, chunks[c] * rows, axis=0)
+        got.append(swap(part))
+    tables = prepare(points, vel_index)
     table, _, weights = tables
+    lowest = pick(side, flat, lambda s: s * (half // size), half, size, [(0, 3)], [table])
+    below = against_flow(lowest)
     gram = jnp.asarray(target_moments(points))
     mat = jnp.asarray(macro_matrix())
 
@@ -719,7 +682,7 @@
     flow_fluid = 1.0 - flow(wall, other_cells[rows:])
     cells = jnp.concatenate([flow_fluid * (1.0 - flow_rate), flow_fluid])
 
-    home = sum_groups(home_moments(flat, weights, size))
+    home = sum_groups(home_moments(flat, weights, 2 * size))
     home = jnp.concatenate(
         [home[:13], collision_rate.reshape(1, -1), wall.reshape(1, -1), jnp.zeros((1, rows * cols), F32)]
     )
@@ -728,17 +691,23 @@
 
     width = BLOCK_ROWS * LANES
     sums = jnp.zeros((16, width), F32)
+    above = []
+    for c in order:
+        edges = pick(side, got[c], lambda s: 0, chunks[c], size, [(2, 1), (3, 0)])
+        above.append(with_flow(edges))
     kept = []
-    for c in order:
-        edge_here, mid_here, below = got[c]
-        above = with_flow(edge_here)
-        first, middle, edge, sums = transport(
-            side, [flat, mid_here, edge_here, above, below],
-            tables, cells, sums, half, chunks[c], firsts[c], size,
-        )
-        above = with_flow(edge)
-        below = against_flow(first)
-        kept.append((first, middle, edge, above, below))
+    for number, members in enumerate(groups_of):
+        start = firsts[members[0]]
+        length = sum(chunks[c] for c in members)
+        held = None
+        for c in members:
+            *held, sums = transport(
+                side, [flat, got[c], above[c], below], tables, cells, sums, half,
+                chunks[c], firsts[c], size, skip=firsts[c] - start, group=length, into=held,
+            )
+        next_above = with_flow(held[2])
+        next_below = against_flow(held[0])
+        kept.append((*held, next_above, next_below))
 
     total = sum_groups(sums)
     total = total + swap(total)
@@ -754,12 +723,15 @@
     )
 
     sums = jnp.zeros((16, width), F32)
-    near, far, back = {}, {}, {}
-    for c in reversed(order):
-        near[c], far[c], sums = transport(
-            side, list(kept[c]), tables, cells, sums, half, chunks[c], firsts[c], size, change
+    near, back = {}, {}
+    for c in order:
+        number = int(c >= cut)
+        start = firsts[groups_of[number][0]]
+        near[c], far, sums = transport(
+            side, list(kept[number]), tables, cells, sums, half,
+            chunks[c], firsts[c], size, change, skip=firsts[c] - start,
         )
-        back[c] = swap(far[c])
+        back[c] = swap(far)
     total = sum_groups(sums)
     total = total + swap(total)
     sum_a, sum_b = both_z(total)
@@ -773,8 +745,11 @@
         [pltpu.VMEM((16, SPAN * LANES), F32)],
     )
     out = None
-    for c in reversed(order):
-        out = finish(side, out, near[c], back[c], table, change, half, chunks[c], firsts[c], size)
+    for own, parts in ((True, near), (False, back)):
+        for c in order:
+            out = finish(
+                side, out, parts[c], own, table, change, half, chunks[c], firsts[c], size
+            )
     return out.reshape(dist.shape), state[:5].reshape(5, rows, cols)
 
 

time: 386 us -> 322 us (0.83)
  starting transfers between devices: 105 us -> 60.6 us
  Pallas kernels: 144 us -> 124 us
  local copies, waits for them, and re-layouts: 8.14 us -> 13.3 us
    ppermute x8 -> x3, starting transfers between devices: 28 us -> 11.5 us  [against_flow(): return lax.ppermute(value, 'strip', up_pairs)]
    ppermute x3, starting transfers between devices: 36 us -> 21.7 us  [both_z(): lax.ppermute(value, 'strip', pair_a)]
    ppermute x16 -> x12, starting transfers between devices: 24.1 us -> 11.2 us  [swap(): return lax.ppermute(value, 'strip', swap_pairs)]
    ppermute x8 -> x6, waiting for transfers between devices: 0.02 us -> 9.92 us  [with_flow(): return lax.ppermute(value, 'strip', down_pairs)]
    pallas_call x1, Pallas kernels: 12.9 us -> 3.76 us  [prepare(): pl.pallas_call(functools.partial(prepare_kernel, points), out_shape=(jax....]
    pallas_call x1, Pallas kernels: 15 us -> 6.47 us  [home_moments(): pl.pallas_call(functools.partial(moment_kernel, size), out_shape=jax.Shap...]
    ppermute x16 -> x12, waiting for transfers between devices: 100 us -> 93.1 us  [swap(): return lax.ppermute(value, 'strip', swap_pairs)]
    ppermute x8 -> x3, waiting for transfers between devices: 7.26 us -> 0.01 us  [against_flow(): return lax.ppermute(value, 'strip', up_pairs)]
  transfers between devices with their start and end apart: 47 -> 36, of which waited for: 13 -> 13; matrix products, arithmetic and copies ran while one was open for 2% -> 2% of each run, Pallas kernels for 33% -> 38%
where the time goes in v3:
time: 322 us; the launch traced here: 318 us
  Pallas kernels  124 us (39%)
  waiting for transfers between devices  116 us (36%)
  starting transfers between devices  60.6 us (19%)
  local copies, waits for them, and re-layouts  13.3 us (4%)
    ppermute x12, waiting for transfers between devices, swap(): return lax.ppermute(value, 'strip', swap_pairs)  93.1 us
    pallas_call x8, Pallas kernels, transport(): pl.pallas_call(functools.partial(transport_kernel, size, second_pass), ou...  77.7 us
    ppermute x3, starting transfers between devices, both_z(): lax.ppermute(value, 'strip', pair_a)  21.7 us
    pallas_call x8, Pallas kernels, finish(): pl.pallas_call(functools.partial(finish_kernel, size, own), out_shape=jax...  17.9 us
    pallas_call x5, Pallas kernels, pick(): pl.pallas_call(functools.partial(pick_kernel, size, picks), out_shape=jax...  12.4 us
    ppermute x3, starting transfers between devices, against_flow(): return lax.ppermute(value, 'strip', up_pairs)  11.5 us
    ppermute x12, starting transfers between devices, swap(): return lax.ppermute(value, 'strip', swap_pairs)  11.2 us
    ppermute x6, waiting for transfers between devices, with_flow(): return lax.ppermute(value, 'strip', down_pairs)  9.92 us
  transfers between devices with their start and end apart: 36, of which 13 were waited for; matrix products, arithmetic and copies ran while one was open for 2% of the time, Pallas kernels for 38%

profile of v3, /device:TPU:24, one launch (start us, length us, event | category | flops | bytes accessed | tf_op | source)
XLA Modules:
  0.0 318.5 jit_solution(10087340295186782809)
XLA Ops:
  0.7 2.8 constant_dynamic-slice_fusion.1
  3.5 1.5 collective-permute-start.6
  5.5 1.6 collective-permute-start.3
  7.1 2.4 constant_dynamic-slice_fusion
  10.0 1.5 collective-permute-start
  11.6 3.8 %prepare.1 = (bf16[3456,48]{1,0:T(8,128)(2,1)}, f32[3456,8]{1,0:T(8,128)}, bf16[3456,32]{1,0:T(8,128)(2,1)}) custom-call(s32[3,3456]{1,0:T(4,128)} %vel_ref.1), custom_call_target="tpu_custom_call" | custom-call | flops 691200 | bytes 3456000 | tf_op jit(solution)/shard_map/prepare/pallas_call | solution.py:182
  15.3 6.5 %home_moments.1 = f32[16,512]{1,0:T(8,128)} custom-call(f32[13824,128]{1,0:T(8,128)} %bitcast.15, bf16[3456,32]{1,0:T(8,128)(2,1)} %get-tuple-element.39.refs_5_.weight_ref.refs_8_), custom_call_target="tpu_custom_call" | custom-call | flops 169869312 | bytes 7077888 | tf_op jit(solution)/shard_map/home_moments/pallas_call | solution.py:228
  21.9 4.8 %shard_map.78 = f32[1,1728,128]{2,1,0:T(8,128)} custom-call(s32[1]{0:T(128)} %bitcast.side_ref, f32[13824,128]{1,0:T(8,128)} %bitcast.16, bf16[3456,48]{1,0:T(8,128)(2,1)} %get-tuple-element.37.rest_0_.refs_0_.table_ref), custom_call_target="tpu_custom_call" | custom-call | bytes 4423680 | tf_op jit(solution)/shard_map/pallas_call | solution.py:129
  26.7 31.0 %collective-permute-done.3 = f32[8,128]{1,0:T(8,128)S(1)} collective-permute-done((f32[8,128]{1,0:T(8,128)S(1)}, f32[8,128]{1,0:T(8,128)S(1)}, u32[]{:S(2)}, u32[]{:S(2)}) %collective-permute-start.3) | collective-permute-done | bytes 4128 | tf_op jit(solution)/shard_map/ppermute | solution.py:639
  57.8 2.4 collective-permute-start.2
  60.2 2.0 shard_map.80
  62.2 1.3 collective-permute-start.7
  63.5 2.0 shard_map.79
  65.5 1.3 collective-permute-start.5
  66.8 3.6 %collective-permute-done.8.strip_ref.refs_1_ = f32[1152,128]{1,0:T(8,128)} collective-permute-done((f32[1152,128]{1,0:T(8,128)}, f32[1152,128]{1,0:T(8,128)}, u32[]{:S(2)}, u32[]{:S(2)}) %collective-permute-start.8) | collective-permute-done | bytes 589856 | tf_op jit(solution)/shard_map/ppermute | solution.py:639
  70.4 1.5 collective-permute-start.17
  71.9 9.9 %collective-permute-done.strip_ref.refs_1_ = f32[1152,128]{1,0:T(8,128)S(1)} collective-permute-done((f32[1152,128]{1,0:T(8,128)}, f32[1152,128]{1,0:T(8,128)S(1)}, u32[]{:S(2)}, u32[]{:S(2)}) %collective-permute-start) | collective-permute-done | bytes 589856 | tf_op jit(solution)/shard_map/ppermute | solution.py:639
  82.5 1.8 shard_map.81
  84.3 1.8 shard_map.77
  86.1 1.3 collective-permute-start.9
  87.4 1.3 collective-permute-start.1
  88.8 9.9 %collective-permute-done.9.refs_2_ = f32[2,288,128]{2,1,0:T(8,128)S(1)} collective-permute-done((f32[2,288,128]{2,1,0:T(8,128)}, f32[2,288,128]{2,1,0:T(8,128)S(1)}, u32[]{:S(2)}, u32[]{:S(2)}) %collective-permute-start.9) | collective-permute-done | bytes 294944 | tf_op jit(solution)/shard_map/ppermute | solution.py:642
  100.0 6.9 %transport_first.4 = (f32[1,864,128]{2,1,0:T(8,128)}, f32[5,864,128]{2,1,0:T(8,128)}, f32[2,864,128]{2,1,0:T(8,128)}, f32[16,1024]{1,0:T(8,128)}) custom-call(s32[1]{0:T(128)} %bitcast.side_ref, f32[13824,128]{1,0:T(8,128)} %bitcast.17, f32[1152,128]{1,0:T(8,128)} %collective-permute-done.8.strip_ref.refs_1_, f32[2,288,128]{2,1,0:T(8,128)} %copy-done.8, ...), custom_call_target="tpu_custom_call" | custom-call | flops 17694720 | bytes 2801664 | tf_op jit(solution)/shard_map/transport_first/pallas_call | solution.py:402
  107.0 11.7 %transport_first.5 = (f32[1,864,128]{2,1,0:T(8,128)}, f32[5,864,128]{2,1,0:T(8,128)}, f32[2,864,128]{2,1,0:T(8,128)}, f32[16,1024]{1,0:T(8,128)}) custom-call(s32[1]{0:T(128)} %bitcast.side_ref, f32[13824,128]{1,0:T(8,128)} %bitcast.18, ...), custom_call_target="tpu_custom_call", output_to_operand_aliasing={{0}: (9, {}), {1}: (10, {}), {2}: (11, {})} | custom-call | flops 35389440 | bytes 5603328 | tf_op jit(solution)/shard_map/transport_first/pallas_call | solution.py:402
  118.7 1.3 collective-permute-start.24
  120.0 11.7 %transport_first.6 = (f32[1,864,128]{2,1,0:T(8,128)}, f32[5,864,128]{2,1,0:T(8,128)}, f32[2,864,128]{2,1,0:T(8,128)}, f32[16,1024]{1,0:T(8,128)}) custom-call(s32[1]{0:T(128)} %bitcast.side_ref, f32[13824,128]{1,0:T(8,128)} %bitcast.19, f32[2304,128]{1,0:T(8,128)} %collective-permute-done.4.strip_ref.refs_1_, f32[2,576,128]{2,1,0:T(8,128)} %collective-permute-done.5.refs_2_, ...), custom_call_target="tpu_custom_call" | custom-call | flops 35389440 | bytes 5603328 | tf_op jit(solution)/shard_map/transport_first/pallas_call | solution.py:402
  132.5 7.0 %transport_first.7 = (f32[1,864,128]{2,1,0:T(8,128)}, f32[5,864,128]{2,1,0:T(8,128)}, f32[2,864,128]{2,1,0:T(8,128)}, f32[16,1024]{1,0:T(8,128)}) custom-call(s32[1]{0:T(128)} %bitcast.side_ref, f32[13824,128]{1,0:T(8,128)} %bitcast.20, f32[1152,128]{1,0:T(8,128)} %copy-done.3, ...), custom_call_target="tpu_custom_call", output_to_operand_aliasing={{0}: (9, {}), {1}: (10, {}), {2}: (11, {})} | custom-call | flops 17694720 | bytes 2801664 | tf_op jit(solution)/shard_map/transport_first/pallas_call | solution.py:402
  139.5 1.3 collective-permute-start.22
  141.1 2.1 collective-permute-start.11
  144.1 3.1 collective-permute-done.11
  147.2 6.1 %collective-permute-start.25 = (f32[1,864,128]{2,1,0:T(8,128)S(1)}, f32[1,864,128]{2,1,0:T(8,128)}, u32[]{:S(2)}, u32[]{:S(2)}) collective-permute-start(f32[1,864,128]{2,1,0:T(8,128)S(1)} %copy-done.1), channel_id=1, source_target_pairs={{2,0},{4,2},{1,3},{6,4},{3,5},{5,7},{10,8},{12,10},{9,11},{14,12},... | collective-permute-start | bytes 1327112 | tf_op jit(solution)/shard_map/ppermute | solution.py:645
  153.3 3.0 collective-permute-start.23
  157.3 4.6 %collective-permute-done.13 = f32[16,1024]{1,0:T(8,128)S(1)} collective-permute-done((f32[16,1024]{1,0:T(8,128)S(1)}, f32[16,1024]{1,0:T(8,128)S(1)}, u32[]{:S(2)}, u32[]{:S(2)}) %collective-permute-start.13) | collective-permute-done | bytes 65568 | tf_op jit(solution)/shard_map/ppermute | solution.py:639
  162.2 4.3 %collective-permute-done.21.far_ref = f32[3,16,512]{2,1,0:T(8,128)S(1)} collective-permute-done((f32[3,16,512]{2,1,0:T(8,128)S(1)}, f32[3,16,512]{2,1,0:T(8,128)S(1)}, u32[]{:S(2)}, u32[]{:S(2)}) %collective-permute-start.21) | collective-permute-done | bytes 98336 | tf_op jit(solution)/shard_map/ppermute | solution.py:639
  167.9 13.9 %collective-permute-start.14 = (f32[16,1024]{1,0:T(8,128)S(1)}, f32[16,1024]{1,0:T(8,128)}, u32[]{:S(2)}, u32[]{:S(2)}) collective-permute-start(f32[16,1024]{1,0:T(8,128)S(1)} %add.81.sum_ref), channel_id=1, source_target_pairs={{0,2},{1,3},{2,0},{3,1},{4,6},{5,7},{6,4},{7,5},{8,10},{9,11},{10,... | collective-permute-start | bytes 196616 | tf_op jit(solution)/shard_map/ppermute | solution.py:648
  182.4 1.7 collective-permute-done.14.sum_a_ref
  184.1 3.2 %shard_map.82 = (bf16[48,1408]{1,0:T(8,128)(2,1)}, f32[16,3072]{1,0:T(8,128)}) custom-call(s32[2]{0:T(128)} %pad_add_fusion.info_ref, f32[16,1024]{1,0:T(8,128)} %copy-done.10, f32[16,1024]{1,0:T(8,128)} %collective-permute-done.14.sum_a_ref, f32[16,1024]{1,0:T(8,128)} %copy-done.14, f32[3,16,512]{2,1,0:T(8,128)} %copy-done.7, f32[3,16,512]{2,1,0:T(8,128)} %copy-done.13, ...), custom_call_target="tpu_custom_call" | custom-call | flops 4000000 | bytes 1000000 | tf_op jit(solution)/shard_map/pallas_call | solution.py:548
  188.3 7.3 %transport_second.4 = (f32[4,288,128]{2,1,0:T(8,128)}, f32[4,288,128]{2,1,0:T(8,128)}, f32[16,1024]{1,0:T(8,128)}) custom-call(s32[1]{0:T(128)} %bitcast.side_ref, bf16[3456,48]{1,0:T(8,128)(2,1)} %get-tuple-element.37.rest_0_.refs_0_.table_ref, bf16[48,1408]{1,0:T(8,128)(2,1)} %get-tuple-element.50.refs_1_, f32[1,864,128]{2,1,0:T(8,128)} %get-tuple-element.54.refs_2_, ...), custom_call_target="tpu_custom_call" | custom-call | flops 17694720 | bytes 2801664 | tf_op jit(solution)/shard_map/transport_second/pallas_call | solution.py:402
  195.6 12.9 %transport_second.5 = (f32[4,576,128]{2,1,0:T(8,128)}, f32[4,576,128]{2,1,0:T(8,128)}, f32[16,1024]{1,0:T(8,128)}) custom-call(s32[1]{0:T(128)} %bitcast.side_ref, bf16[3456,48]{1,0:T(8,128)(2,1)} %get-tuple-element.37.rest_0_.refs_0_.table_ref, bf16[48,1408]{1,0:T(8,128)(2,1)} %get-tuple-element.50.refs_1_, f32[1,864,128]{2,1,0:T(8,128)} %get-tuple-element.54.refs_2_, ...), custom_call_target="tpu_custom_call" | custom-call | flops 35389440 | bytes 5603328 | tf_op jit(solution)/shard_map/transport_second/pallas_call | solution.py:402
  208.5 1.1 collective-permute-start.34
  210.3 12.9 %transport_second.6 = (f32[4,576,128]{2,1,0:T(8,128)}, f32[4,576,128]{2,1,0:T(8,128)}, f32[16,1024]{1,0:T(8,128)}) custom-call(s32[1]{0:T(128)} %bitcast.side_ref, bf16[3456,48]{1,0:T(8,128)(2,1)} %get-tuple-element.37.rest_0_.refs_0_.table_ref, bf16[48,1408]{1,0:T(8,128)(2,1)} %get-tuple-element.50.refs_1_, f32[1,864,128]{2,1,0:T(8,128)} %get-tuple-element.51.refs_2_, ...), custom_call_target="tpu_custom_call" | custom-call | flops 35389440 | bytes 5603328 | tf_op jit(solution)/shard_map/transport_second/pallas_call | solution.py:402
  223.2 1.1 collective-permute-start.33
  224.3 7.3 %transport_second.7 = (f32[4,288,128]{2,1,0:T(8,128)}, f32[4,288,128]{2,1,0:T(8,128)}, f32[16,1024]{1,0:T(8,128)}) custom-call(s32[1]{0:T(128)} %bitcast.side_ref, bf16[3456,48]{1,0:T(8,128)(2,1)} %get-tuple-element.37.rest_0_.refs_0_.table_ref, bf16[48,1408]{1,0:T(8,128)(2,1)} %get-tuple-element.50.refs_1_, f32[1,864,128]{2,1,0:T(8,128)} %get-tuple-element.51.refs_2_, ...), custom_call_target="tpu_custom_call" | custom-call | flops 17694720 | bytes 2801664 | tf_op jit(solution)/shard_map/transport_second/pallas_call | solution.py:402
  231.6 1.0 collective-permute-start.35
  232.6 1.0 collective-permute-start.26
  233.8 1.4 collective-permute-start.28
  235.3 3.0 collective-permute-done.28
  238.3 1.0 collective-permute-start.27
  239.3 3.0 collective-permute-done.27
  243.2 1.0 collective-permute-start.30
  244.2 39.6 %collective-permute-done.30 = f32[16,1024]{1,0:T(8,128)S(1)} collective-permute-done((f32[16,1024]{1,0:T(8,128)S(1)}, f32[16,1024]{1,0:T(8,128)S(1)}, u32[]{:S(2)}, u32[]{:S(2)}) %collective-permute-start.30) | collective-permute-done | bytes 65568 | tf_op jit(solution)/shard_map/ppermute | solution.py:639
  284.5 7.4 %collective-permute-start.31 = (f32[16,1024]{1,0:T(8,128)S(1)}, f32[16,1024]{1,0:T(8,128)S(1)}, u32[]{:S(2)}, u32[]{:S(2)}) collective-permute-start(f32[16,1024]{1,0:T(8,128)S(1)} %add.88.sum_ref), channel_id=1, source_target_pairs={{0,2},{1,3},{2,0},{3,1},{4,6},{5,7},{6,4},{7,5},{8,10},{9,11},{10,... | collective-permute-start | bytes 196616 | tf_op jit(solution)/shard_map/ppermute | solution.py:648
  291.9 2.2 collective-permute-done.31.sum_a_ref
  294.8 2.6 shard_map.83
  297.3 1.3 reshape.27
  298.6 2.1 finish.8.rest_0_
  300.8 2.3 finish.9.rest_0_
  303.1 2.3 finish.10.rest_0_
  305.5 2.1 finish.11.rest_0_
  307.6 2.1 finish.12.rest_0_
  309.7 1.1 copy-done.5
  310.8 2.3 finish.13.rest_0_
  313.1 2.4 finish.14.rest_0_
  316.4 2.1 finish.15
  (97 shorter events, 13.2 us)
Async XLA Ops:
  0.7 4.9 %copy-start.18 = (s32[4,128]{1,0:T(4,128)S(1)}, s32[4,128]{1,0:T(4,128)}, u32[]{:S(2)}) copy-start(s32[4,128]{1,0:T(4,128)} %param.7) | copy-start | bytes 6148
  0.7 4.8 %copy-start.17 = (f32[4,128]{1,0:T(4,128)S(1)}, f32[4,128]{1,0:T(4,128)}, u32[]{:S(2)}) copy-start(f32[4,128]{1,0:T(4,128)} %param.8) | copy-start | bytes 6148
  3.5 54.3 %collective-permute-start.6 = (f32[2304,128]{1,0:T(8,128)S(1)}, f32[2304,128]{1,0:T(8,128)}, u32[]{:S(2)}, u32[]{:S(2)}) collective-permute-start(f32[2304,128]{1,0:T(8,128)S(1)} %get-tuple-element.74), channel_id=1, source_target_pairs={{0,1},{1,0},{2,3},{3,2},{4,5},{5,4},{6,7},{7,6},{8,9},{9,8},{10,11... | collective-permute-start | bytes 3538952 | tf_op jit(solution)/shard_map/ppermute | solution.py:639
  5.0 57.2 %collective-permute-start.4 = (f32[2304,128]{1,0:T(8,128)}, f32[2304,128]{1,0:T(8,128)}, u32[]{:S(2)}, u32[]{:S(2)}) collective-permute-start(f32[2304,128]{1,0:T(8,128)} %get-tuple-element.75), channel_id=1, source_target_pairs={{0,1},{1,0},{2,3},{3,2},{4,5},{5,4},{6,7},{7,6},{8,9},{9,8},{10,11... | collective-permute-start | bytes 3538952 | tf_op jit(solution)/shard_map/ppermute | solution.py:639
  5.5 52.2 %collective-permute-start.3 = (f32[8,128]{1,0:T(8,128)S(1)}, f32[8,128]{1,0:T(8,128)S(1)}, u32[]{:S(2)}, u32[]{:S(2)}) collective-permute-start(f32[8,128]{1,0:T(8,128)S(1)} %pad_maximum_fusion.2), channel_id=1, source_target_pairs={{0,1},{1,0},{2,3},{3,2},{4,5},{5,4},{6,7},{7,6},{8,9},{9,8},{10,11... | collective-permute-start | bytes 12296 | tf_op jit(solution)/shard_map/ppermute | solution.py:639
  9.5 60.9 %collective-permute-start.8 = (f32[1152,128]{1,0:T(8,128)}, f32[1152,128]{1,0:T(8,128)}, u32[]{:S(2)}, u32[]{:S(2)}) collective-permute-start(f32[1152,128]{1,0:T(8,128)} %get-tuple-element.72), channel_id=1, source_target_pairs={{0,1},{1,0},{2,3},{3,2},{4,5},{5,4},{6,7},{7,6},{8,9},{9,8},{10,11... | collective-permute-start | bytes 1769480 | tf_op jit(solution)/shard_map/ppermute | solution.py:639
  10.0 71.8 %collective-permute-start = (f32[1152,128]{1,0:T(8,128)}, f32[1152,128]{1,0:T(8,128)S(1)}, u32[]{:S(2)}, u32[]{:S(2)}) collective-permute-start(f32[1152,128]{1,0:T(8,128)} %get-tuple-element.73), channel_id=1, source_target_pairs={{0,1},{1,0},{2,3},{3,2},{4,5},{5,4},{6,7},{7,6},{8,9},{9,8},{10,11... | collective-permute-start | bytes 1769480 | tf_op jit(solution)/shard_map/ppermute | solution.py:639
  21.9 35.8 %copy-start.12 = (f32[16,512]{1,0:T(8,128)S(1)}, f32[16,512]{1,0:T(8,128)}, u32[]{:S(2)}) copy-start(f32[16,512]{1,0:T(8,128)} %home_moments.1) | copy-start | bytes 98308
  57.7 7.8 %collective-permute-start.18 = (f32[16,512]{1,0:T(8,128)S(1)}, f32[16,512]{1,0:T(8,128)S(1)}, u32[]{:S(2)}, u32[]{:S(2)}) collective-permute-start(f32[16,512]{1,0:T(8,128)S(1)} %copy-done.12), channel_id=1, source_target_pairs={{0,24},{8,0},{16,8},{24,16},{1,25},{9,1},{17,9},{25,17},{2,26},{10... | collective-permute-start | bytes 98312 | tf_op jit(solution)/shard_map/ppermute | solution.py:653
  57.8 41.3 %collective-permute-start.2 = (f32[1,1728,128]{2,1,0:T(8,128)}, f32[1,1728,128]{2,1,0:T(8,128)S(1)}, u32[]{:S(2)}, u32[]{:S(2)}) collective-permute-start(f32[1,1728,128]{2,1,0:T(8,128)} %shard_map.78), channel_id=1, source_target_pairs={{2,0},{4,2},{1,3},{6,4},{3,5},{5,7},{10,8},{12,10},{9,11},{14,12},... | collective-permute-start | bytes 2654216 | tf_op jit(solution)/shard_map/ppermute | solution.py:645
  62.2 44.8 %collective-permute-start.7 = (f32[2,576,128]{2,1,0:T(8,128)}, f32[2,576,128]{2,1,0:T(8,128)}, u32[]{:S(2)}, u32[]{:S(2)}) collective-permute-start(f32[2,576,128]{2,1,0:T(8,128)} %shard_map.80), channel_id=1, source_target_pairs={{0,2},{2,4},{3,1},{4,6},{5,3},{7,5},{8,10},{10,12},{11,9},{12,14},... | collective-permute-start | bytes 1769480 | tf_op jit(solution)/shard_map/ppermute | solution.py:642
  65.5 54.5 %collective-permute-start.5 = (f32[2,576,128]{2,1,0:T(8,128)}, f32[2,576,128]{2,1,0:T(8,128)}, u32[]{:S(2)}, u32[]{:S(2)}) collective-permute-start(f32[2,576,128]{2,1,0:T(8,128)} %shard_map.79), channel_id=1, source_target_pairs={{0,2},{2,4},{3,1},{4,6},{5,3},{7,5},{8,10},{10,12},{11,9},{12,14},... | collective-permute-start | bytes 1769480 | tf_op jit(solution)/shard_map/ppermute | solution.py:642
  70.4 15.7 %collective-permute-start.17 = (f32[16,512]{1,0:T(8,128)S(1)}, f32[16,512]{1,0:T(8,128)S(1)}, u32[]{:S(2)}, u32[]{:S(2)}) collective-permute-start(f32[16,512]{1,0:T(8,128)S(1)} %copy-done.12), channel_id=1, source_target_pairs={{0,16},{8,24},{16,0},{24,8},{1,17},{9,25},{17,1},{25,9},{2,18},{10... | collective-permute-start | bytes 98312 | tf_op jit(solution)/shard_map/ppermute | solution.py:653
  81.8 2.5 copy-start.3
  81.8 5.6 %collective-permute-start.16 = (f32[16,512]{1,0:T(8,128)S(1)}, f32[16,512]{1,0:T(8,128)S(1)}, u32[]{:S(2)}, u32[]{:S(2)}) collective-permute-start(f32[16,512]{1,0:T(8,128)S(1)} %copy-done.12), channel_id=1, source_target_pairs={{0,8},{8,16},{16,24},{24,0},{1,9},{9,17},{17,25},{25,1},{2,10},{10... | collective-permute-start | bytes 98312 | tf_op jit(solution)/shard_map/ppermute | solution.py:653
  86.1 12.6 %collective-permute-start.9 = (f32[2,288,128]{2,1,0:T(8,128)}, f32[2,288,128]{2,1,0:T(8,128)S(1)}, u32[]{:S(2)}, u32[]{:S(2)}) collective-permute-start(f32[2,288,128]{2,1,0:T(8,128)} %shard_map.81), channel_id=1, source_target_pairs={{0,2},{2,4},{3,1},{4,6},{5,3},{7,5},{8,10},{10,12},{11,9},{12,14},... | collective-permute-start | bytes 884744 | tf_op jit(solution)/shard_map/ppermute | solution.py:642
  87.4 44.3 %collective-permute-start.1 = (f32[2,288,128]{2,1,0:T(8,128)}, f32[2,288,128]{2,1,0:T(8,128)S(1)}, u32[]{:S(2)}, u32[]{:S(2)}) collective-permute-start(f32[2,288,128]{2,1,0:T(8,128)} %shard_map.77), channel_id=1, source_target_pairs={{0,2},{2,4},{3,1},{4,6},{5,3},{7,5},{8,10},{10,12},{11,9},{12,14},... | collective-permute-start | bytes 884744 | tf_op jit(solution)/shard_map/ppermute | solution.py:642
  98.7 1.0 copy-start.8
  98.7 44.5 %collective-permute-start.19 = (f32[16,512]{1,0:T(8,128)S(1)}, f32[16,512]{1,0:T(8,128)S(1)}, u32[]{:S(2)}, u32[]{:S(2)}) collective-permute-start(f32[16,512]{1,0:T(8,128)S(1)} %maximum_maximum_fusion), channel_id=1, source_target_pairs={{0,2},{1,3},{2,0},{3,1},{4,6},{5,7},{6,4},{7,5},{8,10},{9,11},{10,... | collective-permute-start | bytes 98312 | tf_op jit(solution)/shard_map/ppermute | solution.py:648
  99.1 0.9 copy-start
  118.7 68.7 %collective-permute-start.24 = (f32[2,864,128]{2,1,0:T(8,128)}, f32[2,864,128]{2,1,0:T(8,128)S(1)}, u32[]{:S(2)}, u32[]{:S(2)}) collective-permute-start(f32[2,864,128]{2,1,0:T(8,128)} %get-tuple-element.56.refs_4_), channel_id=1, source_target_pairs={{0,2},{2,4},{3,1},{4,6},{5,3},{7,5},{8,10},{10,12},{11,9},{12,14},... | collective-permute-start | bytes 2654216 | tf_op jit(solution)/shard_map/ppermute | solution.py:642
  131.7 0.7 copy-start.9
  132.5 14.7 %copy-start.1 = (f32[1,864,128]{2,1,0:T(8,128)S(1)}, f32[1,864,128]{2,1,0:T(8,128)}, u32[]{:S(2)}) copy-start(f32[1,864,128]{2,1,0:T(8,128)} %get-tuple-element.54.refs_2_) | copy-start | bytes 1327108
  139.5 70.1 %collective-permute-start.22 = (f32[2,864,128]{2,1,0:T(8,128)}, f32[2,864,128]{2,1,0:T(8,128)}, u32[]{:S(2)}, u32[]{:S(2)}) collective-permute-start(f32[2,864,128]{2,1,0:T(8,128)} %get-tuple-element.53.refs_4_), channel_id=1, source_target_pairs={{0,2},{2,4},{3,1},{4,6},{5,3},{7,5},{8,10},{10,12},{11,9},{12,14},... | collective-permute-start | bytes 2654216 | tf_op jit(solution)/shard_map/ppermute | solution.py:642
  140.8 2.6 collective-permute-start.12
  141.1 6.1 %collective-permute-start.11 = (f32[16,1024]{1,0:T(8,128)}, f32[16,1024]{1,0:T(8,128)S(1)}, u32[]{:S(2)}, u32[]{:S(2)}) collective-permute-start(f32[16,1024]{1,0:T(8,128)} %get-tuple-element.49), channel_id=1, source_target_pairs={{0,16},{8,24},{16,0},{24,8},{1,17},{9,25},{17,1},{25,9},{2,18},{10... | collective-permute-start | bytes 196616 | tf_op jit(solution)/shard_map/ppermute | solution.py:653
  143.2 10.1 %collective-permute-start.10 = (f32[16,1024]{1,0:T(8,128)}, f32[16,1024]{1,0:T(8,128)S(1)}, u32[]{:S(2)}, u32[]{:S(2)}) collective-permute-start(f32[16,1024]{1,0:T(8,128)} %get-tuple-element.49), channel_id=1, source_target_pairs={{0,8},{8,16},{16,24},{24,0},{1,9},{9,17},{17,25},{25,1},{2,10},{10... | collective-permute-start | bytes 196616 | tf_op jit(solution)/shard_map/ppermute | solution.py:653
  143.4 13.8 %collective-permute-start.20 = (f32[16,512]{1,0:T(8,128)S(1)}, f32[16,512]{1,0:T(8,128)S(1)}, u32[]{:S(2)}, u32[]{:S(2)}) collective-permute-start(f32[16,512]{1,0:T(8,128)S(1)} %maximum_maximum_fusion), channel_id=1, source_target_pairs={{2,4},{3,5},{4,2},{5,3},{10,12},{11,13},{12,10},{13,11},{18,20},{1... | collective-permute-start | bytes 98312 | tf_op jit(solution)/shard_map/ppermute | solution.py:648
  147.2 40.2 %collective-permute-start.25 = (f32[1,864,128]{2,1,0:T(8,128)S(1)}, f32[1,864,128]{2,1,0:T(8,128)}, u32[]{:S(2)}, u32[]{:S(2)}) collective-permute-start(f32[1,864,128]{2,1,0:T(8,128)S(1)} %copy-done.1), channel_id=1, source_target_pairs={{2,0},{4,2},{1,3},{6,4},{3,5},{5,7},{10,8},{12,10},{9,11},{14,12},... | collective-permute-start | bytes 1327112 | tf_op jit(solution)/shard_map/ppermute | solution.py:645
  153.3 56.2 %collective-permute-start.23 = (f32[1,864,128]{2,1,0:T(8,128)}, f32[1,864,128]{2,1,0:T(8,128)S(1)}, u32[]{:S(2)}, u32[]{:S(2)}) collective-permute-start(f32[1,864,128]{2,1,0:T(8,128)} %get-tuple-element.51.refs_2_), channel_id=1, source_target_pairs={{2,0},{4,2},{1,3},{6,4},{3,5},{5,7},{10,8},{12,10},{9,11},{14,12},... | collective-permute-start | bytes 1327112 | tf_op jit(solution)/shard_map/ppermute | solution.py:645
  157.2 4.7 %collective-permute-start.13 = (f32[16,1024]{1,0:T(8,128)S(1)}, f32[16,1024]{1,0:T(8,128)S(1)}, u32[]{:S(2)}, u32[]{:S(2)}) collective-permute-start(f32[16,1024]{1,0:T(8,128)S(1)} %add_add_fusion.1), channel_id=1, source_target_pairs={{0,1},{1,0},{2,3},{3,2},{4,5},{5,4},{6,7},{7,6},{8,9},{9,8},{10,11... | collective-permute-start | bytes 196616 | tf_op jit(solution)/shard_map/ppermute | solution.py:639
  157.3 26.8 %copy-start.7 = (f32[3,16,512]{2,1,0:T(8,128)}, f32[3,16,512]{2,1,0:T(8,128)S(1)}, u32[]{:S(2)}) copy-start(f32[3,16,512]{2,1,0:T(8,128)S(1)} %pad_maximum_fusion.near_ref) | copy-start | bytes 294916
  161.9 4.6 %collective-permute-start.21 = (f32[3,16,512]{2,1,0:T(8,128)S(1)}, f32[3,16,512]{2,1,0:T(8,128)S(1)}, u32[]{:S(2)}, u32[]{:S(2)}) collective-permute-start(f32[3,16,512]{2,1,0:T(8,128)S(1)} %pad_maximum_fusion.near_ref), channel_id=1, source_target_pairs={{0,1},{1,0},{2,3},{3,2},{4,5},{5,4},{6,7},{7,6},{8,9},{9,8},{10,11... | collective-permute-start | bytes 294920 | tf_op jit(solution)/shard_map/ppermute | solution.py:639
  162.2 21.9 %copy-start.10 = (f32[16,1024]{1,0:T(8,128)}, f32[16,1024]{1,0:T(8,128)S(1)}, u32[]{:S(2)}) copy-start(f32[16,1024]{1,0:T(8,128)S(1)} %add.81.sum_ref) | copy-start | bytes 196612
  166.5 17.6 %copy-start.13 = (f32[3,16,512]{2,1,0:T(8,128)}, f32[3,16,512]{2,1,0:T(8,128)S(1)}, u32[]{:S(2)}) copy-start(f32[3,16,512]{2,1,0:T(8,128)S(1)} %collective-permute-done.21.far_ref) | copy-start | bytes 294916
  166.5 0.7 collective-permute-start.15
  167.2 0.6 copy-start.14
  167.9 16.3 %collective-permute-start.14 = (f32[16,1024]{1,0:T(8,128)S(1)}, f32[16,1024]{1,0:T(8,128)}, u32[]{:S(2)}, u32[]{:S(2)}) collective-permute-start(f32[16,1024]{1,0:T(8,128)S(1)} %add.81.sum_ref), channel_id=1, source_target_pairs={{0,2},{1,3},{2,0},{3,1},{4,6},{5,7},{6,4},{7,5},{8,10},{9,11},{10,... | collective-permute-start | bytes 196616 | tf_op jit(solution)/shard_map/ppermute | solution.py:648
  187.4 1.0 copy-start.2
  208.5 101.2 %collective-permute-start.34 = (f32[4,576,128]{2,1,0:T(8,128)}, f32[4,576,128]{2,1,0:T(8,128)S(1)}, u32[]{:S(2)}, u32[]{:S(2)}) collective-permute-start(f32[4,576,128]{2,1,0:T(8,128)} %get-tuple-element.65), channel_id=1, source_target_pairs={{0,1},{1,0},{2,3},{3,2},{4,5},{5,4},{6,7},{7,6},{8,9},{9,8},{10,11... | collective-permute-start | bytes 3538952 | tf_op jit(solution)/shard_map/ppermute | solution.py:639
  209.6 0.8 copy-start.4
  223.2 89.9 %collective-permute-start.33 = (f32[4,576,128]{2,1,0:T(8,128)}, f32[4,576,128]{2,1,0:T(8,128)}, u32[]{:S(2)}, u32[]{:S(2)}) collective-permute-start(f32[4,576,128]{2,1,0:T(8,128)} %get-tuple-element.64), channel_id=1, source_target_pairs={{0,1},{1,0},{2,3},{3,2},{4,5},{5,4},{6,7},{7,6},{8,9},{9,8},{10,11... | collective-permute-start | bytes 3538952 | tf_op jit(solution)/shard_map/ppermute | solution.py:639
  231.6 2.2 collective-permute-start.29
  231.6 76.0 %collective-permute-start.35 = (f32[4,288,128]{2,1,0:T(8,128)}, f32[4,288,128]{2,1,0:T(8,128)}, u32[]{:S(2)}, u32[]{:S(2)}) collective-permute-start(f32[4,288,128]{2,1,0:T(8,128)} %get-tuple-element.66), channel_id=1, source_target_pairs={{0,1},{1,0},{2,3},{3,2},{4,5},{5,4},{6,7},{7,6},{8,9},{9,8},{10,11... | collective-permute-start | bytes 1769480 | tf_op jit(solution)/shard_map/ppermute | solution.py:639
  232.6 82.8 %collective-permute-start.26 = (f32[4,288,128]{2,1,0:T(8,128)}, f32[4,288,128]{2,1,0:T(8,128)S(1)}, u32[]{:S(2)}, u32[]{:S(2)}) collective-permute-start(f32[4,288,128]{2,1,0:T(8,128)} %get-tuple-element.60), channel_id=1, source_target_pairs={{0,1},{1,0},{2,3},{3,2},{4,5},{5,4},{6,7},{7,6},{8,9},{9,8},{10,11... | collective-permute-start | bytes 1769480 | tf_op jit(solution)/shard_map/ppermute | solution.py:639
  233.8 4.5 %collective-permute-start.28 = (f32[16,1024]{1,0:T(8,128)}, f32[16,1024]{1,0:T(8,128)S(1)}, u32[]{:S(2)}, u32[]{:S(2)}) collective-permute-start(f32[16,1024]{1,0:T(8,128)} %get-tuple-element.61), channel_id=1, source_target_pairs={{0,16},{8,24},{16,0},{24,8},{1,17},{9,25},{17,1},{25,9},{2,18},{10... | collective-permute-start | bytes 196616 | tf_op jit(solution)/shard_map/ppermute | solution.py:653
  238.3 4.0 %collective-permute-start.27 = (f32[16,1024]{1,0:T(8,128)}, f32[16,1024]{1,0:T(8,128)S(1)}, u32[]{:S(2)}, u32[]{:S(2)}) collective-permute-start(f32[16,1024]{1,0:T(8,128)} %get-tuple-element.61), channel_id=1, source_target_pairs={{0,8},{8,16},{16,24},{24,0},{1,9},{9,17},{17,25},{25,1},{2,10},{10... | collective-permute-start | bytes 196616 | tf_op jit(solution)/shard_map/ppermute | solution.py:653
  243.2 40.6 %collective-permute-start.30 = (f32[16,1024]{1,0:T(8,128)S(1)}, f32[16,1024]{1,0:T(8,128)S(1)}, u32[]{:S(2)}, u32[]{:S(2)}) collective-permute-start(f32[16,1024]{1,0:T(8,128)S(1)} %add_add_fusion), channel_id=1, source_target_pairs={{0,1},{1,0},{2,3},{3,2},{4,5},{5,4},{6,7},{7,6},{8,9},{9,8},{10,11... | collective-permute-start | bytes 196616 | tf_op jit(solution)/shard_map/ppermute | solution.py:639
  283.8 10.4 %copy-start.11 = (f32[16,1024]{1,0:T(8,128)}, f32[16,1024]{1,0:T(8,128)S(1)}, u32[]{:S(2)}) copy-start(f32[16,1024]{1,0:T(8,128)S(1)} %add.88.sum_ref) | copy-start | bytes 196612
  283.8 0.7 collective-permute-start.32
  284.5 9.7 %copy-start.15 = (f32[16,1024]{1,0:T(8,128)}, f32[16,1024]{1,0:T(8,128)S(1)}, u32[]{:S(2)}) copy-start(f32[16,1024]{1,0:T(8,128)S(1)} %collective-permute-done.32.sum_b_ref) | copy-start | bytes 196612
  284.5 9.6 %collective-permute-start.31 = (f32[16,1024]{1,0:T(8,128)S(1)}, f32[16,1024]{1,0:T(8,128)S(1)}, u32[]{:S(2)}, u32[]{:S(2)}) collective-permute-start(f32[16,1024]{1,0:T(8,128)S(1)} %add.88.sum_ref), channel_id=1, source_target_pairs={{0,2},{1,3},{2,0},{3,1},{4,6},{5,7},{6,4},{7,5},{8,10},{9,11},{10,... | collective-permute-start | bytes 196616 | tf_op jit(solution)/shard_map/ppermute | solution.py:648
  294.1 0.6 copy-start.16
  309.7 1.1 copy-start.5
  315.5 0.9 copy-start.6

commit v4 on v3

--- a/solution.py
+++ b/solution.py
@@ -19,7 +19,6 @@
 STRIP_ROWS = 4
 BLOCK_ROWS = 2 * STRIP_ROWS
 SPAN = 3 * BLOCK_ROWS
-GROUP = 16
 F32 = jnp.float32
 BF16 = jnp.bfloat16
 
@@ -196,12 +195,6 @@
     )(vel_index)
 
 
-def split_store(value, first_ref, second_ref, rows, columns):
-    first = value.astype(BF16)
-    first_ref[rows, columns] = first
-    second_ref[rows, columns] = (value - first.astype(F32)).astype(BF16)
-
-
 def weighted(weights, first, second):
     over_rows = (((0,), (0,)), ((), ()))
     both = lax.dot_general(weights, first, over_rows, preferred_element_type=F32)
@@ -209,17 +202,19 @@
     return both[:16] + both[16:] + rest[:16]
 
 
-def moment_kernel(size, dist_ref, weight_ref, out_ref, first_ref, second_ref):
+def moment_kernel(size, dist_ref, weight_ref, out_ref):
     @pl.when(pl.program_id(0) == 0)
     def _():
         out_ref[...] = jnp.zeros_like(out_ref)
 
-    for row in range(STRIP_ROWS):
-        columns = pl.ds(row * LANES, LANES)
-        split_store(
-            dist_ref[strided(row, size), :], first_ref, second_ref, pl.ds(0, size), columns
+    for pair in range(0, STRIP_ROWS, 2):
+        value = jnp.concatenate(
+            [dist_ref[strided(row, size), :] for row in (pair, pair + 1)], axis=1
         )
-    out_ref[...] += weighted(weight_ref[...], first_ref[...], second_ref[...])
+        high = value.astype(BF16)
+        out_ref[:, pair * LANES : (pair + 2) * LANES] += weighted(
+            weight_ref[...], high, (value - high.astype(F32)).astype(BF16)
+        )
 
 
 def home_moments(flat, weights, size):
@@ -234,7 +229,6 @@
             pl.BlockSpec((size, 32), lambda i: (i, 0)),
         ],
         out_specs=pl.BlockSpec((16, width), lambda i: (0, 0)),
-        scratch_shapes=[pltpu.VMEM((size, width), BF16), pltpu.VMEM((size, width), BF16)],
         compiler_params=params(),
         name="home_moments",
         cost_estimate=pl.CostEstimate(
@@ -250,10 +244,11 @@
         (own_ref, got_ref, up_ref, down_ref, *rest) = refs
     (const_ref, weight_ref, cell_ref, sum_in_ref, *rest) = rest
     if second_pass:
-        (near_out, far_out, sum_ref, first_ref, second_ref, lift_ref) = rest
+        (near_out, far_out, sum_ref, lift_ref) = rest[-4:]
     else:
-        (first_out, mid_out, edge_out, sum_ref, first_ref, second_ref) = rest[-6:]
+        (first_out, mid_out, edge_out, sum_ref) = rest[-4:]
     side = side_ref[0]
+    group_size = 32 if size % 32 == 0 else 16
 
     @pl.when(pl.program_id(0) == 0)
     def _():
@@ -262,13 +257,20 @@
     if second_pass:
         lift_ref[...] = jnp.dot(table_ref[...], change_ref[...], preferred_element_type=F32)
 
-    lane = lax.broadcasted_iota(jnp.int32, (GROUP, LANES), 1)
+    def row_out(row):
+        if second_pass:
+            return near_out.at[row] if row < 4 else far_out.at[row - 4]
+        if row == 0:
+            return first_out
+        return mid_out.at[row - 1] if row < 6 else edge_out.at[row - 6]
+
+    lane = lax.broadcasted_iota(jnp.int32, (group_size, LANES), 1)
     inner_low = jnp.where(lane == 0, 0.0, 1.0)
     inner_high = jnp.where(lane == LANES - 1, 0.0, 1.0)
 
     def body(group, carry):
-        base = pl.multiple_of(group * GROUP, GROUP)
-        rows = pl.ds(base, GROUP)
+        base = pl.multiple_of(group * group_size, group_size)
+        rows = pl.ds(base, group_size)
 
         def load(row):
             if row < 0:
@@ -285,13 +287,13 @@
             else:
                 ref = own_ref if row < 4 else got_ref
                 local = jnp.where(side == 1, 3 - row % 4, row % 4)
-                value = ref[strided(base * STRIP_ROWS + local, GROUP), :]
+                value = ref[strided(base * STRIP_ROWS + local, group_size), :]
             if second_pass:
                 value = value + lift_ref[rows, pl.ds((row + 2) * LANES, LANES)]
             return value
 
         def wide(column):
-            return jnp.broadcast_to(const_ref[rows, column : column + 1], (GROUP, LANES))
+            return jnp.broadcast_to(const_ref[rows, column : column + 1], (group_size, LANES))
 
         speed_x = wide(0)
         speed_y = wide(1)
@@ -317,30 +319,22 @@
             face = here + half_sign * minmod(left, right)
             other = jnp.where(forward, pltpu.roll(face, 1, 1), pltpu.roll(face, LANES - 1, 1))
             drift = drift + speed_y * (face - other * open_end)
-            keep = jnp.broadcast_to(cell_ref[row : row + 1, :], (GROUP, LANES))
-            fluid = jnp.broadcast_to(cell_ref[row + 8 : row + 9, :], (GROUP, LANES))
+            keep = jnp.broadcast_to(cell_ref[row : row + 1, :], (group_size, LANES))
+            fluid = jnp.broadcast_to(cell_ref[row + 8 : row + 9, :], (group_size, LANES))
             value = keep * here - fluid * drift
-            split_store(value, first_ref, second_ref, rows, pl.ds(row * LANES, LANES))
-            if second_pass:
-                if row < 4:
-                    near_out[row, rows, :] = value
-                else:
-                    far_out[row - 4, rows, :] = value
-            elif row == 0:
-                first_out[rows, :] = value
-            elif row < 6:
-                mid_out[row - 1, rows, :] = value
-            else:
-                edge_out[row - 6, rows, :] = value
+            row_out(row)[rows, :] = value
             here = ahead
         return carry
 
-    lax.fori_loop(0, size // GROUP, body, 0)
-    part = weighted(weight_ref[...], first_ref[...], second_ref[...])
-    for row in range(BLOCK_ROWS):
-        place = jnp.where(side == 1, 7 - row, row)
-        columns = pl.ds(pl.multiple_of(place * LANES, LANES), LANES)
-        sum_ref[:, columns] += part[:, row * LANES : (row + 1) * LANES]
+    lax.fori_loop(0, size // group_size, body, 0)
+    for pair in range(0, BLOCK_ROWS, 2):
+        value = jnp.concatenate([row_out(pair)[...], row_out(pair + 1)[...]], axis=1)
+        high = value.astype(BF16)
+        part = weighted(weight_ref[...], high, (value - high.astype(F32)).astype(BF16))
+        for row in (pair, pair + 1):
+            place = jnp.where(side == 1, 7 - row, row)
+            columns = pl.ds(pl.multiple_of(place * LANES, LANES), LANES)
+            sum_ref[:, columns] += part[:, (row - pair) * LANES : (row - pair + 1) * LANES]
 
 
 def transport(
@@ -372,8 +366,8 @@
             stack_of(2, offset),
             stack_of(None, offset),
         ]
-        outs = [jax.ShapeDtypeStruct((4, chunk, LANES), F32)] * 2
-        out_specs = [stack_of(4, 0)] * 2
+        outs = [jax.ShapeDtypeStruct((4, n, LANES), F32) for n in (half, chunk)]
+        out_specs = [stack_of(4, begin), stack_of(4, 0)]
         scratch = [pltpu.VMEM((size, 11 * LANES), F32)]
     else:
         args = []
@@ -396,9 +390,9 @@
         whole,
     ]
     if into is not None:
-        aliases = {len(args) + n: n for n in range(3)}
+        aliases = {len(args) + n: n for n in range(len(into))}
         args = [*args, *into]
-        specs = [*specs, *[pl.BlockSpec(memory_space=pl.ANY)] * 3]
+        specs = [*specs, *[pl.BlockSpec(memory_space=pl.ANY)] * len(into)]
     return pl.pallas_call(
         functools.partial(transport_kernel, size, second_pass),
         out_shape=(*outs, jax.ShapeDtypeStruct((16, width), F32)),
@@ -407,11 +401,7 @@
             grid=(steps,),
             in_specs=specs,
             out_specs=[*out_specs, whole],
-            scratch_shapes=[
-                pltpu.VMEM((size, width), BF16),
-                pltpu.VMEM((size, width), BF16),
-                *scratch,
-            ],
+            scratch_shapes=scratch,
         ),
         input_output_aliases=aliases,
         compiler_params=params(),
@@ -665,10 +655,10 @@
         far_start = ((1 - strip % 2) * half + firsts[c]) * rows
         part = lax.dynamic_slice_in_dim(flat, far_start, chunks[c] * rows, axis=0)
         got.append(swap(part))
+    lowest = pick(side, flat, lambda s: s * (half // size), half, size, [(0, 3)])
+    below = against_flow(lowest)
     tables = prepare(points, vel_index)
     table, _, weights = tables
-    lowest = pick(side, flat, lambda s: s * (half // size), half, size, [(0, 3)], [table])
-    below = against_flow(lowest)
     gram = jnp.asarray(target_moments(points))
     mat = jnp.asarray(macro_matrix())
 
@@ -723,15 +713,16 @@
     )
 
     sums = jnp.zeros((16, width), F32)
-    near, back = {}, {}
+    near, back = None, []
     for c in order:
         number = int(c >= cut)
         start = firsts[groups_of[number][0]]
-        near[c], far, sums = transport(
+        near, far, sums = transport(
             side, list(kept[number]), tables, cells, sums, half,
             chunks[c], firsts[c], size, change, skip=firsts[c] - start,
+            into=None if near is None else [near],
         )
-        back[c] = swap(far)
+        back.append(swap(far))
     total = sum_groups(sums)
     total = total + swap(total)
     sum_a, sum_b = both_z(total)
@@ -744,12 +735,9 @@
         ],
         [pltpu.VMEM((16, SPAN * LANES), F32)],
     )
-    out = None
-    for own, parts in ((True, near), (False, back)):
-        for c in order:
-            out = finish(
-                side, out, parts[c], own, table, change, half, chunks[c], firsts[c], size
-            )
+    out = finish(side, None, near, True, table, change, half, half, 0, size)
+    for c in order:
+        out = finish(side, out, back[c], False, table, change, half, chunks[c], firsts[c], size)
     return out.reshape(dist.shape), state[:5].reshape(5, rows, cols)
 
 

time: 322 us -> 322 us (level)
  the two profiles are of different devices: /device:TPU:24 before, /device:TPU:12 now
where the time goes in v4:
time: 322 us; the launch traced here: 321 us
  waiting for transfers between devices  154 us (48%)
  Pallas kernels  105 us (33%)
  starting transfers between devices  44.6 us (14%)
  local copies, waits for them, and re-layouts  12.9 us (4%)
    ppermute x12, waiting for transfers between devices, swap(): return lax.ppermute(value, 'strip', swap_pairs)  99 us
    pallas_call x8, Pallas kernels, transport(): pl.pallas_call(functools.partial(transport_kernel, size, second_pass), ou...  61.8 us
    ppermute x6, waiting for transfers between devices, with_flow(): return lax.ppermute(value, 'strip', down_pairs)  19.9 us
    ppermute x3, waiting for transfers between devices, both_z(): lax.ppermute(value, 'strip', pair_b)  17.8 us
    pallas_call x5, Pallas kernels, finish(): pl.pallas_call(functools.partial(finish_kernel, size, own), out_shape=jax...  14.9 us
    ppermute x6, starting transfers between devices, with_flow(): return lax.ppermute(value, 'strip', down_pairs)  13.5 us
    pallas_call x5, Pallas kernels, pick(): pl.pallas_call(functools.partial(pick_kernel, size, picks), out_shape=jax...  12.4 us
    ppermute x12, starting transfers between devices, swap(): return lax.ppermute(value, 'strip', swap_pairs)  8.95 us
  transfers between devices with their start and end apart: 36, of which 14 were waited for; matrix products, arithmetic and copies ran while one was open for 2% of the time, Pallas kernels for 32%

profile of v4, /device:TPU:12, one launch (start us, length us, event | category | flops | bytes accessed | tf_op | source)
XLA Modules:
  0.0 320.6 jit_solution(911640159265436944)
XLA Ops:
  0.7 3.2 constant_dynamic-slice_fusion.1
  4.3 1.5 collective-permute-start.4
  5.9 2.3 constant_dynamic-slice_fusion
  8.7 1.6 collective-permute-start.3
  10.9 3.8 %prepare.1 = (bf16[3456,48]{1,0:T(8,128)(2,1)}, f32[3456,8]{1,0:T(8,128)}, bf16[3456,32]{1,0:T(8,128)(2,1)}) custom-call(s32[3,3456]{1,0:T(4,128)} %vel_ref.1), custom_call_target="tpu_custom_call" | custom-call | flops 691200 | bytes 3456000 | tf_op jit(solution)/shard_map/prepare/pallas_call | solution.py:181
  14.7 6.1 %home_moments.1 = f32[16,512]{1,0:T(8,128)} custom-call(f32[13824,128]{1,0:T(8,128)} %bitcast.14, bf16[3456,32]{1,0:T(8,128)(2,1)} %get-tuple-element.39.refs_5_.weight_ref.refs_8_), custom_call_target="tpu_custom_call" | custom-call | flops 169869312 | bytes 7077888 | tf_op jit(solution)/shard_map/home_moments/pallas_call | solution.py:223
  20.8 4.8 %shard_map.78 = f32[1,1728,128]{2,1,0:T(8,128)} custom-call(s32[1]{0:T(128)} %bitcast.side_ref, f32[13824,128]{1,0:T(8,128)} %bitcast.15), custom_call_target="tpu_custom_call" | custom-call | bytes 4423680 | tf_op jit(solution)/shard_map/pallas_call | solution.py:128
  25.7 45.2 %collective-permute-done.3 = f32[8,128]{1,0:T(8,128)S(1)} collective-permute-done((f32[8,128]{1,0:T(8,128)S(1)}, f32[8,128]{1,0:T(8,128)S(1)}, u32[]{:S(2)}, u32[]{:S(2)}) %collective-permute-start.3) | collective-permute-done | bytes 4128 | tf_op jit(solution)/shard_map/ppermute | solution.py:629
  71.0 3.5 %collective-permute-start.2 = (f32[1,1728,128]{2,1,0:T(8,128)}, f32[1,1728,128]{2,1,0:T(8,128)S(1)}, u32[]{:S(2)}, u32[]{:S(2)}) collective-permute-start(f32[1,1728,128]{2,1,0:T(8,128)} %shard_map.78), channel_id=1, source_target_pairs={{2,0},{4,2},{1,3},{6,4},{3,5},{5,7},{10,8},{12,10},{9,11},{14,12},... | collective-permute-start | bytes 2654216 | tf_op jit(solution)/shard_map/ppermute | solution.py:635
  74.5 2.0 shard_map.80
  76.5 2.4 collective-permute-start.7
  78.9 2.0 shard_map.79
  80.9 1.9 collective-permute-start.5
  82.9 1.6 collective-permute-start.17
  84.4 0.9 collective-permute-start.18
  85.9 1.8 shard_map.81
  87.8 1.8 shard_map.77
  89.6 1.9 collective-permute-start.9
  91.5 1.9 collective-permute-start.1
  93.5 19.9 %collective-permute-done.9.refs_2_ = f32[2,288,128]{2,1,0:T(8,128)S(1)} collective-permute-done((f32[2,288,128]{2,1,0:T(8,128)}, f32[2,288,128]{2,1,0:T(8,128)S(1)}, u32[]{:S(2)}, u32[]{:S(2)}) %collective-permute-start.9) | collective-permute-done | bytes 294944 | tf_op jit(solution)/shard_map/ppermute | solution.py:632
  114.9 5.6 %transport_first.4 = (f32[1,864,128]{2,1,0:T(8,128)}, f32[5,864,128]{2,1,0:T(8,128)}, f32[2,864,128]{2,1,0:T(8,128)}, f32[16,1024]{1,0:T(8,128)}) custom-call(s32[1]{0:T(128)} %bitcast.side_ref, f32[13824,128]{1,0:T(8,128)} %bitcast.16, f32[1152,128]{1,0:T(8,128)} %collective-permute-done.8.strip_ref.refs_1_, f32[2,288,128]{2,1,0:T(8,128)} %copy-done.8, ...), custom_call_target="tpu_custom_call" | custom-call | flops 17694720 | bytes 2801664 | tf_op jit(solution)/shard_map/transport_first/pallas_call | solution.py:396
  120.5 9.0 %transport_first.5 = (f32[1,864,128]{2,1,0:T(8,128)}, f32[5,864,128]{2,1,0:T(8,128)}, f32[2,864,128]{2,1,0:T(8,128)}, f32[16,1024]{1,0:T(8,128)}) custom-call(s32[1]{0:T(128)} %bitcast.side_ref, f32[13824,128]{1,0:T(8,128)} %bitcast.17, ...), custom_call_target="tpu_custom_call", output_to_operand_aliasing={{0}: (9, {}), {1}: (10, {}), {2}: (11, {})} | custom-call | flops 35389440 | bytes 5603328 | tf_op jit(solution)/shard_map/transport_first/pallas_call | solution.py:396
  129.5 3.4 %collective-permute-start.24 = (f32[2,864,128]{2,1,0:T(8,128)}, f32[2,864,128]{2,1,0:T(8,128)}, u32[]{:S(2)}, u32[]{:S(2)}) collective-permute-start(f32[2,864,128]{2,1,0:T(8,128)} %get-tuple-element.56.refs_4_), channel_id=1, source_target_pairs={{0,2},{2,4},{3,1},{4,6},{5,3},{7,5},{8,10},{10,12},{11,9},{12,14},... | collective-permute-start | bytes 2654216 | tf_op jit(solution)/shard_map/ppermute | solution.py:632
  133.0 9.0 %transport_first.6 = (f32[1,864,128]{2,1,0:T(8,128)}, f32[5,864,128]{2,1,0:T(8,128)}, f32[2,864,128]{2,1,0:T(8,128)}, f32[16,1024]{1,0:T(8,128)}) custom-call(s32[1]{0:T(128)} %bitcast.side_ref, f32[13824,128]{1,0:T(8,128)} %bitcast.18, f32[2304,128]{1,0:T(8,128)} %collective-permute-done.4.strip_ref.refs_1_, f32[2,576,128]{2,1,0:T(8,128)} %collective-permute-done.5.refs_2_, ...), custom_call_target="tpu_custom_call" | custom-call | flops 35389440 | bytes 5603328 | tf_op jit(solution)/shard_map/transport_first/pallas_call | solution.py:396
  142.0 0.7 copy-done.9
  142.7 5.7 %transport_first.7 = (f32[1,864,128]{2,1,0:T(8,128)}, f32[5,864,128]{2,1,0:T(8,128)}, f32[2,864,128]{2,1,0:T(8,128)}, f32[16,1024]{1,0:T(8,128)}) custom-call(s32[1]{0:T(128)} %bitcast.side_ref, f32[13824,128]{1,0:T(8,128)} %bitcast.19, f32[1152,128]{1,0:T(8,128)} %copy-done.3, ...), custom_call_target="tpu_custom_call", output_to_operand_aliasing={{0}: (9, {}), {1}: (10, {}), {2}: (11, {})} | custom-call | flops 17694720 | bytes 2801664 | tf_op jit(solution)/shard_map/transport_first/pallas_call | solution.py:396
  148.4 1.9 collective-permute-start.22
  150.7 1.7 collective-permute-start.11
  152.3 1.4 collective-permute-start.12
  154.3 4.0 %collective-permute-start.20 = (f32[16,512]{1,0:T(8,128)S(1)}, f32[16,512]{1,0:T(8,128)S(1)}, u32[]{:S(2)}, u32[]{:S(2)}) collective-permute-start(f32[16,512]{1,0:T(8,128)S(1)} %maximum_maximum_fusion), channel_id=1, source_target_pairs={{2,4},{3,5},{4,2},{5,3},{10,12},{11,13},{12,10},{13,11},{18,20},{1... | collective-permute-start | bytes 98312 | tf_op jit(solution)/shard_map/ppermute | solution.py:638
  158.3 1.9 collective-permute-start.25
  160.2 1.9 collective-permute-start.23
  162.2 0.9 add_add_fusion.1
  163.0 10.3 %collective-permute-done.20 = f32[16,512]{1,0:T(8,128)S(1)} collective-permute-done((f32[16,512]{1,0:T(8,128)S(1)}, f32[16,512]{1,0:T(8,128)S(1)}, u32[]{:S(2)}, u32[]{:S(2)}) %collective-permute-start.20) | collective-permute-done | bytes 32800 | tf_op jit(solution)/shard_map/ppermute | solution.py:638
  173.4 4.2 %collective-permute-done.13 = f32[16,1024]{1,0:T(8,128)S(1)} collective-permute-done((f32[16,1024]{1,0:T(8,128)S(1)}, f32[16,1024]{1,0:T(8,128)S(1)}, u32[]{:S(2)}, u32[]{:S(2)}) %collective-permute-start.13) | collective-permute-done | bytes 65568 | tf_op jit(solution)/shard_map/ppermute | solution.py:629
  177.7 4.6 %collective-permute-done.21.far_ref = f32[3,16,512]{2,1,0:T(8,128)S(1)} collective-permute-done((f32[3,16,512]{2,1,0:T(8,128)S(1)}, f32[3,16,512]{2,1,0:T(8,128)S(1)}, u32[]{:S(2)}, u32[]{:S(2)}) %collective-permute-start.21) | collective-permute-done | bytes 98336 | tf_op jit(solution)/shard_map/ppermute | solution.py:629
  182.3 4.3 %collective-permute-done.14.sum_a_ref = f32[16,1024]{1,0:T(8,128)S(1)} collective-permute-done((f32[16,1024]{1,0:T(8,128)S(1)}, f32[16,1024]{1,0:T(8,128)S(1)}, u32[]{:S(2)}, u32[]{:S(2)}) %collective-permute-start.14) | collective-permute-done | bytes 65568 | tf_op jit(solution)/shard_map/ppermute | solution.py:638
  187.2 2.1 collective-permute-start.15
  189.9 3.5 %collective-permute-done.15.sum_b_ref = f32[16,1024]{1,0:T(8,128)} collective-permute-done((f32[16,1024]{1,0:T(8,128)S(1)}, f32[16,1024]{1,0:T(8,128)}, u32[]{:S(2)}, u32[]{:S(2)}) %collective-permute-start.15) | collective-permute-done | bytes 65568 | tf_op jit(solution)/shard_map/ppermute | solution.py:638
  193.4 3.2 shard_map.82
  196.6 6.2 %transport_second.4 = (f32[4,1728,128]{2,1,0:T(8,128)}, f32[4,288,128]{2,1,0:T(8,128)}, f32[16,1024]{1,0:T(8,128)}) custom-call(s32[1]{0:T(128)} %bitcast.side_ref, bf16[3456,48]{1,0:T(8,128)(2,1)} %get-tuple-element.37.refs_0_.table_ref, bf16[48,1408]{1,0:T(8,128)(2,1)} %get-tuple-element.50.refs_1_, f32[1,864,128]{2,1,0:T(8,128)} %get-tuple-element.54.refs_2_, ...), custom_call_target="tpu_custom_call" | custom-call | flops 17694720 | bytes 2801664 | tf_op jit(solution)/shard_map/transport_second/pallas_call | solution.py:396
  202.8 10.0 %transport_second.5 = (f32[4,1728,128]{2,1,0:T(8,128)}, f32[4,576,128]{2,1,0:T(8,128)}, f32[16,1024]{1,0:T(8,128)}) custom-call(s32[1]{0:T(128)} %bitcast.side_ref, bf16[3456,48]{1,0:T(8,128)(2,1)} %get-tuple-element.37.refs_0_.table_ref, bf16[48,1408]{1,0:T(8,128)(2,1)} %get-tuple-element.50.refs_1_, ...), custom_call_target="tpu_custom_call", output_to_operand_aliasing={{0}: (12, {})} | custom-call | flops 35389440 | bytes 5603328 | tf_op jit(solution)/shard_map/transport_second/pallas_call | solution.py:396
  213.0 0.8 copy-done.4
  214.0 10.0 %transport_second.6 = (f32[4,1728,128]{2,1,0:T(8,128)}, f32[4,576,128]{2,1,0:T(8,128)}, f32[16,1024]{1,0:T(8,128)}) custom-call(s32[1]{0:T(128)} %bitcast.side_ref, bf16[3456,48]{1,0:T(8,128)(2,1)} %get-tuple-element.37.refs_0_.table_ref, bf16[48,1408]{1,0:T(8,128)(2,1)} %get-tuple-element.50.refs_1_, ...), custom_call_target="tpu_custom_call", output_to_operand_aliasing={{0}: (12, {})} | custom-call | flops 35389440 | bytes 5603328 | tf_op jit(solution)/shard_map/transport_second/pallas_call | solution.py:396
  224.0 2.0 collective-permute-start.33
  226.1 6.2 %transport_second.7 = (f32[4,1728,128]{2,1,0:T(8,128)}, f32[4,288,128]{2,1,0:T(8,128)}, f32[16,1024]{1,0:T(8,128)}) custom-call(s32[1]{0:T(128)} %bitcast.side_ref, bf16[3456,48]{1,0:T(8,128)(2,1)} %get-tuple-element.37.refs_0_.table_ref, bf16[48,1408]{1,0:T(8,128)(2,1)} %get-tuple-element.50.refs_1_, ...), custom_call_target="tpu_custom_call", output_to_operand_aliasing={{0}: (12, {})} | custom-call | flops 17694720 | bytes 2801664 | tf_op jit(solution)/shard_map/transport_second/pallas_call | solution.py:396
  232.3 1.9 collective-permute-start.26
  234.3 1.9 collective-permute-done.27
  236.3 4.3 %collective-permute-done.28 = f32[16,1024]{1,0:T(8,128)S(1)} collective-permute-done((f32[16,1024]{1,0:T(8,128)}, f32[16,1024]{1,0:T(8,128)S(1)}, u32[]{:S(2)}, u32[]{:S(2)}) %collective-permute-start.28) | collective-permute-done | bytes 65568 | tf_op jit(solution)/shard_map/ppermute | solution.py:643
  240.6 2.2 collective-permute-done.29
  242.9 0.9 add_add_fusion
  243.9 44.9 %collective-permute-done.30 = f32[16,1024]{1,0:T(8,128)S(1)} collective-permute-done((f32[16,1024]{1,0:T(8,128)S(1)}, f32[16,1024]{1,0:T(8,128)S(1)}, u32[]{:S(2)}, u32[]{:S(2)}) %collective-permute-start.30) | collective-permute-done | bytes 65568 | tf_op jit(solution)/shard_map/ppermute | solution.py:629
  288.9 4.3 %collective-permute-done.31.sum_a_ref = f32[16,1024]{1,0:T(8,128)S(1)} collective-permute-done((f32[16,1024]{1,0:T(8,128)S(1)}, f32[16,1024]{1,0:T(8,128)S(1)}, u32[]{:S(2)}, u32[]{:S(2)}) %collective-permute-start.31) | collective-permute-done | bytes 65568 | tf_op jit(solution)/shard_map/ppermute | solution.py:638
  293.1 2.2 collective-permute-start.32
  295.3 4.0 %collective-permute-done.32.sum_b_ref = f32[16,1024]{1,0:T(8,128)S(1)} collective-permute-done((f32[16,1024]{1,0:T(8,128)S(1)}, f32[16,1024]{1,0:T(8,128)S(1)}, u32[]{:S(2)}, u32[]{:S(2)}) %collective-permute-start.32) | collective-permute-done | bytes 65568 | tf_op jit(solution)/shard_map/ppermute | solution.py:638
  299.9 2.6 shard_map.83
  302.5 1.3 reshape.27
  303.8 6.0 %finish.5.rest_0_ = f32[13824,128]{1,0:T(8,128)} custom-call(s32[1]{0:T(128)} %bitcast.side_ref, f32[4,1728,128]{2,1,0:T(8,128)} %get-tuple-element.70.rows_ref, bf16[3456,48]{1,0:T(8,128)(2,1)} %get-tuple-element.37.refs_0_.table_ref, bf16[48,512]{1,0:T(8,128)(2,1)} %get-tuple-element.66.change_ref), custom_call_target="tpu_custom_call" | custom-call | flops 84934656 | bytes 7077888 | tf_op jit(solution)/shard_map/finish/pallas_call | solution.py:578
  309.7 2.1 finish.6.rest_0_
  311.9 2.4 finish.7.rest_0_
  314.3 1.1 copy-done.5
  315.3 2.3 finish.8.rest_0_
  317.7 0.9 copy-done.6
  318.5 2.1 finish.9
  (94 shorter events, 7.7 us)
Async XLA Ops:
  3.8 4.9 %copy-start.18 = (s32[4,128]{1,0:T(4,128)S(1)}, s32[4,128]{1,0:T(4,128)}, u32[]{:S(2)}) copy-start(s32[4,128]{1,0:T(4,128)} %param.7) | copy-start | bytes 6148
  3.8 4.9 %copy-start.17 = (f32[4,128]{1,0:T(4,128)S(1)}, f32[4,128]{1,0:T(4,128)}, u32[]{:S(2)}) copy-start(f32[4,128]{1,0:T(4,128)} %param.8) | copy-start | bytes 6148
  3.8 67.2 %collective-permute-start.6 = (f32[2304,128]{1,0:T(8,128)}, f32[2304,128]{1,0:T(8,128)}, u32[]{:S(2)}, u32[]{:S(2)}) collective-permute-start(f32[2304,128]{1,0:T(8,128)} %get-tuple-element.74), channel_id=1, source_target_pairs={{0,1},{1,0},{2,3},{3,2},{4,5},{5,4},{6,7},{7,6},{8,9},{9,8},{10,11... | collective-permute-start | bytes 3538952 | tf_op jit(solution)/shard_map/ppermute | solution.py:629
  4.3 72.2 %collective-permute-start.4 = (f32[2304,128]{1,0:T(8,128)}, f32[2304,128]{1,0:T(8,128)}, u32[]{:S(2)}, u32[]{:S(2)}) collective-permute-start(f32[2304,128]{1,0:T(8,128)} %get-tuple-element.75), channel_id=1, source_target_pairs={{0,1},{1,0},{2,3},{3,2},{4,5},{5,4},{6,7},{7,6},{8,9},{9,8},{10,11... | collective-permute-start | bytes 3538952 | tf_op jit(solution)/shard_map/ppermute | solution.py:629
  8.2 74.7 %collective-permute-start.8 = (f32[1152,128]{1,0:T(8,128)}, f32[1152,128]{1,0:T(8,128)}, u32[]{:S(2)}, u32[]{:S(2)}) collective-permute-start(f32[1152,128]{1,0:T(8,128)} %get-tuple-element.72), channel_id=1, source_target_pairs={{0,1},{1,0},{2,3},{3,2},{4,5},{5,4},{6,7},{7,6},{8,9},{9,8},{10,11... | collective-permute-start | bytes 1769480 | tf_op jit(solution)/shard_map/ppermute | solution.py:629
  8.7 62.2 %collective-permute-start.3 = (f32[8,128]{1,0:T(8,128)S(1)}, f32[8,128]{1,0:T(8,128)S(1)}, u32[]{:S(2)}, u32[]{:S(2)}) collective-permute-start(f32[8,128]{1,0:T(8,128)S(1)} %pad_maximum_fusion.2), channel_id=1, source_target_pairs={{0,1},{1,0},{2,3},{3,2},{4,5},{5,4},{6,7},{7,6},{8,9},{9,8},{10,11... | collective-permute-start | bytes 12296 | tf_op jit(solution)/shard_map/ppermute | solution.py:629
  10.3 74.1 %collective-permute-start = (f32[1152,128]{1,0:T(8,128)}, f32[1152,128]{1,0:T(8,128)S(1)}, u32[]{:S(2)}, u32[]{:S(2)}) collective-permute-start(f32[1152,128]{1,0:T(8,128)} %get-tuple-element.73), channel_id=1, source_target_pairs={{0,1},{1,0},{2,3},{3,2},{4,5},{5,4},{6,7},{7,6},{8,9},{9,8},{10,11... | collective-permute-start | bytes 1769480 | tf_op jit(solution)/shard_map/ppermute | solution.py:629
  20.8 50.1 %copy-start.12 = (f32[16,512]{1,0:T(8,128)S(1)}, f32[16,512]{1,0:T(8,128)}, u32[]{:S(2)}) copy-start(f32[16,512]{1,0:T(8,128)} %home_moments.1) | copy-start | bytes 98308
  70.9 10.0 %collective-permute-start.16 = (f32[16,512]{1,0:T(8,128)S(1)}, f32[16,512]{1,0:T(8,128)S(1)}, u32[]{:S(2)}, u32[]{:S(2)}) collective-permute-start(f32[16,512]{1,0:T(8,128)S(1)} %copy-done.12), channel_id=1, source_target_pairs={{0,8},{8,16},{16,24},{24,0},{1,9},{9,17},{17,25},{25,1},{2,10},{10... | collective-permute-start | bytes 98312 | tf_op jit(solution)/shard_map/ppermute | solution.py:643
  71.0 42.9 %collective-permute-start.2 = (f32[1,1728,128]{2,1,0:T(8,128)}, f32[1,1728,128]{2,1,0:T(8,128)S(1)}, u32[]{:S(2)}, u32[]{:S(2)}) collective-permute-start(f32[1,1728,128]{2,1,0:T(8,128)} %shard_map.78), channel_id=1, source_target_pairs={{2,0},{4,2},{1,3},{6,4},{3,5},{5,7},{10,8},{12,10},{9,11},{14,12},... | collective-permute-start | bytes 2654216 | tf_op jit(solution)/shard_map/ppermute | solution.py:635
  76.5 44.0 %collective-permute-start.7 = (f32[2,576,128]{2,1,0:T(8,128)}, f32[2,576,128]{2,1,0:T(8,128)}, u32[]{:S(2)}, u32[]{:S(2)}) collective-permute-start(f32[2,576,128]{2,1,0:T(8,128)} %shard_map.80), channel_id=1, source_target_pairs={{0,2},{2,4},{3,1},{4,6},{5,3},{7,5},{8,10},{10,12},{11,9},{12,14},... | collective-permute-start | bytes 1769480 | tf_op jit(solution)/shard_map/ppermute | solution.py:632
  80.9 52.0 %collective-permute-start.5 = (f32[2,576,128]{2,1,0:T(8,128)}, f32[2,576,128]{2,1,0:T(8,128)}, u32[]{:S(2)}, u32[]{:S(2)}) collective-permute-start(f32[2,576,128]{2,1,0:T(8,128)} %shard_map.79), channel_id=1, source_target_pairs={{0,2},{2,4},{3,1},{4,6},{5,3},{7,5},{8,10},{10,12},{11,9},{12,14},... | collective-permute-start | bytes 1769480 | tf_op jit(solution)/shard_map/ppermute | solution.py:632
  82.9 6.7 %collective-permute-start.17 = (f32[16,512]{1,0:T(8,128)S(1)}, f32[16,512]{1,0:T(8,128)S(1)}, u32[]{:S(2)}, u32[]{:S(2)}) collective-permute-start(f32[16,512]{1,0:T(8,128)S(1)} %copy-done.12), channel_id=1, source_target_pairs={{0,16},{8,24},{16,0},{24,8},{1,17},{9,25},{17,1},{25,9},{2,18},{10... | collective-permute-start | bytes 98312 | tf_op jit(solution)/shard_map/ppermute | solution.py:643
  84.4 3.3 %copy-start.3 = (f32[1152,128]{1,0:T(8,128)}, f32[1152,128]{1,0:T(8,128)S(1)}, u32[]{:S(2)}) copy-start(f32[1152,128]{1,0:T(8,128)S(1)} %collective-permute-done.strip_ref.refs_1_) | copy-start | bytes 1769476
  84.4 7.1 %collective-permute-start.18 = (f32[16,512]{1,0:T(8,128)S(1)}, f32[16,512]{1,0:T(8,128)S(1)}, u32[]{:S(2)}, u32[]{:S(2)}) collective-permute-start(f32[16,512]{1,0:T(8,128)S(1)} %copy-done.12), channel_id=1, source_target_pairs={{0,24},{8,0},{16,8},{24,16},{1,25},{9,1},{17,9},{25,17},{2,26},{10... | collective-permute-start | bytes 98312 | tf_op jit(solution)/shard_map/ppermute | solution.py:643
  89.6 23.8 %collective-permute-start.9 = (f32[2,288,128]{2,1,0:T(8,128)}, f32[2,288,128]{2,1,0:T(8,128)S(1)}, u32[]{:S(2)}, u32[]{:S(2)}) collective-permute-start(f32[2,288,128]{2,1,0:T(8,128)} %shard_map.81), channel_id=1, source_target_pairs={{0,2},{2,4},{3,1},{4,6},{5,3},{7,5},{8,10},{10,12},{11,9},{12,14},... | collective-permute-start | bytes 884744 | tf_op jit(solution)/shard_map/ppermute | solution.py:632
  91.5 50.5 %collective-permute-start.1 = (f32[2,288,128]{2,1,0:T(8,128)}, f32[2,288,128]{2,1,0:T(8,128)S(1)}, u32[]{:S(2)}, u32[]{:S(2)}) collective-permute-start(f32[2,288,128]{2,1,0:T(8,128)} %shard_map.77), channel_id=1, source_target_pairs={{0,2},{2,4},{3,1},{4,6},{5,3},{7,5},{8,10},{10,12},{11,9},{12,14},... | collective-permute-start | bytes 884744 | tf_op jit(solution)/shard_map/ppermute | solution.py:632
  113.4 1.2 copy-start.8
  113.4 38.9 %collective-permute-start.19 = (f32[16,512]{1,0:T(8,128)S(1)}, f32[16,512]{1,0:T(8,128)S(1)}, u32[]{:S(2)}, u32[]{:S(2)}) collective-permute-start(f32[16,512]{1,0:T(8,128)S(1)} %maximum_maximum_fusion), channel_id=1, source_target_pairs={{0,2},{1,3},{2,0},{3,1},{4,6},{5,7},{6,4},{7,5},{8,10},{9,11},{10,... | collective-permute-start | bytes 98312 | tf_op jit(solution)/shard_map/ppermute | solution.py:638
  113.9 1.0 copy-start
  129.5 67.1 %collective-permute-start.24 = (f32[2,864,128]{2,1,0:T(8,128)}, f32[2,864,128]{2,1,0:T(8,128)}, u32[]{:S(2)}, u32[]{:S(2)}) collective-permute-start(f32[2,864,128]{2,1,0:T(8,128)} %get-tuple-element.56.refs_4_), channel_id=1, source_target_pairs={{0,2},{2,4},{3,1},{4,6},{5,3},{7,5},{8,10},{10,12},{11,9},{12,14},... | collective-permute-start | bytes 2654216 | tf_op jit(solution)/shard_map/ppermute | solution.py:632
  142.0 0.7 copy-start.9
  142.7 15.6 %copy-start.1 = (f32[1,864,128]{2,1,0:T(8,128)S(1)}, f32[1,864,128]{2,1,0:T(8,128)}, u32[]{:S(2)}) copy-start(f32[1,864,128]{2,1,0:T(8,128)} %get-tuple-element.54.refs_2_) | copy-start | bytes 1327108
  148.4 64.5 %collective-permute-start.22 = (f32[2,864,128]{2,1,0:T(8,128)}, f32[2,864,128]{2,1,0:T(8,128)S(1)}, u32[]{:S(2)}, u32[]{:S(2)}) collective-permute-start(f32[2,864,128]{2,1,0:T(8,128)} %get-tuple-element.53.refs_4_), channel_id=1, source_target_pairs={{0,2},{2,4},{3,1},{4,6},{5,3},{7,5},{8,10},{10,12},{11,9},{12,14},... | collective-permute-start | bytes 2654216 | tf_op jit(solution)/shard_map/ppermute | solution.py:632
  150.4 4.0 %collective-permute-start.10 = (f32[16,1024]{1,0:T(8,128)}, f32[16,1024]{1,0:T(8,128)S(1)}, u32[]{:S(2)}, u32[]{:S(2)}) collective-permute-start(f32[16,1024]{1,0:T(8,128)} %get-tuple-element.49), channel_id=1, source_target_pairs={{0,8},{8,16},{16,24},{24,0},{1,9},{9,17},{17,25},{25,1},{2,10},{10... | collective-permute-start | bytes 196616 | tf_op jit(solution)/shard_map/ppermute | solution.py:643
  150.7 7.6 %collective-permute-start.11 = (f32[16,1024]{1,0:T(8,128)}, f32[16,1024]{1,0:T(8,128)S(1)}, u32[]{:S(2)}, u32[]{:S(2)}) collective-permute-start(f32[16,1024]{1,0:T(8,128)} %get-tuple-element.49), channel_id=1, source_target_pairs={{0,16},{8,24},{16,0},{24,8},{1,17},{9,25},{17,1},{25,9},{2,18},{10... | collective-permute-start | bytes 196616 | tf_op jit(solution)/shard_map/ppermute | solution.py:643
  152.3 7.9 %collective-permute-start.12 = (f32[16,1024]{1,0:T(8,128)}, f32[16,1024]{1,0:T(8,128)S(1)}, u32[]{:S(2)}, u32[]{:S(2)}) collective-permute-start(f32[16,1024]{1,0:T(8,128)} %get-tuple-element.49), channel_id=1, source_target_pairs={{0,24},{8,0},{16,8},{24,16},{1,25},{9,1},{17,9},{25,17},{2,26},{10... | collective-permute-start | bytes 196616 | tf_op jit(solution)/shard_map/ppermute | solution.py:643
  154.3 19.1 %collective-permute-start.20 = (f32[16,512]{1,0:T(8,128)S(1)}, f32[16,512]{1,0:T(8,128)S(1)}, u32[]{:S(2)}, u32[]{:S(2)}) collective-permute-start(f32[16,512]{1,0:T(8,128)S(1)} %maximum_maximum_fusion), channel_id=1, source_target_pairs={{2,4},{3,5},{4,2},{5,3},{10,12},{11,13},{12,10},{13,11},{18,20},{1... | collective-permute-start | bytes 98312 | tf_op jit(solution)/shard_map/ppermute | solution.py:638
  158.3 38.3 %collective-permute-start.25 = (f32[1,864,128]{2,1,0:T(8,128)S(1)}, f32[1,864,128]{2,1,0:T(8,128)}, u32[]{:S(2)}, u32[]{:S(2)}) collective-permute-start(f32[1,864,128]{2,1,0:T(8,128)S(1)} %copy-done.1), channel_id=1, source_target_pairs={{2,0},{4,2},{1,3},{6,4},{3,5},{5,7},{10,8},{12,10},{9,11},{14,12},... | collective-permute-start | bytes 1327112 | tf_op jit(solution)/shard_map/ppermute | solution.py:635
  160.2 52.7 %collective-permute-start.23 = (f32[1,864,128]{2,1,0:T(8,128)}, f32[1,864,128]{2,1,0:T(8,128)S(1)}, u32[]{:S(2)}, u32[]{:S(2)}) collective-permute-start(f32[1,864,128]{2,1,0:T(8,128)} %get-tuple-element.51.refs_2_), channel_id=1, source_target_pairs={{2,0},{4,2},{1,3},{6,4},{3,5},{5,7},{10,8},{12,10},{9,11},{14,12},... | collective-permute-start | bytes 1327112 | tf_op jit(solution)/shard_map/ppermute | solution.py:635
  173.4 4.3 %collective-permute-start.13 = (f32[16,1024]{1,0:T(8,128)S(1)}, f32[16,1024]{1,0:T(8,128)S(1)}, u32[]{:S(2)}, u32[]{:S(2)}) collective-permute-start(f32[16,1024]{1,0:T(8,128)S(1)} %add_add_fusion.1), channel_id=1, source_target_pairs={{0,1},{1,0},{2,3},{3,2},{4,5},{5,4},{6,7},{7,6},{8,9},{9,8},{10,11... | collective-permute-start | bytes 196616 | tf_op jit(solution)/shard_map/ppermute | solution.py:629
  173.4 20.0 %copy-start.7 = (f32[3,16,512]{2,1,0:T(8,128)}, f32[3,16,512]{2,1,0:T(8,128)S(1)}, u32[]{:S(2)}) copy-start(f32[3,16,512]{2,1,0:T(8,128)S(1)} %pad_maximum_fusion.near_ref) | copy-start | bytes 294916
  177.6 4.6 %collective-permute-start.21 = (f32[3,16,512]{2,1,0:T(8,128)S(1)}, f32[3,16,512]{2,1,0:T(8,128)S(1)}, u32[]{:S(2)}, u32[]{:S(2)}) collective-permute-start(f32[3,16,512]{2,1,0:T(8,128)S(1)} %pad_maximum_fusion.near_ref), channel_id=1, source_target_pairs={{0,1},{1,0},{2,3},{3,2},{4,5},{5,4},{6,7},{7,6},{8,9},{9,8},{10,11... | collective-permute-start | bytes 294920 | tf_op jit(solution)/shard_map/ppermute | solution.py:629
  177.7 15.8 %copy-start.10 = (f32[16,1024]{1,0:T(8,128)}, f32[16,1024]{1,0:T(8,128)S(1)}, u32[]{:S(2)}) copy-start(f32[16,1024]{1,0:T(8,128)S(1)} %add.81.sum_ref) | copy-start | bytes 196612
  182.3 11.2 %copy-start.13 = (f32[3,16,512]{2,1,0:T(8,128)}, f32[3,16,512]{2,1,0:T(8,128)S(1)}, u32[]{:S(2)}) copy-start(f32[3,16,512]{2,1,0:T(8,128)S(1)} %collective-permute-done.21.far_ref) | copy-start | bytes 294916
  182.3 4.3 %collective-permute-start.14 = (f32[16,1024]{1,0:T(8,128)S(1)}, f32[16,1024]{1,0:T(8,128)S(1)}, u32[]{:S(2)}, u32[]{:S(2)}) collective-permute-start(f32[16,1024]{1,0:T(8,128)S(1)} %add.81.sum_ref), channel_id=1, source_target_pairs={{0,2},{1,3},{2,0},{3,1},{4,6},{5,7},{6,4},{7,5},{8,10},{9,11},{10,... | collective-permute-start | bytes 196616 | tf_op jit(solution)/shard_map/ppermute | solution.py:638
  186.5 0.6 copy-start.14
  187.2 6.3 %collective-permute-start.15 = (f32[16,1024]{1,0:T(8,128)S(1)}, f32[16,1024]{1,0:T(8,128)}, u32[]{:S(2)}, u32[]{:S(2)}) collective-permute-start(f32[16,1024]{1,0:T(8,128)S(1)} %add.81.sum_ref), channel_id=1, source_target_pairs={{2,4},{3,5},{4,2},{5,3},{10,12},{11,13},{12,10},{13,11},{18,20},{1... | collective-permute-start | bytes 196616 | tf_op jit(solution)/shard_map/ppermute | solution.py:638
  212.8 99.1 %collective-permute-start.34 = (f32[4,576,128]{2,1,0:T(8,128)}, f32[4,576,128]{2,1,0:T(8,128)}, u32[]{:S(2)}, u32[]{:S(2)}) collective-permute-start(f32[4,576,128]{2,1,0:T(8,128)} %get-tuple-element.68), channel_id=1, source_target_pairs={{0,1},{1,0},{2,3},{3,2},{4,5},{5,4},{6,7},{7,6},{8,9},{9,8},{10,11... | collective-permute-start | bytes 3538952 | tf_op jit(solution)/shard_map/ppermute | solution.py:629
  213.0 0.8 copy-start.4
  213.0 1.0 copy-start.2
  224.0 90.2 %collective-permute-start.33 = (f32[4,576,128]{2,1,0:T(8,128)}, f32[4,576,128]{2,1,0:T(8,128)S(1)}, u32[]{:S(2)}, u32[]{:S(2)}) collective-permute-start(f32[4,576,128]{2,1,0:T(8,128)} %get-tuple-element.67), channel_id=1, source_target_pairs={{0,1},{1,0},{2,3},{3,2},{4,5},{5,4},{6,7},{7,6},{8,9},{9,8},{10,11... | collective-permute-start | bytes 3538952 | tf_op jit(solution)/shard_map/ppermute | solution.py:629
  232.3 3.9 %collective-permute-start.27 = (f32[16,1024]{1,0:T(8,128)}, f32[16,1024]{1,0:T(8,128)S(1)}, u32[]{:S(2)}, u32[]{:S(2)}) collective-permute-start(f32[16,1024]{1,0:T(8,128)} %get-tuple-element.64), channel_id=1, source_target_pairs={{0,8},{8,16},{16,24},{24,0},{1,9},{9,17},{17,25},{25,1},{2,10},{10... | collective-permute-start | bytes 196616 | tf_op jit(solution)/shard_map/ppermute | solution.py:643
  232.3 77.5 %collective-permute-start.35 = (f32[4,288,128]{2,1,0:T(8,128)}, f32[4,288,128]{2,1,0:T(8,128)}, u32[]{:S(2)}, u32[]{:S(2)}) collective-permute-start(f32[4,288,128]{2,1,0:T(8,128)} %get-tuple-element.69), channel_id=1, source_target_pairs={{0,1},{1,0},{2,3},{3,2},{4,5},{5,4},{6,7},{7,6},{8,9},{9,8},{10,11... | collective-permute-start | bytes 1769480 | tf_op jit(solution)/shard_map/ppermute | solution.py:629
  232.3 85.3 %collective-permute-start.26 = (f32[4,288,128]{2,1,0:T(8,128)}, f32[4,288,128]{2,1,0:T(8,128)S(1)}, u32[]{:S(2)}, u32[]{:S(2)}) collective-permute-start(f32[4,288,128]{2,1,0:T(8,128)} %get-tuple-element.63), channel_id=1, source_target_pairs={{0,1},{1,0},{2,3},{3,2},{4,5},{5,4},{6,7},{7,6},{8,9},{9,8},{10,11... | collective-permute-start | bytes 1769480 | tf_op jit(solution)/shard_map/ppermute | solution.py:629
  236.2 4.5 %collective-permute-start.28 = (f32[16,1024]{1,0:T(8,128)}, f32[16,1024]{1,0:T(8,128)S(1)}, u32[]{:S(2)}, u32[]{:S(2)}) collective-permute-start(f32[16,1024]{1,0:T(8,128)} %get-tuple-element.64), channel_id=1, source_target_pairs={{0,16},{8,24},{16,0},{24,8},{1,17},{9,25},{17,1},{25,9},{2,18},{10... | collective-permute-start | bytes 196616 | tf_op jit(solution)/shard_map/ppermute | solution.py:643
  240.6 2.2 collective-permute-start.29
  243.7 45.1 %collective-permute-start.30 = (f32[16,1024]{1,0:T(8,128)S(1)}, f32[16,1024]{1,0:T(8,128)S(1)}, u32[]{:S(2)}, u32[]{:S(2)}) collective-permute-start(f32[16,1024]{1,0:T(8,128)S(1)} %add_add_fusion), channel_id=1, source_target_pairs={{0,1},{1,0},{2,3},{3,2},{4,5},{5,4},{6,7},{7,6},{8,9},{9,8},{10,11... | collective-permute-start | bytes 196616 | tf_op jit(solution)/shard_map/ppermute | solution.py:629
  288.8 10.5 %copy-start.11 = (f32[16,1024]{1,0:T(8,128)}, f32[16,1024]{1,0:T(8,128)S(1)}, u32[]{:S(2)}) copy-start(f32[16,1024]{1,0:T(8,128)S(1)} %add.88.sum_ref) | copy-start | bytes 196612
  288.8 4.3 %collective-permute-start.31 = (f32[16,1024]{1,0:T(8,128)S(1)}, f32[16,1024]{1,0:T(8,128)S(1)}, u32[]{:S(2)}, u32[]{:S(2)}) collective-permute-start(f32[16,1024]{1,0:T(8,128)S(1)} %add.88.sum_ref), channel_id=1, source_target_pairs={{0,2},{1,3},{2,0},{3,1},{4,6},{5,7},{6,4},{7,5},{8,10},{9,11},{10,... | collective-permute-start | bytes 196616 | tf_op jit(solution)/shard_map/ppermute | solution.py:638
  293.1 6.2 %copy-start.15 = (f32[16,1024]{1,0:T(8,128)}, f32[16,1024]{1,0:T(8,128)S(1)}, u32[]{:S(2)}) copy-start(f32[16,1024]{1,0:T(8,128)S(1)} %collective-permute-done.31.sum_a_ref) | copy-start | bytes 196612
  293.1 6.1 %collective-permute-start.32 = (f32[16,1024]{1,0:T(8,128)S(1)}, f32[16,1024]{1,0:T(8,128)S(1)}, u32[]{:S(2)}, u32[]{:S(2)}) collective-permute-start(f32[16,1024]{1,0:T(8,128)S(1)} %add.88.sum_ref), channel_id=1, source_target_pairs={{2,4},{3,5},{4,2},{5,3},{10,12},{11,13},{12,10},{13,11},{18,20},{1... | collective-permute-start | bytes 196616 | tf_op jit(solution)/shard_map/ppermute | solution.py:638
  299.3 0.6 copy-start.16
  314.2 1.1 copy-start.5
  317.7 0.9 copy-start.6

commit v5 on v4

--- a/solution.py
+++ b/solution.py
@@ -32,8 +32,13 @@
     blocks = half // block
     if blocks % 6 == 0:
         unit = block * (blocks // 6)
-        return block, [unit, 2 * unit, 2 * unit, unit]
+        return block, [2 * unit, unit, unit, unit, unit]
     return block, [block * (blocks - 2), block, block]
+
+
+def second_order(pieces):
+    cut = (pieces + 1) // 2
+    return [*range(1, cut), 0, *range(cut, pieces)], cut
 
 
 def moment_rows(vel_x, vel_y, vel_z, volume, lib):
@@ -202,10 +207,18 @@
     return both[:16] + both[16:] + rest[:16]
 
 
-def moment_kernel(size, dist_ref, weight_ref, out_ref):
-    @pl.when(pl.program_id(0) == 0)
+def moment_kernel(size, side_ref, dist_ref, weight_ref, out_ref, lowest_ref):
+    side = side_ref[0]
+    step = pl.program_id(0)
+    half_steps = pl.num_programs(0) // 2
+
+    @pl.when(step == 0)
     def _():
         out_ref[...] = jnp.zeros_like(out_ref)
+
+    @pl.when(jnp.where(step >= half_steps, 1, 0) == side)
+    def _():
+        lowest_ref[...] = dist_ref[strided(jnp.where(side == 1, 3, 0), size), :]
 
     for pair in range(0, STRIP_ROWS, 2):
         value = jnp.concatenate(
@@ -217,24 +230,36 @@
         )
 
 
-def home_moments(flat, weights, size):
+def home_moments(side, flat, weights, size):
     count = flat.shape[0] // STRIP_ROWS
     width = STRIP_ROWS * LANES
+    half_steps = count // size // 2
     return pl.pallas_call(
         functools.partial(moment_kernel, size),
-        out_shape=jax.ShapeDtypeStruct((16, width), F32),
-        grid=(count // size,),
-        in_specs=[
-            pl.BlockSpec((4 * size, LANES), lambda i: (i, 0)),
-            pl.BlockSpec((size, 32), lambda i: (i, 0)),
-        ],
-        out_specs=pl.BlockSpec((16, width), lambda i: (0, 0)),
+        out_shape=(
+            jax.ShapeDtypeStruct((16, width), F32),
+            jax.ShapeDtypeStruct((count // 2, LANES), F32),
+        ),
+        grid_spec=pltpu.PrefetchScalarGridSpec(
+            num_scalar_prefetch=1,
+            grid=(2 * half_steps,),
+            in_specs=[
+                pl.BlockSpec((4 * size, LANES), lambda i, s: (i, 0)),
+                pl.BlockSpec((size, 32), lambda i, s: (i, 0)),
+            ],
+            out_specs=[
+                pl.BlockSpec((16, width), lambda i, s: (0, 0)),
+                pl.BlockSpec(
+                    (size, LANES), lambda i, s: (jnp.clip(i - s[0] * half_steps, 0, half_steps - 1), 0)
+                ),
+            ],
+        ),
         compiler_params=params(),
         name="home_moments",
         cost_estimate=pl.CostEstimate(
-            flops=2 * 48 * count * width, transcendentals=0, bytes_accessed=count * width * 4
-        ),
-    )(flat, weights)
+            flops=2 * 64 * count * width, transcendentals=0, bytes_accessed=count * width * 4
+        ),
+    )(side, flat, weights)
 
 
 def transport_kernel(size, second_pass, side_ref, *refs):
@@ -375,7 +400,7 @@
             pl.BlockSpec((4 * size, LANES), lambda i, s: (mine(i, s), 0)),
             pl.BlockSpec((4 * size, LANES), lambda i, s: (i, 0)),
             stack_of(2, 0),
-            stack_of(None, begin),
+            pl.BlockSpec((size, LANES), lambda i, s: (begin + i, 0)),
         ]
         outs = [jax.ShapeDtypeStruct((n, group, LANES), F32) for n in (1, 5, 2)]
         out_specs = [stack_of(None, offset), stack_of(5, offset), stack_of(2, offset)]
@@ -602,7 +627,7 @@
     size, chunks = plan(half)
     firsts = [sum(chunks[:c]) for c in range(len(chunks))]
     order = range(len(chunks))
-    cut = len(chunks) // 2
+    later, cut = second_order(len(chunks))
     groups_of = [order[:cut], order[cut:]]
     side = (strip % 2).astype(jnp.int32).reshape(1)
     info = jnp.stack([strip % 2, (strip // 2) % 2]).astype(jnp.int32)
@@ -655,10 +680,10 @@
         far_start = ((1 - strip % 2) * half + firsts[c]) * rows
         part = lax.dynamic_slice_in_dim(flat, far_start, chunks[c] * rows, axis=0)
         got.append(swap(part))
-    lowest = pick(side, flat, lambda s: s * (half // size), half, size, [(0, 3)])
-    below = against_flow(lowest)
     tables = prepare(points, vel_index)
     table, _, weights = tables
+    home, lowest = home_moments(side, flat, weights, size)
+    below = against_flow(lowest)
     gram = jnp.asarray(target_moments(points))
     mat = jnp.asarray(macro_matrix())
 
@@ -672,7 +697,7 @@
     flow_fluid = 1.0 - flow(wall, other_cells[rows:])
     cells = jnp.concatenate([flow_fluid * (1.0 - flow_rate), flow_fluid])
 
-    home = sum_groups(home_moments(flat, weights, 2 * size))
+    home = sum_groups(home)
     home = jnp.concatenate(
         [home[:13], collision_rate.reshape(1, -1), wall.reshape(1, -1), jnp.zeros((1, rows * cols), F32)]
     )
@@ -713,8 +738,8 @@
     )
 
     sums = jnp.zeros((16, width), F32)
-    near, back = None, []
-    for c in order:
+    near, back = None, {}
+    for c in later:
         number = int(c >= cut)
         start = firsts[groups_of[number][0]]
         near, far, sums = transport(
@@ -722,7 +747,7 @@
             chunks[c], firsts[c], size, change, skip=firsts[c] - start,
             into=None if near is None else [near],
         )
-        back.append(swap(far))
+        back[c] = swap(far)
     total = sum_groups(sums)
     total = total + swap(total)
     sum_a, sum_b = both_z(total)
@@ -736,7 +761,7 @@
         [pltpu.VMEM((16, SPAN * LANES), F32)],
     )
     out = finish(side, None, near, True, table, change, half, half, 0, size)
-    for c in order:
+    for c in later:
         out = finish(side, out, back[c], False, table, change, half, chunks[c], firsts[c], size)
     return out.reshape(dist.shape), state[:5].reshape(5, rows, cols)
 

time: 322 us -> 288 us (0.89)
  the two profiles are of different devices: /device:TPU:12 before, /device:TPU:0 now
where the time goes in v5:
time: 288 us; the launch traced here: 286 us
  Pallas kernels  111 us (39%)
  waiting for transfers between devices  87.3 us (30%)
  starting transfers between devices  70.3 us (24%)
  local copies, waits for them, and re-layouts  12.6 us (4%)
  other arithmetic  3.15 us (1%)
    ppermute x14, waiting for transfers between devices, swap(): return lax.ppermute(value, 'strip', swap_pairs)  75 us
    pallas_call x10, Pallas kernels, transport(): pl.pallas_call(functools.partial(transport_kernel, size, second_pass), ou...  66.3 us
    ppermute x7, starting transfers between devices, with_flow(): return lax.ppermute(value, 'strip', down_pairs)  26.8 us
    ppermute x14, starting transfers between devices, swap(): return lax.ppermute(value, 'strip', swap_pairs)  19.1 us
    pallas_call x6, Pallas kernels, finish(): pl.pallas_call(functools.partial(finish_kernel, size, own), out_shape=jax...  16.9 us
    ppermute x3, starting transfers between devices, both_z(): lax.ppermute(value, 'strip', pair_a)  9.59 us
    pallas_call x1, Pallas kernels, home_moments(): pl.pallas_call(functools.partial(moment_kernel, size), out_shape=(jax.Sha...  9.37 us
    pallas_call x5, Pallas kernels, pick(): pl.pallas_call(functools.partial(pick_kernel, size, picks), out_shape=jax...  9.31 us
  transfers between devices with their start and end apart: 39, of which 15 were waited for; matrix products, arithmetic and copies ran while one was open for 3% of the time, Pallas kernels for 38%

profile of v5, /device:TPU:0, one launch (start us, length us, event | category | flops | bytes accessed | tf_op | source)
XLA Modules:
  0.0 285.9 jit_solution(12296653072310288130)
XLA Ops:
  0.6 2.4 constant_dynamic-slice_fusion
  3.0 3.0 %collective-permute-start.10 = (f32[2304,128]{1,0:T(8,128)}, f32[2304,128]{1,0:T(8,128)}, u32[]{:S(2)}, u32[]{:S(2)}) collective-permute-start(f32[2304,128]{1,0:T(8,128)} %constant_dynamic-slice_fusion), channel_id=1, source_target_pairs={{0,1},{1,0},{2,3},{3,2},{4,5},{5,4},{6,7},{7,6},{8,9},{9,8},{10,11... | collective-permute-start | bytes 3538952 | tf_op jit(solution)/shard_map/ppermute | solution.py:654
  6.0 3.1 %constant_dynamic-slice_fusion.1 = (f32[1152,128]{1,0:T(8,128)}, f32[1152,128]{1,0:T(8,128)}, f32[1152,128]{1,0:T(8,128)}, f32[1152,128]{1,0:T(8,128)}) fusion(f32[13824,128]{1,0:T(8,128)} %bitcast.13, s32[]{:T(128)S(6)} %select_n.77, s32[]{:T(128)S(6)} %select_n.76, s32[]{:T(128)S(6)} %select_n.75, s32[]{:T(128)S(6)} %select_n.69), kind=kLoop, calls=%fused_computation.14 | loop fusion | bytes 4718608 | tf_op jit(solution)/shard_map/dynamic_slice | solution.py:681
  9.1 3.9 %prepare.1 = (bf16[3456,48]{1,0:T(8,128)(2,1)}, f32[3456,8]{1,0:T(8,128)}, bf16[3456,32]{1,0:T(8,128)(2,1)}) custom-call(s32[3,3456]{1,0:T(4,128)} %vel_ref.1), custom_call_target="tpu_custom_call" | custom-call | flops 691200 | bytes 3456000 | tf_op jit(solution)/shard_map/prepare/pallas_call | solution.py:186
  13.0 9.4 %home_moments.1 = (f32[16,512]{1,0:T(8,128)}, f32[1728,128]{1,0:T(8,128)}) custom-call(s32[1]{0:T(128)} %bitcast.side_ref, f32[13824,128]{1,0:T(8,128)} %bitcast.14, bf16[3456,32]{1,0:T(8,128)(2,1)} %get-tuple-element.47.weight_ref.refs_5_.refs_8_), custom_call_target="tpu_custom_call" | custom-call | flops 226492416 | bytes 7077888 | tf_op jit(solution)/shard_map/home_moments/pallas_call | solution.py:237
  22.4 1.4 collective-permute-start.2
  23.8 4.2 %collective-permute-start.6 = (f32[1152,128]{1,0:T(8,128)}, f32[1152,128]{1,0:T(8,128)}, u32[]{:S(2)}, u32[]{:S(2)}) collective-permute-start(f32[1152,128]{1,0:T(8,128)} %get-tuple-element.91), channel_id=1, source_target_pairs={{0,1},{1,0},{2,3},{3,2},{4,5},{5,4},{6,7},{7,6},{8,9},{9,8},{10,11... | collective-permute-start | bytes 1769480 | tf_op jit(solution)/shard_map/ppermute | solution.py:654
  28.1 5.0 %collective-permute-done.10.strip_ref.refs_1_ = f32[2304,128]{1,0:T(8,128)} collective-permute-done((f32[2304,128]{1,0:T(8,128)}, f32[2304,128]{1,0:T(8,128)}, u32[]{:S(2)}, u32[]{:S(2)}) %collective-permute-start.10) | collective-permute-done | bytes 1179680 | tf_op jit(solution)/shard_map/ppermute | solution.py:654
  33.1 2.0 collective-permute-start.3
  35.2 2.0 shard_map.81
  37.2 33.0 %collective-permute-done.3 = f32[8,128]{1,0:T(8,128)S(1)} collective-permute-done((f32[8,128]{1,0:T(8,128)S(1)}, f32[8,128]{1,0:T(8,128)S(1)}, u32[]{:S(2)}, u32[]{:S(2)}) %collective-permute-start.3) | collective-permute-done | bytes 4128 | tf_op jit(solution)/shard_map/ppermute | solution.py:654
  70.2 1.7 collective-permute-start
  71.9 4.3 %collective-permute-start.11 = (f32[2,576,128]{2,1,0:T(8,128)}, f32[2,576,128]{2,1,0:T(8,128)}, u32[]{:S(2)}, u32[]{:S(2)}) collective-permute-start(f32[2,576,128]{2,1,0:T(8,128)} %shard_map.81), channel_id=1, source_target_pairs={{0,2},{2,4},{3,1},{4,6},{5,3},{7,5},{8,10},{10,12},{11,9},{12,14},... | collective-permute-start | bytes 1769480 | tf_op jit(solution)/shard_map/ppermute | solution.py:657
  76.4 1.8 shard_map.80
  78.2 2.7 collective-permute-start.9
  80.9 1.8 shard_map.79
  82.7 4.2 %collective-permute-start.7 = (f32[2,288,128]{2,1,0:T(8,128)}, f32[2,288,128]{2,1,0:T(8,128)}, u32[]{:S(2)}, u32[]{:S(2)}) collective-permute-start(f32[2,288,128]{2,1,0:T(8,128)} %shard_map.79), channel_id=1, source_target_pairs={{0,2},{2,4},{3,1},{4,6},{5,3},{7,5},{8,10},{10,12},{11,9},{12,14},... | collective-permute-start | bytes 884744 | tf_op jit(solution)/shard_map/ppermute | solution.py:657
  87.1 1.6 collective-permute-start.19
  90.6 1.8 shard_map.78
  92.4 1.8 shard_map.77
  94.9 9.0 %transport_first.5 = (f32[1,1152,128]{2,1,0:T(8,128)}, f32[5,1152,128]{2,1,0:T(8,128)}, f32[2,1152,128]{2,1,0:T(8,128)}, f32[16,1024]{1,0:T(8,128)}) custom-call(s32[1]{0:T(128)} %bitcast.side_ref, f32[13824,128]{1,0:T(8,128)} %bitcast.15, f32[2304,128]{1,0:T(8,128)} %collective-permute-done.10.strip_ref.refs_1_, ...), custom_call_target="tpu_custom_call" | custom-call | flops 35389440 | bytes 5603328 | tf_op jit(solution)/shard_map/transport_first/pallas_call | solution.py:421
  103.9 3.8 %collective-permute-start.5 = (f32[2,288,128]{2,1,0:T(8,128)}, f32[2,288,128]{2,1,0:T(8,128)S(1)}, u32[]{:S(2)}, u32[]{:S(2)}) collective-permute-start(f32[2,288,128]{2,1,0:T(8,128)} %shard_map.78), channel_id=1, source_target_pairs={{0,2},{2,4},{3,1},{4,6},{5,3},{7,5},{8,10},{10,12},{11,9},{12,14},... | collective-permute-start | bytes 884744 | tf_op jit(solution)/shard_map/ppermute | solution.py:657
  107.7 5.6 %transport_first.6 = (f32[1,1152,128]{2,1,0:T(8,128)}, f32[5,1152,128]{2,1,0:T(8,128)}, f32[2,1152,128]{2,1,0:T(8,128)}, f32[16,1024]{1,0:T(8,128)}) custom-call(s32[1]{0:T(128)} %bitcast.side_ref, f32[13824,128]{1,0:T(8,128)} %bitcast.16, ...), custom_call_target="tpu_custom_call", output_to_operand_aliasing={{0}: (9, {}), {1}: (10, {}), {2}: (11, {})} | custom-call | flops 17694720 | bytes 2801664 | tf_op jit(solution)/shard_map/transport_first/pallas_call | solution.py:421
  113.4 3.5 %collective-permute-start.1 = (f32[2,288,128]{2,1,0:T(8,128)}, f32[2,288,128]{2,1,0:T(8,128)S(1)}, u32[]{:S(2)}, u32[]{:S(2)}) collective-permute-start(f32[2,288,128]{2,1,0:T(8,128)} %shard_map.77), channel_id=1, source_target_pairs={{0,2},{2,4},{3,1},{4,6},{5,3},{7,5},{8,10},{10,12},{11,9},{12,14},... | collective-permute-start | bytes 884744 | tf_op jit(solution)/shard_map/ppermute | solution.py:657
  116.9 5.6 %transport_first.7 = (f32[1,1152,128]{2,1,0:T(8,128)}, f32[5,1152,128]{2,1,0:T(8,128)}, f32[2,1152,128]{2,1,0:T(8,128)}, f32[16,1024]{1,0:T(8,128)}) custom-call(s32[1]{0:T(128)} %bitcast.side_ref, f32[13824,128]{1,0:T(8,128)} %bitcast.17, ...), custom_call_target="tpu_custom_call", output_to_operand_aliasing={{0}: (9, {}), {1}: (10, {}), {2}: (11, {})} | custom-call | flops 17694720 | bytes 2801664 | tf_op jit(solution)/shard_map/transport_first/pallas_call | solution.py:421
  122.5 3.5 %collective-permute-start.26 = (f32[2,1152,128]{2,1,0:T(8,128)}, f32[2,1152,128]{2,1,0:T(8,128)S(1)}, u32[]{:S(2)}, u32[]{:S(2)}) collective-permute-start(f32[2,1152,128]{2,1,0:T(8,128)} %get-tuple-element.71.refs_4_), channel_id=1, source_target_pairs={{0,2},{2,4},{3,1},{4,6},{5,3},{7,5},{8,10},{10,12},{11,9},{12,14},... | collective-permute-start | bytes 3538952 | tf_op jit(solution)/shard_map/ppermute | solution.py:657
  126.9 5.7 %transport_first.8 = (f32[1,576,128]{2,1,0:T(8,128)}, f32[5,576,128]{2,1,0:T(8,128)}, f32[2,576,128]{2,1,0:T(8,128)}, f32[16,1024]{1,0:T(8,128)}) custom-call(s32[1]{0:T(128)} %bitcast.side_ref, f32[13824,128]{1,0:T(8,128)} %bitcast.18, f32[1152,128]{1,0:T(8,128)} %copy-done.3, f32[2,288,128]{2,1,0:T(8,128)} %copy-done.7, f32[1728,128]{1,0:T(8,128)} %copy-done, ...), custom_call_target="tpu_custom_call" | custom-call | flops 17694720 | bytes 2801664 | tf_op jit(solution)/shard_map/transport_first/pallas_call | solution.py:421
  133.2 5.7 %transport_first.9 = (f32[1,576,128]{2,1,0:T(8,128)}, f32[5,576,128]{2,1,0:T(8,128)}, f32[2,576,128]{2,1,0:T(8,128)}, f32[16,1024]{1,0:T(8,128)}) custom-call(s32[1]{0:T(128)} %bitcast.side_ref, f32[13824,128]{1,0:T(8,128)} %bitcast.19, ...), custom_call_target="tpu_custom_call", output_to_operand_aliasing={{0}: (9, {}), {1}: (10, {}), {2}: (11, {})} | custom-call | flops 17694720 | bytes 2801664 | tf_op jit(solution)/shard_map/transport_first/pallas_call | solution.py:421
  138.9 1.5 collective-permute-start.13
  140.5 1.4 collective-permute-start.14
  141.9 1.3 collective-permute-start.27
  143.2 2.7 collective-permute-start.21
  146.6 4.8 %collective-permute-start.24 = (f32[2,576,128]{2,1,0:T(8,128)}, f32[2,576,128]{2,1,0:T(8,128)}, u32[]{:S(2)}, u32[]{:S(2)}) collective-permute-start(f32[2,576,128]{2,1,0:T(8,128)} %get-tuple-element.68.refs_4_), channel_id=1, source_target_pairs={{0,2},{2,4},{3,1},{4,6},{5,3},{7,5},{8,10},{10,12},{11,9},{12,14},... | collective-permute-start | bytes 1769480 | tf_op jit(solution)/shard_map/ppermute | solution.py:657
  152.2 6.6 %collective-permute-done.21 = f32[16,512]{1,0:T(8,128)S(1)} collective-permute-done((f32[16,512]{1,0:T(8,128)S(1)}, f32[16,512]{1,0:T(8,128)S(1)}, u32[]{:S(2)}, u32[]{:S(2)}) %collective-permute-start.21) | collective-permute-done | bytes 32800 | tf_op jit(solution)/shard_map/ppermute | solution.py:663
  158.8 2.1 collective-permute-start.23
  160.9 2.1 collective-permute-done.15
  164.1 1.3 collective-permute-start.25
  165.4 2.7 collective-permute-done.16.sum_a_ref
  168.7 1.3 collective-permute-start.17
  170.6 3.2 %shard_map.82 = (bf16[48,1408]{1,0:T(8,128)(2,1)}, f32[16,3072]{1,0:T(8,128)}) custom-call(s32[2]{0:T(128)} %pad_add_fusion.info_ref, f32[16,1024]{1,0:T(8,128)} %copy-done.10, f32[16,1024]{1,0:T(8,128)} %copy-done.13, f32[16,1024]{1,0:T(8,128)} %collective-permute-done.17.sum_b_ref, f32[3,16,512]{2,1,0:T(8,128)} %copy-done.6, f32[3,16,512]{2,1,0:T(8,128)} %copy-done.12, ...), custom_call_target="tpu_custom_call" | custom-call | flops 4000000 | bytes 1000000 | tf_op jit(solution)/shard_map/pallas_call | solution.py:563
  174.9 6.2 %transport_second.5 = (f32[4,1728,128]{2,1,0:T(8,128)}, f32[4,288,128]{2,1,0:T(8,128)}, f32[16,1024]{1,0:T(8,128)}) custom-call(s32[1]{0:T(128)} %bitcast.side_ref, bf16[3456,48]{1,0:T(8,128)(2,1)} %get-tuple-element.46.refs_0_.table_ref, bf16[48,1408]{1,0:T(8,128)(2,1)} %get-tuple-element.65.refs_1_, f32[1,1152,128]{2,1,0:T(8,128)} %get-tuple-element.69.refs_2_, ...), custom_call_target="tpu_custom_call" | custom-call | flops 17694720 | bytes 2801664 | tf_op jit(solution)/shard_map/transport_second/pallas_call | solution.py:421
  181.0 6.2 %transport_second.6 = (f32[4,1728,128]{2,1,0:T(8,128)}, f32[4,288,128]{2,1,0:T(8,128)}, f32[16,1024]{1,0:T(8,128)}) custom-call(s32[1]{0:T(128)} %bitcast.side_ref, bf16[3456,48]{1,0:T(8,128)(2,1)} %get-tuple-element.46.refs_0_.table_ref, bf16[48,1408]{1,0:T(8,128)(2,1)} %get-tuple-element.65.refs_1_, ...), custom_call_target="tpu_custom_call", output_to_operand_aliasing={{0}: (12, {})} | custom-call | flops 17694720 | bytes 2801664 | tf_op jit(solution)/shard_map/transport_second/pallas_call | solution.py:421
  187.2 10.0 %transport_second.7 = (f32[4,1728,128]{2,1,0:T(8,128)}, f32[4,576,128]{2,1,0:T(8,128)}, f32[16,1024]{1,0:T(8,128)}) custom-call(s32[1]{0:T(128)} %bitcast.side_ref, bf16[3456,48]{1,0:T(8,128)(2,1)} %get-tuple-element.46.refs_0_.table_ref, bf16[48,1408]{1,0:T(8,128)(2,1)} %get-tuple-element.65.refs_1_, ...), custom_call_target="tpu_custom_call", output_to_operand_aliasing={{0}: (12, {})} | custom-call | flops 35389440 | bytes 5603328 | tf_op jit(solution)/shard_map/transport_second/pallas_call | solution.py:421
  197.3 6.2 %transport_second.8 = (f32[4,1728,128]{2,1,0:T(8,128)}, f32[4,288,128]{2,1,0:T(8,128)}, f32[16,1024]{1,0:T(8,128)}) custom-call(s32[1]{0:T(128)} %bitcast.side_ref, bf16[3456,48]{1,0:T(8,128)(2,1)} %get-tuple-element.46.refs_0_.table_ref, bf16[48,1408]{1,0:T(8,128)(2,1)} %get-tuple-element.65.refs_1_, ...), custom_call_target="tpu_custom_call", output_to_operand_aliasing={{0}: (12, {})} | custom-call | flops 17694720 | bytes 2801664 | tf_op jit(solution)/shard_map/transport_second/pallas_call | solution.py:421
  203.5 6.2 %transport_second.9 = (f32[4,1728,128]{2,1,0:T(8,128)}, f32[4,288,128]{2,1,0:T(8,128)}, f32[16,1024]{1,0:T(8,128)}) custom-call(s32[1]{0:T(128)} %bitcast.side_ref, bf16[3456,48]{1,0:T(8,128)(2,1)} %get-tuple-element.46.refs_0_.table_ref, bf16[48,1408]{1,0:T(8,128)(2,1)} %get-tuple-element.65.refs_1_, ...), custom_call_target="tpu_custom_call", output_to_operand_aliasing={{0}: (12, {})} | custom-call | flops 17694720 | bytes 2801664 | tf_op jit(solution)/shard_map/transport_second/pallas_call | solution.py:421
  209.7 1.7 collective-permute-start.30
  211.4 1.5 collective-permute-start.31
  215.9 1.7 collective-permute-start.32
  217.7 6.3 %collective-permute-done.32 = f32[16,1024]{1,0:T(8,128)S(1)} collective-permute-done((f32[16,1024]{1,0:T(8,128)S(1)}, f32[16,1024]{1,0:T(8,128)S(1)}, u32[]{:S(2)}, u32[]{:S(2)}) %collective-permute-start.32) | collective-permute-done | bytes 65568 | tf_op jit(solution)/shard_map/ppermute | solution.py:654
  224.0 6.9 %collective-permute-start.33 = (f32[16,1024]{1,0:T(8,128)S(1)}, f32[16,1024]{1,0:T(8,128)S(1)}, u32[]{:S(2)}, u32[]{:S(2)}) collective-permute-start(f32[16,1024]{1,0:T(8,128)S(1)} %add.97.sum_ref), channel_id=1, source_target_pairs={{0,2},{1,3},{2,0},{3,1},{4,6},{5,7},{6,4},{7,5},{8,10},{9,11},{10,... | collective-permute-start | bytes 196616 | tf_op jit(solution)/shard_map/ppermute | solution.py:663
  231.9 1.7 collective-permute-start.37
  233.9 1.7 collective-permute-start.28
  235.7 2.6 shard_map.83
  238.2 1.3 reshape.27
  239.6 6.0 %finish.6.rest_0_ = f32[13824,128]{1,0:T(8,128)} custom-call(s32[1]{0:T(128)} %bitcast.side_ref, f32[4,1728,128]{2,1,0:T(8,128)} %get-tuple-element.88.rows_ref, bf16[3456,48]{1,0:T(8,128)(2,1)} %get-tuple-element.46.refs_0_.table_ref, bf16[48,512]{1,0:T(8,128)(2,1)} %get-tuple-element.83.change_ref), custom_call_target="tpu_custom_call" | custom-call | flops 84934656 | bytes 7077888 | tf_op jit(solution)/shard_map/finish/pallas_call | solution.py:603
  245.5 2.6 collective-permute-done.38.rows_ref
  248.1 2.1 finish.7.rest_0_
  250.3 10.5 %collective-permute-done.37.rows_ref = f32[4,288,128]{2,1,0:T(8,128)} collective-permute-done((f32[4,288,128]{2,1,0:T(8,128)}, f32[4,288,128]{2,1,0:T(8,128)}, u32[]{:S(2)}, u32[]{:S(2)}) %collective-permute-start.37) | collective-permute-done | bytes 589856 | tf_op jit(solution)/shard_map/ppermute | solution.py:654
  260.8 2.1 finish.8.rest_0_
  263.9 2.3 finish.9.rest_0_
  266.3 7.1 %collective-permute-done.35.rows_ref = f32[4,288,128]{2,1,0:T(8,128)} collective-permute-done((f32[4,288,128]{2,1,0:T(8,128)}, f32[4,288,128]{2,1,0:T(8,128)}, u32[]{:S(2)}, u32[]{:S(2)}) %collective-permute-start.35) | collective-permute-done | bytes 589856 | tf_op jit(solution)/shard_map/ppermute | solution.py:654
  273.4 2.1 finish.10.rest_0_
  275.5 7.3 %collective-permute-done.28.rows_ref = f32[4,288,128]{2,1,0:T(8,128)S(1)} collective-permute-done((f32[4,288,128]{2,1,0:T(8,128)}, f32[4,288,128]{2,1,0:T(8,128)S(1)}, u32[]{:S(2)}, u32[]{:S(2)}) %collective-permute-start.28) | collective-permute-done | bytes 589856 | tf_op jit(solution)/shard_map/ppermute | solution.py:654
  283.7 2.1 finish.11
  (103 shorter events, 15.8 us)
Async XLA Ops:
  3.0 30.1 %collective-permute-start.10 = (f32[2304,128]{1,0:T(8,128)}, f32[2304,128]{1,0:T(8,128)}, u32[]{:S(2)}, u32[]{:S(2)}) collective-permute-start(f32[2304,128]{1,0:T(8,128)} %constant_dynamic-slice_fusion), channel_id=1, source_target_pairs={{0,1},{1,0},{2,3},{3,2},{4,5},{5,4},{6,7},{7,6},{8,9},{9,8},{10,11... | collective-permute-start | bytes 3538952 | tf_op jit(solution)/shard_map/ppermute | solution.py:654
  9.1 62.8 %collective-permute-start.8 = (f32[1152,128]{1,0:T(8,128)}, f32[1152,128]{1,0:T(8,128)}, u32[]{:S(2)}, u32[]{:S(2)}) collective-permute-start(f32[1152,128]{1,0:T(8,128)} %get-tuple-element.90), channel_id=1, source_target_pairs={{0,1},{1,0},{2,3},{3,2},{4,5},{5,4},{6,7},{7,6},{8,9},{9,8},{10,11... | collective-permute-start | bytes 1769480 | tf_op jit(solution)/shard_map/ppermute | solution.py:654
  13.0 15.1 %copy-start.18 = (s32[4,128]{1,0:T(4,128)S(1)}, s32[4,128]{1,0:T(4,128)}, u32[]{:S(2)}) copy-start(s32[4,128]{1,0:T(4,128)} %param.7) | copy-start | bytes 6148
  13.0 15.1 %copy-start.16 = (f32[4,128]{1,0:T(4,128)S(1)}, f32[4,128]{1,0:T(4,128)}, u32[]{:S(2)}) copy-start(f32[4,128]{1,0:T(4,128)} %param.8) | copy-start | bytes 6148
  22.4 64.6 %copy-start.17 = (f32[16,512]{1,0:T(8,128)S(1)}, f32[16,512]{1,0:T(8,128)}, u32[]{:S(2)}) copy-start(f32[16,512]{1,0:T(8,128)} %get-tuple-element.64) | copy-start | bytes 98308
  22.4 64.7 %collective-permute-start.2 = (f32[1728,128]{1,0:T(8,128)}, f32[1728,128]{1,0:T(8,128)S(1)}, u32[]{:S(2)}, u32[]{:S(2)}) collective-permute-start(f32[1728,128]{1,0:T(8,128)} %get-tuple-element.48), channel_id=1, source_target_pairs={{2,0},{4,2},{1,3},{6,4},{3,5},{5,7},{10,8},{12,10},{9,11},{14,12},... | collective-permute-start | bytes 2654216 | tf_op jit(solution)/shard_map/ppermute | solution.py:660
  23.8 54.4 %collective-permute-start.6 = (f32[1152,128]{1,0:T(8,128)}, f32[1152,128]{1,0:T(8,128)}, u32[]{:S(2)}, u32[]{:S(2)}) collective-permute-start(f32[1152,128]{1,0:T(8,128)} %get-tuple-element.91), channel_id=1, source_target_pairs={{0,1},{1,0},{2,3},{3,2},{4,5},{5,4},{6,7},{7,6},{8,9},{9,8},{10,11... | collective-permute-start | bytes 1769480 | tf_op jit(solution)/shard_map/ppermute | solution.py:654
  28.0 54.7 %collective-permute-start.4 = (f32[1152,128]{1,0:T(8,128)}, f32[1152,128]{1,0:T(8,128)S(1)}, u32[]{:S(2)}, u32[]{:S(2)}) collective-permute-start(f32[1152,128]{1,0:T(8,128)} %get-tuple-element.92), channel_id=1, source_target_pairs={{0,1},{1,0},{2,3},{3,2},{4,5},{5,4},{6,7},{7,6},{8,9},{9,8},{10,11... | collective-permute-start | bytes 1769480 | tf_op jit(solution)/shard_map/ppermute | solution.py:654
  33.1 37.1 %collective-permute-start.3 = (f32[8,128]{1,0:T(8,128)S(1)}, f32[8,128]{1,0:T(8,128)S(1)}, u32[]{:S(2)}, u32[]{:S(2)}) collective-permute-start(f32[8,128]{1,0:T(8,128)S(1)} %pad_maximum_fusion.2), channel_id=1, source_target_pairs={{0,1},{1,0},{2,3},{3,2},{4,5},{5,4},{6,7},{7,6},{8,9},{9,8},{10,11... | collective-permute-start | bytes 12296 | tf_op jit(solution)/shard_map/ppermute | solution.py:654
  70.2 16.8 %collective-permute-start = (f32[1152,128]{1,0:T(8,128)}, f32[1152,128]{1,0:T(8,128)}, u32[]{:S(2)}, u32[]{:S(2)}) collective-permute-start(f32[1152,128]{1,0:T(8,128)} %get-tuple-element.93), channel_id=1, source_target_pairs={{0,1},{1,0},{2,3},{3,2},{4,5},{5,4},{6,7},{7,6},{8,9},{9,8},{10,11... | collective-permute-start | bytes 1769480 | tf_op jit(solution)/shard_map/ppermute | solution.py:654
  71.9 17.5 %collective-permute-start.11 = (f32[2,576,128]{2,1,0:T(8,128)}, f32[2,576,128]{2,1,0:T(8,128)}, u32[]{:S(2)}, u32[]{:S(2)}) collective-permute-start(f32[2,576,128]{2,1,0:T(8,128)} %shard_map.81), channel_id=1, source_target_pairs={{0,2},{2,4},{3,1},{4,6},{5,3},{7,5},{8,10},{10,12},{11,9},{12,14},... | collective-permute-start | bytes 1769480 | tf_op jit(solution)/shard_map/ppermute | solution.py:657
  78.2 25.7 %collective-permute-start.9 = (f32[2,288,128]{2,1,0:T(8,128)}, f32[2,288,128]{2,1,0:T(8,128)S(1)}, u32[]{:S(2)}, u32[]{:S(2)}) collective-permute-start(f32[2,288,128]{2,1,0:T(8,128)} %shard_map.80), channel_id=1, source_target_pairs={{0,2},{2,4},{3,1},{4,6},{5,3},{7,5},{8,10},{10,12},{11,9},{12,14},... | collective-permute-start | bytes 884744 | tf_op jit(solution)/shard_map/ppermute | solution.py:657
  82.7 7.9 %copy-start.3 = (f32[1152,128]{1,0:T(8,128)}, f32[1152,128]{1,0:T(8,128)S(1)}, u32[]{:S(2)}) copy-start(f32[1152,128]{1,0:T(8,128)S(1)} %collective-permute-done.4.strip_ref.refs_1_) | copy-start | bytes 1769476
  82.7 30.6 %collective-permute-start.7 = (f32[2,288,128]{2,1,0:T(8,128)}, f32[2,288,128]{2,1,0:T(8,128)}, u32[]{:S(2)}, u32[]{:S(2)}) collective-permute-start(f32[2,288,128]{2,1,0:T(8,128)} %shard_map.79), channel_id=1, source_target_pairs={{0,2},{2,4},{3,1},{4,6},{5,3},{7,5},{8,10},{10,12},{11,9},{12,14},... | collective-permute-start | bytes 884744 | tf_op jit(solution)/shard_map/ppermute | solution.py:657
  87.0 35.5 %collective-permute-start.18 = (f32[16,512]{1,0:T(8,128)S(1)}, f32[16,512]{1,0:T(8,128)S(1)}, u32[]{:S(2)}, u32[]{:S(2)}) collective-permute-start(f32[16,512]{1,0:T(8,128)S(1)} %copy-done.17), channel_id=1, source_target_pairs={{0,8},{8,16},{16,24},{24,0},{1,9},{9,17},{17,25},{25,1},{2,10},{10... | collective-permute-start | bytes 98312 | tf_op jit(solution)/shard_map/ppermute | solution.py:668
  87.0 7.8 %copy-start = (f32[1728,128]{1,0:T(8,128)}, f32[1728,128]{1,0:T(8,128)S(1)}, u32[]{:S(2)}) copy-start(f32[1728,128]{1,0:T(8,128)S(1)} %collective-permute-done.2.refs_3_) | copy-start | bytes 2654212
  87.1 39.0 %collective-permute-start.19 = (f32[16,512]{1,0:T(8,128)S(1)}, f32[16,512]{1,0:T(8,128)S(1)}, u32[]{:S(2)}, u32[]{:S(2)}) collective-permute-start(f32[16,512]{1,0:T(8,128)S(1)} %copy-done.17), channel_id=1, source_target_pairs={{0,16},{8,24},{16,0},{24,8},{1,17},{9,25},{17,1},{25,9},{2,18},{10... | collective-permute-start | bytes 98312 | tf_op jit(solution)/shard_map/ppermute | solution.py:668
  89.4 36.6 %collective-permute-start.20 = (f32[16,512]{1,0:T(8,128)S(1)}, f32[16,512]{1,0:T(8,128)S(1)}, u32[]{:S(2)}, u32[]{:S(2)}) collective-permute-start(f32[16,512]{1,0:T(8,128)S(1)} %copy-done.17), channel_id=1, source_target_pairs={{0,24},{8,0},{16,8},{24,16},{1,25},{9,1},{17,9},{25,17},{2,26},{10... | collective-permute-start | bytes 98312 | tf_op jit(solution)/shard_map/ppermute | solution.py:668
  103.9 3.9 %copy-start.9 = (f32[2,288,128]{2,1,0:T(8,128)}, f32[2,288,128]{2,1,0:T(8,128)S(1)}, u32[]{:S(2)}) copy-start(f32[2,288,128]{2,1,0:T(8,128)S(1)} %collective-permute-done.9.refs_2_) | copy-start | bytes 884740
  103.9 22.3 %collective-permute-start.5 = (f32[2,288,128]{2,1,0:T(8,128)}, f32[2,288,128]{2,1,0:T(8,128)S(1)}, u32[]{:S(2)}, u32[]{:S(2)}) collective-permute-start(f32[2,288,128]{2,1,0:T(8,128)} %shard_map.78), channel_id=1, source_target_pairs={{0,2},{2,4},{3,1},{4,6},{5,3},{7,5},{8,10},{10,12},{11,9},{12,14},... | collective-permute-start | bytes 884744 | tf_op jit(solution)/shard_map/ppermute | solution.py:657
  113.4 19.1 %collective-permute-start.1 = (f32[2,288,128]{2,1,0:T(8,128)}, f32[2,288,128]{2,1,0:T(8,128)S(1)}, u32[]{:S(2)}, u32[]{:S(2)}) collective-permute-start(f32[2,288,128]{2,1,0:T(8,128)} %shard_map.77), channel_id=1, source_target_pairs={{0,2},{2,4},{3,1},{4,6},{5,3},{7,5},{8,10},{10,12},{11,9},{12,14},... | collective-permute-start | bytes 884744 | tf_op jit(solution)/shard_map/ppermute | solution.py:657
  122.5 51.4 %collective-permute-start.26 = (f32[2,1152,128]{2,1,0:T(8,128)}, f32[2,1152,128]{2,1,0:T(8,128)S(1)}, u32[]{:S(2)}, u32[]{:S(2)}) collective-permute-start(f32[2,1152,128]{2,1,0:T(8,128)} %get-tuple-element.71.refs_4_), channel_id=1, source_target_pairs={{0,2},{2,4},{3,1},{4,6},{5,3},{7,5},{8,10},{10,12},{11,9},{12,14},... | collective-permute-start | bytes 3538952 | tf_op jit(solution)/shard_map/ppermute | solution.py:657
  126.1 0.7 copy-start.7
  132.5 0.7 copy-start.8
  133.2 8.7 %copy-start.1 = (f32[1,1152,128]{2,1,0:T(8,128)S(1)}, f32[1,1152,128]{2,1,0:T(8,128)}, u32[]{:S(2)}) copy-start(f32[1,1152,128]{2,1,0:T(8,128)} %get-tuple-element.69.refs_2_) | copy-start | bytes 1769476
  138.9 4.3 %collective-permute-start.12 = (f32[16,1024]{1,0:T(8,128)}, f32[16,1024]{1,0:T(8,128)S(1)}, u32[]{:S(2)}, u32[]{:S(2)}) collective-permute-start(f32[16,1024]{1,0:T(8,128)} %get-tuple-element.63), channel_id=1, source_target_pairs={{0,8},{8,16},{16,24},{24,0},{1,9},{9,17},{17,25},{25,1},{2,10},{10... | collective-permute-start | bytes 196616 | tf_op jit(solution)/shard_map/ppermute | solution.py:668
  138.9 7.0 %collective-permute-start.13 = (f32[16,1024]{1,0:T(8,128)}, f32[16,1024]{1,0:T(8,128)S(1)}, u32[]{:S(2)}, u32[]{:S(2)}) collective-permute-start(f32[16,1024]{1,0:T(8,128)} %get-tuple-element.63), channel_id=1, source_target_pairs={{0,16},{8,24},{16,0},{24,8},{1,17},{9,25},{17,1},{25,9},{2,18},{10... | collective-permute-start | bytes 196616 | tf_op jit(solution)/shard_map/ppermute | solution.py:668
  140.5 6.1 %collective-permute-start.14 = (f32[16,1024]{1,0:T(8,128)}, f32[16,1024]{1,0:T(8,128)S(1)}, u32[]{:S(2)}, u32[]{:S(2)}) collective-permute-start(f32[16,1024]{1,0:T(8,128)} %get-tuple-element.63), channel_id=1, source_target_pairs={{0,24},{8,0},{16,8},{24,16},{1,25},{9,1},{17,9},{25,17},{2,26},{10... | collective-permute-start | bytes 196616 | tf_op jit(solution)/shard_map/ppermute | solution.py:668
  141.9 32.0 %collective-permute-start.27 = (f32[1,1152,128]{2,1,0:T(8,128)S(1)}, f32[1,1152,128]{2,1,0:T(8,128)}, u32[]{:S(2)}, u32[]{:S(2)}) collective-permute-start(f32[1,1152,128]{2,1,0:T(8,128)S(1)} %copy-done.1), channel_id=1, source_target_pairs={{2,0},{4,2},{1,3},{6,4},{3,5},{5,7},{10,8},{12,10},{9,11},{14,12},... | collective-permute-start | bytes 1769480 | tf_op jit(solution)/shard_map/ppermute | solution.py:660
  143.2 15.5 %collective-permute-start.21 = (f32[16,512]{1,0:T(8,128)S(1)}, f32[16,512]{1,0:T(8,128)S(1)}, u32[]{:S(2)}, u32[]{:S(2)}) collective-permute-start(f32[16,512]{1,0:T(8,128)S(1)} %maximum_maximum_fusion), channel_id=1, source_target_pairs={{0,2},{1,3},{2,0},{3,1},{4,6},{5,7},{6,4},{7,5},{8,10},{9,11},{10,... | collective-permute-start | bytes 98312 | tf_op jit(solution)/shard_map/ppermute | solution.py:663
  145.9 12.9 %collective-permute-start.22 = (f32[16,512]{1,0:T(8,128)S(1)}, f32[16,512]{1,0:T(8,128)S(1)}, u32[]{:S(2)}, u32[]{:S(2)}) collective-permute-start(f32[16,512]{1,0:T(8,128)S(1)} %maximum_maximum_fusion), channel_id=1, source_target_pairs={{2,4},{3,5},{4,2},{5,3},{10,12},{11,13},{12,10},{13,11},{18,20},{1... | collective-permute-start | bytes 98312 | tf_op jit(solution)/shard_map/ppermute | solution.py:663
  146.6 50.7 %collective-permute-start.24 = (f32[2,576,128]{2,1,0:T(8,128)}, f32[2,576,128]{2,1,0:T(8,128)}, u32[]{:S(2)}, u32[]{:S(2)}) collective-permute-start(f32[2,576,128]{2,1,0:T(8,128)} %get-tuple-element.68.refs_4_), channel_id=1, source_target_pairs={{0,2},{2,4},{3,1},{4,6},{5,3},{7,5},{8,10},{10,12},{11,9},{12,14},... | collective-permute-start | bytes 1769480 | tf_op jit(solution)/shard_map/ppermute | solution.py:657
  158.8 4.3 %collective-permute-start.15 = (f32[16,1024]{1,0:T(8,128)S(1)}, f32[16,1024]{1,0:T(8,128)S(1)}, u32[]{:S(2)}, u32[]{:S(2)}) collective-permute-start(f32[16,1024]{1,0:T(8,128)S(1)} %add_add_fusion.1), channel_id=1, source_target_pairs={{0,1},{1,0},{2,3},{3,2},{4,5},{5,4},{6,7},{7,6},{8,9},{9,8},{10,11... | collective-permute-start | bytes 196616 | tf_op jit(solution)/shard_map/ppermute | solution.py:654
  158.8 11.8 %copy-start.6 = (f32[3,16,512]{2,1,0:T(8,128)}, f32[3,16,512]{2,1,0:T(8,128)S(1)}, u32[]{:S(2)}) copy-start(f32[3,16,512]{2,1,0:T(8,128)S(1)} %pad_maximum_fusion.near_ref) | copy-start | bytes 294916
  158.8 5.3 %collective-permute-start.23 = (f32[3,16,512]{2,1,0:T(8,128)S(1)}, f32[3,16,512]{2,1,0:T(8,128)S(1)}, u32[]{:S(2)}, u32[]{:S(2)}) collective-permute-start(f32[3,16,512]{2,1,0:T(8,128)S(1)} %pad_maximum_fusion.near_ref), channel_id=1, source_target_pairs={{0,1},{1,0},{2,3},{3,2},{4,5},{5,4},{6,7},{7,6},{8,9},{9,8},{10,11... | collective-permute-start | bytes 294920 | tf_op jit(solution)/shard_map/ppermute | solution.py:654
  163.1 7.6 %copy-start.10 = (f32[16,1024]{1,0:T(8,128)}, f32[16,1024]{1,0:T(8,128)S(1)}, u32[]{:S(2)}) copy-start(f32[16,1024]{1,0:T(8,128)S(1)} %add.90.sum_ref) | copy-start | bytes 196612
  163.1 5.0 %collective-permute-start.16 = (f32[16,1024]{1,0:T(8,128)S(1)}, f32[16,1024]{1,0:T(8,128)S(1)}, u32[]{:S(2)}, u32[]{:S(2)}) collective-permute-start(f32[16,1024]{1,0:T(8,128)S(1)} %add.90.sum_ref), channel_id=1, source_target_pairs={{0,2},{1,3},{2,0},{3,1},{4,6},{5,7},{6,4},{7,5},{8,10},{9,11},{10,... | collective-permute-start | bytes 196616 | tf_op jit(solution)/shard_map/ppermute | solution.py:663
  164.1 6.5 %copy-start.12 = (f32[3,16,512]{2,1,0:T(8,128)}, f32[3,16,512]{2,1,0:T(8,128)S(1)}, u32[]{:S(2)}) copy-start(f32[3,16,512]{2,1,0:T(8,128)S(1)} %collective-permute-done.23.far_ref) | copy-start | bytes 294916
  164.1 33.2 %collective-permute-start.25 = (f32[1,576,128]{2,1,0:T(8,128)}, f32[1,576,128]{2,1,0:T(8,128)}, u32[]{:S(2)}, u32[]{:S(2)}) collective-permute-start(f32[1,576,128]{2,1,0:T(8,128)} %get-tuple-element.66.refs_2_), channel_id=1, source_target_pairs={{2,0},{4,2},{1,3},{6,4},{3,5},{5,7},{10,8},{12,10},{9,11},{14,12},... | collective-permute-start | bytes 884744 | tf_op jit(solution)/shard_map/ppermute | solution.py:660
  168.1 0.6 copy-start.13
  168.7 1.9 collective-permute-start.17
  173.9 1.0 copy-start.2
  197.2 65.7 %collective-permute-start.36 = (f32[4,576,128]{2,1,0:T(8,128)}, f32[4,576,128]{2,1,0:T(8,128)S(1)}, u32[]{:S(2)}, u32[]{:S(2)}) collective-permute-start(f32[4,576,128]{2,1,0:T(8,128)} %get-tuple-element.85), channel_id=1, source_target_pairs={{0,1},{1,0},{2,3},{3,2},{4,5},{5,4},{6,7},{7,6},{8,9},{9,8},{10,11... | collective-permute-start | bytes 3538952 | tf_op jit(solution)/shard_map/ppermute | solution.py:654
  209.7 4.0 %collective-permute-start.29 = (f32[16,1024]{1,0:T(8,128)}, f32[16,1024]{1,0:T(8,128)S(1)}, u32[]{:S(2)}, u32[]{:S(2)}) collective-permute-start(f32[16,1024]{1,0:T(8,128)} %get-tuple-element.81), channel_id=1, source_target_pairs={{0,8},{8,16},{16,24},{24,0},{1,9},{9,17},{17,25},{25,1},{2,10},{10... | collective-permute-start | bytes 196616 | tf_op jit(solution)/shard_map/ppermute | solution.py:668
  209.7 4.6 %collective-permute-start.30 = (f32[16,1024]{1,0:T(8,128)}, f32[16,1024]{1,0:T(8,128)S(1)}, u32[]{:S(2)}, u32[]{:S(2)}) collective-permute-start(f32[16,1024]{1,0:T(8,128)} %get-tuple-element.81), channel_id=1, source_target_pairs={{0,16},{8,24},{16,0},{24,8},{1,17},{9,25},{17,1},{25,9},{2,18},{10... | collective-permute-start | bytes 196616 | tf_op jit(solution)/shard_map/ppermute | solution.py:668
  211.4 3.7 %collective-permute-start.31 = (f32[16,1024]{1,0:T(8,128)}, f32[16,1024]{1,0:T(8,128)S(1)}, u32[]{:S(2)}, u32[]{:S(2)}) collective-permute-start(f32[16,1024]{1,0:T(8,128)} %get-tuple-element.81), channel_id=1, source_target_pairs={{0,24},{8,0},{16,8},{24,16},{1,25},{9,1},{17,9},{25,17},{2,26},{10... | collective-permute-start | bytes 196616 | tf_op jit(solution)/shard_map/ppermute | solution.py:668
  215.9 8.1 %collective-permute-start.32 = (f32[16,1024]{1,0:T(8,128)S(1)}, f32[16,1024]{1,0:T(8,128)S(1)}, u32[]{:S(2)}, u32[]{:S(2)}) collective-permute-start(f32[16,1024]{1,0:T(8,128)S(1)} %add_add_fusion), channel_id=1, source_target_pairs={{0,1},{1,0},{2,3},{3,2},{4,5},{5,4},{6,7},{7,6},{8,9},{9,8},{10,11... | collective-permute-start | bytes 196616 | tf_op jit(solution)/shard_map/ppermute | solution.py:654
  224.0 11.7 %copy-start.11 = (f32[16,1024]{1,0:T(8,128)}, f32[16,1024]{1,0:T(8,128)S(1)}, u32[]{:S(2)}) copy-start(f32[16,1024]{1,0:T(8,128)S(1)} %add.97.sum_ref) | copy-start | bytes 196612
  224.0 9.6 %collective-permute-start.33 = (f32[16,1024]{1,0:T(8,128)S(1)}, f32[16,1024]{1,0:T(8,128)S(1)}, u32[]{:S(2)}, u32[]{:S(2)}) collective-permute-start(f32[16,1024]{1,0:T(8,128)S(1)} %add.97.sum_ref), channel_id=1, source_target_pairs={{0,2},{1,3},{2,0},{3,1},{4,6},{5,7},{6,4},{7,5},{8,10},{9,11},{10,... | collective-permute-start | bytes 196616 | tf_op jit(solution)/shard_map/ppermute | solution.py:663
  230.9 3.0 %collective-permute-start.34 = (f32[16,1024]{1,0:T(8,128)S(1)}, f32[16,1024]{1,0:T(8,128)S(1)}, u32[]{:S(2)}, u32[]{:S(2)}) collective-permute-start(f32[16,1024]{1,0:T(8,128)S(1)} %add.97.sum_ref), channel_id=1, source_target_pairs={{2,4},{3,5},{4,2},{5,3},{10,12},{11,13},{12,10},{13,11},{18,20},{1... | collective-permute-start | bytes 196616 | tf_op jit(solution)/shard_map/ppermute | solution.py:663
  231.5 16.6 %collective-permute-start.38 = (f32[4,288,128]{2,1,0:T(8,128)}, f32[4,288,128]{2,1,0:T(8,128)}, u32[]{:S(2)}, u32[]{:S(2)}) collective-permute-start(f32[4,288,128]{2,1,0:T(8,128)} %get-tuple-element.87), channel_id=1, source_target_pairs={{0,1},{1,0},{2,3},{3,2},{4,5},{5,4},{6,7},{7,6},{8,9},{9,8},{10,11... | collective-permute-start | bytes 1769480 | tf_op jit(solution)/shard_map/ppermute | solution.py:654
  231.9 28.9 %collective-permute-start.37 = (f32[4,288,128]{2,1,0:T(8,128)}, f32[4,288,128]{2,1,0:T(8,128)}, u32[]{:S(2)}, u32[]{:S(2)}) collective-permute-start(f32[4,288,128]{2,1,0:T(8,128)} %get-tuple-element.86), channel_id=1, source_target_pairs={{0,1},{1,0},{2,3},{3,2},{4,5},{5,4},{6,7},{7,6},{8,9},{9,8},{10,11... | collective-permute-start | bytes 1769480 | tf_op jit(solution)/shard_map/ppermute | solution.py:654
  233.6 2.0 copy-start.14
  233.6 39.8 %collective-permute-start.35 = (f32[4,288,128]{2,1,0:T(8,128)}, f32[4,288,128]{2,1,0:T(8,128)}, u32[]{:S(2)}, u32[]{:S(2)}) collective-permute-start(f32[4,288,128]{2,1,0:T(8,128)} %get-tuple-element.84), channel_id=1, source_target_pairs={{0,1},{1,0},{2,3},{3,2},{4,5},{5,4},{6,7},{7,6},{8,9},{9,8},{10,11... | collective-permute-start | bytes 1769480 | tf_op jit(solution)/shard_map/ppermute | solution.py:654
  233.9 1.8 copy-start.15
  233.9 48.9 %collective-permute-start.28 = (f32[4,288,128]{2,1,0:T(8,128)}, f32[4,288,128]{2,1,0:T(8,128)S(1)}, u32[]{:S(2)}, u32[]{:S(2)}) collective-permute-start(f32[4,288,128]{2,1,0:T(8,128)} %get-tuple-element.80), channel_id=1, source_target_pairs={{0,1},{1,0},{2,3},{3,2},{4,5},{5,4},{6,7},{7,6},{8,9},{9,8},{10,11... | collective-permute-start | bytes 1769480 | tf_op jit(solution)/shard_map/ppermute | solution.py:654
  262.9 1.0 copy-start.4
  282.9 0.9 copy-start.5

commit v6 on v5

--- a/solution.py
+++ b/solution.py
@@ -122,31 +122,50 @@
     return pl.ds(start, count, stride=STRIP_ROWS)
 
 
-def pick_kernel(size, picks, side_ref, strip_ref, *rest):
-    out_ref = rest[-1]
+def pack_kernel(size, begins, counts, side_ref, far_ref, *rest):
+    outs = rest[-2 * len(begins) :]
     side = side_ref[0]
-    for index, (even, odd) in enumerate(picks):
-        out_ref[index] = strip_ref[strided(jnp.where(side == 1, odd, even), size), :]
-
-
-def pick(side, flat, start, count, size, picks, earlier=()):
-    return pl.pallas_call(
-        functools.partial(pick_kernel, size, picks),
-        out_shape=jax.ShapeDtypeStruct((len(picks), count, LANES), F32),
+    step = pl.program_id(0)
+    for c, (begin, count) in enumerate(zip(begins, counts)):
+
+        @pl.when((step >= begin) & (step < begin + count))
+        def _():
+            for i in range(STRIP_ROWS):
+                row = jnp.where(side == 1, i, 3 - i)
+                outs[2 * c + (1 if i < 2 else 0)][i % 2] = far_ref[strided(row, size), :]
+
+
+def pack(side, flat, half, chunks, first, size):
+    counts = [n // size for n in chunks]
+    begins = [sum(counts[:c]) for c in range(len(chunks))]
+    shift = half // size
+    start = first // size
+
+    def out_spec(c):
+        return pl.BlockSpec(
+            (2, size, LANES), lambda i, s: (0, jnp.clip(i - begins[c], 0, counts[c] - 1), 0)
+        )
+
+    outs = pl.pallas_call(
+        functools.partial(pack_kernel, size, begins, counts),
+        out_shape=[
+            jax.ShapeDtypeStruct((2, n, LANES), F32) for n in chunks for _ in range(2)
+        ],
         grid_spec=pltpu.PrefetchScalarGridSpec(
             num_scalar_prefetch=1,
-            grid=(count // size,),
+            grid=(sum(counts),),
             in_specs=[
-                pl.BlockSpec((4 * size, LANES), lambda i, s: (start(s[0]) + i, 0)),
-                *[pl.BlockSpec(memory_space=pl.ANY)] * len(earlier),
+                pl.BlockSpec((4 * size, LANES), lambda i, s: ((1 - s[0]) * shift + start + i, 0))
             ],
-            out_specs=pl.BlockSpec((len(picks), size, LANES), lambda i, s: (0, i, 0)),
+            out_specs=[out_spec(c) for c in range(len(chunks)) for _ in range(2)],
         ),
         compiler_params=params(),
+        name="pack",
         cost_estimate=pl.CostEstimate(
-            flops=0, transcendentals=0, bytes_accessed=count * LANES * 4 * (4 + len(picks))
-        ),
-    )(side, flat, *earlier)
+            flops=0, transcendentals=0, bytes_accessed=sum(chunks) * LANES * 4 * 8
+        ),
+    )(side, flat)
+    return [(outs[2 * c], outs[2 * c + 1]) for c in range(len(chunks))]
 
 
 def prepare_kernel(points, vel_ref, table_ref, const_ref, weight_ref):
@@ -200,11 +219,19 @@
     )(vel_index)
 
 
-def weighted(weights, first, second):
+def weighted(weight_ref, values):
     over_rows = (((0,), (0,)), ((), ()))
-    both = lax.dot_general(weights, first, over_rows, preferred_element_type=F32)
-    rest = lax.dot_general(weights, second, over_rows, preferred_element_type=F32)
-    return both[:16] + both[16:] + rest[:16]
+    total = None
+    for start in range(0, weight_ref.shape[0], 144):
+        weights = weight_ref[start : start + 144, :]
+        value = jnp.concatenate(values(start), axis=1)
+        high = value.astype(BF16)
+        low = (value - high.astype(F32)).astype(BF16)
+        both = lax.dot_general(weights, high, over_rows, preferred_element_type=F32)
+        rest = lax.dot_general(weights, low, over_rows, preferred_element_type=F32)
+        part = both[:16] + both[16:] + rest[:16]
+        total = part if total is None else total + part
+    return total
 
 
 def moment_kernel(size, side_ref, dist_ref, weight_ref, out_ref, lowest_ref):
@@ -221,13 +248,12 @@
         lowest_ref[...] = dist_ref[strided(jnp.where(side == 1, 3, 0), size), :]
 
     for pair in range(0, STRIP_ROWS, 2):
-        value = jnp.concatenate(
-            [dist_ref[strided(row, size), :] for row in (pair, pair + 1)], axis=1
-        )
-        high = value.astype(BF16)
-        out_ref[:, pair * LANES : (pair + 2) * LANES] += weighted(
-            weight_ref[...], high, (value - high.astype(F32)).astype(BF16)
-        )
+        def values(start, pair=pair):
+            return [
+                dist_ref[strided(STRIP_ROWS * start + row, 144), :] for row in (pair, pair + 1)
+            ]
+
+        out_ref[:, pair * LANES : (pair + 2) * LANES] += weighted(weight_ref, values)
 
 
 def home_moments(side, flat, weights, size):
@@ -266,7 +292,7 @@
     if second_pass:
         (table_ref, change_ref, q_first, q_mid, q_edge, up_ref, down_ref, *rest) = refs
     else:
-        (own_ref, got_ref, up_ref, down_ref, *rest) = refs
+        (own_ref, mid_ref, edge_ref, up_ref, down_ref, *rest) = refs
     (const_ref, weight_ref, cell_ref, sum_in_ref, *rest) = rest
     if second_pass:
         (near_out, far_out, sum_ref, lift_ref) = rest[-4:]
@@ -309,10 +335,13 @@
                     value = q_mid[row - 1, rows, :]
                 else:
                     value = q_edge[row - 6, rows, :]
+            elif row < 4:
+                local = jnp.where(side == 1, 3 - row, row)
+                value = own_ref[strided(base * STRIP_ROWS + local, group_size), :]
+            elif row < 6:
+                value = mid_ref[row - 4, rows, :]
             else:
-                ref = own_ref if row < 4 else got_ref
-                local = jnp.where(side == 1, 3 - row % 4, row % 4)
-                value = ref[strided(base * STRIP_ROWS + local, group_size), :]
+                value = edge_ref[row - 6, rows, :]
             if second_pass:
                 value = value + lift_ref[rows, pl.ds((row + 2) * LANES, LANES)]
             return value
@@ -353,9 +382,10 @@
 
     lax.fori_loop(0, size // group_size, body, 0)
     for pair in range(0, BLOCK_ROWS, 2):
-        value = jnp.concatenate([row_out(pair)[...], row_out(pair + 1)[...]], axis=1)
-        high = value.astype(BF16)
-        part = weighted(weight_ref[...], high, (value - high.astype(F32)).astype(BF16))
+        def values(start, pair=pair):
+            return [row_out(row)[start : start + 144, :] for row in (pair, pair + 1)]
+
+        part = weighted(weight_ref, values)
         for row in (pair, pair + 1):
             place = jnp.where(side == 1, 7 - row, row)
             columns = pl.ds(pl.multiple_of(place * LANES, LANES), LANES)
@@ -398,7 +428,8 @@
         args = []
         specs = [
             pl.BlockSpec((4 * size, LANES), lambda i, s: (mine(i, s), 0)),
-            pl.BlockSpec((4 * size, LANES), lambda i, s: (i, 0)),
+            stack_of(2, 0),
+            stack_of(2, 0),
             stack_of(2, 0),
             pl.BlockSpec((size, LANES), lambda i, s: (begin + i, 0)),
         ]
@@ -555,7 +586,9 @@
     part = STRIP_ROWS * LANES
     spot = pl.ds(pl.multiple_of(2 * part + side * part, part), part)
     change_ref[...] = stacked(span_ref[0:8, spot])
-    state_ref[...] = span_ref[8:16, spot]
+    state = span_ref[8:16, spot]
+    for row in range(STRIP_ROWS):
+        state_ref[:, row, :] = state[:5, row * LANES : (row + 1) * LANES]
 
 
 def macro(kernel, info, args, outs, scratch):
@@ -571,41 +604,62 @@
     )(info, *args)
 
 
-def finish_kernel(size, own, side_ref, rows_ref, table_ref, change_ref, *rest):
-    out_ref = rest[-1]
-    flipped = side_ref[0] == (1 if own else 0)
+def finish_kernel(size, parts, side_ref, *refs):
+    out_ref = refs[-1]
+    rows = refs[: len(parts)]
+    table_ref, change_ref = refs[len(parts) : len(parts) + 2]
+    side = side_ref[0]
+    step = pl.program_id(0)
     lift = jnp.dot(table_ref[...], change_ref[...], preferred_element_type=F32)
-    for row in range(STRIP_ROWS):
-        index = jnp.where(flipped, 3 - row, row)
-        out_ref[strided(row, size), :] = (
-            rows_ref[index] + lift[:, row * LANES : (row + 1) * LANES]
+    for ref, (own, begin, count, _) in zip(rows, parts):
+
+        @pl.when((step >= begin) & (step < begin + count))
+        def _(ref=ref, flipped=(side == (1 if own else 0))):
+            for row in range(STRIP_ROWS):
+                index = jnp.where(flipped, 3 - row, row)
+                out_ref[strided(row, size), :] = (
+                    ref[index] + lift[:, row * LANES : (row + 1) * LANES]
+                )
+
+
+def finish(side, out, pieces, table, change, half, size):
+    shift = half // size
+    parts = []
+    steps = 0
+    for rows, own, first in pieces:
+        count = rows.shape[1] // size
+        parts.append((own, steps, count, first // size))
+        steps += count
+
+    def place(i, s):
+        spot = 0
+        for own, begin, count, at in parts:
+            here = (s[0] if own else 1 - s[0]) * shift + at + i - begin
+            spot = jnp.where(i >= begin, here, spot)
+        return spot
+
+    def rows_spec(begin, count):
+        return pl.BlockSpec(
+            (4, size, LANES), lambda i, s: (0, jnp.clip(i - begin, 0, count - 1), 0)
         )
 
-
-def finish(side, out, rows, own, table, change, half, chunk, first, size):
-    shift = half // size
-    begin = first // size
-
-    def place(i, s):
-        return (s[0] if own else 1 - s[0]) * shift + begin + i
-
     specs = [
-        pl.BlockSpec((4, size, LANES), lambda i, s: (0, i, 0)),
+        *[rows_spec(begin, count) for _, begin, count, _ in parts],
         pl.BlockSpec((size, 48), lambda i, s: (place(i, s), 0)),
         pl.BlockSpec(change.shape, lambda i, s: (0, 0)),
     ]
-    args = [side, rows, table, change]
+    args = [side, *[rows for rows, _, _ in pieces], table, change]
     aliases = {}
     if out is not None:
         specs.append(pl.BlockSpec(memory_space=pl.ANY))
+        aliases = {len(args): 0}
         args.append(out)
-        aliases = {4: 0}
     return pl.pallas_call(
-        functools.partial(finish_kernel, size, own),
+        functools.partial(finish_kernel, size, parts),
         out_shape=jax.ShapeDtypeStruct((2 * half * STRIP_ROWS, LANES), F32),
         grid_spec=pltpu.PrefetchScalarGridSpec(
             num_scalar_prefetch=1,
-            grid=(chunk // size,),
+            grid=(steps,),
             in_specs=specs,
             out_specs=pl.BlockSpec((4 * size, LANES), lambda i, s: (place(i, s), 0)),
         ),
@@ -613,7 +667,9 @@
         compiler_params=params(),
         name="finish",
         cost_estimate=pl.CostEstimate(
-            flops=2 * 48 * 4 * LANES * chunk, transcendentals=0, bytes_accessed=chunk * LANES * 4 * 8
+            flops=2 * 48 * 4 * LANES * steps * size,
+            transcendentals=0,
+            bytes_accessed=steps * size * LANES * 4 * 8,
         ),
     )(*args)
 
@@ -675,14 +731,17 @@
     cell_pair = jnp.concatenate([collision_rate, wall])
     other_cells = swap(cell_pair)
 
-    got = []
-    for c in order:
-        far_start = ((1 - strip % 2) * half + firsts[c]) * rows
-        part = lax.dynamic_slice_in_dim(flat, far_start, chunks[c] * rows, axis=0)
-        got.append(swap(part))
+    packed = pack(side, flat, half, chunks[:1], 0, size)
+    packed += pack(side, flat, half, chunks[1:], firsts[1], size)
+    got, above = [], []
+    for edge, mid in packed:
+        edge = swap(edge)
+        mid = swap(mid)
+        above.append(with_flow(edge))
+        got.append((mid, edge))
     tables = prepare(points, vel_index)
     table, _, weights = tables
-    home, lowest = home_moments(side, flat, weights, size)
+    home, lowest = home_moments(side, flat, weights, half // 3)
     below = against_flow(lowest)
     gram = jnp.asarray(target_moments(points))
     mat = jnp.asarray(macro_matrix())
@@ -706,10 +765,6 @@
 
     width = BLOCK_ROWS * LANES
     sums = jnp.zeros((16, width), F32)
-    above = []
-    for c in order:
-        edges = pick(side, got[c], lambda s: 0, chunks[c], size, [(2, 1), (3, 0)])
-        above.append(with_flow(edges))
     kept = []
     for number, members in enumerate(groups_of):
         start = firsts[members[0]]
@@ -717,7 +772,7 @@
         held = None
         for c in members:
             *held, sums = transport(
-                side, [flat, got[c], above[c], below], tables, cells, sums, half,
+                side, [flat, *got[c], above[c], below], tables, cells, sums, half,
                 chunks[c], firsts[c], size, skip=firsts[c] - start, group=length, into=held,
             )
         next_above = with_flow(held[2])
@@ -756,14 +811,15 @@
         [total, sum_a, sum_b, keep, gram, mat],
         [
             jax.ShapeDtypeStruct((48, STRIP_ROWS * LANES), BF16),
-            jax.ShapeDtypeStruct((8, STRIP_ROWS * LANES), F32),
+            jax.ShapeDtypeStruct((5, STRIP_ROWS, LANES), F32),
         ],
         [pltpu.VMEM((16, SPAN * LANES), F32)],
     )
-    out = finish(side, None, near, True, table, change, half, half, 0, size)
-    for c in later:
-        out = finish(side, out, back[c], False, table, change, half, chunks[c], firsts[c], size)
-    return out.reshape(dist.shape), state[:5].reshape(5, rows, cols)
+    pieces = [(near, True, 0), *[(back[c], False, firsts[c]) for c in later[:cut]]]
+    out = finish(side, None, pieces, table, change, half, size)
+    for c in later[cut:]:
+        out = finish(side, out, [(back[c], False, firsts[c])], table, change, half, size)
+    return out.reshape(dist.shape), state
 
 
 def solution(mesh):

time: 288 us -> 283 us (0.983)
  the two profiles are of different devices: /device:TPU:0 before, /device:TPU:24 now
where the time goes in v6:
time: 283 us; the launch traced here: 279 us
  waiting for transfers between devices  112 us (40%)
  Pallas kernels  102 us (36%)
  starting transfers between devices  55 us (19%)
  local copies, waits for them, and re-layouts  5.57 us (2%)
  other arithmetic  3.1 us (1%)
    ppermute x19, waiting for transfers between devices, swap(): return lax.ppermute(value, 'strip', swap_pairs)  75 us
    pallas_call x10, Pallas kernels, transport(): pl.pallas_call(functools.partial(transport_kernel, size, second_pass), ou...  66 us
    ppermute x7, waiting for transfers between devices, with_flow(): return lax.ppermute(value, 'strip', down_pairs)  22.1 us
    ppermute x19, starting transfers between devices, swap(): return lax.ppermute(value, 'strip', swap_pairs)  19.7 us
    pallas_call x3, Pallas kernels, finish(): pl.pallas_call(functools.partial(finish_kernel, size, parts), out_shape=j...  13.9 us
    ppermute x3, waiting for transfers between devices, both_z(): lax.ppermute(value, 'strip', pair_a)  13 us
    ppermute x3, starting transfers between devices, against_flow(): return lax.ppermute(value, 'strip', up_pairs)  10.7 us
    ppermute x7, starting transfers between devices, with_flow(): return lax.ppermute(value, 'strip', down_pairs)  9.02 us
  transfers between devices with their start and end apart: 44, of which 17 were waited for; matrix products, arithmetic and copies ran while one was open for 1% of the time, Pallas kernels for 35%

profile of v6, /device:TPU:24, one launch (start us, length us, event | category | flops | bytes accessed | tf_op | source)
XLA Modules:
  0.0 278.9 jit_solution(5035210423532421920)
XLA Ops:
  0.6 2.2 pack.3
  2.8 1.5 collective-permute-start.15
  4.4 4.0 %pack.2 = (f32[2,288,128]{2,1,0:T(8,128)}, f32[2,288,128]{2,1,0:T(8,128)}, f32[2,288,128]{2,1,0:T(8,128)}, f32[2,288,128]{2,1,0:T(8,128)}, f32[2,288,128]{2,1,0:...) custom-call(s32[1]{0:T(128)} %bitcast.side_ref, f32[13824,128]{1,0:T(8,128)} %bitcast.12), custom_call_target="tpu_custom_call" | custom-call | bytes 4718592 | tf_op jit(solution)/shard_map/pack/pallas_call | solution.py:149
  8.9 1.5 collective-permute-start.11
  10.9 1.6 collective-permute-start.4
  12.5 24.8 %collective-permute-done.4 = f32[8,128]{1,0:T(8,128)S(1)} collective-permute-done((f32[8,128]{1,0:T(8,128)S(1)}, f32[8,128]{1,0:T(8,128)S(1)}, u32[]{:S(2)}, u32[]{:S(2)}) %collective-permute-start.4) | collective-permute-done | bytes 4128 | tf_op jit(solution)/shard_map/ppermute | solution.py:710
  37.3 1.5 collective-permute-start.14
  38.8 3.9 %prepare.1 = (bf16[3456,48]{1,0:T(8,128)(2,1)}, f32[3456,8]{1,0:T(8,128)}, bf16[3456,32]{1,0:T(8,128)(2,1)}) custom-call(s32[3,3456]{1,0:T(4,128)} %vel_ref.1), custom_call_target="tpu_custom_call" | custom-call | flops 691200 | bytes 3456000 | tf_op jit(solution)/shard_map/prepare/pallas_call | solution.py:205
  42.7 6.2 %home_moments.1 = (f32[16,512]{1,0:T(8,128)}, f32[1728,128]{1,0:T(8,128)}) custom-call(s32[1]{0:T(128)} %bitcast.side_ref, f32[13824,128]{1,0:T(8,128)} %bitcast.13, bf16[3456,32]{1,0:T(8,128)(2,1)} %get-tuple-element.59.weight_ref.refs_6_.refs_8_), custom_call_target="tpu_custom_call" | custom-call | flops 226492416 | bytes 7077888 | tf_op jit(solution)/shard_map/home_moments/pallas_call | solution.py:263
  48.9 2.4 collective-permute-start.3
  51.4 1.3 collective-permute-start.13
  52.8 1.3 collective-permute-start.16
  54.2 4.8 %collective-permute-done.8.refs_1_ = f32[2,288,128]{2,1,0:T(8,128)S(1)} collective-permute-done((f32[2,288,128]{2,1,0:T(8,128)}, f32[2,288,128]{2,1,0:T(8,128)S(1)}, u32[]{:S(2)}, u32[]{:S(2)}) %collective-permute-start.8) | collective-permute-done | bytes 294944 | tf_op jit(solution)/shard_map/ppermute | solution.py:710
  59.6 1.5 collective-permute-start.1
  61.0 2.4 collective-permute-done.13.refs_3_
  63.4 1.3 collective-permute-start.10
  64.7 15.1 %collective-permute-done.10.refs_3_ = f32[2,288,128]{2,1,0:T(8,128)S(1)} collective-permute-done((f32[2,288,128]{2,1,0:T(8,128)}, f32[2,288,128]{2,1,0:T(8,128)S(1)}, u32[]{:S(2)}, u32[]{:S(2)}) %collective-permute-start.10) | collective-permute-done | bytes 294944 | tf_op jit(solution)/shard_map/ppermute | solution.py:713
  79.9 1.6 collective-permute-start.24
  82.3 1.4 collective-permute-start.25
  85.0 8.9 %transport_first.5 = (f32[1,1152,128]{2,1,0:T(8,128)}, f32[5,1152,128]{2,1,0:T(8,128)}, f32[2,1152,128]{2,1,0:T(8,128)}, f32[16,1024]{1,0:T(8,128)}) custom-call(s32[1]{0:T(128)} %bitcast.side_ref, f32[13824,128]{1,0:T(8,128)} %bitcast.14, f32[2,576,128]{2,1,0:T(8,128)} %collective-permute-done.14.refs_1_, f32[2,576,128]{2,1,0:T(8,128)} %copy-done.4, ...), custom_call_target="tpu_custom_call" | custom-call | flops 35389440 | bytes 5603328 | tf_op jit(solution)/shard_map/transport_first/pallas_call | solution.py:452
  93.8 5.6 %transport_first.6 = (f32[1,1152,128]{2,1,0:T(8,128)}, f32[5,1152,128]{2,1,0:T(8,128)}, f32[2,1152,128]{2,1,0:T(8,128)}, f32[16,1024]{1,0:T(8,128)}) custom-call(s32[1]{0:T(128)} %bitcast.side_ref, f32[13824,128]{1,0:T(8,128)} %bitcast.15, f32[2,288,128]{2,1,0:T(8,128)} %copy-done.10, ...), custom_call_target="tpu_custom_call", output_to_operand_aliasing={{0}: (10, {}), {1}: (11, {}), {2}: (12, {})} | custom-call | flops 17694720 | bytes 2801664 | tf_op jit(solution)/shard_map/transport_first/pallas_call | solution.py:452
  99.4 5.6 %transport_first.7 = (f32[1,1152,128]{2,1,0:T(8,128)}, f32[5,1152,128]{2,1,0:T(8,128)}, f32[2,1152,128]{2,1,0:T(8,128)}, f32[16,1024]{1,0:T(8,128)}) custom-call(s32[1]{0:T(128)} %bitcast.side_ref, f32[13824,128]{1,0:T(8,128)} %bitcast.16, f32[2,288,128]{2,1,0:T(8,128)} %copy-done.11, ...), custom_call_target="tpu_custom_call", output_to_operand_aliasing={{0}: (10, {}), {1}: (11, {}), {2}: (12, {})} | custom-call | flops 17694720 | bytes 2801664 | tf_op jit(solution)/shard_map/transport_first/pallas_call | solution.py:452
  105.1 2.0 collective-permute-start
  107.1 1.3 collective-permute-start.7
  108.4 1.3 collective-permute-start.2
  109.7 1.3 collective-permute-start.31
  111.1 4.1 %collective-permute-done.5.refs_1_ = f32[2,288,128]{2,1,0:T(8,128)} collective-permute-done((f32[2,288,128]{2,1,0:T(8,128)}, f32[2,288,128]{2,1,0:T(8,128)}, u32[]{:S(2)}, u32[]{:S(2)}) %collective-permute-start.5) | collective-permute-done | bytes 294944 | tf_op jit(solution)/shard_map/ppermute | solution.py:710
  115.3 3.9 %collective-permute-done.7.refs_3_ = f32[2,288,128]{2,1,0:T(8,128)} collective-permute-done((f32[2,288,128]{2,1,0:T(8,128)}, f32[2,288,128]{2,1,0:T(8,128)}, u32[]{:S(2)}, u32[]{:S(2)}) %collective-permute-start.7) | collective-permute-done | bytes 294944 | tf_op jit(solution)/shard_map/ppermute | solution.py:713
  119.2 5.6 %transport_first.8 = (f32[1,576,128]{2,1,0:T(8,128)}, f32[5,576,128]{2,1,0:T(8,128)}, f32[2,576,128]{2,1,0:T(8,128)}, f32[16,1024]{1,0:T(8,128)}) custom-call(s32[1]{0:T(128)} %bitcast.side_ref, f32[13824,128]{1,0:T(8,128)} %bitcast.17, f32[2,288,128]{2,1,0:T(8,128)} %collective-permute-done.5.refs_1_, f32[2,288,128]{2,1,0:T(8,128)} %collective-permute-done.6.refs_2_, ...), custom_call_target="tpu_custom_call" | custom-call | flops 17694720 | bytes 2801664 | tf_op jit(solution)/shard_map/transport_first/pallas_call | solution.py:452
  125.5 5.7 %transport_first.9 = (f32[1,576,128]{2,1,0:T(8,128)}, f32[5,576,128]{2,1,0:T(8,128)}, f32[2,576,128]{2,1,0:T(8,128)}, f32[16,1024]{1,0:T(8,128)}) custom-call(s32[1]{0:T(128)} %bitcast.side_ref, f32[13824,128]{1,0:T(8,128)} %bitcast.18, f32[2,288,128]{2,1,0:T(8,128)} %copy-done.9, ...), custom_call_target="tpu_custom_call", output_to_operand_aliasing={{0}: (10, {}), {1}: (11, {}), {2}: (12, {})} | custom-call | flops 17694720 | bytes 2801664 | tf_op jit(solution)/shard_map/transport_first/pallas_call | solution.py:452
  131.9 1.4 collective-permute-start.19
  133.3 4.4 %collective-permute-start.32 = (f32[1,1152,128]{2,1,0:T(8,128)S(1)}, f32[1,1152,128]{2,1,0:T(8,128)}, u32[]{:S(2)}, u32[]{:S(2)}) collective-permute-start(f32[1,1152,128]{2,1,0:T(8,128)S(1)} %copy-done.1), channel_id=1, source_target_pairs={{2,0},{4,2},{1,3},{6,4},{3,5},{5,7},{10,8},{12,10},{9,11},{14,12},... | collective-permute-start | bytes 1769480 | tf_op jit(solution)/shard_map/ppermute | solution.py:716
  138.5 1.3 collective-permute-start.29
  140.6 10.7 %collective-permute-done.26 = f32[16,512]{1,0:T(8,128)S(1)} collective-permute-done((f32[16,512]{1,0:T(8,128)S(1)}, f32[16,512]{1,0:T(8,128)S(1)}, u32[]{:S(2)}, u32[]{:S(2)}) %collective-permute-start.26) | collective-permute-done | bytes 32800 | tf_op jit(solution)/shard_map/ppermute | solution.py:719
  151.4 2.1 collective-permute-start.28
  153.5 2.1 collective-permute-done.20
  155.7 1.2 collective-permute-start.21
  156.9 3.9 %collective-permute-start.30 = (f32[1,576,128]{2,1,0:T(8,128)}, f32[1,576,128]{2,1,0:T(8,128)}, u32[]{:S(2)}, u32[]{:S(2)}) collective-permute-start(f32[1,576,128]{2,1,0:T(8,128)} %get-tuple-element.86.refs_2_), channel_id=1, source_target_pairs={{2,0},{4,2},{1,3},{6,4},{3,5},{5,7},{10,8},{12,10},{9,11},{14,12},... | collective-permute-start | bytes 884744 | tf_op jit(solution)/shard_map/ppermute | solution.py:716
  160.8 2.2 collective-permute-done.21.sum_a_ref
  163.6 1.3 collective-permute-start.22
  165.5 3.2 %shard_map.77 = (bf16[48,1408]{1,0:T(8,128)(2,1)}, f32[16,3072]{1,0:T(8,128)}) custom-call(s32[2]{0:T(128)} %pad_add_fusion.info_ref, f32[16,1024]{1,0:T(8,128)} %copy-done.14, f32[16,1024]{1,0:T(8,128)} %copy-done.17, f32[16,1024]{1,0:T(8,128)} %collective-permute-done.22.sum_b_ref, f32[3,16,512]{2,1,0:T(8,128)} %copy-done.7, f32[3,16,512]{2,1,0:T(8,128)} %copy-done.16, ...), custom_call_target="tpu_custom_call" | custom-call | flops 4000000 | bytes 1000000 | tf_op jit(solution)/shard_map/pallas_call | solution.py:596
  168.7 1.0 copy-done.2
  169.7 6.2 %transport_second.5 = (f32[4,1728,128]{2,1,0:T(8,128)}, f32[4,288,128]{2,1,0:T(8,128)}, f32[16,1024]{1,0:T(8,128)}) custom-call(s32[1]{0:T(128)} %bitcast.side_ref, bf16[3456,48]{1,0:T(8,128)(2,1)} %get-tuple-element.56.refs_0_.refs_4_.refs_1_, bf16[48,1408]{1,0:T(8,128)(2,1)} %get-tuple-element.85.refs_1_, f32[1,1152,128]{2,1,0:T(8,128)} %get-tuple-element.89.refs_2_, ...), custom_call_target="tpu_custom_call" | custom-call | flops 17694720 | bytes 2801664 | tf_op jit(solution)/shard_map/transport_second/pallas_call | solution.py:452
  175.8 6.2 %transport_second.6 = (f32[4,1728,128]{2,1,0:T(8,128)}, f32[4,288,128]{2,1,0:T(8,128)}, f32[16,1024]{1,0:T(8,128)}) custom-call(s32[1]{0:T(128)} %bitcast.side_ref, bf16[3456,48]{1,0:T(8,128)(2,1)} %get-tuple-element.56.refs_0_.refs_4_.refs_1_, bf16[48,1408]{1,0:T(8,128)(2,1)} %get-tuple-element.85.refs_1_, ...), custom_call_target="tpu_custom_call", output_to_operand_aliasing={{0}: (12, {})} | custom-call | flops 17694720 | bytes 2801664 | tf_op jit(solution)/shard_map/transport_second/pallas_call | solution.py:452
  182.0 9.9 %transport_second.7 = (f32[4,1728,128]{2,1,0:T(8,128)}, f32[4,576,128]{2,1,0:T(8,128)}, f32[16,1024]{1,0:T(8,128)}) custom-call(s32[1]{0:T(128)} %bitcast.side_ref, bf16[3456,48]{1,0:T(8,128)(2,1)} %get-tuple-element.56.refs_0_.refs_4_.refs_1_, bf16[48,1408]{1,0:T(8,128)(2,1)} %get-tuple-element.85.refs_1_, ...), custom_call_target="tpu_custom_call", output_to_operand_aliasing={{0}: (12, {})} | custom-call | flops 35389440 | bytes 5603328 | tf_op jit(solution)/shard_map/transport_second/pallas_call | solution.py:452
  192.1 6.2 %transport_second.8 = (f32[4,1728,128]{2,1,0:T(8,128)}, f32[4,288,128]{2,1,0:T(8,128)}, f32[16,1024]{1,0:T(8,128)}) custom-call(s32[1]{0:T(128)} %bitcast.side_ref, bf16[3456,48]{1,0:T(8,128)(2,1)} %get-tuple-element.56.refs_0_.refs_4_.refs_1_, bf16[48,1408]{1,0:T(8,128)(2,1)} %get-tuple-element.85.refs_1_, ...), custom_call_target="tpu_custom_call", output_to_operand_aliasing={{0}: (12, {})} | custom-call | flops 17694720 | bytes 2801664 | tf_op jit(solution)/shard_map/transport_second/pallas_call | solution.py:452
  198.2 6.2 %transport_second.9 = (f32[4,1728,128]{2,1,0:T(8,128)}, f32[4,288,128]{2,1,0:T(8,128)}, f32[16,1024]{1,0:T(8,128)}) custom-call(s32[1]{0:T(128)} %bitcast.side_ref, bf16[3456,48]{1,0:T(8,128)(2,1)} %get-tuple-element.56.refs_0_.refs_4_.refs_1_, bf16[48,1408]{1,0:T(8,128)(2,1)} %get-tuple-element.85.refs_1_, ...), custom_call_target="tpu_custom_call", output_to_operand_aliasing={{0}: (12, {})} | custom-call | flops 17694720 | bytes 2801664 | tf_op jit(solution)/shard_map/transport_second/pallas_call | solution.py:452
  204.4 1.3 collective-permute-start.35
  205.7 1.5 collective-permute-start.36
  207.2 1.3 collective-permute-done.34
  210.3 2.1 collective-permute-start.37
  212.3 7.0 %collective-permute-done.37 = f32[16,1024]{1,0:T(8,128)S(1)} collective-permute-done((f32[16,1024]{1,0:T(8,128)S(1)}, f32[16,1024]{1,0:T(8,128)S(1)}, u32[]{:S(2)}, u32[]{:S(2)}) %collective-permute-start.37) | collective-permute-done | bytes 65568 | tf_op jit(solution)/shard_map/ppermute | solution.py:710
  219.4 4.0 %collective-permute-start.38 = (f32[16,1024]{1,0:T(8,128)S(1)}, f32[16,1024]{1,0:T(8,128)S(1)}, u32[]{:S(2)}, u32[]{:S(2)}) collective-permute-start(f32[16,1024]{1,0:T(8,128)S(1)} %add.56.sum_ref), channel_id=1, source_target_pairs={{0,2},{1,3},{2,0},{3,1},{4,6},{5,7},{6,4},{7,5},{8,10},{9,11},{10,... | collective-permute-start | bytes 196616 | tf_op jit(solution)/shard_map/ppermute | solution.py:719
  224.0 1.8 collective-permute-start.42
  226.1 1.7 collective-permute-start.40
  228.4 2.6 shard_map.78
  231.0 9.6 %collective-permute-done.42.refs_2_ = f32[4,288,128]{2,1,0:T(8,128)} collective-permute-done((f32[4,288,128]{2,1,0:T(8,128)}, f32[4,288,128]{2,1,0:T(8,128)}, u32[]{:S(2)}, u32[]{:S(2)}) %collective-permute-start.42) | collective-permute-done | bytes 589856 | tf_op jit(solution)/shard_map/ppermute | solution.py:710
  240.6 12.6 %collective-permute-done.41.refs_1_ = f32[4,288,128]{2,1,0:T(8,128)} collective-permute-done((f32[4,288,128]{2,1,0:T(8,128)}, f32[4,288,128]{2,1,0:T(8,128)}, u32[]{:S(2)}, u32[]{:S(2)}) %collective-permute-start.41) | collective-permute-done | bytes 589856 | tf_op jit(solution)/shard_map/ppermute | solution.py:710
  253.2 1.1 copy-done.3
  254.3 9.6 %finish.3.refs_3_ = f32[13824,128]{1,0:T(8,128)} custom-call(s32[1]{0:T(128)} %bitcast.side_ref, f32[4,1728,128]{2,1,0:T(8,128)} %get-tuple-element.105.refs_0_, f32[4,288,128]{2,1,0:T(8,128)} %collective-permute-done.41.refs_1_, f32[4,288,128]{2,1,0:T(8,128)} %collective-permute-done.42.refs_2_, f32[4,576,128]{2,1,0:T(8,128)} %copy-done.3, ...), custom_call_target="tpu_custom_call" | custom-call | flops 141557760 | bytes 11796480 | tf_op jit(solution)/shard_map/finish/pallas_call | solution.py:657
  263.9 2.0 collective-permute-done.40.refs_0_
  265.9 2.1 finish.4.refs_3_
  268.0 7.9 %collective-permute-done.33.refs_0_ = f32[4,288,128]{2,1,0:T(8,128)S(1)} collective-permute-done((f32[4,288,128]{2,1,0:T(8,128)}, f32[4,288,128]{2,1,0:T(8,128)S(1)}, u32[]{:S(2)}, u32[]{:S(2)}) %collective-permute-start.33) | collective-permute-done | bytes 589856 | tf_op jit(solution)/shard_map/ppermute | solution.py:710
  276.8 2.1 finish.5
  (112 shorter events, 12.8 us)
Async XLA Ops:
  2.8 8.0 %copy-start.22 = (s32[4,128]{1,0:T(4,128)S(1)}, s32[4,128]{1,0:T(4,128)}, u32[]{:S(2)}) copy-start(s32[4,128]{1,0:T(4,128)} %param.7) | copy-start | bytes 6148
  2.8 8.0 %copy-start.20 = (f32[4,128]{1,0:T(4,128)S(1)}, f32[4,128]{1,0:T(4,128)}, u32[]{:S(2)}) copy-start(f32[4,128]{1,0:T(4,128)} %param.8) | copy-start | bytes 6148
  2.8 49.9 %collective-permute-start.15 = (f32[2,576,128]{2,1,0:T(8,128)}, f32[2,576,128]{2,1,0:T(8,128)S(1)}, u32[]{:S(2)}, u32[]{:S(2)}) collective-permute-start(f32[2,576,128]{2,1,0:T(8,128)} %get-tuple-element.69), channel_id=1, source_target_pairs={{0,1},{1,0},{2,3},{3,2},{4,5},{5,4},{6,7},{7,6},{8,9},{9,8},{10,11... | collective-permute-start | bytes 1769480 | tf_op jit(solution)/shard_map/ppermute | solution.py:710
  8.3 40.5 %collective-permute-start.12 = (f32[2,288,128]{2,1,0:T(8,128)}, f32[2,288,128]{2,1,0:T(8,128)}, u32[]{:S(2)}, u32[]{:S(2)}) collective-permute-start(f32[2,288,128]{2,1,0:T(8,128)} %get-tuple-element.67), channel_id=1, source_target_pairs={{0,1},{1,0},{2,3},{3,2},{4,5},{5,4},{6,7},{7,6},{8,9},{9,8},{10,11... | collective-permute-start | bytes 884744 | tf_op jit(solution)/shard_map/ppermute | solution.py:710
  8.9 42.5 %collective-permute-start.11 = (f32[2,288,128]{2,1,0:T(8,128)}, f32[2,288,128]{2,1,0:T(8,128)S(1)}, u32[]{:S(2)}, u32[]{:S(2)}) collective-permute-start(f32[2,288,128]{2,1,0:T(8,128)} %get-tuple-element.66), channel_id=1, source_target_pairs={{0,1},{1,0},{2,3},{3,2},{4,5},{5,4},{6,7},{7,6},{8,9},{9,8},{10,11... | collective-permute-start | bytes 884744 | tf_op jit(solution)/shard_map/ppermute | solution.py:710
  10.4 41.1 %collective-permute-start.9 = (f32[2,288,128]{2,1,0:T(8,128)}, f32[2,288,128]{2,1,0:T(8,128)}, u32[]{:S(2)}, u32[]{:S(2)}) collective-permute-start(f32[2,288,128]{2,1,0:T(8,128)} %get-tuple-element.65), channel_id=1, source_target_pairs={{0,1},{1,0},{2,3},{3,2},{4,5},{5,4},{6,7},{7,6},{8,9},{9,8},{10,11... | collective-permute-start | bytes 884744 | tf_op jit(solution)/shard_map/ppermute | solution.py:710
  10.9 26.4 %collective-permute-start.4 = (f32[8,128]{1,0:T(8,128)S(1)}, f32[8,128]{1,0:T(8,128)S(1)}, u32[]{:S(2)}, u32[]{:S(2)}) collective-permute-start(f32[8,128]{1,0:T(8,128)S(1)} %pad_maximum_fusion.2), channel_id=1, source_target_pairs={{0,1},{1,0},{2,3},{3,2},{4,5},{5,4},{6,7},{7,6},{8,9},{9,8},{10,11... | collective-permute-start | bytes 12296 | tf_op jit(solution)/shard_map/ppermute | solution.py:710
  37.3 22.3 %collective-permute-start.14 = (f32[2,576,128]{2,1,0:T(8,128)}, f32[2,576,128]{2,1,0:T(8,128)}, u32[]{:S(2)}, u32[]{:S(2)}) collective-permute-start(f32[2,576,128]{2,1,0:T(8,128)} %get-tuple-element.68), channel_id=1, source_target_pairs={{0,1},{1,0},{2,3},{3,2},{4,5},{5,4},{6,7},{7,6},{8,9},{9,8},{10,11... | collective-permute-start | bytes 1769480 | tf_op jit(solution)/shard_map/ppermute | solution.py:710
  48.9 31.0 %collective-permute-start.3 = (f32[1728,128]{1,0:T(8,128)}, f32[1728,128]{1,0:T(8,128)S(1)}, u32[]{:S(2)}, u32[]{:S(2)}) collective-permute-start(f32[1728,128]{1,0:T(8,128)} %get-tuple-element.60), channel_id=1, source_target_pairs={{2,0},{4,2},{1,3},{6,4},{3,5},{5,7},{10,8},{12,10},{9,11},{14,12},... | collective-permute-start | bytes 2654216 | tf_op jit(solution)/shard_map/ppermute | solution.py:716
  51.4 8.2 %copy-start.10 = (f32[2,288,128]{2,1,0:T(8,128)}, f32[2,288,128]{2,1,0:T(8,128)S(1)}, u32[]{:S(2)}) copy-start(f32[2,288,128]{2,1,0:T(8,128)S(1)} %collective-permute-done.11.refs_1_) | copy-start | bytes 884740
  51.4 7.7 %collective-permute-start.8 = (f32[2,288,128]{2,1,0:T(8,128)}, f32[2,288,128]{2,1,0:T(8,128)S(1)}, u32[]{:S(2)}, u32[]{:S(2)}) collective-permute-start(f32[2,288,128]{2,1,0:T(8,128)} %get-tuple-element.64), channel_id=1, source_target_pairs={{0,1},{1,0},{2,3},{3,2},{4,5},{5,4},{6,7},{7,6},{8,9},{9,8},{10,11... | collective-permute-start | bytes 884744 | tf_op jit(solution)/shard_map/ppermute | solution.py:710
  51.4 12.0 %collective-permute-start.13 = (f32[2,288,128]{2,1,0:T(8,128)}, f32[2,288,128]{2,1,0:T(8,128)S(1)}, u32[]{:S(2)}, u32[]{:S(2)}) collective-permute-start(f32[2,288,128]{2,1,0:T(8,128)} %collective-permute-done.12.refs_2_), channel_id=1, source_target_pairs={{0,2},{2,4},{3,1},{4,6},{5,3},{7,5},{8,10},{10,12},{11,9},{12,14},... | collective-permute-start | bytes 884744 | tf_op jit(solution)/shard_map/ppermute | solution.py:713
  52.8 32.2 %copy-start.4 = (f32[2,576,128]{2,1,0:T(8,128)}, f32[2,576,128]{2,1,0:T(8,128)S(1)}, u32[]{:S(2)}) copy-start(f32[2,576,128]{2,1,0:T(8,128)S(1)} %collective-permute-done.15.refs_2_) | copy-start | bytes 1769476
  52.8 28.7 %collective-permute-start.16 = (f32[2,576,128]{2,1,0:T(8,128)S(1)}, f32[2,576,128]{2,1,0:T(8,128)S(1)}, u32[]{:S(2)}, u32[]{:S(2)}) collective-permute-start(f32[2,576,128]{2,1,0:T(8,128)S(1)} %collective-permute-done.15.refs_2_), channel_id=1, source_target_pairs={{0,2},{2,4},{3,1},{4,6},{5,3},{7,5},{8,10},{10,12},{11,9},{12,14},... | collective-permute-start | bytes 1769480 | tf_op jit(solution)/shard_map/ppermute | solution.py:713
  59.0 24.7 %copy-start.11 = (f32[2,288,128]{2,1,0:T(8,128)}, f32[2,288,128]{2,1,0:T(8,128)S(1)}, u32[]{:S(2)}) copy-start(f32[2,288,128]{2,1,0:T(8,128)S(1)} %collective-permute-done.8.refs_1_) | copy-start | bytes 884740
  59.0 48.1 %collective-permute-start.6 = (f32[2,288,128]{2,1,0:T(8,128)}, f32[2,288,128]{2,1,0:T(8,128)}, u32[]{:S(2)}, u32[]{:S(2)}) collective-permute-start(f32[2,288,128]{2,1,0:T(8,128)} %get-tuple-element.63), channel_id=1, source_target_pairs={{0,1},{1,0},{2,3},{3,2},{4,5},{5,4},{6,7},{7,6},{8,9},{9,8},{10,11... | collective-permute-start | bytes 884744 | tf_op jit(solution)/shard_map/ppermute | solution.py:710
  59.6 48.8 %collective-permute-start.1 = (f32[2,288,128]{2,1,0:T(8,128)}, f32[2,288,128]{2,1,0:T(8,128)S(1)}, u32[]{:S(2)}, u32[]{:S(2)}) collective-permute-start(f32[2,288,128]{2,1,0:T(8,128)} %get-tuple-element.58), channel_id=1, source_target_pairs={{0,1},{1,0},{2,3},{3,2},{4,5},{5,4},{6,7},{7,6},{8,9},{9,8},{10,11... | collective-permute-start | bytes 884744 | tf_op jit(solution)/shard_map/ppermute | solution.py:710
  63.4 20.3 %copy-start.12 = (f32[2,288,128]{2,1,0:T(8,128)}, f32[2,288,128]{2,1,0:T(8,128)S(1)}, u32[]{:S(2)}) copy-start(f32[2,288,128]{2,1,0:T(8,128)S(1)} %collective-permute-done.13.refs_3_) | copy-start | bytes 884740
  63.4 16.5 %collective-permute-start.10 = (f32[2,288,128]{2,1,0:T(8,128)}, f32[2,288,128]{2,1,0:T(8,128)S(1)}, u32[]{:S(2)}, u32[]{:S(2)}) collective-permute-start(f32[2,288,128]{2,1,0:T(8,128)} %collective-permute-done.9.refs_2_), channel_id=1, source_target_pairs={{0,2},{2,4},{3,1},{4,6},{5,3},{7,5},{8,10},{10,12},{11,9},{12,14},... | collective-permute-start | bytes 884744 | tf_op jit(solution)/shard_map/ppermute | solution.py:713
  79.9 3.8 %copy-start.13 = (f32[2,288,128]{2,1,0:T(8,128)}, f32[2,288,128]{2,1,0:T(8,128)S(1)}, u32[]{:S(2)}) copy-start(f32[2,288,128]{2,1,0:T(8,128)S(1)} %collective-permute-done.10.refs_3_) | copy-start | bytes 884740
  79.9 25.1 %collective-permute-start.23 = (f32[16,512]{1,0:T(8,128)}, f32[16,512]{1,0:T(8,128)S(1)}, u32[]{:S(2)}, u32[]{:S(2)}) collective-permute-start(f32[16,512]{1,0:T(8,128)} %get-tuple-element.84), channel_id=1, source_target_pairs={{0,8},{8,16},{16,24},{24,0},{1,9},{9,17},{17,25},{25,1},{2,10},{10... | collective-permute-start | bytes 98312 | tf_op jit(solution)/shard_map/ppermute | solution.py:724
  79.9 5.1 %copy-start = (f32[1728,128]{1,0:T(8,128)}, f32[1728,128]{1,0:T(8,128)S(1)}, u32[]{:S(2)}) copy-start(f32[1728,128]{1,0:T(8,128)S(1)} %collective-permute-done.3.refs_4_) | copy-start | bytes 2654212
  79.9 25.2 %collective-permute-start.24 = (f32[16,512]{1,0:T(8,128)}, f32[16,512]{1,0:T(8,128)S(1)}, u32[]{:S(2)}, u32[]{:S(2)}) collective-permute-start(f32[16,512]{1,0:T(8,128)} %get-tuple-element.84), channel_id=1, source_target_pairs={{0,16},{8,24},{16,0},{24,8},{1,17},{9,25},{17,1},{25,9},{2,18},{10... | collective-permute-start | bytes 98312 | tf_op jit(solution)/shard_map/ppermute | solution.py:724
  81.5 0.9 copy-start.5
  82.3 27.4 %collective-permute-start.25 = (f32[16,512]{1,0:T(8,128)}, f32[16,512]{1,0:T(8,128)S(1)}, u32[]{:S(2)}, u32[]{:S(2)}) collective-permute-start(f32[16,512]{1,0:T(8,128)} %get-tuple-element.84), channel_id=1, source_target_pairs={{0,24},{8,0},{16,8},{24,16},{1,25},{9,1},{17,9},{25,17},{2,26},{10... | collective-permute-start | bytes 98312 | tf_op jit(solution)/shard_map/ppermute | solution.py:724
  99.4 11.6 %copy-start.21 = (f32[16,512]{1,0:T(8,128)S(1)}, f32[16,512]{1,0:T(8,128)}, u32[]{:S(2)}) copy-start(f32[16,512]{1,0:T(8,128)} %get-tuple-element.84) | copy-start | bytes 98308
  105.0 10.2 %collective-permute-start.5 = (f32[2,288,128]{2,1,0:T(8,128)}, f32[2,288,128]{2,1,0:T(8,128)}, u32[]{:S(2)}, u32[]{:S(2)}) collective-permute-start(f32[2,288,128]{2,1,0:T(8,128)} %get-tuple-element.62), channel_id=1, source_target_pairs={{0,1},{1,0},{2,3},{3,2},{4,5},{5,4},{6,7},{7,6},{8,9},{9,8},{10,11... | collective-permute-start | bytes 884744 | tf_op jit(solution)/shard_map/ppermute | solution.py:710
  105.1 19.7 %collective-permute-start = (f32[2,288,128]{2,1,0:T(8,128)}, f32[2,288,128]{2,1,0:T(8,128)S(1)}, u32[]{:S(2)}, u32[]{:S(2)}) collective-permute-start(f32[2,288,128]{2,1,0:T(8,128)} %get-tuple-element.57), channel_id=1, source_target_pairs={{0,1},{1,0},{2,3},{3,2},{4,5},{5,4},{6,7},{7,6},{8,9},{9,8},{10,11... | collective-permute-start | bytes 884744 | tf_op jit(solution)/shard_map/ppermute | solution.py:710
  107.1 12.1 %collective-permute-start.7 = (f32[2,288,128]{2,1,0:T(8,128)}, f32[2,288,128]{2,1,0:T(8,128)}, u32[]{:S(2)}, u32[]{:S(2)}) collective-permute-start(f32[2,288,128]{2,1,0:T(8,128)} %collective-permute-done.6.refs_2_), channel_id=1, source_target_pairs={{0,2},{2,4},{3,1},{4,6},{5,3},{7,5},{8,10},{10,12},{11,9},{12,14},... | collective-permute-start | bytes 884744 | tf_op jit(solution)/shard_map/ppermute | solution.py:713
  108.4 16.4 %copy-start.8 = (f32[2,288,128]{2,1,0:T(8,128)}, f32[2,288,128]{2,1,0:T(8,128)S(1)}, u32[]{:S(2)}) copy-start(f32[2,288,128]{2,1,0:T(8,128)S(1)} %collective-permute-done.1.refs_2_) | copy-start | bytes 884740
  108.4 17.1 %collective-permute-start.2 = (f32[2,288,128]{2,1,0:T(8,128)S(1)}, f32[2,288,128]{2,1,0:T(8,128)}, u32[]{:S(2)}, u32[]{:S(2)}) collective-permute-start(f32[2,288,128]{2,1,0:T(8,128)S(1)} %collective-permute-done.1.refs_2_), channel_id=1, source_target_pairs={{0,2},{2,4},{3,1},{4,6},{5,3},{7,5},{8,10},{10,12},{11,9},{12,14},... | collective-permute-start | bytes 884744 | tf_op jit(solution)/shard_map/ppermute | solution.py:713
  109.7 59.0 %collective-permute-start.31 = (f32[2,1152,128]{2,1,0:T(8,128)}, f32[2,1152,128]{2,1,0:T(8,128)S(1)}, u32[]{:S(2)}, u32[]{:S(2)}) collective-permute-start(f32[2,1152,128]{2,1,0:T(8,128)} %get-tuple-element.91.refs_4_), channel_id=1, source_target_pairs={{0,2},{2,4},{3,1},{4,6},{5,3},{7,5},{8,10},{10,12},{11,9},{12,14},... | collective-permute-start | bytes 3538952 | tf_op jit(solution)/shard_map/ppermute | solution.py:713
  125.5 7.8 %copy-start.1 = (f32[1,1152,128]{2,1,0:T(8,128)S(1)}, f32[1,1152,128]{2,1,0:T(8,128)}, u32[]{:S(2)}) copy-start(f32[1,1152,128]{2,1,0:T(8,128)} %get-tuple-element.89.refs_2_) | copy-start | bytes 1769476
  131.2 6.5 %collective-permute-start.17 = (f32[16,1024]{1,0:T(8,128)}, f32[16,1024]{1,0:T(8,128)S(1)}, u32[]{:S(2)}, u32[]{:S(2)}) collective-permute-start(f32[16,1024]{1,0:T(8,128)} %get-tuple-element.83), channel_id=1, source_target_pairs={{0,8},{8,16},{16,24},{24,0},{1,9},{9,17},{17,25},{25,1},{2,10},{10... | collective-permute-start | bytes 196616 | tf_op jit(solution)/shard_map/ppermute | solution.py:724
  131.2 6.6 %collective-permute-start.18 = (f32[16,1024]{1,0:T(8,128)}, f32[16,1024]{1,0:T(8,128)S(1)}, u32[]{:S(2)}, u32[]{:S(2)}) collective-permute-start(f32[16,1024]{1,0:T(8,128)} %get-tuple-element.83), channel_id=1, source_target_pairs={{0,16},{8,24},{16,0},{24,8},{1,17},{9,25},{17,1},{25,9},{2,18},{10... | collective-permute-start | bytes 196616 | tf_op jit(solution)/shard_map/ppermute | solution.py:724
  131.9 6.6 %collective-permute-start.19 = (f32[16,1024]{1,0:T(8,128)}, f32[16,1024]{1,0:T(8,128)S(1)}, u32[]{:S(2)}, u32[]{:S(2)}) collective-permute-start(f32[16,1024]{1,0:T(8,128)} %get-tuple-element.83), channel_id=1, source_target_pairs={{0,24},{8,0},{16,8},{24,16},{1,25},{9,1},{17,9},{25,17},{2,26},{10... | collective-permute-start | bytes 196616 | tf_op jit(solution)/shard_map/ppermute | solution.py:724
  133.3 35.4 %collective-permute-start.32 = (f32[1,1152,128]{2,1,0:T(8,128)S(1)}, f32[1,1152,128]{2,1,0:T(8,128)}, u32[]{:S(2)}, u32[]{:S(2)}) collective-permute-start(f32[1,1152,128]{2,1,0:T(8,128)S(1)} %copy-done.1), channel_id=1, source_target_pairs={{2,0},{4,2},{1,3},{6,4},{3,5},{5,7},{10,8},{12,10},{9,11},{14,12},... | collective-permute-start | bytes 1769480 | tf_op jit(solution)/shard_map/ppermute | solution.py:716
  137.7 13.6 %collective-permute-start.26 = (f32[16,512]{1,0:T(8,128)S(1)}, f32[16,512]{1,0:T(8,128)S(1)}, u32[]{:S(2)}, u32[]{:S(2)}) collective-permute-start(f32[16,512]{1,0:T(8,128)S(1)} %maximum_maximum_fusion), channel_id=1, source_target_pairs={{0,2},{1,3},{2,0},{3,1},{4,6},{5,7},{6,4},{7,5},{8,10},{9,11},{10,... | collective-permute-start | bytes 98312 | tf_op jit(solution)/shard_map/ppermute | solution.py:719
  137.8 13.6 %collective-permute-start.27 = (f32[16,512]{1,0:T(8,128)S(1)}, f32[16,512]{1,0:T(8,128)S(1)}, u32[]{:S(2)}, u32[]{:S(2)}) collective-permute-start(f32[16,512]{1,0:T(8,128)S(1)} %maximum_maximum_fusion), channel_id=1, source_target_pairs={{2,4},{3,5},{4,2},{5,3},{10,12},{11,13},{12,10},{13,11},{18,20},{1... | collective-permute-start | bytes 98312 | tf_op jit(solution)/shard_map/ppermute | solution.py:719
  138.5 53.6 %collective-permute-start.29 = (f32[2,576,128]{2,1,0:T(8,128)}, f32[2,576,128]{2,1,0:T(8,128)}, u32[]{:S(2)}, u32[]{:S(2)}) collective-permute-start(f32[2,576,128]{2,1,0:T(8,128)} %get-tuple-element.88.refs_4_), channel_id=1, source_target_pairs={{0,2},{2,4},{3,1},{4,6},{5,3},{7,5},{8,10},{10,12},{11,9},{12,14},... | collective-permute-start | bytes 1769480 | tf_op jit(solution)/shard_map/ppermute | solution.py:713
  151.4 4.3 %collective-permute-start.20 = (f32[16,1024]{1,0:T(8,128)S(1)}, f32[16,1024]{1,0:T(8,128)S(1)}, u32[]{:S(2)}, u32[]{:S(2)}) collective-permute-start(f32[16,1024]{1,0:T(8,128)S(1)} %add_add_fusion.1), channel_id=1, source_target_pairs={{0,1},{1,0},{2,3},{3,2},{4,5},{5,4},{6,7},{7,6},{8,9},{9,8},{10,11... | collective-permute-start | bytes 196616 | tf_op jit(solution)/shard_map/ppermute | solution.py:710
  151.4 14.1 %copy-start.7 = (f32[3,16,512]{2,1,0:T(8,128)}, f32[3,16,512]{2,1,0:T(8,128)S(1)}, u32[]{:S(2)}) copy-start(f32[3,16,512]{2,1,0:T(8,128)S(1)} %pad_maximum_fusion.near_ref) | copy-start | bytes 294916
  151.4 5.5 %collective-permute-start.28 = (f32[3,16,512]{2,1,0:T(8,128)S(1)}, f32[3,16,512]{2,1,0:T(8,128)S(1)}, u32[]{:S(2)}, u32[]{:S(2)}) collective-permute-start(f32[3,16,512]{2,1,0:T(8,128)S(1)} %pad_maximum_fusion.near_ref), channel_id=1, source_target_pairs={{0,1},{1,0},{2,3},{3,2},{4,5},{5,4},{6,7},{7,6},{8,9},{9,8},{10,11... | collective-permute-start | bytes 294920 | tf_op jit(solution)/shard_map/ppermute | solution.py:710
  155.7 9.8 %copy-start.14 = (f32[16,1024]{1,0:T(8,128)}, f32[16,1024]{1,0:T(8,128)S(1)}, u32[]{:S(2)}) copy-start(f32[16,1024]{1,0:T(8,128)S(1)} %add.49.sum_ref) | copy-start | bytes 196612
  155.7 7.4 %collective-permute-start.21 = (f32[16,1024]{1,0:T(8,128)S(1)}, f32[16,1024]{1,0:T(8,128)S(1)}, u32[]{:S(2)}, u32[]{:S(2)}) collective-permute-start(f32[16,1024]{1,0:T(8,128)S(1)} %add.49.sum_ref), channel_id=1, source_target_pairs={{0,2},{1,3},{2,0},{3,1},{4,6},{5,7},{6,4},{7,5},{8,10},{9,11},{10,... | collective-permute-start | bytes 196616 | tf_op jit(solution)/shard_map/ppermute | solution.py:719
  156.9 8.6 %copy-start.16 = (f32[3,16,512]{2,1,0:T(8,128)}, f32[3,16,512]{2,1,0:T(8,128)S(1)}, u32[]{:S(2)}) copy-start(f32[3,16,512]{2,1,0:T(8,128)S(1)} %collective-permute-done.28.far_ref) | copy-start | bytes 294916
  156.9 35.2 %collective-permute-start.30 = (f32[1,576,128]{2,1,0:T(8,128)}, f32[1,576,128]{2,1,0:T(8,128)}, u32[]{:S(2)}, u32[]{:S(2)}) collective-permute-start(f32[1,576,128]{2,1,0:T(8,128)} %get-tuple-element.86.refs_2_), channel_id=1, source_target_pairs={{2,0},{4,2},{1,3},{6,4},{3,5},{5,7},{10,8},{12,10},{9,11},{14,12},... | collective-permute-start | bytes 884744 | tf_op jit(solution)/shard_map/ppermute | solution.py:716
  163.6 1.8 collective-permute-start.22
  168.7 1.0 copy-start.2
  192.0 61.2 %collective-permute-start.43 = (f32[4,576,128]{2,1,0:T(8,128)}, f32[4,576,128]{2,1,0:T(8,128)S(1)}, u32[]{:S(2)}, u32[]{:S(2)}) collective-permute-start(f32[4,576,128]{2,1,0:T(8,128)} %get-tuple-element.108), channel_id=1, source_target_pairs={{0,1},{1,0},{2,3},{3,2},{4,5},{5,4},{6,7},{7,6},{8,9},{9,8},{10,11... | collective-permute-start | bytes 3538952 | tf_op jit(solution)/shard_map/ppermute | solution.py:710
  204.4 4.0 %collective-permute-start.34 = (f32[16,1024]{1,0:T(8,128)}, f32[16,1024]{1,0:T(8,128)S(1)}, u32[]{:S(2)}, u32[]{:S(2)}) collective-permute-start(f32[16,1024]{1,0:T(8,128)} %get-tuple-element.101), channel_id=1, source_target_pairs={{0,8},{8,16},{16,24},{24,0},{1,9},{9,17},{17,25},{25,1},{2,10},{10... | collective-permute-start | bytes 196616 | tf_op jit(solution)/shard_map/ppermute | solution.py:724
  204.4 5.0 %collective-permute-start.35 = (f32[16,1024]{1,0:T(8,128)}, f32[16,1024]{1,0:T(8,128)S(1)}, u32[]{:S(2)}, u32[]{:S(2)}) collective-permute-start(f32[16,1024]{1,0:T(8,128)} %get-tuple-element.101), channel_id=1, source_target_pairs={{0,16},{8,24},{16,0},{24,8},{1,17},{9,25},{17,1},{25,9},{2,18},{10... | collective-permute-start | bytes 196616 | tf_op jit(solution)/shard_map/ppermute | solution.py:724
  205.7 3.7 %collective-permute-start.36 = (f32[16,1024]{1,0:T(8,128)}, f32[16,1024]{1,0:T(8,128)S(1)}, u32[]{:S(2)}, u32[]{:S(2)}) collective-permute-start(f32[16,1024]{1,0:T(8,128)} %get-tuple-element.101), channel_id=1, source_target_pairs={{0,24},{8,0},{16,8},{24,16},{1,25},{9,1},{17,9},{25,17},{2,26},{10... | collective-permute-start | bytes 196616 | tf_op jit(solution)/shard_map/ppermute | solution.py:724
  210.3 9.1 %collective-permute-start.37 = (f32[16,1024]{1,0:T(8,128)S(1)}, f32[16,1024]{1,0:T(8,128)S(1)}, u32[]{:S(2)}, u32[]{:S(2)}) collective-permute-start(f32[16,1024]{1,0:T(8,128)S(1)} %add_add_fusion), channel_id=1, source_target_pairs={{0,1},{1,0},{2,3},{3,2},{4,5},{5,4},{6,7},{7,6},{8,9},{9,8},{10,11... | collective-permute-start | bytes 196616 | tf_op jit(solution)/shard_map/ppermute | solution.py:710
  219.3 8.8 %copy-start.15 = (f32[16,1024]{1,0:T(8,128)}, f32[16,1024]{1,0:T(8,128)S(1)}, u32[]{:S(2)}) copy-start(f32[16,1024]{1,0:T(8,128)S(1)} %add.56.sum_ref) | copy-start | bytes 196612
  219.4 6.7 %collective-permute-start.38 = (f32[16,1024]{1,0:T(8,128)S(1)}, f32[16,1024]{1,0:T(8,128)S(1)}, u32[]{:S(2)}, u32[]{:S(2)}) collective-permute-start(f32[16,1024]{1,0:T(8,128)S(1)} %add.56.sum_ref), channel_id=1, source_target_pairs={{0,2},{1,3},{2,0},{3,1},{4,6},{5,7},{6,4},{7,5},{8,10},{9,11},{10,... | collective-permute-start | bytes 196616 | tf_op jit(solution)/shard_map/ppermute | solution.py:719
  223.3 4.5 %collective-permute-start.39 = (f32[16,1024]{1,0:T(8,128)S(1)}, f32[16,1024]{1,0:T(8,128)S(1)}, u32[]{:S(2)}, u32[]{:S(2)}) collective-permute-start(f32[16,1024]{1,0:T(8,128)S(1)} %add.56.sum_ref), channel_id=1, source_target_pairs={{2,4},{3,5},{4,2},{5,3},{10,12},{11,13},{12,10},{13,11},{18,20},{1... | collective-permute-start | bytes 196616 | tf_op jit(solution)/shard_map/ppermute | solution.py:719
  224.0 16.6 %collective-permute-start.42 = (f32[4,288,128]{2,1,0:T(8,128)}, f32[4,288,128]{2,1,0:T(8,128)}, u32[]{:S(2)}, u32[]{:S(2)}) collective-permute-start(f32[4,288,128]{2,1,0:T(8,128)} %get-tuple-element.107), channel_id=1, source_target_pairs={{0,1},{1,0},{2,3},{3,2},{4,5},{5,4},{6,7},{7,6},{8,9},{9,8},{10,11... | collective-permute-start | bytes 1769480 | tf_op jit(solution)/shard_map/ppermute | solution.py:710
  225.8 27.4 %collective-permute-start.41 = (f32[4,288,128]{2,1,0:T(8,128)}, f32[4,288,128]{2,1,0:T(8,128)}, u32[]{:S(2)}, u32[]{:S(2)}) collective-permute-start(f32[4,288,128]{2,1,0:T(8,128)} %get-tuple-element.106), channel_id=1, source_target_pairs={{0,1},{1,0},{2,3},{3,2},{4,5},{5,4},{6,7},{7,6},{8,9},{9,8},{10,11... | collective-permute-start | bytes 1769480 | tf_op jit(solution)/shard_map/ppermute | solution.py:710
  226.1 2.0 copy-start.18
  226.1 39.8 %collective-permute-start.40 = (f32[4,288,128]{2,1,0:T(8,128)}, f32[4,288,128]{2,1,0:T(8,128)}, u32[]{:S(2)}, u32[]{:S(2)}) collective-permute-start(f32[4,288,128]{2,1,0:T(8,128)} %get-tuple-element.104), channel_id=1, source_target_pairs={{0,1},{1,0},{2,3},{3,2},{4,5},{5,4},{6,7},{7,6},{8,9},{9,8},{10,11... | collective-permute-start | bytes 1769480 | tf_op jit(solution)/shard_map/ppermute | solution.py:710
  227.8 48.1 %collective-permute-start.33 = (f32[4,288,128]{2,1,0:T(8,128)}, f32[4,288,128]{2,1,0:T(8,128)S(1)}, u32[]{:S(2)}, u32[]{:S(2)}) collective-permute-start(f32[4,288,128]{2,1,0:T(8,128)} %get-tuple-element.100), channel_id=1, source_target_pairs={{0,1},{1,0},{2,3},{3,2},{4,5},{5,4},{6,7},{7,6},{8,9},{9,8},{10,11... | collective-permute-start | bytes 1769480 | tf_op jit(solution)/shard_map/ppermute | solution.py:710
  253.2 1.1 copy-start.3
  275.9 0.8 copy-start.6
  (3 other events, 1.9 us)

commit v7 on v6

--- a/solution.py
+++ b/solution.py
@@ -23,8 +23,8 @@
 BF16 = jnp.bfloat16
 
 
-def params(**more):
-    return pltpu.CompilerParams(vmem_limit_bytes=62 * 1024 * 1024, **more)
+def params(limit=67043328):
+    return pltpu.CompilerParams(vmem_limit_bytes=limit)
 
 
 def plan(half):
@@ -567,11 +567,23 @@
         change_ref[:, (row + 2) * LANES : (row + 3) * LANES] = stacked(piece)
 
 
-def second_macro_kernel(
-    info_ref, sum_ref, sum_a_ref, sum_b_ref, keep_ref, gram_ref, mat_ref,
-    change_ref, state_ref, span_ref,
+def last_kernel(
+    size, half, blocks, info_ref, sum_ref, sum_a_ref, sum_b_ref, keep_ref, gram_ref, mat_ref,
+    table_ref, *refs
 ):
+    count = len({source for source, *_ in blocks})
+    sources = refs[:count]
+    out_ref, change_ref, state_ref, span_ref, held_ref, ready_ref, in_sems, out_sems = refs[count:]
     side = info_ref[0]
+
+    def copy_in(k):
+        source, offset, _, _ = blocks[k]
+        return pltpu.make_async_copy(
+            sources[source].at[:, pl.ds(offset, size), :], held_ref.at[k], in_sems.at[k]
+        )
+
+    for k in range(len(blocks)):
+        copy_in(k).start()
     place_blocks(info_ref, span_ref, sum_ref[...], sum_a_ref[...], sum_b_ref[...])
     fields = keep_ref[0:8, :]
     rate = keep_ref[8:9, :]
@@ -590,6 +602,69 @@
     for row in range(STRIP_ROWS):
         state_ref[:, row, :] = state[:5, row * LANES : (row + 1) * LANES]
 
+    def copy_out(k):
+        _, offset, own, first = blocks[k]
+        begin = (side if own else 1 - side) * half + first + offset
+        return begin, pltpu.make_async_copy(
+            ready_ref.at[k],
+            out_ref.at[pl.ds(pl.multiple_of(begin * STRIP_ROWS, STRIP_ROWS * size), STRIP_ROWS * size), :],
+            out_sems.at[k],
+        )
+
+    for k, (_, _, own, _) in enumerate(blocks):
+        begin, copy = copy_out(k)
+        lift = jnp.dot(
+            table_ref[pl.ds(pl.multiple_of(begin, size), size), :],
+            change_ref[...],
+            preferred_element_type=F32,
+        )
+        copy_in(k).wait()
+        flipped = side == (1 if own else 0)
+        for row in range(STRIP_ROWS):
+            index = jnp.where(flipped, 3 - row, row)
+            ready_ref[k, strided(row, size), :] = (
+                held_ref[k, index] + lift[:, row * LANES : (row + 1) * LANES]
+            )
+        copy.start()
+    for k in range(len(blocks)):
+        copy_out(k)[1].wait()
+
+
+def last_macro(info, args, table, pieces, half, size):
+    blocks = [
+        (source, offset, own, first)
+        for source, (rows, own, first) in enumerate(pieces)
+        for offset in range(0, rows.shape[1], size)
+    ]
+    whole = pl.BlockSpec(memory_space=pltpu.VMEM)
+    anywhere = pl.BlockSpec(memory_space=pl.ANY)
+    return pl.pallas_call(
+        functools.partial(last_kernel, size, half, blocks),
+        out_shape=[
+            jax.ShapeDtypeStruct((2 * half * STRIP_ROWS, LANES), F32),
+            jax.ShapeDtypeStruct((48, STRIP_ROWS * LANES), BF16),
+            jax.ShapeDtypeStruct((5, STRIP_ROWS, LANES), F32),
+        ],
+        in_specs=[
+            pl.BlockSpec(memory_space=pltpu.SMEM),
+            *[whole] * (len(args) + 1),
+            *[anywhere] * len(pieces),
+        ],
+        out_specs=[anywhere, whole, whole],
+        scratch_shapes=[
+            pltpu.VMEM((16, SPAN * LANES), F32),
+            pltpu.VMEM((len(blocks), STRIP_ROWS, size, LANES), F32),
+            pltpu.VMEM((len(blocks), STRIP_ROWS * size, LANES), F32),
+            pltpu.SemaphoreType.DMA((len(blocks),)),
+            pltpu.SemaphoreType.DMA((len(blocks),)),
+        ],
+        compiler_params=params(63 * 1024 * 1024),
+        name="last_macro",
+        cost_estimate=pl.CostEstimate(
+            flops=4000000, transcendentals=0, bytes_accessed=len(blocks) * size * LANES * 32
+        ),
+    )(info, *args, table, *[rows for rows, _, _ in pieces])
+
 
 def macro(kernel, info, args, outs, scratch):
     vmem = pl.BlockSpec(memory_space=pltpu.VMEM)
@@ -599,7 +674,7 @@
         in_specs=[pl.BlockSpec(memory_space=pltpu.SMEM)] + [vmem] * len(args),
         out_specs=[vmem] * len(outs),
         scratch_shapes=scratch,
-        compiler_params=params(),
+        compiler_params=params(48 * 1024 * 1024),
         cost_estimate=pl.CostEstimate(flops=4000000, transcendentals=0, bytes_accessed=1000000),
     )(info, *args)
 
@@ -806,17 +881,10 @@
     total = sum_groups(sums)
     total = total + swap(total)
     sum_a, sum_b = both_z(total)
-    change, state = macro(
-        second_macro_kernel, info,
-        [total, sum_a, sum_b, keep, gram, mat],
-        [
-            jax.ShapeDtypeStruct((48, STRIP_ROWS * LANES), BF16),
-            jax.ShapeDtypeStruct((5, STRIP_ROWS, LANES), F32),
-        ],
-        [pltpu.VMEM((16, SPAN * LANES), F32)],
+    pieces = [(near, True, 0), *[(back[c], False, firsts[c]) for c in later[:cut]]]
+    out, change, state = last_macro(
+        info, [total, sum_a, sum_b, keep, gram, mat], table, pieces, half, size
     )
-    pieces = [(near, True, 0), *[(back[c], False, firsts[c]) for c in later[:cut]]]
-    out = finish(side, None, pieces, table, change, half, size)
     for c in later[cut:]:
         out = finish(side, out, [(back[c], False, firsts[c])], table, change, half, size)
     return out.reshape(dist.shape), state

time: 283 us -> 284 us (level)
  other arithmetic: 3.1 us -> 9 us
  Pallas kernels: 102 us -> 96.2 us
    pallas_call x3 -> x2, Pallas kernels: 13.9 us -> 4.26 us  [finish(): pl.pallas_call(functools.partial(finish_kernel, size, parts), out_shape=j...]
    pallas_call x0 -> x1, Pallas kernels: none -> 7.73 us  [last_macro(): pl.pallas_call(functools.partial(last_kernel, size, half, blocks), out_sh...]
    pallas_call x2 -> x1, Pallas kernels: 5.77 us -> 1.95 us  [macro(): pl.pallas_call(kernel, out_shape=outs, in_specs=[pl.BlockSpec(memory_spac...]
  transfers between devices with their start and end apart: 44 -> 44, of which waited for: 17 -> 19; matrix products, arithmetic and copies ran while one was open for 1% -> 4% of each run, Pallas kernels for 35% -> 33%
where the time goes in v7:
time: 284 us; the launch traced here: 280 us
  waiting for transfers between devices  111 us (39%)
  Pallas kernels  96.2 us (34%)
  starting transfers between devices  54 us (19%)
  other arithmetic  9 us (3%)
  local copies, waits for them, and re-layouts  8.13 us (3%)
    ppermute x19, waiting for transfers between devices, swap(): return lax.ppermute(value, 'strip', swap_pairs)  73.5 us
    pallas_call x10, Pallas kernels, transport(): pl.pallas_call(functools.partial(transport_kernel, size, second_pass), ou...  65.9 us
    ppermute x7, waiting for transfers between devices, with_flow(): return lax.ppermute(value, 'strip', down_pairs)  21.5 us
    ppermute x19, starting transfers between devices, swap(): return lax.ppermute(value, 'strip', swap_pairs)  19.6 us
    ppermute x3, waiting for transfers between devices, both_z(): lax.ppermute(value, 'strip', pair_a)  14 us
    ppermute x3, starting transfers between devices, against_flow(): return lax.ppermute(value, 'strip', up_pairs)  9.63 us
    ppermute x7, starting transfers between devices, with_flow(): return lax.ppermute(value, 'strip', down_pairs)  9.02 us
    ppermute x9, starting transfers between devices, sum_groups(): lax.ppermute(value, 'vel', [(g, (g + shift) % groups) for g in range(grou...  7.78 us
  transfers between devices with their start and end apart: 44, of which 19 were waited for; matrix products, arithmetic and copies ran while one was open for 4% of the time, Pallas kernels for 33%

profile of v7, /device:TPU:24, one launch (start us, length us, event | category | flops | bytes accessed | tf_op | source)
XLA Modules:
  0.0 279.5 jit_solution(12933880003184795082)
XLA Ops:
  0.6 2.2 pack.3
  2.8 1.5 collective-permute-start.15
  4.3 4.1 %pack.2 = (f32[2,288,128]{2,1,0:T(8,128)}, f32[2,288,128]{2,1,0:T(8,128)}, f32[2,288,128]{2,1,0:T(8,128)}, f32[2,288,128]{2,1,0:T(8,128)}, f32[2,288,128]{2,1,0:...) custom-call(s32[1]{0:T(128)} %bitcast.side_ref, f32[13824,128]{1,0:T(8,128)} %bitcast.12), custom_call_target="tpu_custom_call" | custom-call | bytes 4718592 | tf_op jit(solution)/shard_map/pack/pallas_call | solution.py:149
  8.9 1.5 collective-permute-start.11
  12.9 1.5 collective-permute-start.4
  14.4 22.8 %collective-permute-done.4 = f32[8,128]{1,0:T(8,128)} collective-permute-done((f32[8,128]{1,0:T(8,128)S(1)}, f32[8,128]{1,0:T(8,128)}, u32[]{:S(2)}, u32[]{:S(2)}) %collective-permute-start.4) | collective-permute-done | bytes 4128 | tf_op jit(solution)/shard_map/ppermute | solution.py:785
  37.3 1.5 collective-permute-start.14
  38.8 3.9 %prepare.1 = (bf16[3456,48]{1,0:T(8,128)(2,1)}, f32[3456,8]{1,0:T(8,128)}, bf16[3456,32]{1,0:T(8,128)(2,1)}) custom-call(s32[3,3456]{1,0:T(4,128)} %vel_ref.1), custom_call_target="tpu_custom_call" | custom-call | flops 691200 | bytes 3456000 | tf_op jit(solution)/shard_map/prepare/pallas_call | solution.py:205
  42.7 6.2 %home_moments.1 = (f32[16,512]{1,0:T(8,128)}, f32[1728,128]{1,0:T(8,128)}) custom-call(s32[1]{0:T(128)} %bitcast.side_ref, f32[13824,128]{1,0:T(8,128)} %bitcast.13, bf16[3456,32]{1,0:T(8,128)(2,1)} %get-tuple-element.60.weight_ref.refs_6_.refs_8_), custom_call_target="tpu_custom_call" | custom-call | flops 226492416 | bytes 7077888 | tf_op jit(solution)/shard_map/home_moments/pallas_call | solution.py:263
  48.9 3.3 %collective-permute-start.3 = (f32[1728,128]{1,0:T(8,128)}, f32[1728,128]{1,0:T(8,128)}, u32[]{:S(2)}, u32[]{:S(2)}) collective-permute-start(f32[1728,128]{1,0:T(8,128)} %get-tuple-element.61), channel_id=1, source_target_pairs={{2,0},{4,2},{1,3},{6,4},{3,5},{5,7},{10,8},{12,10},{9,11},{14,12},... | collective-permute-start | bytes 2654216 | tf_op jit(solution)/shard_map/ppermute | solution.py:791
  53.6 1.3 collective-permute-start.13
  54.9 1.3 collective-permute-start.16
  59.1 2.1 collective-permute-done.8.refs_1_
  61.2 1.9 collective-permute-start.6
  63.3 2.4 collective-permute-done.13.refs_3_
  65.7 1.3 collective-permute-start.10
  67.7 14.4 %collective-permute-done.10.refs_3_ = f32[2,288,128]{2,1,0:T(8,128)} collective-permute-done((f32[2,288,128]{2,1,0:T(8,128)}, f32[2,288,128]{2,1,0:T(8,128)}, u32[]{:S(2)}, u32[]{:S(2)}) %collective-permute-start.10) | collective-permute-done | bytes 294944 | tf_op jit(solution)/shard_map/ppermute | solution.py:788
  82.1 1.5 collective-permute-start.24
  83.6 1.5 collective-permute-start.25
  86.3 8.9 %transport_first.5 = (f32[1,1152,128]{2,1,0:T(8,128)}, f32[5,1152,128]{2,1,0:T(8,128)}, f32[2,1152,128]{2,1,0:T(8,128)}, f32[16,1024]{1,0:T(8,128)}) custom-call(s32[1]{0:T(128)} %bitcast.side_ref, f32[13824,128]{1,0:T(8,128)} %bitcast.14, f32[2,576,128]{2,1,0:T(8,128)} %collective-permute-done.14.refs_1_, f32[2,576,128]{2,1,0:T(8,128)} %collective-permute-done.15.refs_2_, ...), custom_call_target="tpu_custom_call" | custom-call | flops 35389440 | bytes 5603328 | tf_op jit(solution)/shard_map/transport_first/pallas_call | solution.py:452
  95.2 5.6 %transport_first.6 = (f32[1,1152,128]{2,1,0:T(8,128)}, f32[5,1152,128]{2,1,0:T(8,128)}, f32[2,1152,128]{2,1,0:T(8,128)}, f32[16,1024]{1,0:T(8,128)}) custom-call(s32[1]{0:T(128)} %bitcast.side_ref, f32[13824,128]{1,0:T(8,128)} %bitcast.15, ...), custom_call_target="tpu_custom_call", output_to_operand_aliasing={{0}: (10, {}), {1}: (11, {}), {2}: (12, {})} | custom-call | flops 17694720 | bytes 2801664 | tf_op jit(solution)/shard_map/transport_first/pallas_call | solution.py:452
  100.8 5.6 %transport_first.7 = (f32[1,1152,128]{2,1,0:T(8,128)}, f32[5,1152,128]{2,1,0:T(8,128)}, f32[2,1152,128]{2,1,0:T(8,128)}, f32[16,1024]{1,0:T(8,128)}) custom-call(s32[1]{0:T(128)} %bitcast.side_ref, f32[13824,128]{1,0:T(8,128)} %bitcast.16, ...), custom_call_target="tpu_custom_call", output_to_operand_aliasing={{0}: (10, {}), {1}: (11, {}), {2}: (12, {})} | custom-call | flops 17694720 | bytes 2801664 | tf_op jit(solution)/shard_map/transport_first/pallas_call | solution.py:452
  106.5 2.0 collective-permute-start
  108.5 1.3 collective-permute-start.7
  109.8 1.3 collective-permute-start.2
  111.1 1.3 collective-permute-start.31
  113.8 1.4 maximum_maximum_fusion
  115.2 1.5 collective-permute-done.5.refs_1_
  116.6 3.9 %collective-permute-done.7.refs_3_ = f32[2,288,128]{2,1,0:T(8,128)} collective-permute-done((f32[2,288,128]{2,1,0:T(8,128)}, f32[2,288,128]{2,1,0:T(8,128)}, u32[]{:S(2)}, u32[]{:S(2)}) %collective-permute-start.7) | collective-permute-done | bytes 294944 | tf_op jit(solution)/shard_map/ppermute | solution.py:788
  120.6 5.6 %transport_first.8 = (f32[1,576,128]{2,1,0:T(8,128)}, f32[5,576,128]{2,1,0:T(8,128)}, f32[2,576,128]{2,1,0:T(8,128)}, f32[16,1024]{1,0:T(8,128)}) custom-call(s32[1]{0:T(128)} %bitcast.side_ref, f32[13824,128]{1,0:T(8,128)} %bitcast.17, f32[2,288,128]{2,1,0:T(8,128)} %collective-permute-done.5.refs_1_, f32[2,288,128]{2,1,0:T(8,128)} %collective-permute-done.6.refs_2_, ...), custom_call_target="tpu_custom_call" | custom-call | flops 17694720 | bytes 2801664 | tf_op jit(solution)/shard_map/transport_first/pallas_call | solution.py:452
  126.9 5.6 %transport_first.9 = (f32[1,576,128]{2,1,0:T(8,128)}, f32[5,576,128]{2,1,0:T(8,128)}, f32[2,576,128]{2,1,0:T(8,128)}, f32[16,1024]{1,0:T(8,128)}) custom-call(s32[1]{0:T(128)} %bitcast.side_ref, f32[13824,128]{1,0:T(8,128)} %bitcast.18, f32[2,288,128]{2,1,0:T(8,128)} %collective-permute-done.refs_1_, ...), custom_call_target="tpu_custom_call", output_to_operand_aliasing={{0}: (10, {}), {1}: (11, {}), {2}: (12, {})} | custom-call | flops 17694720 | bytes 2801664 | tf_op jit(solution)/shard_map/transport_first/pallas_call | solution.py:452
  133.1 1.4 collective-permute-start.19
  134.5 2.7 collective-permute-start.32
  137.2 0.9 fusion.1
  139.2 1.3 collective-permute-start.29
  140.5 0.9 add_add_fusion.1
  141.3 11.4 %collective-permute-done.26 = f32[16,512]{1,0:T(8,128)S(1)} collective-permute-done((f32[16,512]{1,0:T(8,128)}, f32[16,512]{1,0:T(8,128)S(1)}, u32[]{:S(2)}, u32[]{:S(2)}) %collective-permute-start.26) | collective-permute-done | bytes 32800 | tf_op jit(solution)/shard_map/ppermute | solution.py:794
  152.8 2.1 collective-permute-start.28
  154.9 2.2 collective-permute-done.20
  158.1 3.7 %collective-permute-start.30 = (f32[1,576,128]{2,1,0:T(8,128)}, f32[1,576,128]{2,1,0:T(8,128)}, u32[]{:S(2)}, u32[]{:S(2)}) collective-permute-start(f32[1,576,128]{2,1,0:T(8,128)} %get-tuple-element.87.refs_2_), channel_id=1, source_target_pairs={{2,0},{4,2},{1,3},{6,4},{3,5},{5,7},{10,8},{12,10},{9,11},{14,12},... | collective-permute-start | bytes 884744 | tf_op jit(solution)/shard_map/ppermute | solution.py:791
  161.7 2.6 collective-permute-done.21.sum_a_ref
  166.7 1.9 shard_map.77
  170.8 6.2 %transport_second.5 = (f32[4,1728,128]{2,1,0:T(8,128)}, f32[4,288,128]{2,1,0:T(8,128)}, f32[16,1024]{1,0:T(8,128)}) custom-call(s32[1]{0:T(128)} %bitcast.side_ref, bf16[3456,48]{1,0:T(8,128)(2,1)} %get-tuple-element.57.refs_0_.table_ref.refs_1_, bf16[48,1408]{1,0:T(8,128)(2,1)} %copy-done, f32[1,1152,128]{2,1,0:T(8,128)} %get-tuple-element.90.refs_2_, ...), custom_call_target="tpu_custom_call" | custom-call | flops 17694720 | bytes 2801664 | tf_op jit(solution)/shard_map/transport_second/pallas_call | solution.py:452
  176.9 6.2 %transport_second.6 = (f32[4,1728,128]{2,1,0:T(8,128)}, f32[4,288,128]{2,1,0:T(8,128)}, f32[16,1024]{1,0:T(8,128)}) custom-call(s32[1]{0:T(128)} %bitcast.side_ref, bf16[3456,48]{1,0:T(8,128)(2,1)} %get-tuple-element.57.refs_0_.table_ref.refs_1_, bf16[48,1408]{1,0:T(8,128)(2,1)} %copy-done, ...), custom_call_target="tpu_custom_call", output_to_operand_aliasing={{0}: (12, {})} | custom-call | flops 17694720 | bytes 2801664 | tf_op jit(solution)/shard_map/transport_second/pallas_call | solution.py:452
  183.1 9.9 %transport_second.7 = (f32[4,1728,128]{2,1,0:T(8,128)}, f32[4,576,128]{2,1,0:T(8,128)}, f32[16,1024]{1,0:T(8,128)}) custom-call(s32[1]{0:T(128)} %bitcast.side_ref, bf16[3456,48]{1,0:T(8,128)(2,1)} %get-tuple-element.57.refs_0_.table_ref.refs_1_, bf16[48,1408]{1,0:T(8,128)(2,1)} %copy-done, ...), custom_call_target="tpu_custom_call", output_to_operand_aliasing={{0}: (12, {})} | custom-call | flops 35389440 | bytes 5603328 | tf_op jit(solution)/shard_map/transport_second/pallas_call | solution.py:452
  193.1 6.2 %transport_second.8 = (f32[4,1728,128]{2,1,0:T(8,128)}, f32[4,288,128]{2,1,0:T(8,128)}, f32[16,1024]{1,0:T(8,128)}) custom-call(s32[1]{0:T(128)} %bitcast.side_ref, bf16[3456,48]{1,0:T(8,128)(2,1)} %get-tuple-element.57.refs_0_.table_ref.refs_1_, bf16[48,1408]{1,0:T(8,128)(2,1)} %copy-done, ...), custom_call_target="tpu_custom_call", output_to_operand_aliasing={{0}: (12, {})} | custom-call | flops 17694720 | bytes 2801664 | tf_op jit(solution)/shard_map/transport_second/pallas_call | solution.py:452
  199.3 6.2 %transport_second.9 = (f32[4,1728,128]{2,1,0:T(8,128)}, f32[4,288,128]{2,1,0:T(8,128)}, f32[16,1024]{1,0:T(8,128)}) custom-call(s32[1]{0:T(128)} %bitcast.side_ref, bf16[3456,48]{1,0:T(8,128)(2,1)} %get-tuple-element.57.refs_0_.table_ref.refs_1_, bf16[48,1408]{1,0:T(8,128)(2,1)} %copy-done, ...), custom_call_target="tpu_custom_call", output_to_operand_aliasing={{0}: (12, {})} | custom-call | flops 17694720 | bytes 2801664 | tf_op jit(solution)/shard_map/transport_second/pallas_call | solution.py:452
  205.5 1.4 collective-permute-start.35
  206.8 1.5 collective-permute-start.36
  208.3 1.2 collective-permute-done.34
  209.5 0.9 collective-permute-done.35
  210.5 0.9 add_add_fusion
  211.4 2.1 collective-permute-start.37
  213.4 6.9 %collective-permute-done.37 = f32[16,1024]{1,0:T(8,128)S(1)} collective-permute-done((f32[16,1024]{1,0:T(8,128)S(1)}, f32[16,1024]{1,0:T(8,128)S(1)}, u32[]{:S(2)}, u32[]{:S(2)}) %collective-permute-start.37) | collective-permute-done | bytes 65568 | tf_op jit(solution)/shard_map/ppermute | solution.py:785
  220.4 4.9 %collective-permute-start.38 = (f32[16,1024]{1,0:T(8,128)S(1)}, f32[16,1024]{1,0:T(8,128)S(1)}, u32[]{:S(2)}, u32[]{:S(2)}) collective-permute-start(f32[16,1024]{1,0:T(8,128)S(1)} %add.56.sum_ref), channel_id=1, source_target_pairs={{0,2},{1,3},{2,0},{3,1},{4,6},{5,7},{6,4},{7,5},{8,10},{9,11},{10,... | collective-permute-start | bytes 196616 | tf_op jit(solution)/shard_map/ppermute | solution.py:794
  225.9 1.8 collective-permute-start.41
  228.0 1.7 collective-permute-start.43
  230.0 12.3 %collective-permute-done.41.refs_2_ = f32[4,288,128]{2,1,0:T(8,128)S(1)} collective-permute-done((f32[4,288,128]{2,1,0:T(8,128)}, f32[4,288,128]{2,1,0:T(8,128)S(1)}, u32[]{:S(2)}, u32[]{:S(2)}) %collective-permute-start.41) | collective-permute-done | bytes 589856 | tf_op jit(solution)/shard_map/ppermute | solution.py:785
  242.4 12.7 %collective-permute-done.40.refs_1_ = f32[4,288,128]{2,1,0:T(8,128)} collective-permute-done((f32[4,288,128]{2,1,0:T(8,128)}, f32[4,288,128]{2,1,0:T(8,128)}, u32[]{:S(2)}, u32[]{:S(2)}) %collective-permute-start.40) | collective-permute-done | bytes 589856 | tf_op jit(solution)/shard_map/ppermute | solution.py:785
  255.2 7.7 %last_macro.1 = (f32[13824,128]{1,0:T(8,128)}, bf16[48,512]{1,0:T(8,128)(2,1)}, f32[5,4,128]{2,1,0:T(4,128)}) custom-call(s32[2]{0:T(128)} %copy-done.4, f32[16,1024]{1,0:T(8,128)} %copy-done.8, f32[16,1024]{1,0:T(8,128)} %copy-done.9, f32[16,1024]{1,0:T(8,128)} %copy-done.10, f32[16,3072]{1,0:T(8,128)} %copy-done.1, f32[16,8]{1,0:T(8,128)} %constant.49.clone.gram_ref, ...), custom_call_target="tpu_custom_call" | custom-call | flops 4000000 | bytes 11796480 | tf_op jit(solution)/shard_map/last_macro/pallas_call | solution.py:641
  262.9 4.9 %collective-permute-done.43.refs_0_ = f32[4,288,128]{2,1,0:T(8,128)} collective-permute-done((f32[4,288,128]{2,1,0:T(8,128)}, f32[4,288,128]{2,1,0:T(8,128)}, u32[]{:S(2)}, u32[]{:S(2)}) %collective-permute-start.43) | collective-permute-done | bytes 589856 | tf_op jit(solution)/shard_map/ppermute | solution.py:785
  267.8 2.1 finish.2.refs_3_
  269.9 7.5 %collective-permute-done.33.refs_0_ = f32[4,288,128]{2,1,0:T(8,128)} collective-permute-done((f32[4,288,128]{2,1,0:T(8,128)}, f32[4,288,128]{2,1,0:T(8,128)}, u32[]{:S(2)}, u32[]{:S(2)}) %collective-permute-start.33) | collective-permute-done | bytes 589856 | tf_op jit(solution)/shard_map/ppermute | solution.py:785
  277.4 2.1 finish.3
  (89 shorter events, 20.2 us)
Async XLA Ops:
  2.8 52.1 %collective-permute-start.15 = (f32[2,576,128]{2,1,0:T(8,128)}, f32[2,576,128]{2,1,0:T(8,128)}, u32[]{:S(2)}, u32[]{:S(2)}) collective-permute-start(f32[2,576,128]{2,1,0:T(8,128)} %get-tuple-element.70), channel_id=1, source_target_pairs={{0,1},{1,0},{2,3},{3,2},{4,5},{5,4},{6,7},{7,6},{8,9},{9,8},{10,11... | collective-permute-start | bytes 1769480 | tf_op jit(solution)/shard_map/ppermute | solution.py:785
  8.4 40.5 %collective-permute-start.12 = (f32[2,288,128]{2,1,0:T(8,128)}, f32[2,288,128]{2,1,0:T(8,128)}, u32[]{:S(2)}, u32[]{:S(2)}) collective-permute-start(f32[2,288,128]{2,1,0:T(8,128)} %get-tuple-element.68), channel_id=1, source_target_pairs={{0,1},{1,0},{2,3},{3,2},{4,5},{5,4},{6,7},{7,6},{8,9},{9,8},{10,11... | collective-permute-start | bytes 884744 | tf_op jit(solution)/shard_map/ppermute | solution.py:785
  8.9 44.6 %collective-permute-start.11 = (f32[2,288,128]{2,1,0:T(8,128)}, f32[2,288,128]{2,1,0:T(8,128)}, u32[]{:S(2)}, u32[]{:S(2)}) collective-permute-start(f32[2,288,128]{2,1,0:T(8,128)} %get-tuple-element.67), channel_id=1, source_target_pairs={{0,1},{1,0},{2,3},{3,2},{4,5},{5,4},{6,7},{7,6},{8,9},{9,8},{10,11... | collective-permute-start | bytes 884744 | tf_op jit(solution)/shard_map/ppermute | solution.py:785
  10.4 43.2 %collective-permute-start.9 = (f32[2,288,128]{2,1,0:T(8,128)}, f32[2,288,128]{2,1,0:T(8,128)}, u32[]{:S(2)}, u32[]{:S(2)}) collective-permute-start(f32[2,288,128]{2,1,0:T(8,128)} %get-tuple-element.66), channel_id=1, source_target_pairs={{0,1},{1,0},{2,3},{3,2},{4,5},{5,4},{6,7},{7,6},{8,9},{9,8},{10,11... | collective-permute-start | bytes 884744 | tf_op jit(solution)/shard_map/ppermute | solution.py:785
  11.6 0.6 copy-start.11
  12.9 24.4 %collective-permute-start.4 = (f32[8,128]{1,0:T(8,128)S(1)}, f32[8,128]{1,0:T(8,128)}, u32[]{:S(2)}, u32[]{:S(2)}) collective-permute-start(f32[8,128]{1,0:T(8,128)S(1)} %pad_maximum_fusion.2), channel_id=1, source_target_pairs={{0,1},{1,0},{2,3},{3,2},{4,5},{5,4},{6,7},{7,6},{8,9},{9,8},{10,11... | collective-permute-start | bytes 12296 | tf_op jit(solution)/shard_map/ppermute | solution.py:785
  37.3 25.9 %collective-permute-start.14 = (f32[2,576,128]{2,1,0:T(8,128)}, f32[2,576,128]{2,1,0:T(8,128)}, u32[]{:S(2)}, u32[]{:S(2)}) collective-permute-start(f32[2,576,128]{2,1,0:T(8,128)} %get-tuple-element.69), channel_id=1, source_target_pairs={{0,1},{1,0},{2,3},{3,2},{4,5},{5,4},{6,7},{7,6},{8,9},{9,8},{10,11... | collective-permute-start | bytes 1769480 | tf_op jit(solution)/shard_map/ppermute | solution.py:785
  48.9 33.2 %collective-permute-start.3 = (f32[1728,128]{1,0:T(8,128)}, f32[1728,128]{1,0:T(8,128)}, u32[]{:S(2)}, u32[]{:S(2)}) collective-permute-start(f32[1728,128]{1,0:T(8,128)} %get-tuple-element.61), channel_id=1, source_target_pairs={{2,0},{4,2},{1,3},{6,4},{3,5},{5,7},{10,8},{12,10},{9,11},{14,12},... | collective-permute-start | bytes 2654216 | tf_op jit(solution)/shard_map/ppermute | solution.py:791
  53.5 7.7 %collective-permute-start.8 = (f32[2,288,128]{2,1,0:T(8,128)}, f32[2,288,128]{2,1,0:T(8,128)}, u32[]{:S(2)}, u32[]{:S(2)}) collective-permute-start(f32[2,288,128]{2,1,0:T(8,128)} %get-tuple-element.65), channel_id=1, source_target_pairs={{0,1},{1,0},{2,3},{3,2},{4,5},{5,4},{6,7},{7,6},{8,9},{9,8},{10,11... | collective-permute-start | bytes 884744 | tf_op jit(solution)/shard_map/ppermute | solution.py:785
  53.6 12.1 %collective-permute-start.13 = (f32[2,288,128]{2,1,0:T(8,128)}, f32[2,288,128]{2,1,0:T(8,128)}, u32[]{:S(2)}, u32[]{:S(2)}) collective-permute-start(f32[2,288,128]{2,1,0:T(8,128)} %collective-permute-done.12.refs_2_), channel_id=1, source_target_pairs={{0,2},{2,4},{3,1},{4,6},{5,3},{7,5},{8,10},{10,12},{11,9},{12,14},... | collective-permute-start | bytes 884744 | tf_op jit(solution)/shard_map/ppermute | solution.py:788
  54.9 28.7 %collective-permute-start.16 = (f32[2,576,128]{2,1,0:T(8,128)}, f32[2,576,128]{2,1,0:T(8,128)}, u32[]{:S(2)}, u32[]{:S(2)}) collective-permute-start(f32[2,576,128]{2,1,0:T(8,128)} %collective-permute-done.15.refs_2_), channel_id=1, source_target_pairs={{0,2},{2,4},{3,1},{4,6},{5,3},{7,5},{8,10},{10,12},{11,9},{12,14},... | collective-permute-start | bytes 1769480 | tf_op jit(solution)/shard_map/ppermute | solution.py:788
  61.2 47.2 %collective-permute-start.6 = (f32[2,288,128]{2,1,0:T(8,128)}, f32[2,288,128]{2,1,0:T(8,128)}, u32[]{:S(2)}, u32[]{:S(2)}) collective-permute-start(f32[2,288,128]{2,1,0:T(8,128)} %get-tuple-element.64), channel_id=1, source_target_pairs={{0,1},{1,0},{2,3},{3,2},{4,5},{5,4},{6,7},{7,6},{8,9},{9,8},{10,11... | collective-permute-start | bytes 884744 | tf_op jit(solution)/shard_map/ppermute | solution.py:785
  63.2 46.6 %collective-permute-start.1 = (f32[2,288,128]{2,1,0:T(8,128)}, f32[2,288,128]{2,1,0:T(8,128)}, u32[]{:S(2)}, u32[]{:S(2)}) collective-permute-start(f32[2,288,128]{2,1,0:T(8,128)} %get-tuple-element.59), channel_id=1, source_target_pairs={{0,1},{1,0},{2,3},{3,2},{4,5},{5,4},{6,7},{7,6},{8,9},{9,8},{10,11... | collective-permute-start | bytes 884744 | tf_op jit(solution)/shard_map/ppermute | solution.py:785
  65.7 16.4 %collective-permute-start.10 = (f32[2,288,128]{2,1,0:T(8,128)}, f32[2,288,128]{2,1,0:T(8,128)}, u32[]{:S(2)}, u32[]{:S(2)}) collective-permute-start(f32[2,288,128]{2,1,0:T(8,128)} %collective-permute-done.9.refs_2_), channel_id=1, source_target_pairs={{0,2},{2,4},{3,1},{4,6},{5,3},{7,5},{8,10},{10,12},{11,9},{12,14},... | collective-permute-start | bytes 884744 | tf_op jit(solution)/shard_map/ppermute | solution.py:788
  82.1 24.3 %collective-permute-start.23 = (f32[16,512]{1,0:T(8,128)}, f32[16,512]{1,0:T(8,128)}, u32[]{:S(2)}, u32[]{:S(2)}) collective-permute-start(f32[16,512]{1,0:T(8,128)} %get-tuple-element.85), channel_id=1, source_target_pairs={{0,8},{8,16},{16,24},{24,0},{1,9},{9,17},{17,25},{25,1},{2,10},{10... | collective-permute-start | bytes 98312 | tf_op jit(solution)/shard_map/ppermute | solution.py:799
  82.1 24.3 %collective-permute-start.24 = (f32[16,512]{1,0:T(8,128)}, f32[16,512]{1,0:T(8,128)}, u32[]{:S(2)}, u32[]{:S(2)}) collective-permute-start(f32[16,512]{1,0:T(8,128)} %get-tuple-element.85), channel_id=1, source_target_pairs={{0,16},{8,24},{16,0},{24,8},{1,17},{9,25},{17,1},{25,9},{2,18},{10... | collective-permute-start | bytes 98312 | tf_op jit(solution)/shard_map/ppermute | solution.py:799
  83.6 27.4 %collective-permute-start.25 = (f32[16,512]{1,0:T(8,128)}, f32[16,512]{1,0:T(8,128)}, u32[]{:S(2)}, u32[]{:S(2)}) collective-permute-start(f32[16,512]{1,0:T(8,128)} %get-tuple-element.85), channel_id=1, source_target_pairs={{0,24},{8,0},{16,8},{24,16},{1,25},{9,1},{17,9},{25,17},{2,26},{10... | collective-permute-start | bytes 98312 | tf_op jit(solution)/shard_map/ppermute | solution.py:799
  106.4 10.2 %collective-permute-start.5 = (f32[2,288,128]{2,1,0:T(8,128)}, f32[2,288,128]{2,1,0:T(8,128)}, u32[]{:S(2)}, u32[]{:S(2)}) collective-permute-start(f32[2,288,128]{2,1,0:T(8,128)} %get-tuple-element.63), channel_id=1, source_target_pairs={{0,1},{1,0},{2,3},{3,2},{4,5},{5,4},{6,7},{7,6},{8,9},{9,8},{10,11... | collective-permute-start | bytes 884744 | tf_op jit(solution)/shard_map/ppermute | solution.py:785
  106.5 19.7 %collective-permute-start = (f32[2,288,128]{2,1,0:T(8,128)}, f32[2,288,128]{2,1,0:T(8,128)}, u32[]{:S(2)}, u32[]{:S(2)}) collective-permute-start(f32[2,288,128]{2,1,0:T(8,128)} %get-tuple-element.58), channel_id=1, source_target_pairs={{0,1},{1,0},{2,3},{3,2},{4,5},{5,4},{6,7},{7,6},{8,9},{9,8},{10,11... | collective-permute-start | bytes 884744 | tf_op jit(solution)/shard_map/ppermute | solution.py:785
  108.5 12.1 %collective-permute-start.7 = (f32[2,288,128]{2,1,0:T(8,128)}, f32[2,288,128]{2,1,0:T(8,128)}, u32[]{:S(2)}, u32[]{:S(2)}) collective-permute-start(f32[2,288,128]{2,1,0:T(8,128)} %collective-permute-done.6.refs_2_), channel_id=1, source_target_pairs={{0,2},{2,4},{3,1},{4,6},{5,3},{7,5},{8,10},{10,12},{11,9},{12,14},... | collective-permute-start | bytes 884744 | tf_op jit(solution)/shard_map/ppermute | solution.py:788
  109.8 17.1 %collective-permute-start.2 = (f32[2,288,128]{2,1,0:T(8,128)}, f32[2,288,128]{2,1,0:T(8,128)}, u32[]{:S(2)}, u32[]{:S(2)}) collective-permute-start(f32[2,288,128]{2,1,0:T(8,128)} %collective-permute-done.1.refs_2_), channel_id=1, source_target_pairs={{0,2},{2,4},{3,1},{4,6},{5,3},{7,5},{8,10},{10,12},{11,9},{12,14},... | collective-permute-start | bytes 884744 | tf_op jit(solution)/shard_map/ppermute | solution.py:788
  111.1 59.7 %collective-permute-start.31 = (f32[2,1152,128]{2,1,0:T(8,128)}, f32[2,1152,128]{2,1,0:T(8,128)}, u32[]{:S(2)}, u32[]{:S(2)}) collective-permute-start(f32[2,1152,128]{2,1,0:T(8,128)} %get-tuple-element.92.refs_4_), channel_id=1, source_target_pairs={{0,2},{2,4},{3,1},{4,6},{5,3},{7,5},{8,10},{10,12},{11,9},{12,14},... | collective-permute-start | bytes 3538952 | tf_op jit(solution)/shard_map/ppermute | solution.py:788
  113.2 0.6 copy-start.7
  132.5 5.6 %collective-permute-start.17 = (f32[16,1024]{1,0:T(8,128)}, f32[16,1024]{1,0:T(8,128)S(1)}, u32[]{:S(2)}, u32[]{:S(2)}) collective-permute-start(f32[16,1024]{1,0:T(8,128)} %get-tuple-element.84), channel_id=1, source_target_pairs={{0,8},{8,16},{16,24},{24,0},{1,9},{9,17},{17,25},{25,1},{2,10},{10... | collective-permute-start | bytes 196616 | tf_op jit(solution)/shard_map/ppermute | solution.py:799
  132.5 6.0 %collective-permute-start.18 = (f32[16,1024]{1,0:T(8,128)}, f32[16,1024]{1,0:T(8,128)S(1)}, u32[]{:S(2)}, u32[]{:S(2)}) collective-permute-start(f32[16,1024]{1,0:T(8,128)} %get-tuple-element.84), channel_id=1, source_target_pairs={{0,16},{8,24},{16,0},{24,8},{1,17},{9,25},{17,1},{25,9},{2,18},{10... | collective-permute-start | bytes 196616 | tf_op jit(solution)/shard_map/ppermute | solution.py:799
  133.1 6.1 %collective-permute-start.19 = (f32[16,1024]{1,0:T(8,128)}, f32[16,1024]{1,0:T(8,128)S(1)}, u32[]{:S(2)}, u32[]{:S(2)}) collective-permute-start(f32[16,1024]{1,0:T(8,128)} %get-tuple-element.84), channel_id=1, source_target_pairs={{0,24},{8,0},{16,8},{24,16},{1,25},{9,1},{17,9},{25,17},{2,26},{10... | collective-permute-start | bytes 196616 | tf_op jit(solution)/shard_map/ppermute | solution.py:799
  134.5 35.5 %collective-permute-start.32 = (f32[1,1152,128]{2,1,0:T(8,128)}, f32[1,1152,128]{2,1,0:T(8,128)S(1)}, u32[]{:S(2)}, u32[]{:S(2)}) collective-permute-start(f32[1,1152,128]{2,1,0:T(8,128)} %get-tuple-element.90.refs_2_), channel_id=1, source_target_pairs={{2,0},{4,2},{1,3},{6,4},{3,5},{5,7},{10,8},{12,10},{9,11},{14,12},... | collective-permute-start | bytes 1769480 | tf_op jit(solution)/shard_map/ppermute | solution.py:791
  138.1 14.7 %collective-permute-start.26 = (f32[16,512]{1,0:T(8,128)}, f32[16,512]{1,0:T(8,128)S(1)}, u32[]{:S(2)}, u32[]{:S(2)}) collective-permute-start(f32[16,512]{1,0:T(8,128)} %maximum_maximum_fusion), channel_id=1, source_target_pairs={{0,2},{1,3},{2,0},{3,1},{4,6},{5,7},{6,4},{7,5},{8,10},{9,11},{10,... | collective-permute-start | bytes 98312 | tf_op jit(solution)/shard_map/ppermute | solution.py:794
  138.5 14.2 %collective-permute-start.27 = (f32[16,512]{1,0:T(8,128)}, f32[16,512]{1,0:T(8,128)S(1)}, u32[]{:S(2)}, u32[]{:S(2)}) collective-permute-start(f32[16,512]{1,0:T(8,128)} %maximum_maximum_fusion), channel_id=1, source_target_pairs={{2,4},{3,5},{4,2},{5,3},{10,12},{11,13},{12,10},{13,11},{18,20},{1... | collective-permute-start | bytes 98312 | tf_op jit(solution)/shard_map/ppermute | solution.py:794
  139.2 54.0 %collective-permute-start.29 = (f32[2,576,128]{2,1,0:T(8,128)}, f32[2,576,128]{2,1,0:T(8,128)}, u32[]{:S(2)}, u32[]{:S(2)}) collective-permute-start(f32[2,576,128]{2,1,0:T(8,128)} %get-tuple-element.89.refs_4_), channel_id=1, source_target_pairs={{0,2},{2,4},{3,1},{4,6},{5,3},{7,5},{8,10},{10,12},{11,9},{12,14},... | collective-permute-start | bytes 1769480 | tf_op jit(solution)/shard_map/ppermute | solution.py:788
  152.8 4.3 %collective-permute-start.20 = (f32[16,1024]{1,0:T(8,128)S(1)}, f32[16,1024]{1,0:T(8,128)S(1)}, u32[]{:S(2)}, u32[]{:S(2)}) collective-permute-start(f32[16,1024]{1,0:T(8,128)S(1)} %add_add_fusion.1), channel_id=1, source_target_pairs={{0,1},{1,0},{2,3},{3,2},{4,5},{5,4},{6,7},{7,6},{8,9},{9,8},{10,11... | collective-permute-start | bytes 196616 | tf_op jit(solution)/shard_map/ppermute | solution.py:785
  152.8 5.3 %collective-permute-start.28 = (f32[3,16,512]{2,1,0:T(8,128)S(1)}, f32[3,16,512]{2,1,0:T(8,128)S(1)}, u32[]{:S(2)}, u32[]{:S(2)}) collective-permute-start(f32[3,16,512]{2,1,0:T(8,128)S(1)} %pad_maximum_fusion.near_ref), channel_id=1, source_target_pairs={{0,1},{1,0},{2,3},{3,2},{4,5},{5,4},{6,7},{7,6},{8,9},{9,8},{10,11... | collective-permute-start | bytes 294920 | tf_op jit(solution)/shard_map/ppermute | solution.py:785
  157.0 7.3 %collective-permute-start.21 = (f32[16,1024]{1,0:T(8,128)S(1)}, f32[16,1024]{1,0:T(8,128)S(1)}, u32[]{:S(2)}, u32[]{:S(2)}) collective-permute-start(f32[16,1024]{1,0:T(8,128)S(1)} %add.49.sum_ref), channel_id=1, source_target_pairs={{0,2},{1,3},{2,0},{3,1},{4,6},{5,7},{6,4},{7,5},{8,10},{9,11},{10,... | collective-permute-start | bytes 196616 | tf_op jit(solution)/shard_map/ppermute | solution.py:794
  158.1 35.1 %collective-permute-start.30 = (f32[1,576,128]{2,1,0:T(8,128)}, f32[1,576,128]{2,1,0:T(8,128)}, u32[]{:S(2)}, u32[]{:S(2)}) collective-permute-start(f32[1,576,128]{2,1,0:T(8,128)} %get-tuple-element.87.refs_2_), channel_id=1, source_target_pairs={{2,0},{4,2},{1,3},{6,4},{3,5},{5,7},{10,8},{12,10},{9,11},{14,12},... | collective-permute-start | bytes 884744 | tf_op jit(solution)/shard_map/ppermute | solution.py:791
  164.3 0.9 collective-permute-start.22
  165.2 3.4 %copy-start.4 = (s32[2]{0:T(128)}, s32[2]{0:T(128)S(1)}, u32[]{:S(2)}) copy-start(s32[2]{0:T(128)S(1)} %pad_add_fusion.info_ref) | copy-start | bytes 28
  165.2 0.7 copy-start.2
  166.0 0.7 copy-start.3
  168.6 0.7 copy-start
  169.3 0.7 copy-start.1
  170.0 0.8 copy-start.5
  193.0 62.1 %collective-permute-start.42 = (f32[4,576,128]{2,1,0:T(8,128)}, f32[4,576,128]{2,1,0:T(8,128)}, u32[]{:S(2)}, u32[]{:S(2)}) collective-permute-start(f32[4,576,128]{2,1,0:T(8,128)} %get-tuple-element.107), channel_id=1, source_target_pairs={{0,1},{1,0},{2,3},{3,2},{4,5},{5,4},{6,7},{7,6},{8,9},{9,8},{10,11... | collective-permute-start | bytes 3538952 | tf_op jit(solution)/shard_map/ppermute | solution.py:785
  205.5 4.0 %collective-permute-start.34 = (f32[16,1024]{1,0:T(8,128)}, f32[16,1024]{1,0:T(8,128)S(1)}, u32[]{:S(2)}, u32[]{:S(2)}) collective-permute-start(f32[16,1024]{1,0:T(8,128)} %get-tuple-element.102), channel_id=1, source_target_pairs={{0,8},{8,16},{16,24},{24,0},{1,9},{9,17},{17,25},{25,1},{2,10},{10... | collective-permute-start | bytes 196616 | tf_op jit(solution)/shard_map/ppermute | solution.py:799
  205.5 4.9 %collective-permute-start.35 = (f32[16,1024]{1,0:T(8,128)}, f32[16,1024]{1,0:T(8,128)S(1)}, u32[]{:S(2)}, u32[]{:S(2)}) collective-permute-start(f32[16,1024]{1,0:T(8,128)} %get-tuple-element.102), channel_id=1, source_target_pairs={{0,16},{8,24},{16,0},{24,8},{1,17},{9,25},{17,1},{25,9},{2,18},{10... | collective-permute-start | bytes 196616 | tf_op jit(solution)/shard_map/ppermute | solution.py:799
  206.8 3.7 %collective-permute-start.36 = (f32[16,1024]{1,0:T(8,128)}, f32[16,1024]{1,0:T(8,128)S(1)}, u32[]{:S(2)}, u32[]{:S(2)}) collective-permute-start(f32[16,1024]{1,0:T(8,128)} %get-tuple-element.102), channel_id=1, source_target_pairs={{0,24},{8,0},{16,8},{24,16},{1,25},{9,1},{17,9},{25,17},{2,26},{10... | collective-permute-start | bytes 196616 | tf_op jit(solution)/shard_map/ppermute | solution.py:799
  211.4 9.0 %collective-permute-start.37 = (f32[16,1024]{1,0:T(8,128)S(1)}, f32[16,1024]{1,0:T(8,128)S(1)}, u32[]{:S(2)}, u32[]{:S(2)}) collective-permute-start(f32[16,1024]{1,0:T(8,128)S(1)} %add_add_fusion), channel_id=1, source_target_pairs={{0,1},{1,0},{2,3},{3,2},{4,5},{5,4},{6,7},{7,6},{8,9},{9,8},{10,11... | collective-permute-start | bytes 196616 | tf_op jit(solution)/shard_map/ppermute | solution.py:785
  220.3 34.8 %copy-start.8 = (f32[16,1024]{1,0:T(8,128)}, f32[16,1024]{1,0:T(8,128)S(1)}, u32[]{:S(2)}) copy-start(f32[16,1024]{1,0:T(8,128)S(1)} %add.56.sum_ref) | copy-start | bytes 196612
  220.4 7.7 %collective-permute-start.38 = (f32[16,1024]{1,0:T(8,128)S(1)}, f32[16,1024]{1,0:T(8,128)S(1)}, u32[]{:S(2)}, u32[]{:S(2)}) collective-permute-start(f32[16,1024]{1,0:T(8,128)S(1)} %add.56.sum_ref), channel_id=1, source_target_pairs={{0,2},{1,3},{2,0},{3,1},{4,6},{5,7},{6,4},{7,5},{8,10},{9,11},{10,... | collective-permute-start | bytes 196616 | tf_op jit(solution)/shard_map/ppermute | solution.py:794
  225.3 4.5 %collective-permute-start.39 = (f32[16,1024]{1,0:T(8,128)S(1)}, f32[16,1024]{1,0:T(8,128)S(1)}, u32[]{:S(2)}, u32[]{:S(2)}) collective-permute-start(f32[16,1024]{1,0:T(8,128)S(1)} %add.56.sum_ref), channel_id=1, source_target_pairs={{2,4},{3,5},{4,2},{5,3},{10,12},{11,13},{12,10},{13,11},{18,20},{1... | collective-permute-start | bytes 196616 | tf_op jit(solution)/shard_map/ppermute | solution.py:794
  225.9 16.5 %collective-permute-start.41 = (f32[4,288,128]{2,1,0:T(8,128)}, f32[4,288,128]{2,1,0:T(8,128)S(1)}, u32[]{:S(2)}, u32[]{:S(2)}) collective-permute-start(f32[4,288,128]{2,1,0:T(8,128)} %get-tuple-element.106), channel_id=1, source_target_pairs={{0,1},{1,0},{2,3},{3,2},{4,5},{5,4},{6,7},{7,6},{8,9},{9,8},{10,11... | collective-permute-start | bytes 1769480 | tf_op jit(solution)/shard_map/ppermute | solution.py:785
  227.7 27.4 %collective-permute-start.40 = (f32[4,288,128]{2,1,0:T(8,128)}, f32[4,288,128]{2,1,0:T(8,128)}, u32[]{:S(2)}, u32[]{:S(2)}) collective-permute-start(f32[4,288,128]{2,1,0:T(8,128)} %get-tuple-element.105), channel_id=1, source_target_pairs={{0,1},{1,0},{2,3},{3,2},{4,5},{5,4},{6,7},{7,6},{8,9},{9,8},{10,11... | collective-permute-start | bytes 1769480 | tf_op jit(solution)/shard_map/ppermute | solution.py:785
  228.0 27.1 %copy-start.9 = (f32[16,1024]{1,0:T(8,128)}, f32[16,1024]{1,0:T(8,128)S(1)}, u32[]{:S(2)}) copy-start(f32[16,1024]{1,0:T(8,128)S(1)} %collective-permute-done.38.sum_a_ref) | copy-start | bytes 196612
  228.0 39.8 %collective-permute-start.43 = (f32[4,288,128]{2,1,0:T(8,128)}, f32[4,288,128]{2,1,0:T(8,128)}, u32[]{:S(2)}, u32[]{:S(2)}) collective-permute-start(f32[4,288,128]{2,1,0:T(8,128)} %get-tuple-element.109), channel_id=1, source_target_pairs={{0,1},{1,0},{2,3},{3,2},{4,5},{5,4},{6,7},{7,6},{8,9},{9,8},{10,11... | collective-permute-start | bytes 1769480 | tf_op jit(solution)/shard_map/ppermute | solution.py:785
  229.8 25.4 %copy-start.10 = (f32[16,1024]{1,0:T(8,128)}, f32[16,1024]{1,0:T(8,128)S(1)}, u32[]{:S(2)}) copy-start(f32[16,1024]{1,0:T(8,128)S(1)} %collective-permute-done.39.sum_b_ref) | copy-start | bytes 196612
  229.8 47.6 %collective-permute-start.33 = (f32[4,288,128]{2,1,0:T(8,128)}, f32[4,288,128]{2,1,0:T(8,128)}, u32[]{:S(2)}, u32[]{:S(2)}) collective-permute-start(f32[4,288,128]{2,1,0:T(8,128)} %get-tuple-element.101), channel_id=1, source_target_pairs={{0,1},{1,0},{2,3},{3,2},{4,5},{5,4},{6,7},{7,6},{8,9},{9,8},{10,11... | collective-permute-start | bytes 1769480 | tf_op jit(solution)/shard_map/ppermute | solution.py:785
  242.4 12.8 %copy-start.6 = (f32[4,288,128]{2,1,0:T(8,128)}, f32[4,288,128]{2,1,0:T(8,128)S(1)}, u32[]{:S(2)}) copy-start(f32[4,288,128]{2,1,0:T(8,128)S(1)} %collective-permute-done.41.refs_2_) | copy-start | bytes 1769476

commit v8 on v7

--- a/solution.py
+++ b/solution.py
@@ -23,7 +23,7 @@
 BF16 = jnp.bfloat16
 
 
-def params(limit=67043328):
+def params(limit=66584576):
     return pltpu.CompilerParams(vmem_limit_bytes=limit)
 
 
@@ -32,13 +32,16 @@
     blocks = half // block
     if blocks % 6 == 0:
         unit = block * (blocks // 6)
-        return block, [2 * unit, unit, unit, unit, unit]
+        return block, [2 * unit, 2 * unit, unit, unit]
     return block, [block * (blocks - 2), block, block]
 
 
-def second_order(pieces):
-    cut = (pieces + 1) // 2
-    return [*range(1, cut), 0, *range(cut, pieces)], cut
+def second_items(chunks):
+    firsts = [sum(chunks[:c]) for c in range(len(chunks))]
+    unit = chunks[-1]
+    items = [(1, first, unit) for first in range(firsts[1], firsts[2], unit)]
+    items.append((0, 0, chunks[0]))
+    return items + [(2, firsts[c], chunks[c]) for c in range(2, len(chunks))]
 
 
 def moment_rows(vel_x, vel_y, vel_z, volume, lib):
@@ -532,18 +535,19 @@
 
 
 def first_macro_kernel(
-    info_ref, sum_ref, sum_a_ref, sum_b_ref, near_ref, far_ref, gram_ref, mat_ref,
+    info_ref, sum_ref, home_own_ref, both_a_ref, both_b_ref, gram_ref, mat_ref,
     change_ref, keep_ref, span_ref, home_ref,
 ):
     side = info_ref[0]
     odd = info_ref[1]
     width = BLOCK_ROWS * LANES
     part = STRIP_ROWS * LANES
-    place_blocks(info_ref, span_ref, sum_ref[...], sum_a_ref[...], sum_b_ref[...])
-    for ref, where in ((near_ref, side), (far_ref, 1 - side)):
-        for index, block in enumerate((1, (1 - odd) * 2, odd * 2)):
+    place_blocks(info_ref, span_ref, sum_ref[...], both_a_ref[:16, :], both_b_ref[:16, :])
+    homes = (home_own_ref[...], both_a_ref[16:, :], both_b_ref[16:, :])
+    for block, both in zip((1, (1 - odd) * 2, odd * 2), homes):
+        for where, rows in ((side, both[:, :part]), (1 - side, both[:, part:])):
             spot = pl.multiple_of(block * width + where * part, part)
-            home_ref[:, pl.ds(spot, part)] = ref[index]
+            home_ref[:, pl.ds(spot, part)] = rows
     home = home_ref[...]
     rate = home[13:14, :]
     ratio = jnp.where(home[14:15, :] > 0.5, 1.0, rate)
@@ -674,7 +678,7 @@
         in_specs=[pl.BlockSpec(memory_space=pltpu.SMEM)] + [vmem] * len(args),
         out_specs=[vmem] * len(outs),
         scratch_shapes=scratch,
-        compiler_params=params(48 * 1024 * 1024),
+        compiler_params=params(),
         cost_estimate=pl.CostEstimate(flops=4000000, transcendentals=0, bytes_accessed=1000000),
     )(info, *args)
 
@@ -739,7 +743,7 @@
             out_specs=pl.BlockSpec((4 * size, LANES), lambda i, s: (place(i, s), 0)),
         ),
         input_output_aliases=aliases,
-        compiler_params=params(),
+        compiler_params=params(67043328),
         name="finish",
         cost_estimate=pl.CostEstimate(
             flops=2 * 48 * 4 * LANES * steps * size,
@@ -758,8 +762,9 @@
     size, chunks = plan(half)
     firsts = [sum(chunks[:c]) for c in range(len(chunks))]
     order = range(len(chunks))
-    later, cut = second_order(len(chunks))
-    groups_of = [order[:cut], order[cut:]]
+    groups_of = [order[:1], order[1:2], order[2:]]
+    items = second_items(chunks)
+    early = len(items) - len(groups_of[2])
     side = (strip % 2).astype(jnp.int32).reshape(1)
     info = jnp.stack([strip % 2, (strip // 2) % 2]).astype(jnp.int32)
 
@@ -835,13 +840,12 @@
     home = jnp.concatenate(
         [home[:13], collision_rate.reshape(1, -1), wall.reshape(1, -1), jnp.zeros((1, rows * cols), F32)]
     )
-    near_home = jnp.stack([home, *both_z(home)])
-    far_home = swap(near_home)
+    home = jnp.concatenate([home, swap(home)], axis=1)
 
     width = BLOCK_ROWS * LANES
     sums = jnp.zeros((16, width), F32)
     kept = []
-    for number, members in enumerate(groups_of):
+    for members in groups_of:
         start = firsts[members[0]]
         length = sum(chunks[c] for c in members)
         held = None
@@ -856,10 +860,10 @@
 
     total = sum_groups(sums)
     total = total + swap(total)
-    sum_a, sum_b = both_z(total)
+    both_a, both_b = both_z(jnp.concatenate([total, home]))
     change, keep = macro(
         first_macro_kernel, info,
-        [total, sum_a, sum_b, near_home, far_home, gram, mat],
+        [total, home, both_a, both_b, gram, mat],
         [
             jax.ShapeDtypeStruct((48, 11 * LANES), BF16),
             jax.ShapeDtypeStruct((16, SPAN * LANES), F32),
@@ -868,25 +872,24 @@
     )
 
     sums = jnp.zeros((16, width), F32)
-    near, back = None, {}
-    for c in later:
-        number = int(c >= cut)
+    near, back = None, []
+    for number, first, length in items:
         start = firsts[groups_of[number][0]]
         near, far, sums = transport(
-            side, list(kept[number]), tables, cells, sums, half,
-            chunks[c], firsts[c], size, change, skip=firsts[c] - start,
-            into=None if near is None else [near],
+            side, list(kept[number]), tables, cells, sums, half, length, first, size, change,
+            skip=first - start, into=None if near is None else [near],
         )
-        back[c] = swap(far)
+        back.append(swap(far))
     total = sum_groups(sums)
     total = total + swap(total)
     sum_a, sum_b = both_z(total)
-    pieces = [(near, True, 0), *[(back[c], False, firsts[c]) for c in later[:cut]]]
+    returned = [(rows, False, first) for rows, (_, first, _) in zip(back, items)]
+    pieces = [(near, True, 0), *returned[:early]]
     out, change, state = last_macro(
         info, [total, sum_a, sum_b, keep, gram, mat], table, pieces, half, size
     )
-    for c in later[cut:]:
-        out = finish(side, out, [(back[c], False, firsts[c])], table, change, half, size)
+    for piece in returned[early:]:
+        out = finish(side, out, [piece], table, change, half, size)
     return out.reshape(dist.shape), state
 
 

time: 284 us -> 316 us (1.11)
  waiting for transfers between devices: 111 us -> 141 us
  starting transfers between devices: 54 us -> 64.7 us
  other arithmetic: 9 us -> 4.45 us
  local copies, waits for them, and re-layouts: 8.13 us -> 3.65 us
    ppermute x19 -> x17, waiting for transfers between devices: 73.5 us -> 89.4 us  [swap(): return lax.ppermute(value, 'strip', swap_pairs)]
    ppermute x3 -> x2, waiting for transfers between devices: 14 us -> 25.8 us  [both_z(): lax.ppermute(value, 'strip', pair_a)]
    ppermute x3 -> x4, starting transfers between devices: 9.63 us -> 21.2 us  [against_flow(): return lax.ppermute(value, 'strip', up_pairs)]
    ppermute x19 -> x17, starting transfers between devices: 19.6 us -> 23.2 us  [swap(): return lax.ppermute(value, 'strip', swap_pairs)]
    pallas_call x10 -> x9, Pallas kernels: 65.9 us -> 63.9 us  [transport(): pl.pallas_call(functools.partial(transport_kernel, size, second_pass), ou...]
  transfers between devices with their start and end apart: 44 -> 41, of which waited for: 19 -> 19; matrix products, arithmetic and copies ran while one was open for 4% -> 1% of each run, Pallas kernels for 33% -> 29%
where the time goes in v8:
time: 316 us; the launch traced here: 311 us
  waiting for transfers between devices  141 us (45%)
  Pallas kernels  95.7 us (30%)
  starting transfers between devices  64.7 us (20%)
  other arithmetic  4.45 us (1%)
  local copies, waits for them, and re-layouts  3.65 us (1%)
    ppermute x17, waiting for transfers between devices, swap(): return lax.ppermute(value, 'strip', swap_pairs)  89.4 us
    pallas_call x9, Pallas kernels, transport(): pl.pallas_call(functools.partial(transport_kernel, size, second_pass), ou...  63.9 us
    ppermute x2, waiting for transfers between devices, both_z(): lax.ppermute(value, 'strip', pair_a)  25.8 us
    ppermute x17, starting transfers between devices, swap(): return lax.ppermute(value, 'strip', swap_pairs)  23.2 us
    ppermute x7, waiting for transfers between devices, with_flow(): return lax.ppermute(value, 'strip', down_pairs)  21.4 us
    ppermute x4, starting transfers between devices, against_flow(): return lax.ppermute(value, 'strip', up_pairs)  21.2 us
    ppermute x7, starting transfers between devices, with_flow(): return lax.ppermute(value, 'strip', down_pairs)  9.02 us
    pallas_call x1, Pallas kernels, last_macro(): pl.pallas_call(functools.partial(last_kernel, size, half, blocks), out_sh...  7.73 us
  transfers between devices with their start and end apart: 41, of which 19 were waited for; matrix products, arithmetic and copies ran while one was open for 1% of the time, Pallas kernels for 29%

profile of v8, /device:TPU:24, one launch (start us, length us, event | category | flops | bytes accessed | tf_op | source)
XLA Modules:
  0.0 311.0 jit_solution(18038327531569210718)
XLA Ops:
  0.6 2.2 pack.3
  2.9 1.5 collective-permute-start.12
  4.9 4.4 %pack.2 = (f32[2,576,128]{2,1,0:T(8,128)}, f32[2,576,128]{2,1,0:T(8,128)}, f32[2,288,128]{2,1,0:T(8,128)}, f32[2,288,128]{2,1,0:T(8,128)}, f32[2,288,128]{2,1,0:T(8,128)}, /*index=5*/f32[2,288,128]{2,1,0:T(8,128)}) custom-call(s32[1]{0:T(128)} %bitcast.side_ref, f32[13824,128]{1,0:T(8,128)} %bitcast.7), custom_call_target="tpu_custom_call" | custom-call | bytes 4718592 | tf_op jit(solution)/shard_map/pack/pallas_call | solution.py:152
  9.3 1.5 collective-permute-start.9
  11.3 1.6 collective-permute-start.4
  12.9 36.9 %collective-permute-done.4 = f32[8,128]{1,0:T(8,128)S(1)} collective-permute-done((f32[8,128]{1,0:T(8,128)S(1)}, f32[8,128]{1,0:T(8,128)S(1)}, u32[]{:S(2)}, u32[]{:S(2)}) %collective-permute-start.4) | collective-permute-done | bytes 4128 | tf_op jit(solution)/shard_map/ppermute | solution.py:790
  49.8 1.5 collective-permute-start.5
  51.9 8.2 %collective-permute-done.5.refs_1_ = f32[2,288,128]{2,1,0:T(8,128)} collective-permute-done((f32[2,288,128]{2,1,0:T(8,128)}, f32[2,288,128]{2,1,0:T(8,128)}, u32[]{:S(2)}, u32[]{:S(2)}) %collective-permute-start.5) | collective-permute-done | bytes 294944 | tf_op jit(solution)/shard_map/ppermute | solution.py:790
  60.0 1.5 collective-permute-start.8
  61.6 3.8 %prepare.1 = (bf16[3456,48]{1,0:T(8,128)(2,1)}, f32[3456,8]{1,0:T(8,128)}, bf16[3456,32]{1,0:T(8,128)(2,1)}) custom-call(s32[3,3456]{1,0:T(4,128)} %vel_ref.1), custom_call_target="tpu_custom_call" | custom-call | flops 691200 | bytes 3456000 | tf_op jit(solution)/shard_map/prepare/pallas_call | solution.py:208
  65.3 6.3 %home_moments.1 = (f32[16,512]{1,0:T(8,128)}, f32[1728,128]{1,0:T(8,128)}) custom-call(s32[1]{0:T(128)} %bitcast.side_ref, f32[13824,128]{1,0:T(8,128)} %bitcast.8, bf16[3456,32]{1,0:T(8,128)(2,1)} %get-tuple-element.54.weight_ref.refs_6_.refs_8_), custom_call_target="tpu_custom_call" | custom-call | flops 226492416 | bytes 7077888 | tf_op jit(solution)/shard_map/home_moments/pallas_call | solution.py:266
  71.6 3.3 %collective-permute-start.3 = (f32[1728,128]{1,0:T(8,128)}, f32[1728,128]{1,0:T(8,128)}, u32[]{:S(2)}, u32[]{:S(2)}) collective-permute-start(f32[1728,128]{1,0:T(8,128)} %get-tuple-element.55), channel_id=1, source_target_pairs={{2,0},{4,2},{1,3},{6,4},{3,5},{5,7},{10,8},{12,10},{9,11},{14,12},... | collective-permute-start | bytes 2654216 | tf_op jit(solution)/shard_map/ppermute | solution.py:796
  75.0 1.3 collective-permute-start.7
  76.3 1.3 collective-permute-start.13
  77.6 1.3 collective-permute-start.10
  79.0 5.6 %collective-permute-start = (f32[2,288,128]{2,1,0:T(8,128)}, f32[2,288,128]{2,1,0:T(8,128)}, u32[]{:S(2)}, u32[]{:S(2)}) collective-permute-start(f32[2,288,128]{2,1,0:T(8,128)} %get-tuple-element.52), channel_id=1, source_target_pairs={{0,1},{1,0},{2,3},{3,2},{4,5},{5,4},{6,7},{7,6},{8,9},{9,8},{10,11... | collective-permute-start | bytes 884744 | tf_op jit(solution)/shard_map/ppermute | solution.py:790
  84.6 2.2 collective-permute-done.7.refs_3_
  86.8 0.7 copy-done.6
  87.5 1.3 collective-permute-start.2
  89.2 10.3 %collective-permute-done.13.refs_3_ = f32[2,576,128]{2,1,0:T(8,128)} collective-permute-done((f32[2,576,128]{2,1,0:T(8,128)}, f32[2,576,128]{2,1,0:T(8,128)}, u32[]{:S(2)}, u32[]{:S(2)}) %collective-permute-start.13) | collective-permute-done | bytes 589856 | tf_op jit(solution)/shard_map/ppermute | solution.py:793
  99.5 1.5 collective-permute-start.19
  101.0 8.9 %collective-permute-done.10.refs_3_ = f32[2,576,128]{2,1,0:T(8,128)} collective-permute-done((f32[2,576,128]{2,1,0:T(8,128)}, f32[2,576,128]{2,1,0:T(8,128)}, u32[]{:S(2)}, u32[]{:S(2)}) %collective-permute-start.10) | collective-permute-done | bytes 589856 | tf_op jit(solution)/shard_map/ppermute | solution.py:793
  111.2 8.9 %transport_first.4 = (f32[1,576,128]{2,1,0:T(8,128)}, f32[5,576,128]{2,1,0:T(8,128)}, f32[2,576,128]{2,1,0:T(8,128)}, f32[16,1024]{1,0:T(8,128)}) custom-call(s32[1]{0:T(128)} %bitcast.side_ref, f32[13824,128]{1,0:T(8,128)} %bitcast.9, f32[2,576,128]{2,1,0:T(8,128)} %collective-permute-done.11.refs_1_, f32[2,576,128]{2,1,0:T(8,128)} %collective-permute-done.12.refs_2_, ...), custom_call_target="tpu_custom_call" | custom-call | flops 35389440 | bytes 5603328 | tf_op jit(solution)/shard_map/transport_first/pallas_call | solution.py:455
  120.1 9.0 %transport_first.5 = (f32[1,576,128]{2,1,0:T(8,128)}, f32[5,576,128]{2,1,0:T(8,128)}, f32[2,576,128]{2,1,0:T(8,128)}, f32[16,1024]{1,0:T(8,128)}) custom-call(s32[1]{0:T(128)} %bitcast.side_ref, f32[13824,128]{1,0:T(8,128)} %bitcast.10, f32[2,576,128]{2,1,0:T(8,128)} %collective-permute-done.8.refs_1_, f32[2,576,128]{2,1,0:T(8,128)} %collective-permute-done.9.refs_2_, ...), custom_call_target="tpu_custom_call" | custom-call | flops 35389440 | bytes 5603328 | tf_op jit(solution)/shard_map/transport_first/pallas_call | solution.py:455
  129.1 5.7 %transport_first.6 = (f32[1,576,128]{2,1,0:T(8,128)}, f32[5,576,128]{2,1,0:T(8,128)}, f32[2,576,128]{2,1,0:T(8,128)}, f32[16,1024]{1,0:T(8,128)}) custom-call(s32[1]{0:T(128)} %bitcast.side_ref, f32[13824,128]{1,0:T(8,128)} %bitcast.11, f32[2,288,128]{2,1,0:T(8,128)} %collective-permute-done.5.refs_1_, f32[2,288,128]{2,1,0:T(8,128)} %copy-done.5, ...), custom_call_target="tpu_custom_call" | custom-call | flops 17694720 | bytes 2801664 | tf_op jit(solution)/shard_map/transport_first/pallas_call | solution.py:455
  135.5 5.7 %transport_first.7 = (f32[1,576,128]{2,1,0:T(8,128)}, f32[5,576,128]{2,1,0:T(8,128)}, f32[2,576,128]{2,1,0:T(8,128)}, f32[16,1024]{1,0:T(8,128)}) custom-call(s32[1]{0:T(128)} %bitcast.side_ref, f32[13824,128]{1,0:T(8,128)} %bitcast.12, f32[2,288,128]{2,1,0:T(8,128)} %collective-permute-done.refs_1_, ...), custom_call_target="tpu_custom_call", output_to_operand_aliasing={{0}: (10, {}), {1}: (11, {}), {2}: (12, {})} | custom-call | flops 17694720 | bytes 2801664 | tf_op jit(solution)/shard_map/transport_first/pallas_call | solution.py:455
  141.7 1.5 collective-permute-start.15
  143.2 1.0 collective-permute-start.16
  144.2 0.8 slice_add_fusion
  145.1 1.7 collective-permute-done.15
  146.8 0.9 add_add_fusion.1
  147.7 2.1 collective-permute-start.21
  149.8 1.3 collective-permute-start.28
  151.1 1.3 collective-permute-start.26
  153.1 2.7 collective-permute-start.22
  155.8 1.9 collective-permute-start.29
  157.8 1.3 collective-permute-start.24
  159.1 24.5 %collective-permute-done.22.both_a_ref = f32[32,1024]{1,0:T(8,128)S(1)} collective-permute-done((f32[32,1024]{1,0:T(8,128)S(1)}, f32[32,1024]{1,0:T(8,128)S(1)}, u32[]{:S(2)}, u32[]{:S(2)}) %collective-permute-start.22) | collective-permute-done | bytes 131104 | tf_op jit(solution)/shard_map/ppermute | solution.py:799
  184.2 14.4 %collective-permute-start.27 = (f32[1,576,128]{2,1,0:T(8,128)}, f32[1,576,128]{2,1,0:T(8,128)}, u32[]{:S(2)}, u32[]{:S(2)}) collective-permute-start(f32[1,576,128]{2,1,0:T(8,128)} %get-tuple-element.75.refs_2_), channel_id=1, source_target_pairs={{2,0},{4,2},{1,3},{6,4},{3,5},{5,7},{10,8},{12,10},{9,11},{14,12},... | collective-permute-start | bytes 884744 | tf_op jit(solution)/shard_map/ppermute | solution.py:796
  198.7 0.7 copy-done.1
  199.4 1.5 collective-permute-start.25
  202.2 3.2 %shard_map.77 = (bf16[48,1408]{1,0:T(8,128)(2,1)}, f32[16,3072]{1,0:T(8,128)}) custom-call(s32[2]{0:T(128)} %pad_add_fusion.info_ref, f32[16,1024]{1,0:T(8,128)} %copy-done.4, f32[16,1024]{1,0:T(8,128)} %pad_maximum_fusion.home_own_ref, f32[32,1024]{1,0:T(8,128)} %copy-done.9, f32[32,1024]{1,0:T(8,128)} %copy-done.10, f32[16,8]{1,0:T(8,128)} %constant.49.clone.gram_ref, ...), custom_call_target="tpu_custom_call" | custom-call | flops 4000000 | bytes 1000000 | tf_op jit(solution)/shard_map/pallas_call | solution.py:675
  205.3 6.2 %transport_second.5 = (f32[4,1728,128]{2,1,0:T(8,128)}, f32[4,288,128]{2,1,0:T(8,128)}, f32[16,1024]{1,0:T(8,128)}) custom-call(s32[1]{0:T(128)} %bitcast.side_ref, bf16[3456,48]{1,0:T(8,128)(2,1)} %get-tuple-element.51.refs_0_.table_ref.refs_1_, bf16[48,1408]{1,0:T(8,128)(2,1)} %get-tuple-element.71.refs_1_, f32[1,576,128]{2,1,0:T(8,128)} %get-tuple-element.78.refs_2_, ...), custom_call_target="tpu_custom_call" | custom-call | flops 17694720 | bytes 2801664 | tf_op jit(solution)/shard_map/transport_second/pallas_call | solution.py:455
  211.5 6.2 %transport_second.6 = (f32[4,1728,128]{2,1,0:T(8,128)}, f32[4,288,128]{2,1,0:T(8,128)}, f32[16,1024]{1,0:T(8,128)}) custom-call(s32[1]{0:T(128)} %bitcast.side_ref, bf16[3456,48]{1,0:T(8,128)(2,1)} %get-tuple-element.51.refs_0_.table_ref.refs_1_, bf16[48,1408]{1,0:T(8,128)(2,1)} %get-tuple-element.71.refs_1_, ...), custom_call_target="tpu_custom_call", output_to_operand_aliasing={{0}: (12, {})} | custom-call | flops 17694720 | bytes 2801664 | tf_op jit(solution)/shard_map/transport_second/pallas_call | solution.py:455
  217.7 9.9 %transport_second.7 = (f32[4,1728,128]{2,1,0:T(8,128)}, f32[4,576,128]{2,1,0:T(8,128)}, f32[16,1024]{1,0:T(8,128)}) custom-call(s32[1]{0:T(128)} %bitcast.side_ref, bf16[3456,48]{1,0:T(8,128)(2,1)} %get-tuple-element.51.refs_0_.table_ref.refs_1_, bf16[48,1408]{1,0:T(8,128)(2,1)} %get-tuple-element.71.refs_1_, ...), custom_call_target="tpu_custom_call", output_to_operand_aliasing={{0}: (12, {})} | custom-call | flops 35389440 | bytes 5603328 | tf_op jit(solution)/shard_map/transport_second/pallas_call | solution.py:455
  228.4 6.2 %transport_second.8 = (f32[4,1728,128]{2,1,0:T(8,128)}, f32[4,288,128]{2,1,0:T(8,128)}, f32[16,1024]{1,0:T(8,128)}) custom-call(s32[1]{0:T(128)} %bitcast.side_ref, bf16[3456,48]{1,0:T(8,128)(2,1)} %get-tuple-element.51.refs_0_.table_ref.refs_1_, bf16[48,1408]{1,0:T(8,128)(2,1)} %get-tuple-element.71.refs_1_, ...), custom_call_target="tpu_custom_call", output_to_operand_aliasing={{0}: (12, {})} | custom-call | flops 17694720 | bytes 2801664 | tf_op jit(solution)/shard_map/transport_second/pallas_call | solution.py:455
  234.6 6.2 %transport_second.9 = (f32[4,1728,128]{2,1,0:T(8,128)}, f32[4,288,128]{2,1,0:T(8,128)}, f32[16,1024]{1,0:T(8,128)}) custom-call(s32[1]{0:T(128)} %bitcast.side_ref, bf16[3456,48]{1,0:T(8,128)(2,1)} %get-tuple-element.51.refs_0_.table_ref.refs_1_, bf16[48,1408]{1,0:T(8,128)(2,1)} %get-tuple-element.71.refs_1_, ...), custom_call_target="tpu_custom_call", output_to_operand_aliasing={{0}: (12, {})} | custom-call | flops 17694720 | bytes 2801664 | tf_op jit(solution)/shard_map/transport_second/pallas_call | solution.py:455
  240.8 1.1 collective-permute-start.32
  241.9 1.5 collective-permute-start.33
  243.4 1.4 collective-permute-done.31
  244.8 1.2 collective-permute-done.32
  246.0 0.9 add_add_fusion
  246.8 2.1 collective-permute-start.34
  248.9 7.2 %collective-permute-done.34 = f32[16,1024]{1,0:T(8,128)S(1)} collective-permute-done((f32[16,1024]{1,0:T(8,128)S(1)}, f32[16,1024]{1,0:T(8,128)S(1)}, u32[]{:S(2)}, u32[]{:S(2)}) %collective-permute-start.34) | collective-permute-done | bytes 65568 | tf_op jit(solution)/shard_map/ppermute | solution.py:790
  257.4 1.7 collective-permute-start.37
  259.2 1.3 collective-permute-done.35.sum_a_ref
  260.8 1.7 collective-permute-start.30
  262.5 11.1 %collective-permute-done.38.refs_2_ = f32[4,288,128]{2,1,0:T(8,128)S(1)} collective-permute-done((f32[4,288,128]{2,1,0:T(8,128)}, f32[4,288,128]{2,1,0:T(8,128)S(1)}, u32[]{:S(2)}, u32[]{:S(2)}) %collective-permute-start.38) | collective-permute-done | bytes 589856 | tf_op jit(solution)/shard_map/ppermute | solution.py:790
  273.6 12.7 %collective-permute-done.37.refs_1_ = f32[4,288,128]{2,1,0:T(8,128)} collective-permute-done((f32[4,288,128]{2,1,0:T(8,128)}, f32[4,288,128]{2,1,0:T(8,128)}, u32[]{:S(2)}, u32[]{:S(2)}) %collective-permute-start.37) | collective-permute-done | bytes 589856 | tf_op jit(solution)/shard_map/ppermute | solution.py:790
  286.3 7.7 %last_macro.1 = (f32[13824,128]{1,0:T(8,128)}, bf16[48,512]{1,0:T(8,128)(2,1)}, f32[5,4,128]{2,1,0:T(4,128)}) custom-call(s32[2]{0:T(128)} %pad_add_fusion.info_ref, f32[16,1024]{1,0:T(8,128)} %copy-done.8, f32[16,1024]{1,0:T(8,128)} %copy-done.12, f32[16,1024]{1,0:T(8,128)} %copy-done.13, f32[16,3072]{1,0:T(8,128)} %get-tuple-element.91.keep_ref, ...), custom_call_target="tpu_custom_call" | custom-call | flops 4000000 | bytes 11796480 | tf_op jit(solution)/shard_map/last_macro/pallas_call | solution.py:645
  294.1 4.9 %collective-permute-done.40.refs_0_ = f32[4,288,128]{2,1,0:T(8,128)} collective-permute-done((f32[4,288,128]{2,1,0:T(8,128)}, f32[4,288,128]{2,1,0:T(8,128)}, u32[]{:S(2)}, u32[]{:S(2)}) %collective-permute-start.40) | collective-permute-done | bytes 589856 | tf_op jit(solution)/shard_map/ppermute | solution.py:790
  299.0 2.1 finish.2.refs_3_
  301.1 7.7 %collective-permute-done.30.refs_0_ = f32[4,288,128]{2,1,0:T(8,128)} collective-permute-done((f32[4,288,128]{2,1,0:T(8,128)}, f32[4,288,128]{2,1,0:T(8,128)}, u32[]{:S(2)}, u32[]{:S(2)}) %collective-permute-start.30) | collective-permute-done | bytes 589856 | tf_op jit(solution)/shard_map/ppermute | solution.py:790
  308.8 2.1 finish.3
  (90 shorter events, 9.8 us)
Async XLA Ops:
  2.9 72.1 %collective-permute-start.12 = (f32[2,576,128]{2,1,0:T(8,128)}, f32[2,576,128]{2,1,0:T(8,128)}, u32[]{:S(2)}, u32[]{:S(2)}) collective-permute-start(f32[2,576,128]{2,1,0:T(8,128)} %get-tuple-element.62), channel_id=1, source_target_pairs={{0,1},{1,0},{2,3},{3,2},{4,5},{5,4},{6,7},{7,6},{8,9},{9,8},{10,11... | collective-permute-start | bytes 1769480 | tf_op jit(solution)/shard_map/ppermute | solution.py:790
  4.4 6.9 %copy-start.15 = (s32[4,128]{1,0:T(4,128)S(1)}, s32[4,128]{1,0:T(4,128)}, u32[]{:S(2)}) copy-start(s32[4,128]{1,0:T(4,128)} %param.7) | copy-start | bytes 6148
  4.4 6.9 %copy-start.11 = (f32[4,128]{1,0:T(4,128)S(1)}, f32[4,128]{1,0:T(4,128)}, u32[]{:S(2)}) copy-start(f32[4,128]{1,0:T(4,128)} %param.8) | copy-start | bytes 6148
  4.4 71.9 %collective-permute-start.11 = (f32[2,576,128]{2,1,0:T(8,128)}, f32[2,576,128]{2,1,0:T(8,128)}, u32[]{:S(2)}, u32[]{:S(2)}) collective-permute-start(f32[2,576,128]{2,1,0:T(8,128)} %get-tuple-element.61), channel_id=1, source_target_pairs={{0,1},{1,0},{2,3},{3,2},{4,5},{5,4},{6,7},{7,6},{8,9},{9,8},{10,11... | collective-permute-start | bytes 1769480 | tf_op jit(solution)/shard_map/ppermute | solution.py:790
  9.3 68.4 %collective-permute-start.9 = (f32[2,576,128]{2,1,0:T(8,128)}, f32[2,576,128]{2,1,0:T(8,128)}, u32[]{:S(2)}, u32[]{:S(2)}) collective-permute-start(f32[2,576,128]{2,1,0:T(8,128)} %get-tuple-element.60), channel_id=1, source_target_pairs={{0,1},{1,0},{2,3},{3,2},{4,5},{5,4},{6,7},{7,6},{8,9},{9,8},{10,11... | collective-permute-start | bytes 1769480 | tf_op jit(solution)/shard_map/ppermute | solution.py:790
  10.8 40.6 %collective-permute-start.6 = (f32[2,288,128]{2,1,0:T(8,128)}, f32[2,288,128]{2,1,0:T(8,128)S(1)}, u32[]{:S(2)}, u32[]{:S(2)}) collective-permute-start(f32[2,288,128]{2,1,0:T(8,128)} %get-tuple-element.58), channel_id=1, source_target_pairs={{0,1},{1,0},{2,3},{3,2},{4,5},{5,4},{6,7},{7,6},{8,9},{9,8},{10,11... | collective-permute-start | bytes 884744 | tf_op jit(solution)/shard_map/ppermute | solution.py:790
  11.3 38.5 %collective-permute-start.4 = (f32[8,128]{1,0:T(8,128)S(1)}, f32[8,128]{1,0:T(8,128)S(1)}, u32[]{:S(2)}, u32[]{:S(2)}) collective-permute-start(f32[8,128]{1,0:T(8,128)S(1)} %pad_maximum_fusion.3), channel_id=1, source_target_pairs={{0,1},{1,0},{2,3},{3,2},{4,5},{5,4},{6,7},{7,6},{8,9},{9,8},{10,11... | collective-permute-start | bytes 12296 | tf_op jit(solution)/shard_map/ppermute | solution.py:790
  49.8 10.2 %collective-permute-start.5 = (f32[2,288,128]{2,1,0:T(8,128)}, f32[2,288,128]{2,1,0:T(8,128)}, u32[]{:S(2)}, u32[]{:S(2)}) collective-permute-start(f32[2,288,128]{2,1,0:T(8,128)} %get-tuple-element.57), channel_id=1, source_target_pairs={{0,1},{1,0},{2,3},{3,2},{4,5},{5,4},{6,7},{7,6},{8,9},{9,8},{10,11... | collective-permute-start | bytes 884744 | tf_op jit(solution)/shard_map/ppermute | solution.py:790
  51.4 23.6 %copy-start.5 = (f32[2,288,128]{2,1,0:T(8,128)}, f32[2,288,128]{2,1,0:T(8,128)S(1)}, u32[]{:S(2)}) copy-start(f32[2,288,128]{2,1,0:T(8,128)S(1)} %collective-permute-done.6.refs_2_) | copy-start | bytes 884740
  51.4 20.2 %collective-permute-start.1 = (f32[2,288,128]{2,1,0:T(8,128)}, f32[2,288,128]{2,1,0:T(8,128)}, u32[]{:S(2)}, u32[]{:S(2)}) collective-permute-start(f32[2,288,128]{2,1,0:T(8,128)} %get-tuple-element.53), channel_id=1, source_target_pairs={{0,1},{1,0},{2,3},{3,2},{4,5},{5,4},{6,7},{7,6},{8,9},{9,8},{10,11... | collective-permute-start | bytes 884744 | tf_op jit(solution)/shard_map/ppermute | solution.py:790
  60.0 19.0 %collective-permute-start.8 = (f32[2,576,128]{2,1,0:T(8,128)}, f32[2,576,128]{2,1,0:T(8,128)}, u32[]{:S(2)}, u32[]{:S(2)}) collective-permute-start(f32[2,576,128]{2,1,0:T(8,128)} %get-tuple-element.59), channel_id=1, source_target_pairs={{0,1},{1,0},{2,3},{3,2},{4,5},{5,4},{6,7},{7,6},{8,9},{9,8},{10,11... | collective-permute-start | bytes 1769480 | tf_op jit(solution)/shard_map/ppermute | solution.py:790
  71.6 17.6 %collective-permute-start.3 = (f32[1728,128]{1,0:T(8,128)}, f32[1728,128]{1,0:T(8,128)}, u32[]{:S(2)}, u32[]{:S(2)}) collective-permute-start(f32[1728,128]{1,0:T(8,128)} %get-tuple-element.55), channel_id=1, source_target_pairs={{2,0},{4,2},{1,3},{6,4},{3,5},{5,7},{10,8},{12,10},{9,11},{14,12},... | collective-permute-start | bytes 2654216 | tf_op jit(solution)/shard_map/ppermute | solution.py:796
  75.0 11.8 %collective-permute-start.7 = (f32[2,288,128]{2,1,0:T(8,128)S(1)}, f32[2,288,128]{2,1,0:T(8,128)S(1)}, u32[]{:S(2)}, u32[]{:S(2)}) collective-permute-start(f32[2,288,128]{2,1,0:T(8,128)S(1)} %collective-permute-done.6.refs_2_), channel_id=1, source_target_pairs={{0,2},{2,4},{3,1},{4,6},{5,3},{7,5},{8,10},{10,12},{11,9},{12,14},... | collective-permute-start | bytes 884744 | tf_op jit(solution)/shard_map/ppermute | solution.py:793
  76.3 23.2 %collective-permute-start.13 = (f32[2,576,128]{2,1,0:T(8,128)}, f32[2,576,128]{2,1,0:T(8,128)}, u32[]{:S(2)}, u32[]{:S(2)}) collective-permute-start(f32[2,576,128]{2,1,0:T(8,128)} %collective-permute-done.12.refs_2_), channel_id=1, source_target_pairs={{0,2},{2,4},{3,1},{4,6},{5,3},{7,5},{8,10},{10,12},{11,9},{12,14},... | collective-permute-start | bytes 1769480 | tf_op jit(solution)/shard_map/ppermute | solution.py:793
  77.6 32.3 %collective-permute-start.10 = (f32[2,576,128]{2,1,0:T(8,128)}, f32[2,576,128]{2,1,0:T(8,128)}, u32[]{:S(2)}, u32[]{:S(2)}) collective-permute-start(f32[2,576,128]{2,1,0:T(8,128)} %collective-permute-done.9.refs_2_), channel_id=1, source_target_pairs={{0,2},{2,4},{3,1},{4,6},{5,3},{7,5},{8,10},{10,12},{11,9},{12,14},... | collective-permute-start | bytes 1769480 | tf_op jit(solution)/shard_map/ppermute | solution.py:793
  79.0 55.7 %collective-permute-start = (f32[2,288,128]{2,1,0:T(8,128)}, f32[2,288,128]{2,1,0:T(8,128)}, u32[]{:S(2)}, u32[]{:S(2)}) collective-permute-start(f32[2,288,128]{2,1,0:T(8,128)} %get-tuple-element.52), channel_id=1, source_target_pairs={{0,1},{1,0},{2,3},{3,2},{4,5},{5,4},{6,7},{7,6},{8,9},{9,8},{10,11... | collective-permute-start | bytes 884744 | tf_op jit(solution)/shard_map/ppermute | solution.py:790
  86.8 0.7 copy-start.6
  87.5 47.3 %collective-permute-start.2 = (f32[2,288,128]{2,1,0:T(8,128)}, f32[2,288,128]{2,1,0:T(8,128)S(1)}, u32[]{:S(2)}, u32[]{:S(2)}) collective-permute-start(f32[2,288,128]{2,1,0:T(8,128)} %collective-permute-done.1.refs_2_), channel_id=1, source_target_pairs={{0,2},{2,4},{3,1},{4,6},{5,3},{7,5},{8,10},{10,12},{11,9},{12,14},... | collective-permute-start | bytes 884744 | tf_op jit(solution)/shard_map/ppermute | solution.py:793
  89.2 54.0 %collective-permute-start.18 = (f32[16,512]{1,0:T(8,128)}, f32[16,512]{1,0:T(8,128)S(1)}, u32[]{:S(2)}, u32[]{:S(2)}) collective-permute-start(f32[16,512]{1,0:T(8,128)} %get-tuple-element.70), channel_id=1, source_target_pairs={{0,8},{8,16},{16,24},{24,0},{1,9},{9,17},{17,25},{25,1},{2,10},{10... | collective-permute-start | bytes 98312 | tf_op jit(solution)/shard_map/ppermute | solution.py:804
  99.5 44.7 %collective-permute-start.19 = (f32[16,512]{1,0:T(8,128)}, f32[16,512]{1,0:T(8,128)}, u32[]{:S(2)}, u32[]{:S(2)}) collective-permute-start(f32[16,512]{1,0:T(8,128)} %get-tuple-element.70), channel_id=1, source_target_pairs={{0,16},{8,24},{16,0},{24,8},{1,17},{9,25},{17,1},{25,9},{2,18},{10... | collective-permute-start | bytes 98312 | tf_op jit(solution)/shard_map/ppermute | solution.py:804
  109.9 34.2 %collective-permute-start.20 = (f32[16,512]{1,0:T(8,128)}, f32[16,512]{1,0:T(8,128)}, u32[]{:S(2)}, u32[]{:S(2)}) collective-permute-start(f32[16,512]{1,0:T(8,128)} %get-tuple-element.70), channel_id=1, source_target_pairs={{0,24},{8,0},{16,8},{24,16},{1,25},{9,1},{17,9},{25,17},{2,26},{10... | collective-permute-start | bytes 98312 | tf_op jit(solution)/shard_map/ppermute | solution.py:804
  134.8 0.7 copy-start.7
  135.5 8.7 %copy-start.14 = (f32[16,512]{1,0:T(8,128)S(1)}, f32[16,512]{1,0:T(8,128)}, u32[]{:S(2)}) copy-start(f32[16,512]{1,0:T(8,128)} %get-tuple-element.70) | copy-start | bytes 98308
  135.5 20.3 %copy-start = (f32[1,576,128]{2,1,0:T(8,128)S(1)}, f32[1,576,128]{2,1,0:T(8,128)}, u32[]{:S(2)}) copy-start(f32[1,576,128]{2,1,0:T(8,128)} %get-tuple-element.78.refs_2_) | copy-start | bytes 884740
  141.2 3.9 %collective-permute-start.14 = (f32[16,1024]{1,0:T(8,128)}, f32[16,1024]{1,0:T(8,128)S(1)}, u32[]{:S(2)}, u32[]{:S(2)}) collective-permute-start(f32[16,1024]{1,0:T(8,128)} %get-tuple-element.69), channel_id=1, source_target_pairs={{0,8},{8,16},{16,24},{24,0},{1,9},{9,17},{17,25},{25,1},{2,10},{10... | collective-permute-start | bytes 196616 | tf_op jit(solution)/shard_map/ppermute | solution.py:804
  141.7 5.0 %collective-permute-start.15 = (f32[16,1024]{1,0:T(8,128)}, f32[16,1024]{1,0:T(8,128)S(1)}, u32[]{:S(2)}, u32[]{:S(2)}) collective-permute-start(f32[16,1024]{1,0:T(8,128)} %get-tuple-element.69), channel_id=1, source_target_pairs={{0,16},{8,24},{16,0},{24,8},{1,17},{9,25},{17,1},{25,9},{2,18},{10... | collective-permute-start | bytes 196616 | tf_op jit(solution)/shard_map/ppermute | solution.py:804
  143.2 3.6 %collective-permute-start.16 = (f32[16,1024]{1,0:T(8,128)}, f32[16,1024]{1,0:T(8,128)S(1)}, u32[]{:S(2)}, u32[]{:S(2)}) collective-permute-start(f32[16,1024]{1,0:T(8,128)} %get-tuple-element.69), channel_id=1, source_target_pairs={{0,24},{8,0},{16,8},{24,16},{1,25},{9,1},{17,9},{25,17},{2,26},{10... | collective-permute-start | bytes 196616 | tf_op jit(solution)/shard_map/ppermute | solution.py:804
  147.6 5.0 %collective-permute-start.17 = (f32[16,1024]{1,0:T(8,128)S(1)}, f32[16,1024]{1,0:T(8,128)S(1)}, u32[]{:S(2)}, u32[]{:S(2)}) collective-permute-start(f32[16,1024]{1,0:T(8,128)S(1)} %add_add_fusion.1), channel_id=1, source_target_pairs={{0,1},{1,0},{2,3},{3,2},{4,5},{5,4},{6,7},{7,6},{8,9},{9,8},{10,11... | collective-permute-start | bytes 196616 | tf_op jit(solution)/shard_map/ppermute | solution.py:790
  147.7 5.3 %collective-permute-start.21 = (f32[16,512]{1,0:T(8,128)S(1)}, f32[16,512]{1,0:T(8,128)S(1)}, u32[]{:S(2)}, u32[]{:S(2)}) collective-permute-start(f32[16,512]{1,0:T(8,128)S(1)} %pad_maximum_fusion.1), channel_id=1, source_target_pairs={{0,1},{1,0},{2,3},{3,2},{4,5},{5,4},{6,7},{7,6},{8,9},{9,8},{10,11... | collective-permute-start | bytes 98312 | tf_op jit(solution)/shard_map/ppermute | solution.py:790
  149.8 55.5 %collective-permute-start.28 = (f32[2,576,128]{2,1,0:T(8,128)}, f32[2,576,128]{2,1,0:T(8,128)}, u32[]{:S(2)}, u32[]{:S(2)}) collective-permute-start(f32[2,576,128]{2,1,0:T(8,128)} %get-tuple-element.80.refs_4_), channel_id=1, source_target_pairs={{0,2},{2,4},{3,1},{4,6},{5,3},{7,5},{8,10},{10,12},{11,9},{12,14},... | collective-permute-start | bytes 1769480 | tf_op jit(solution)/shard_map/ppermute | solution.py:793
  151.1 66.6 %collective-permute-start.26 = (f32[2,576,128]{2,1,0:T(8,128)}, f32[2,576,128]{2,1,0:T(8,128)}, u32[]{:S(2)}, u32[]{:S(2)}) collective-permute-start(f32[2,576,128]{2,1,0:T(8,128)} %get-tuple-element.77.refs_4_), channel_id=1, source_target_pairs={{0,2},{2,4},{3,1},{4,6},{5,3},{7,5},{8,10},{10,12},{11,9},{12,14},... | collective-permute-start | bytes 1769480 | tf_op jit(solution)/shard_map/ppermute | solution.py:793
  152.7 49.5 %copy-start.4 = (f32[16,1024]{1,0:T(8,128)}, f32[16,1024]{1,0:T(8,128)S(1)}, u32[]{:S(2)}) copy-start(f32[16,1024]{1,0:T(8,128)S(1)} %add.49.sum_ref) | copy-start | bytes 196612
  153.1 30.5 %collective-permute-start.22 = (f32[32,1024]{1,0:T(8,128)S(1)}, f32[32,1024]{1,0:T(8,128)S(1)}, u32[]{:S(2)}, u32[]{:S(2)}) collective-permute-start(f32[32,1024]{1,0:T(8,128)S(1)} %maximum_maximum_fusion), channel_id=1, source_target_pairs={{0,2},{1,3},{2,0},{3,1},{4,6},{5,7},{6,4},{7,5},{8,10},{9,11},{10,... | collective-permute-start | bytes 393224 | tf_op jit(solution)/shard_map/ppermute | solution.py:799
  155.8 42.9 %collective-permute-start.29 = (f32[1,576,128]{2,1,0:T(8,128)S(1)}, f32[1,576,128]{2,1,0:T(8,128)S(1)}, u32[]{:S(2)}, u32[]{:S(2)}) collective-permute-start(f32[1,576,128]{2,1,0:T(8,128)S(1)} %copy-done), channel_id=1, source_target_pairs={{2,0},{4,2},{1,3},{6,4},{3,5},{5,7},{10,8},{12,10},{9,11},{14,12},... | collective-permute-start | bytes 884744 | tf_op jit(solution)/shard_map/ppermute | solution.py:796
  157.8 70.0 %collective-permute-start.24 = (f32[2,576,128]{2,1,0:T(8,128)}, f32[2,576,128]{2,1,0:T(8,128)}, u32[]{:S(2)}, u32[]{:S(2)}) collective-permute-start(f32[2,576,128]{2,1,0:T(8,128)} %get-tuple-element.74.refs_4_), channel_id=1, source_target_pairs={{0,2},{2,4},{3,1},{4,6},{5,3},{7,5},{8,10},{10,12},{11,9},{12,14},... | collective-permute-start | bytes 1769480 | tf_op jit(solution)/shard_map/ppermute | solution.py:793
  183.6 15.9 %copy-start.9 = (f32[32,1024]{1,0:T(8,128)}, f32[32,1024]{1,0:T(8,128)S(1)}, u32[]{:S(2)}) copy-start(f32[32,1024]{1,0:T(8,128)S(1)} %collective-permute-done.22.both_a_ref) | copy-start | bytes 393220
  183.6 0.7 collective-permute-start.23
  184.2 16.7 %copy-start.10 = (f32[32,1024]{1,0:T(8,128)}, f32[32,1024]{1,0:T(8,128)S(1)}, u32[]{:S(2)}) copy-start(f32[32,1024]{1,0:T(8,128)S(1)} %collective-permute-done.23.both_b_ref) | copy-start | bytes 393220
  184.2 33.5 %collective-permute-start.27 = (f32[1,576,128]{2,1,0:T(8,128)}, f32[1,576,128]{2,1,0:T(8,128)}, u32[]{:S(2)}, u32[]{:S(2)}) collective-permute-start(f32[1,576,128]{2,1,0:T(8,128)} %get-tuple-element.75.refs_2_), channel_id=1, source_target_pairs={{2,0},{4,2},{1,3},{6,4},{3,5},{5,7},{10,8},{12,10},{9,11},{14,12},... | collective-permute-start | bytes 884744 | tf_op jit(solution)/shard_map/ppermute | solution.py:796
  198.7 0.7 copy-start.1
  199.4 28.3 %collective-permute-start.25 = (f32[1,576,128]{2,1,0:T(8,128)}, f32[1,576,128]{2,1,0:T(8,128)S(1)}, u32[]{:S(2)}, u32[]{:S(2)}) collective-permute-start(f32[1,576,128]{2,1,0:T(8,128)} %get-tuple-element.72.refs_2_), channel_id=1, source_target_pairs={{2,0},{4,2},{1,3},{6,4},{3,5},{5,7},{10,8},{12,10},{9,11},{14,12},... | collective-permute-start | bytes 884744 | tf_op jit(solution)/shard_map/ppermute | solution.py:796
  227.6 58.7 %collective-permute-start.39 = (f32[4,576,128]{2,1,0:T(8,128)}, f32[4,576,128]{2,1,0:T(8,128)}, u32[]{:S(2)}, u32[]{:S(2)}) collective-permute-start(f32[4,576,128]{2,1,0:T(8,128)} %get-tuple-element.95), channel_id=1, source_target_pairs={{0,1},{1,0},{2,3},{3,2},{4,5},{5,4},{6,7},{7,6},{8,9},{9,8},{10,11... | collective-permute-start | bytes 3538952 | tf_op jit(solution)/shard_map/ppermute | solution.py:790
  227.7 0.7 copy-start.2
  240.8 4.0 %collective-permute-start.31 = (f32[16,1024]{1,0:T(8,128)}, f32[16,1024]{1,0:T(8,128)S(1)}, u32[]{:S(2)}, u32[]{:S(2)}) collective-permute-start(f32[16,1024]{1,0:T(8,128)} %get-tuple-element.90), channel_id=1, source_target_pairs={{0,8},{8,16},{16,24},{24,0},{1,9},{9,17},{17,25},{25,1},{2,10},{10... | collective-permute-start | bytes 196616 | tf_op jit(solution)/shard_map/ppermute | solution.py:804
  240.8 5.2 %collective-permute-start.32 = (f32[16,1024]{1,0:T(8,128)}, f32[16,1024]{1,0:T(8,128)S(1)}, u32[]{:S(2)}, u32[]{:S(2)}) collective-permute-start(f32[16,1024]{1,0:T(8,128)} %get-tuple-element.90), channel_id=1, source_target_pairs={{0,16},{8,24},{16,0},{24,8},{1,17},{9,25},{17,1},{25,9},{2,18},{10... | collective-permute-start | bytes 196616 | tf_op jit(solution)/shard_map/ppermute | solution.py:804
  241.9 4.1 %collective-permute-start.33 = (f32[16,1024]{1,0:T(8,128)}, f32[16,1024]{1,0:T(8,128)S(1)}, u32[]{:S(2)}, u32[]{:S(2)}) collective-permute-start(f32[16,1024]{1,0:T(8,128)} %get-tuple-element.90), channel_id=1, source_target_pairs={{0,24},{8,0},{16,8},{24,16},{1,25},{9,1},{17,9},{25,17},{2,26},{10... | collective-permute-start | bytes 196616 | tf_op jit(solution)/shard_map/ppermute | solution.py:804
  246.8 9.3 %collective-permute-start.34 = (f32[16,1024]{1,0:T(8,128)S(1)}, f32[16,1024]{1,0:T(8,128)S(1)}, u32[]{:S(2)}, u32[]{:S(2)}) collective-permute-start(f32[16,1024]{1,0:T(8,128)S(1)} %add_add_fusion), channel_id=1, source_target_pairs={{0,1},{1,0},{2,3},{3,2},{4,5},{5,4},{6,7},{7,6},{8,9},{9,8},{10,11... | collective-permute-start | bytes 196616 | tf_op jit(solution)/shard_map/ppermute | solution.py:790
  256.1 30.2 %copy-start.8 = (f32[16,1024]{1,0:T(8,128)}, f32[16,1024]{1,0:T(8,128)S(1)}, u32[]{:S(2)}) copy-start(f32[16,1024]{1,0:T(8,128)S(1)} %add.56.sum_ref) | copy-start | bytes 196612
  256.1 4.3 %collective-permute-start.35 = (f32[16,1024]{1,0:T(8,128)S(1)}, f32[16,1024]{1,0:T(8,128)S(1)}, u32[]{:S(2)}, u32[]{:S(2)}) collective-permute-start(f32[16,1024]{1,0:T(8,128)S(1)} %add.56.sum_ref), channel_id=1, source_target_pairs={{0,2},{1,3},{2,0},{3,1},{4,6},{5,7},{6,4},{7,5},{8,10},{9,11},{10,... | collective-permute-start | bytes 196616 | tf_op jit(solution)/shard_map/ppermute | solution.py:799
  256.4 4.3 %collective-permute-start.36 = (f32[16,1024]{1,0:T(8,128)S(1)}, f32[16,1024]{1,0:T(8,128)S(1)}, u32[]{:S(2)}, u32[]{:S(2)}) collective-permute-start(f32[16,1024]{1,0:T(8,128)S(1)} %add.56.sum_ref), channel_id=1, source_target_pairs={{2,4},{3,5},{4,2},{5,3},{10,12},{11,13},{12,10},{13,11},{18,20},{1... | collective-permute-start | bytes 196616 | tf_op jit(solution)/shard_map/ppermute | solution.py:799
  257.1 16.5 %collective-permute-start.38 = (f32[4,288,128]{2,1,0:T(8,128)}, f32[4,288,128]{2,1,0:T(8,128)S(1)}, u32[]{:S(2)}, u32[]{:S(2)}) collective-permute-start(f32[4,288,128]{2,1,0:T(8,128)} %get-tuple-element.94), channel_id=1, source_target_pairs={{0,1},{1,0},{2,3},{3,2},{4,5},{5,4},{6,7},{7,6},{8,9},{9,8},{10,11... | collective-permute-start | bytes 1769480 | tf_op jit(solution)/shard_map/ppermute | solution.py:790
  257.4 28.9 %collective-permute-start.37 = (f32[4,288,128]{2,1,0:T(8,128)}, f32[4,288,128]{2,1,0:T(8,128)}, u32[]{:S(2)}, u32[]{:S(2)}) collective-permute-start(f32[4,288,128]{2,1,0:T(8,128)} %get-tuple-element.93), channel_id=1, source_target_pairs={{0,1},{1,0},{2,3},{3,2},{4,5},{5,4},{6,7},{7,6},{8,9},{9,8},{10,11... | collective-permute-start | bytes 1769480 | tf_op jit(solution)/shard_map/ppermute | solution.py:790
  260.5 25.8 %copy-start.12 = (f32[16,1024]{1,0:T(8,128)}, f32[16,1024]{1,0:T(8,128)S(1)}, u32[]{:S(2)}) copy-start(f32[16,1024]{1,0:T(8,128)S(1)} %collective-permute-done.35.sum_a_ref) | copy-start | bytes 196612
  260.5 38.5 %collective-permute-start.40 = (f32[4,288,128]{2,1,0:T(8,128)}, f32[4,288,128]{2,1,0:T(8,128)}, u32[]{:S(2)}, u32[]{:S(2)}) collective-permute-start(f32[4,288,128]{2,1,0:T(8,128)} %get-tuple-element.97), channel_id=1, source_target_pairs={{0,1},{1,0},{2,3},{3,2},{4,5},{5,4},{6,7},{7,6},{8,9},{9,8},{10,11... | collective-permute-start | bytes 1769480 | tf_op jit(solution)/shard_map/ppermute | solution.py:790
  260.8 25.6 %copy-start.13 = (f32[16,1024]{1,0:T(8,128)}, f32[16,1024]{1,0:T(8,128)S(1)}, u32[]{:S(2)}) copy-start(f32[16,1024]{1,0:T(8,128)S(1)} %collective-permute-done.36.sum_b_ref) | copy-start | bytes 196612
  260.8 48.1 %collective-permute-start.30 = (f32[4,288,128]{2,1,0:T(8,128)}, f32[4,288,128]{2,1,0:T(8,128)}, u32[]{:S(2)}, u32[]{:S(2)}) collective-permute-start(f32[4,288,128]{2,1,0:T(8,128)} %get-tuple-element.89), channel_id=1, source_target_pairs={{0,1},{1,0},{2,3},{3,2},{4,5},{5,4},{6,7},{7,6},{8,9},{9,8},{10,11... | collective-permute-start | bytes 1769480 | tf_op jit(solution)/shard_map/ppermute | solution.py:790
  273.6 12.8 %copy-start.3 = (f32[4,288,128]{2,1,0:T(8,128)}, f32[4,288,128]{2,1,0:T(8,128)S(1)}, u32[]{:S(2)}) copy-start(f32[4,288,128]{2,1,0:T(8,128)S(1)} %collective-permute-done.38.refs_2_) | copy-start | bytes 1769476

commit v9 on v7

--- a/solution.py
+++ b/solution.py
@@ -23,7 +23,7 @@
 BF16 = jnp.bfloat16
 
 
-def params(limit=67043328):
+def params(limit=66584576):
     return pltpu.CompilerParams(vmem_limit_bytes=limit)
 
 
@@ -532,18 +532,19 @@
 
 
 def first_macro_kernel(
-    info_ref, sum_ref, sum_a_ref, sum_b_ref, near_ref, far_ref, gram_ref, mat_ref,
+    info_ref, sum_ref, home_own_ref, both_a_ref, both_b_ref, gram_ref, mat_ref,
     change_ref, keep_ref, span_ref, home_ref,
 ):
     side = info_ref[0]
     odd = info_ref[1]
     width = BLOCK_ROWS * LANES
     part = STRIP_ROWS * LANES
-    place_blocks(info_ref, span_ref, sum_ref[...], sum_a_ref[...], sum_b_ref[...])
-    for ref, where in ((near_ref, side), (far_ref, 1 - side)):
-        for index, block in enumerate((1, (1 - odd) * 2, odd * 2)):
+    place_blocks(info_ref, span_ref, sum_ref[...], both_a_ref[:16, :], both_b_ref[:16, :])
+    homes = (home_own_ref[...], both_a_ref[16:, :], both_b_ref[16:, :])
+    for block, both in zip((1, (1 - odd) * 2, odd * 2), homes):
+        for where, rows in ((side, both[:, :part]), (1 - side, both[:, part:])):
             spot = pl.multiple_of(block * width + where * part, part)
-            home_ref[:, pl.ds(spot, part)] = ref[index]
+            home_ref[:, pl.ds(spot, part)] = rows
     home = home_ref[...]
     rate = home[13:14, :]
     ratio = jnp.where(home[14:15, :] > 0.5, 1.0, rate)
@@ -674,7 +675,7 @@
         in_specs=[pl.BlockSpec(memory_space=pltpu.SMEM)] + [vmem] * len(args),
         out_specs=[vmem] * len(outs),
         scratch_shapes=scratch,
-        compiler_params=params(48 * 1024 * 1024),
+        compiler_params=params(),
         cost_estimate=pl.CostEstimate(flops=4000000, transcendentals=0, bytes_accessed=1000000),
     )(info, *args)
 
@@ -739,7 +740,7 @@
             out_specs=pl.BlockSpec((4 * size, LANES), lambda i, s: (place(i, s), 0)),
         ),
         input_output_aliases=aliases,
-        compiler_params=params(),
+        compiler_params=params(67043328),
         name="finish",
         cost_estimate=pl.CostEstimate(
             flops=2 * 48 * 4 * LANES * steps * size,
@@ -835,8 +836,7 @@
     home = jnp.concatenate(
         [home[:13], collision_rate.reshape(1, -1), wall.reshape(1, -1), jnp.zeros((1, rows * cols), F32)]
     )
-    near_home = jnp.stack([home, *both_z(home)])
-    far_home = swap(near_home)
+    home = jnp.concatenate([home, swap(home)], axis=1)
 
     width = BLOCK_ROWS * LANES
     sums = jnp.zeros((16, width), F32)
@@ -856,10 +856,10 @@
 
     total = sum_groups(sums)
     total = total + swap(total)
-    sum_a, sum_b = both_z(total)
+    both_a, both_b = both_z(jnp.concatenate([total, home]))
     change, keep = macro(
         first_macro_kernel, info,
-        [total, sum_a, sum_b, near_home, far_home, gram, mat],
+        [total, home, both_a, both_b, gram, mat],
         [
             jax.ShapeDtypeStruct((48, 11 * LANES), BF16),
             jax.ShapeDtypeStruct((16, SPAN * LANES), F32),

time: 284 us -> 268 us (0.944)
  waiting for transfers between devices: 111 us -> 104 us
  local copies, waits for them, and re-layouts: 8.13 us -> 2.11 us
  other arithmetic: 9 us -> 3.69 us
    ppermute x7, waiting for transfers between devices: 21.5 us -> 0.02 us  [with_flow(): return lax.ppermute(value, 'strip', down_pairs)]
    ppermute x19, waiting for transfers between devices: 73.5 us -> 88.2 us  [swap(): return lax.ppermute(value, 'strip', swap_pairs)]
    ppermute x3, starting transfers between devices: 9.63 us -> 13.1 us  [against_flow(): return lax.ppermute(value, 'strip', up_pairs)]
    unnamed x24 -> x26, local copies, waits for them, and re-layouts: 4.74 us -> 1.37 us
    ppermute x3 -> x2, starting transfers between devices: 5.82 us -> 3.79 us  [both_z(): lax.ppermute(value, 'strip', pair_a)]
    ppermute x3 -> x2, waiting for transfers between devices: 14 us -> 12.5 us  [both_z(): lax.ppermute(value, 'strip', pair_a)]
  transfers between devices with their start and end apart: 44 -> 42, of which waited for: 19 -> 13; matrix products, arithmetic and copies ran while one was open for 4% -> 2% of each run, Pallas kernels for 33% -> 35%
where the time goes in v9:
time: 268 us; the launch traced here: 264 us
  waiting for transfers between devices  104 us (39%)
  Pallas kernels  97.3 us (36%)
  starting transfers between devices  55.6 us (21%)
  other arithmetic  3.69 us (1%)
    ppermute x19, waiting for transfers between devices, swap(): return lax.ppermute(value, 'strip', swap_pairs)  88.2 us
    pallas_call x10, Pallas kernels, transport(): pl.pallas_call(functools.partial(transport_kernel, size, second_pass), ou...  65.9 us
    ppermute x19, starting transfers between devices, swap(): return lax.ppermute(value, 'strip', swap_pairs)  20.7 us
    ppermute x3, starting transfers between devices, against_flow(): return lax.ppermute(value, 'strip', up_pairs)  13.1 us
    ppermute x2, waiting for transfers between devices, both_z(): lax.ppermute(value, 'strip', pair_a)  12.5 us
    ppermute x7, starting transfers between devices, with_flow(): return lax.ppermute(value, 'strip', down_pairs)  8.98 us
    pallas_call x1, Pallas kernels, last_macro(): pl.pallas_call(functools.partial(last_kernel, size, half, blocks), out_sh...  7.73 us
    ppermute x9, starting transfers between devices, sum_groups(): lax.ppermute(value, 'vel', [(g, (g + shift) % groups) for g in range(grou...  7 us
  transfers between devices with their start and end apart: 42, of which 13 were waited for; matrix products, arithmetic and copies ran while one was open for 2% of the time, Pallas kernels for 35%

profile of v9, /device:TPU:24, one launch (start us, length us, event | category | flops | bytes accessed | tf_op | source)
XLA Modules:
  0.0 263.6 jit_solution(1570392183583846162)
XLA Ops:
  0.6 2.2 pack.3
  2.8 1.6 collective-permute-start.15
  4.4 4.0 %pack.2 = (f32[2,288,128]{2,1,0:T(8,128)}, f32[2,288,128]{2,1,0:T(8,128)}, f32[2,288,128]{2,1,0:T(8,128)}, f32[2,288,128]{2,1,0:T(8,128)}, f32[2,288,128]{2,1,0:...) custom-call(s32[1]{0:T(128)} %bitcast.side_ref, f32[13824,128]{1,0:T(8,128)} %bitcast.7), custom_call_target="tpu_custom_call" | custom-call | bytes 4718592 | tf_op jit(solution)/shard_map/pack/pallas_call | solution.py:149
  8.8 1.5 collective-permute-start.11
  11.0 1.5 collective-permute-start.9
  12.5 19.5 %collective-permute-done.4 = f32[8,128]{1,0:T(8,128)S(1)} collective-permute-done((f32[8,128]{1,0:T(8,128)S(1)}, f32[8,128]{1,0:T(8,128)S(1)}, u32[]{:S(2)}, u32[]{:S(2)}) %collective-permute-start.4) | collective-permute-done | bytes 4128 | tf_op jit(solution)/shard_map/ppermute | solution.py:786
  32.0 1.5 collective-permute-start.8
  33.5 3.9 %prepare.1 = (bf16[3456,48]{1,0:T(8,128)(2,1)}, f32[3456,8]{1,0:T(8,128)}, bf16[3456,32]{1,0:T(8,128)(2,1)}) custom-call(s32[3,3456]{1,0:T(4,128)} %vel_ref.1), custom_call_target="tpu_custom_call" | custom-call | flops 691200 | bytes 3456000 | tf_op jit(solution)/shard_map/prepare/pallas_call | solution.py:205
  37.4 6.2 %home_moments.1 = (f32[16,512]{1,0:T(8,128)}, f32[1728,128]{1,0:T(8,128)}) custom-call(s32[1]{0:T(128)} %bitcast.side_ref, f32[13824,128]{1,0:T(8,128)} %bitcast.8, bf16[3456,32]{1,0:T(8,128)(2,1)} %get-tuple-element.60.weight_ref.refs_6_.refs_8_), custom_call_target="tpu_custom_call" | custom-call | flops 226492416 | bytes 7077888 | tf_op jit(solution)/shard_map/home_moments/pallas_call | solution.py:263
  43.6 3.3 %collective-permute-start.3 = (f32[1728,128]{1,0:T(8,128)}, f32[1728,128]{1,0:T(8,128)}, u32[]{:S(2)}, u32[]{:S(2)}) collective-permute-start(f32[1728,128]{1,0:T(8,128)} %get-tuple-element.61), channel_id=1, source_target_pairs={{2,0},{4,2},{1,3},{6,4},{3,5},{5,7},{10,8},{12,10},{9,11},{14,12},... | collective-permute-start | bytes 2654216 | tf_op jit(solution)/shard_map/ppermute | solution.py:792
  47.0 2.1 collective-permute-start.14
  49.1 1.3 collective-permute-start.16
  50.5 6.5 %collective-permute-done.6.refs_2_ = f32[2,288,128]{2,1,0:T(8,128)S(1)} collective-permute-done((f32[2,288,128]{2,1,0:T(8,128)}, f32[2,288,128]{2,1,0:T(8,128)S(1)}, u32[]{:S(2)}, u32[]{:S(2)}) %collective-permute-start.6) | collective-permute-done | bytes 294944 | tf_op jit(solution)/shard_map/ppermute | solution.py:786
  57.0 1.3 collective-permute-start.13
  58.3 14.1 %collective-permute-done.1.refs_2_ = f32[2,288,128]{2,1,0:T(8,128)} collective-permute-done((f32[2,288,128]{2,1,0:T(8,128)}, f32[2,288,128]{2,1,0:T(8,128)}, u32[]{:S(2)}, u32[]{:S(2)}) %collective-permute-start.1) | collective-permute-done | bytes 294944 | tf_op jit(solution)/shard_map/ppermute | solution.py:786
  72.5 1.3 collective-permute-start.10
  73.8 2.5 collective-permute-start.5
  77.0 1.3 collective-permute-start.7
  78.3 1.3 collective-permute-start.2
  80.8 8.9 %transport_first.5 = (f32[1,1152,128]{2,1,0:T(8,128)}, f32[5,1152,128]{2,1,0:T(8,128)}, f32[2,1152,128]{2,1,0:T(8,128)}, f32[16,1024]{1,0:T(8,128)}) custom-call(s32[1]{0:T(128)} %bitcast.side_ref, f32[13824,128]{1,0:T(8,128)} %bitcast.9, f32[2,576,128]{2,1,0:T(8,128)} %collective-permute-done.14.refs_1_, f32[2,576,128]{2,1,0:T(8,128)} %collective-permute-done.15.refs_2_, ...), custom_call_target="tpu_custom_call" | custom-call | flops 35389440 | bytes 5603328 | tf_op jit(solution)/shard_map/transport_first/pallas_call | solution.py:452
  89.7 5.6 %transport_first.6 = (f32[1,1152,128]{2,1,0:T(8,128)}, f32[5,1152,128]{2,1,0:T(8,128)}, f32[2,1152,128]{2,1,0:T(8,128)}, f32[16,1024]{1,0:T(8,128)}) custom-call(s32[1]{0:T(128)} %bitcast.side_ref, f32[13824,128]{1,0:T(8,128)} %bitcast.10, ...), custom_call_target="tpu_custom_call", output_to_operand_aliasing={{0}: (10, {}), {1}: (11, {}), {2}: (12, {})} | custom-call | flops 17694720 | bytes 2801664 | tf_op jit(solution)/shard_map/transport_first/pallas_call | solution.py:452
  95.3 5.6 %transport_first.7 = (f32[1,1152,128]{2,1,0:T(8,128)}, f32[5,1152,128]{2,1,0:T(8,128)}, f32[2,1152,128]{2,1,0:T(8,128)}, f32[16,1024]{1,0:T(8,128)}) custom-call(s32[1]{0:T(128)} %bitcast.side_ref, f32[13824,128]{1,0:T(8,128)} %bitcast.11, ...), custom_call_target="tpu_custom_call", output_to_operand_aliasing={{0}: (10, {}), {1}: (11, {}), {2}: (12, {})} | custom-call | flops 17694720 | bytes 2801664 | tf_op jit(solution)/shard_map/transport_first/pallas_call | solution.py:452
  100.9 1.3 collective-permute-start.29
  102.3 1.6 collective-permute-start.22
  103.8 1.4 collective-permute-start.23
  105.2 5.6 %transport_first.8 = (f32[1,576,128]{2,1,0:T(8,128)}, f32[5,576,128]{2,1,0:T(8,128)}, f32[2,576,128]{2,1,0:T(8,128)}, f32[16,1024]{1,0:T(8,128)}) custom-call(s32[1]{0:T(128)} %bitcast.side_ref, f32[13824,128]{1,0:T(8,128)} %bitcast.12, f32[2,288,128]{2,1,0:T(8,128)} %collective-permute-done.5.refs_1_, f32[2,288,128]{2,1,0:T(8,128)} %copy-done.3, ...), custom_call_target="tpu_custom_call" | custom-call | flops 17694720 | bytes 2801664 | tf_op jit(solution)/shard_map/transport_first/pallas_call | solution.py:452
  110.8 5.6 %transport_first.9 = (f32[1,576,128]{2,1,0:T(8,128)}, f32[5,576,128]{2,1,0:T(8,128)}, f32[2,576,128]{2,1,0:T(8,128)}, f32[16,1024]{1,0:T(8,128)}) custom-call(s32[1]{0:T(128)} %bitcast.side_ref, f32[13824,128]{1,0:T(8,128)} %bitcast.13, f32[2,288,128]{2,1,0:T(8,128)} %collective-permute-done.refs_1_, ...), custom_call_target="tpu_custom_call", output_to_operand_aliasing={{0}: (10, {}), {1}: (11, {}), {2}: (12, {})} | custom-call | flops 17694720 | bytes 2801664 | tf_op jit(solution)/shard_map/transport_first/pallas_call | solution.py:452
  117.0 1.4 collective-permute-start.19
  118.5 6.6 %collective-permute-start.30 = (f32[1,1152,128]{2,1,0:T(8,128)}, f32[1,1152,128]{2,1,0:T(8,128)}, u32[]{:S(2)}, u32[]{:S(2)}) collective-permute-start(f32[1,1152,128]{2,1,0:T(8,128)} %get-tuple-element.90.refs_2_), channel_id=1, source_target_pairs={{2,0},{4,2},{1,3},{6,4},{3,5},{5,7},{10,8},{12,10},{9,11},{14,12},... | collective-permute-start | bytes 1769480 | tf_op jit(solution)/shard_map/ppermute | solution.py:792
  125.1 0.9 add_add_fusion.1
  126.0 2.5 collective-permute-start.20
  128.6 1.3 collective-permute-start.27
  129.9 1.4 collective-permute-done.20
  131.3 1.1 collective-permute-done.24
  132.5 0.8 collective-permute-start.25
  133.3 3.2 %collective-permute-start.28 = (f32[1,576,128]{2,1,0:T(8,128)}, f32[1,576,128]{2,1,0:T(8,128)S(1)}, u32[]{:S(2)}, u32[]{:S(2)}) collective-permute-start(f32[1,576,128]{2,1,0:T(8,128)} %get-tuple-element.87.refs_2_), channel_id=1, source_target_pairs={{2,0},{4,2},{1,3},{6,4},{3,5},{5,7},{10,8},{12,10},{9,11},{14,12},... | collective-permute-start | bytes 884744 | tf_op jit(solution)/shard_map/ppermute | solution.py:792
  136.5 12.5 %collective-permute-done.25.both_a_ref = f32[32,1024]{1,0:T(8,128)S(1)} collective-permute-done((f32[32,1024]{1,0:T(8,128)S(1)}, f32[32,1024]{1,0:T(8,128)S(1)}, u32[]{:S(2)}, u32[]{:S(2)}) %collective-permute-start.25) | collective-permute-done | bytes 131104 | tf_op jit(solution)/shard_map/ppermute | solution.py:795
  149.0 1.3 collective-permute-start.26
  151.6 3.2 %shard_map.77 = (bf16[48,1408]{1,0:T(8,128)(2,1)}, f32[16,3072]{1,0:T(8,128)}) custom-call(s32[2]{0:T(128)} %pad_add_fusion.info_ref, f32[16,1024]{1,0:T(8,128)} %copy-done.2, f32[16,1024]{1,0:T(8,128)} %pad_maximum_fusion.home_own_ref, f32[32,1024]{1,0:T(8,128)} %copy-done.7, f32[32,1024]{1,0:T(8,128)} %collective-permute-done.26.both_b_ref, ...), custom_call_target="tpu_custom_call" | custom-call | flops 4000000 | bytes 1000000 | tf_op jit(solution)/shard_map/pallas_call | solution.py:672
  154.8 6.2 %transport_second.5 = (f32[4,1728,128]{2,1,0:T(8,128)}, f32[4,288,128]{2,1,0:T(8,128)}, f32[16,1024]{1,0:T(8,128)}) custom-call(s32[1]{0:T(128)} %bitcast.side_ref, bf16[3456,48]{1,0:T(8,128)(2,1)} %get-tuple-element.57.refs_0_.table_ref.refs_1_, bf16[48,1408]{1,0:T(8,128)(2,1)} %get-tuple-element.86.refs_1_, f32[1,1152,128]{2,1,0:T(8,128)} %get-tuple-element.90.refs_2_, ...), custom_call_target="tpu_custom_call" | custom-call | flops 17694720 | bytes 2801664 | tf_op jit(solution)/shard_map/transport_second/pallas_call | solution.py:452
  161.0 6.2 %transport_second.6 = (f32[4,1728,128]{2,1,0:T(8,128)}, f32[4,288,128]{2,1,0:T(8,128)}, f32[16,1024]{1,0:T(8,128)}) custom-call(s32[1]{0:T(128)} %bitcast.side_ref, bf16[3456,48]{1,0:T(8,128)(2,1)} %get-tuple-element.57.refs_0_.table_ref.refs_1_, bf16[48,1408]{1,0:T(8,128)(2,1)} %get-tuple-element.86.refs_1_, ...), custom_call_target="tpu_custom_call", output_to_operand_aliasing={{0}: (12, {})} | custom-call | flops 17694720 | bytes 2801664 | tf_op jit(solution)/shard_map/transport_second/pallas_call | solution.py:452
  167.2 9.9 %transport_second.7 = (f32[4,1728,128]{2,1,0:T(8,128)}, f32[4,576,128]{2,1,0:T(8,128)}, f32[16,1024]{1,0:T(8,128)}) custom-call(s32[1]{0:T(128)} %bitcast.side_ref, bf16[3456,48]{1,0:T(8,128)(2,1)} %get-tuple-element.57.refs_0_.table_ref.refs_1_, bf16[48,1408]{1,0:T(8,128)(2,1)} %get-tuple-element.86.refs_1_, ...), custom_call_target="tpu_custom_call", output_to_operand_aliasing={{0}: (12, {})} | custom-call | flops 35389440 | bytes 5603328 | tf_op jit(solution)/shard_map/transport_second/pallas_call | solution.py:452
  177.2 0.7 copy-done
  177.9 6.2 %transport_second.8 = (f32[4,1728,128]{2,1,0:T(8,128)}, f32[4,288,128]{2,1,0:T(8,128)}, f32[16,1024]{1,0:T(8,128)}) custom-call(s32[1]{0:T(128)} %bitcast.side_ref, bf16[3456,48]{1,0:T(8,128)(2,1)} %get-tuple-element.57.refs_0_.table_ref.refs_1_, bf16[48,1408]{1,0:T(8,128)(2,1)} %get-tuple-element.86.refs_1_, ...), custom_call_target="tpu_custom_call", output_to_operand_aliasing={{0}: (12, {})} | custom-call | flops 17694720 | bytes 2801664 | tf_op jit(solution)/shard_map/transport_second/pallas_call | solution.py:452
  184.1 6.2 %transport_second.9 = (f32[4,1728,128]{2,1,0:T(8,128)}, f32[4,288,128]{2,1,0:T(8,128)}, f32[16,1024]{1,0:T(8,128)}) custom-call(s32[1]{0:T(128)} %bitcast.side_ref, bf16[3456,48]{1,0:T(8,128)(2,1)} %get-tuple-element.57.refs_0_.table_ref.refs_1_, bf16[48,1408]{1,0:T(8,128)(2,1)} %get-tuple-element.86.refs_1_, ...), custom_call_target="tpu_custom_call", output_to_operand_aliasing={{0}: (12, {})} | custom-call | flops 17694720 | bytes 2801664 | tf_op jit(solution)/shard_map/transport_second/pallas_call | solution.py:452
  190.8 1.5 collective-permute-start.34
  192.3 2.0 collective-permute-done.32
  194.3 1.2 collective-permute-done.33
  195.5 0.9 add_add_fusion
  196.3 2.1 collective-permute-start.35
  198.4 7.7 %collective-permute-done.35 = f32[16,1024]{1,0:T(8,128)S(1)} collective-permute-done((f32[16,1024]{1,0:T(8,128)S(1)}, f32[16,1024]{1,0:T(8,128)S(1)}, u32[]{:S(2)}, u32[]{:S(2)}) %collective-permute-start.35) | collective-permute-done | bytes 65568 | tf_op jit(solution)/shard_map/ppermute | solution.py:786
  206.1 3.0 %collective-permute-start.36 = (f32[16,1024]{1,0:T(8,128)S(1)}, f32[16,1024]{1,0:T(8,128)S(1)}, u32[]{:S(2)}, u32[]{:S(2)}) collective-permute-start(f32[16,1024]{1,0:T(8,128)S(1)} %add.56.sum_ref), channel_id=1, source_target_pairs={{0,2},{1,3},{2,0},{3,1},{4,6},{5,7},{6,4},{7,5},{8,10},{9,11},{10,... | collective-permute-start | bytes 196616 | tf_op jit(solution)/shard_map/ppermute | solution.py:795
  209.1 0.7 collective-permute-start.37
  209.7 1.3 collective-permute-start.39
  211.1 0.7 collective-permute-start.38
  211.8 1.3 collective-permute-start.41
  213.1 0.7 collective-permute-start.31
  213.9 12.3 %collective-permute-done.39.refs_2_ = f32[4,288,128]{2,1,0:T(8,128)S(1)} collective-permute-done((f32[4,288,128]{2,1,0:T(8,128)}, f32[4,288,128]{2,1,0:T(8,128)S(1)}, u32[]{:S(2)}, u32[]{:S(2)}) %collective-permute-start.39) | collective-permute-done | bytes 589856 | tf_op jit(solution)/shard_map/ppermute | solution.py:786
  226.2 12.7 %collective-permute-done.38.refs_1_ = f32[4,288,128]{2,1,0:T(8,128)} collective-permute-done((f32[4,288,128]{2,1,0:T(8,128)}, f32[4,288,128]{2,1,0:T(8,128)}, u32[]{:S(2)}, u32[]{:S(2)}) %collective-permute-start.38) | collective-permute-done | bytes 589856 | tf_op jit(solution)/shard_map/ppermute | solution.py:786
  239.0 7.7 %last_macro.1 = (f32[13824,128]{1,0:T(8,128)}, bf16[48,512]{1,0:T(8,128)(2,1)}, f32[5,4,128]{2,1,0:T(4,128)}) custom-call(s32[2]{0:T(128)} %pad_add_fusion.info_ref, f32[16,1024]{1,0:T(8,128)} %copy-done.6, f32[16,1024]{1,0:T(8,128)} %copy-done.9, f32[16,1024]{1,0:T(8,128)} %copy-done.10, f32[16,3072]{1,0:T(8,128)} %get-tuple-element.103.keep_ref, ...), custom_call_target="tpu_custom_call" | custom-call | flops 4000000 | bytes 11796480 | tf_op jit(solution)/shard_map/last_macro/pallas_call | solution.py:642
  246.7 4.9 %collective-permute-done.41.refs_0_ = f32[4,288,128]{2,1,0:T(8,128)} collective-permute-done((f32[4,288,128]{2,1,0:T(8,128)}, f32[4,288,128]{2,1,0:T(8,128)}, u32[]{:S(2)}, u32[]{:S(2)}) %collective-permute-start.41) | collective-permute-done | bytes 589856 | tf_op jit(solution)/shard_map/ppermute | solution.py:786
  251.6 2.1 finish.2.refs_3_
  253.7 7.8 %collective-permute-done.31.refs_0_ = f32[4,288,128]{2,1,0:T(8,128)} collective-permute-done((f32[4,288,128]{2,1,0:T(8,128)}, f32[4,288,128]{2,1,0:T(8,128)}, u32[]{:S(2)}, u32[]{:S(2)}) %collective-permute-start.31) | collective-permute-done | bytes 589856 | tf_op jit(solution)/shard_map/ppermute | solution.py:786
  261.5 2.1 finish.3
  (87 shorter events, 6.1 us)
Async XLA Ops:
  2.8 7.5 %copy-start.12 = (s32[4,128]{1,0:T(4,128)S(1)}, s32[4,128]{1,0:T(4,128)}, u32[]{:S(2)}) copy-start(s32[4,128]{1,0:T(4,128)} %param.7) | copy-start | bytes 6148
  2.8 7.5 %copy-start.8 = (f32[4,128]{1,0:T(4,128)S(1)}, f32[4,128]{1,0:T(4,128)}, u32[]{:S(2)}) copy-start(f32[4,128]{1,0:T(4,128)} %param.8) | copy-start | bytes 6148
  2.8 46.3 %collective-permute-start.15 = (f32[2,576,128]{2,1,0:T(8,128)}, f32[2,576,128]{2,1,0:T(8,128)}, u32[]{:S(2)}, u32[]{:S(2)}) collective-permute-start(f32[2,576,128]{2,1,0:T(8,128)} %get-tuple-element.70), channel_id=1, source_target_pairs={{0,1},{1,0},{2,3},{3,2},{4,5},{5,4},{6,7},{7,6},{8,9},{9,8},{10,11... | collective-permute-start | bytes 1769480 | tf_op jit(solution)/shard_map/ppermute | solution.py:786
  8.3 35.3 %collective-permute-start.12 = (f32[2,288,128]{2,1,0:T(8,128)}, f32[2,288,128]{2,1,0:T(8,128)S(1)}, u32[]{:S(2)}, u32[]{:S(2)}) collective-permute-start(f32[2,288,128]{2,1,0:T(8,128)} %get-tuple-element.68), channel_id=1, source_target_pairs={{0,1},{1,0},{2,3},{3,2},{4,5},{5,4},{6,7},{7,6},{8,9},{9,8},{10,11... | collective-permute-start | bytes 884744 | tf_op jit(solution)/shard_map/ppermute | solution.py:786
  8.8 38.1 %collective-permute-start.11 = (f32[2,288,128]{2,1,0:T(8,128)}, f32[2,288,128]{2,1,0:T(8,128)}, u32[]{:S(2)}, u32[]{:S(2)}) collective-permute-start(f32[2,288,128]{2,1,0:T(8,128)} %get-tuple-element.67), channel_id=1, source_target_pairs={{0,1},{1,0},{2,3},{3,2},{4,5},{5,4},{6,7},{7,6},{8,9},{9,8},{10,11... | collective-permute-start | bytes 884744 | tf_op jit(solution)/shard_map/ppermute | solution.py:786
  10.4 21.6 %collective-permute-start.4 = (f32[8,128]{1,0:T(8,128)S(1)}, f32[8,128]{1,0:T(8,128)S(1)}, u32[]{:S(2)}, u32[]{:S(2)}) collective-permute-start(f32[8,128]{1,0:T(8,128)S(1)} %pad_maximum_fusion.3), channel_id=1, source_target_pairs={{0,1},{1,0},{2,3},{3,2},{4,5},{5,4},{6,7},{7,6},{8,9},{9,8},{10,11... | collective-permute-start | bytes 12296 | tf_op jit(solution)/shard_map/ppermute | solution.py:786
  11.0 36.0 %collective-permute-start.9 = (f32[2,288,128]{2,1,0:T(8,128)}, f32[2,288,128]{2,1,0:T(8,128)}, u32[]{:S(2)}, u32[]{:S(2)}) collective-permute-start(f32[2,288,128]{2,1,0:T(8,128)} %get-tuple-element.66), channel_id=1, source_target_pairs={{0,1},{1,0},{2,3},{3,2},{4,5},{5,4},{6,7},{7,6},{8,9},{9,8},{10,11... | collective-permute-start | bytes 884744 | tf_op jit(solution)/shard_map/ppermute | solution.py:786
  32.0 17.0 %collective-permute-start.8 = (f32[2,288,128]{2,1,0:T(8,128)}, f32[2,288,128]{2,1,0:T(8,128)}, u32[]{:S(2)}, u32[]{:S(2)}) collective-permute-start(f32[2,288,128]{2,1,0:T(8,128)} %get-tuple-element.65), channel_id=1, source_target_pairs={{0,1},{1,0},{2,3},{3,2},{4,5},{5,4},{6,7},{7,6},{8,9},{9,8},{10,11... | collective-permute-start | bytes 884744 | tf_op jit(solution)/shard_map/ppermute | solution.py:786
  43.6 3.3 %copy-start.4 = (f32[2,288,128]{2,1,0:T(8,128)}, f32[2,288,128]{2,1,0:T(8,128)S(1)}, u32[]{:S(2)}) copy-start(f32[2,288,128]{2,1,0:T(8,128)S(1)} %collective-permute-done.12.refs_2_) | copy-start | bytes 884740
  43.6 33.4 %collective-permute-start.3 = (f32[1728,128]{1,0:T(8,128)}, f32[1728,128]{1,0:T(8,128)}, u32[]{:S(2)}, u32[]{:S(2)}) collective-permute-start(f32[1728,128]{1,0:T(8,128)} %get-tuple-element.61), channel_id=1, source_target_pairs={{2,0},{4,2},{1,3},{6,4},{3,5},{5,7},{10,8},{12,10},{9,11},{14,12},... | collective-permute-start | bytes 2654216 | tf_op jit(solution)/shard_map/ppermute | solution.py:792
  46.9 10.1 %collective-permute-start.6 = (f32[2,288,128]{2,1,0:T(8,128)}, f32[2,288,128]{2,1,0:T(8,128)S(1)}, u32[]{:S(2)}, u32[]{:S(2)}) collective-permute-start(f32[2,288,128]{2,1,0:T(8,128)} %get-tuple-element.64), channel_id=1, source_target_pairs={{0,1},{1,0},{2,3},{3,2},{4,5},{5,4},{6,7},{7,6},{8,9},{9,8},{10,11... | collective-permute-start | bytes 884744 | tf_op jit(solution)/shard_map/ppermute | solution.py:786
  47.0 26.8 %collective-permute-start.14 = (f32[2,576,128]{2,1,0:T(8,128)}, f32[2,576,128]{2,1,0:T(8,128)}, u32[]{:S(2)}, u32[]{:S(2)}) collective-permute-start(f32[2,576,128]{2,1,0:T(8,128)} %get-tuple-element.69), channel_id=1, source_target_pairs={{0,1},{1,0},{2,3},{3,2},{4,5},{5,4},{6,7},{7,6},{8,9},{9,8},{10,11... | collective-permute-start | bytes 1769480 | tf_op jit(solution)/shard_map/ppermute | solution.py:786
  49.0 23.4 %collective-permute-start.1 = (f32[2,288,128]{2,1,0:T(8,128)}, f32[2,288,128]{2,1,0:T(8,128)}, u32[]{:S(2)}, u32[]{:S(2)}) collective-permute-start(f32[2,288,128]{2,1,0:T(8,128)} %get-tuple-element.59), channel_id=1, source_target_pairs={{0,1},{1,0},{2,3},{3,2},{4,5},{5,4},{6,7},{7,6},{8,9},{9,8},{10,11... | collective-permute-start | bytes 884744 | tf_op jit(solution)/shard_map/ppermute | solution.py:786
  49.1 29.1 %collective-permute-start.16 = (f32[2,576,128]{2,1,0:T(8,128)}, f32[2,576,128]{2,1,0:T(8,128)}, u32[]{:S(2)}, u32[]{:S(2)}) collective-permute-start(f32[2,576,128]{2,1,0:T(8,128)} %collective-permute-done.15.refs_2_), channel_id=1, source_target_pairs={{0,2},{2,4},{3,1},{4,6},{5,3},{7,5},{8,10},{10,12},{11,9},{12,14},... | collective-permute-start | bytes 1769480 | tf_op jit(solution)/shard_map/ppermute | solution.py:789
  57.0 32.7 %copy-start.3 = (f32[2,288,128]{2,1,0:T(8,128)}, f32[2,288,128]{2,1,0:T(8,128)S(1)}, u32[]{:S(2)}) copy-start(f32[2,288,128]{2,1,0:T(8,128)S(1)} %collective-permute-done.6.refs_2_) | copy-start | bytes 884740
  57.0 19.2 %collective-permute-start.13 = (f32[2,288,128]{2,1,0:T(8,128)}, f32[2,288,128]{2,1,0:T(8,128)S(1)}, u32[]{:S(2)}, u32[]{:S(2)}) collective-permute-start(f32[2,288,128]{2,1,0:T(8,128)} %copy-done.4), channel_id=1, source_target_pairs={{0,2},{2,4},{3,1},{4,6},{5,3},{7,5},{8,10},{10,12},{11,9},{12,14},... | collective-permute-start | bytes 884744 | tf_op jit(solution)/shard_map/ppermute | solution.py:789
  72.5 22.8 %collective-permute-start.10 = (f32[2,288,128]{2,1,0:T(8,128)}, f32[2,288,128]{2,1,0:T(8,128)}, u32[]{:S(2)}, u32[]{:S(2)}) collective-permute-start(f32[2,288,128]{2,1,0:T(8,128)} %collective-permute-done.9.refs_2_), channel_id=1, source_target_pairs={{0,2},{2,4},{3,1},{4,6},{5,3},{7,5},{8,10},{10,12},{11,9},{12,14},... | collective-permute-start | bytes 884744 | tf_op jit(solution)/shard_map/ppermute | solution.py:789
  73.8 28.4 %collective-permute-start.5 = (f32[2,288,128]{2,1,0:T(8,128)}, f32[2,288,128]{2,1,0:T(8,128)}, u32[]{:S(2)}, u32[]{:S(2)}) collective-permute-start(f32[2,288,128]{2,1,0:T(8,128)} %get-tuple-element.63), channel_id=1, source_target_pairs={{0,1},{1,0},{2,3},{3,2},{4,5},{5,4},{6,7},{7,6},{8,9},{9,8},{10,11... | collective-permute-start | bytes 884744 | tf_op jit(solution)/shard_map/ppermute | solution.py:786
  76.2 0.7 copy-start.5
  76.2 26.0 %collective-permute-start = (f32[2,288,128]{2,1,0:T(8,128)}, f32[2,288,128]{2,1,0:T(8,128)}, u32[]{:S(2)}, u32[]{:S(2)}) collective-permute-start(f32[2,288,128]{2,1,0:T(8,128)} %get-tuple-element.58), channel_id=1, source_target_pairs={{0,1},{1,0},{2,3},{3,2},{4,5},{5,4},{6,7},{7,6},{8,9},{9,8},{10,11... | collective-permute-start | bytes 884744 | tf_op jit(solution)/shard_map/ppermute | solution.py:786
  77.0 26.8 %collective-permute-start.7 = (f32[2,288,128]{2,1,0:T(8,128)S(1)}, f32[2,288,128]{2,1,0:T(8,128)}, u32[]{:S(2)}, u32[]{:S(2)}) collective-permute-start(f32[2,288,128]{2,1,0:T(8,128)S(1)} %collective-permute-done.6.refs_2_), channel_id=1, source_target_pairs={{0,2},{2,4},{3,1},{4,6},{5,3},{7,5},{8,10},{10,12},{11,9},{12,14},... | collective-permute-start | bytes 884744 | tf_op jit(solution)/shard_map/ppermute | solution.py:789
  78.3 32.6 %collective-permute-start.2 = (f32[2,288,128]{2,1,0:T(8,128)}, f32[2,288,128]{2,1,0:T(8,128)}, u32[]{:S(2)}, u32[]{:S(2)}) collective-permute-start(f32[2,288,128]{2,1,0:T(8,128)} %collective-permute-done.1.refs_2_), channel_id=1, source_target_pairs={{0,2},{2,4},{3,1},{4,6},{5,3},{7,5},{8,10},{10,12},{11,9},{12,14},... | collective-permute-start | bytes 884744 | tf_op jit(solution)/shard_map/ppermute | solution.py:789
  95.3 6.9 %copy-start.11 = (f32[16,512]{1,0:T(8,128)S(1)}, f32[16,512]{1,0:T(8,128)}, u32[]{:S(2)}) copy-start(f32[16,512]{1,0:T(8,128)} %get-tuple-element.85) | copy-start | bytes 98308
  100.9 53.9 %collective-permute-start.29 = (f32[2,1152,128]{2,1,0:T(8,128)}, f32[2,1152,128]{2,1,0:T(8,128)}, u32[]{:S(2)}, u32[]{:S(2)}) collective-permute-start(f32[2,1152,128]{2,1,0:T(8,128)} %get-tuple-element.92.refs_4_), channel_id=1, source_target_pairs={{0,2},{2,4},{3,1},{4,6},{5,3},{7,5},{8,10},{10,12},{11,9},{12,14},... | collective-permute-start | bytes 3538952 | tf_op jit(solution)/shard_map/ppermute | solution.py:789
  102.2 14.3 %collective-permute-start.21 = (f32[16,512]{1,0:T(8,128)S(1)}, f32[16,512]{1,0:T(8,128)S(1)}, u32[]{:S(2)}, u32[]{:S(2)}) collective-permute-start(f32[16,512]{1,0:T(8,128)S(1)} %copy-done.11), channel_id=1, source_target_pairs={{0,8},{8,16},{16,24},{24,0},{1,9},{9,17},{17,25},{25,1},{2,10},{10... | collective-permute-start | bytes 98312 | tf_op jit(solution)/shard_map/ppermute | solution.py:800
  102.3 14.8 %collective-permute-start.22 = (f32[16,512]{1,0:T(8,128)S(1)}, f32[16,512]{1,0:T(8,128)S(1)}, u32[]{:S(2)}, u32[]{:S(2)}) collective-permute-start(f32[16,512]{1,0:T(8,128)S(1)} %copy-done.11), channel_id=1, source_target_pairs={{0,16},{8,24},{16,0},{24,8},{1,17},{9,25},{17,1},{25,9},{2,18},{10... | collective-permute-start | bytes 98312 | tf_op jit(solution)/shard_map/ppermute | solution.py:800
  103.8 14.6 %collective-permute-start.23 = (f32[16,512]{1,0:T(8,128)S(1)}, f32[16,512]{1,0:T(8,128)S(1)}, u32[]{:S(2)}, u32[]{:S(2)}) collective-permute-start(f32[16,512]{1,0:T(8,128)S(1)} %copy-done.11), channel_id=1, source_target_pairs={{0,24},{8,0},{16,8},{24,16},{1,25},{9,1},{17,9},{25,17},{2,26},{10... | collective-permute-start | bytes 98312 | tf_op jit(solution)/shard_map/ppermute | solution.py:800
  116.4 8.7 %collective-permute-start.17 = (f32[16,1024]{1,0:T(8,128)}, f32[16,1024]{1,0:T(8,128)S(1)}, u32[]{:S(2)}, u32[]{:S(2)}) collective-permute-start(f32[16,1024]{1,0:T(8,128)} %get-tuple-element.84), channel_id=1, source_target_pairs={{0,8},{8,16},{16,24},{24,0},{1,9},{9,17},{17,25},{25,1},{2,10},{10... | collective-permute-start | bytes 196616 | tf_op jit(solution)/shard_map/ppermute | solution.py:800
  116.4 8.7 %collective-permute-start.18 = (f32[16,1024]{1,0:T(8,128)}, f32[16,1024]{1,0:T(8,128)S(1)}, u32[]{:S(2)}, u32[]{:S(2)}) collective-permute-start(f32[16,1024]{1,0:T(8,128)} %get-tuple-element.84), channel_id=1, source_target_pairs={{0,16},{8,24},{16,0},{24,8},{1,17},{9,25},{17,1},{25,9},{2,18},{10... | collective-permute-start | bytes 196616 | tf_op jit(solution)/shard_map/ppermute | solution.py:800
  117.0 8.1 %collective-permute-start.19 = (f32[16,1024]{1,0:T(8,128)}, f32[16,1024]{1,0:T(8,128)S(1)}, u32[]{:S(2)}, u32[]{:S(2)}) collective-permute-start(f32[16,1024]{1,0:T(8,128)} %get-tuple-element.84), channel_id=1, source_target_pairs={{0,24},{8,0},{16,8},{24,16},{1,25},{9,1},{17,9},{25,17},{2,26},{10... | collective-permute-start | bytes 196616 | tf_op jit(solution)/shard_map/ppermute | solution.py:800
  118.5 36.3 %collective-permute-start.30 = (f32[1,1152,128]{2,1,0:T(8,128)}, f32[1,1152,128]{2,1,0:T(8,128)}, u32[]{:S(2)}, u32[]{:S(2)}) collective-permute-start(f32[1,1152,128]{2,1,0:T(8,128)} %get-tuple-element.90.refs_2_), channel_id=1, source_target_pairs={{2,0},{4,2},{1,3},{6,4},{3,5},{5,7},{10,8},{12,10},{9,11},{14,12},... | collective-permute-start | bytes 1769480 | tf_op jit(solution)/shard_map/ppermute | solution.py:792
  126.0 5.3 %collective-permute-start.20 = (f32[16,1024]{1,0:T(8,128)S(1)}, f32[16,1024]{1,0:T(8,128)S(1)}, u32[]{:S(2)}, u32[]{:S(2)}) collective-permute-start(f32[16,1024]{1,0:T(8,128)S(1)} %add_add_fusion.1), channel_id=1, source_target_pairs={{0,1},{1,0},{2,3},{3,2},{4,5},{5,4},{6,7},{7,6},{8,9},{9,8},{10,11... | collective-permute-start | bytes 196616 | tf_op jit(solution)/shard_map/ppermute | solution.py:786
  128.5 4.0 %collective-permute-start.24 = (f32[16,512]{1,0:T(8,128)S(1)}, f32[16,512]{1,0:T(8,128)S(1)}, u32[]{:S(2)}, u32[]{:S(2)}) collective-permute-start(f32[16,512]{1,0:T(8,128)S(1)} %pad_maximum_fusion.1), channel_id=1, source_target_pairs={{0,1},{1,0},{2,3},{3,2},{4,5},{5,4},{6,7},{7,6},{8,9},{9,8},{10,11... | collective-permute-start | bytes 98312 | tf_op jit(solution)/shard_map/ppermute | solution.py:786
  128.6 48.6 %collective-permute-start.27 = (f32[2,576,128]{2,1,0:T(8,128)}, f32[2,576,128]{2,1,0:T(8,128)}, u32[]{:S(2)}, u32[]{:S(2)}) collective-permute-start(f32[2,576,128]{2,1,0:T(8,128)} %get-tuple-element.89.refs_4_), channel_id=1, source_target_pairs={{0,2},{2,4},{3,1},{4,6},{5,3},{7,5},{8,10},{10,12},{11,9},{12,14},... | collective-permute-start | bytes 1769480 | tf_op jit(solution)/shard_map/ppermute | solution.py:789
  131.3 20.3 %copy-start.2 = (f32[16,1024]{1,0:T(8,128)}, f32[16,1024]{1,0:T(8,128)S(1)}, u32[]{:S(2)}) copy-start(f32[16,1024]{1,0:T(8,128)S(1)} %add.49.sum_ref) | copy-start | bytes 196612
  132.5 16.5 %collective-permute-start.25 = (f32[32,1024]{1,0:T(8,128)S(1)}, f32[32,1024]{1,0:T(8,128)S(1)}, u32[]{:S(2)}, u32[]{:S(2)}) collective-permute-start(f32[32,1024]{1,0:T(8,128)S(1)} %maximum_maximum_fusion), channel_id=1, source_target_pairs={{0,2},{1,3},{2,0},{3,1},{4,6},{5,7},{6,4},{7,5},{8,10},{9,11},{10,... | collective-permute-start | bytes 393224 | tf_op jit(solution)/shard_map/ppermute | solution.py:795
  133.3 43.9 %collective-permute-start.28 = (f32[1,576,128]{2,1,0:T(8,128)}, f32[1,576,128]{2,1,0:T(8,128)S(1)}, u32[]{:S(2)}, u32[]{:S(2)}) collective-permute-start(f32[1,576,128]{2,1,0:T(8,128)} %get-tuple-element.87.refs_2_), channel_id=1, source_target_pairs={{2,0},{4,2},{1,3},{6,4},{3,5},{5,7},{10,8},{12,10},{9,11},{14,12},... | collective-permute-start | bytes 884744 | tf_op jit(solution)/shard_map/ppermute | solution.py:792
  149.0 2.6 copy-start.7
  149.0 2.6 collective-permute-start.26
  177.1 61.9 %collective-permute-start.40 = (f32[4,576,128]{2,1,0:T(8,128)}, f32[4,576,128]{2,1,0:T(8,128)}, u32[]{:S(2)}, u32[]{:S(2)}) collective-permute-start(f32[4,576,128]{2,1,0:T(8,128)} %get-tuple-element.107), channel_id=1, source_target_pairs={{0,1},{1,0},{2,3},{3,2},{4,5},{5,4},{6,7},{7,6},{8,9},{9,8},{10,11... | collective-permute-start | bytes 3538952 | tf_op jit(solution)/shard_map/ppermute | solution.py:786
  177.2 0.7 copy-start
  190.3 4.0 %collective-permute-start.32 = (f32[16,1024]{1,0:T(8,128)}, f32[16,1024]{1,0:T(8,128)S(1)}, u32[]{:S(2)}, u32[]{:S(2)}) collective-permute-start(f32[16,1024]{1,0:T(8,128)} %get-tuple-element.102), channel_id=1, source_target_pairs={{0,8},{8,16},{16,24},{24,0},{1,9},{9,17},{17,25},{25,1},{2,10},{10... | collective-permute-start | bytes 196616 | tf_op jit(solution)/shard_map/ppermute | solution.py:800
  190.3 5.2 %collective-permute-start.33 = (f32[16,1024]{1,0:T(8,128)}, f32[16,1024]{1,0:T(8,128)S(1)}, u32[]{:S(2)}, u32[]{:S(2)}) collective-permute-start(f32[16,1024]{1,0:T(8,128)} %get-tuple-element.102), channel_id=1, source_target_pairs={{0,16},{8,24},{16,0},{24,8},{1,17},{9,25},{17,1},{25,9},{2,18},{10... | collective-permute-start | bytes 196616 | tf_op jit(solution)/shard_map/ppermute | solution.py:800
  190.8 4.6 %collective-permute-start.34 = (f32[16,1024]{1,0:T(8,128)}, f32[16,1024]{1,0:T(8,128)S(1)}, u32[]{:S(2)}, u32[]{:S(2)}) collective-permute-start(f32[16,1024]{1,0:T(8,128)} %get-tuple-element.102), channel_id=1, source_target_pairs={{0,24},{8,0},{16,8},{24,16},{1,25},{9,1},{17,9},{25,17},{2,26},{10... | collective-permute-start | bytes 196616 | tf_op jit(solution)/shard_map/ppermute | solution.py:800
  196.3 9.8 %collective-permute-start.35 = (f32[16,1024]{1,0:T(8,128)S(1)}, f32[16,1024]{1,0:T(8,128)S(1)}, u32[]{:S(2)}, u32[]{:S(2)}) collective-permute-start(f32[16,1024]{1,0:T(8,128)S(1)} %add_add_fusion), channel_id=1, source_target_pairs={{0,1},{1,0},{2,3},{3,2},{4,5},{5,4},{6,7},{7,6},{8,9},{9,8},{10,11... | collective-permute-start | bytes 196616 | tf_op jit(solution)/shard_map/ppermute | solution.py:786
  206.1 32.9 %copy-start.6 = (f32[16,1024]{1,0:T(8,128)}, f32[16,1024]{1,0:T(8,128)S(1)}, u32[]{:S(2)}) copy-start(f32[16,1024]{1,0:T(8,128)S(1)} %add.56.sum_ref) | copy-start | bytes 196612
  206.1 5.7 %collective-permute-start.36 = (f32[16,1024]{1,0:T(8,128)S(1)}, f32[16,1024]{1,0:T(8,128)S(1)}, u32[]{:S(2)}, u32[]{:S(2)}) collective-permute-start(f32[16,1024]{1,0:T(8,128)S(1)} %add.56.sum_ref), channel_id=1, source_target_pairs={{0,2},{1,3},{2,0},{3,1},{4,6},{5,7},{6,4},{7,5},{8,10},{9,11},{10,... | collective-permute-start | bytes 196616 | tf_op jit(solution)/shard_map/ppermute | solution.py:795
  209.1 4.0 %collective-permute-start.37 = (f32[16,1024]{1,0:T(8,128)S(1)}, f32[16,1024]{1,0:T(8,128)S(1)}, u32[]{:S(2)}, u32[]{:S(2)}) collective-permute-start(f32[16,1024]{1,0:T(8,128)S(1)} %add.56.sum_ref), channel_id=1, source_target_pairs={{2,4},{3,5},{4,2},{5,3},{10,12},{11,13},{12,10},{13,11},{18,20},{1... | collective-permute-start | bytes 196616 | tf_op jit(solution)/shard_map/ppermute | solution.py:795
  209.7 16.5 %collective-permute-start.39 = (f32[4,288,128]{2,1,0:T(8,128)}, f32[4,288,128]{2,1,0:T(8,128)S(1)}, u32[]{:S(2)}, u32[]{:S(2)}) collective-permute-start(f32[4,288,128]{2,1,0:T(8,128)} %get-tuple-element.106), channel_id=1, source_target_pairs={{0,1},{1,0},{2,3},{3,2},{4,5},{5,4},{6,7},{7,6},{8,9},{9,8},{10,11... | collective-permute-start | bytes 1769480 | tf_op jit(solution)/shard_map/ppermute | solution.py:786
  211.1 27.9 %collective-permute-start.38 = (f32[4,288,128]{2,1,0:T(8,128)}, f32[4,288,128]{2,1,0:T(8,128)}, u32[]{:S(2)}, u32[]{:S(2)}) collective-permute-start(f32[4,288,128]{2,1,0:T(8,128)} %get-tuple-element.105), channel_id=1, source_target_pairs={{0,1},{1,0},{2,3},{3,2},{4,5},{5,4},{6,7},{7,6},{8,9},{9,8},{10,11... | collective-permute-start | bytes 1769480 | tf_op jit(solution)/shard_map/ppermute | solution.py:786
  211.8 27.1 %copy-start.9 = (f32[16,1024]{1,0:T(8,128)}, f32[16,1024]{1,0:T(8,128)S(1)}, u32[]{:S(2)}) copy-start(f32[16,1024]{1,0:T(8,128)S(1)} %collective-permute-done.36.sum_a_ref) | copy-start | bytes 196612
  211.8 39.8 %collective-permute-start.41 = (f32[4,288,128]{2,1,0:T(8,128)}, f32[4,288,128]{2,1,0:T(8,128)}, u32[]{:S(2)}, u32[]{:S(2)}) collective-permute-start(f32[4,288,128]{2,1,0:T(8,128)} %get-tuple-element.109), channel_id=1, source_target_pairs={{0,1},{1,0},{2,3},{3,2},{4,5},{5,4},{6,7},{7,6},{8,9},{9,8},{10,11... | collective-permute-start | bytes 1769480 | tf_op jit(solution)/shard_map/ppermute | solution.py:786
  213.1 25.9 %copy-start.10 = (f32[16,1024]{1,0:T(8,128)}, f32[16,1024]{1,0:T(8,128)S(1)}, u32[]{:S(2)}) copy-start(f32[16,1024]{1,0:T(8,128)S(1)} %collective-permute-done.37.sum_b_ref) | copy-start | bytes 196612
  213.1 48.4 %collective-permute-start.31 = (f32[4,288,128]{2,1,0:T(8,128)}, f32[4,288,128]{2,1,0:T(8,128)}, u32[]{:S(2)}, u32[]{:S(2)}) collective-permute-start(f32[4,288,128]{2,1,0:T(8,128)} %get-tuple-element.101), channel_id=1, source_target_pairs={{0,1},{1,0},{2,3},{3,2},{4,5},{5,4},{6,7},{7,6},{8,9},{9,8},{10,11... | collective-permute-start | bytes 1769480 | tf_op jit(solution)/shard_map/ppermute | solution.py:786
  226.2 12.8 %copy-start.1 = (f32[4,288,128]{2,1,0:T(8,128)}, f32[4,288,128]{2,1,0:T(8,128)S(1)}, u32[]{:S(2)}) copy-start(f32[4,288,128]{2,1,0:T(8,128)S(1)} %collective-permute-done.39.refs_2_) | copy-start | bytes 1769476
